TPU v7x, 128 devices: a whole 4x4x4 slice. The times are simulated.
128 devices in a mesh: layer: 16 (over x, z_lo, core), dp: 8 (over z_hi, y).
Axes of the slice: x: 4, y: 4, z: 4 (z_hi: 2, z_lo: 2; z = z_hi * 2 + z_lo), core: 2. Of those that a mesh axis runs over, the one named last changes fastest.
Arguments:
- resid_in: bfloat16 [4, 256, 3584], P(None, 'dp'), may hold values from -6 to 6
- resid_out: bfloat16 [4, 256, 3584], P(None, ('layer', 'dp')), may hold values from -4 to 4
- encoder: bfloat16 [2, 3584, 32768], P(None, None, ('layer', 'dp')), may hold values from -0.09375 to 0.09375
- enc_bias: float32 [2, 32768], P(None, ('layer', 'dp')), may hold values from -3 to 3
- decoder: bfloat16 [5, 32768, 3584], P(None, ('layer', 'dp')), may hold values from -0.046875 to 0.046875
- active: int32 [4, 8, 32], replicated, may hold values from 0 to 127, all different within a row
Outputs:
- recon: bfloat16 [4, 256, 3584], P(None, ('layer', 'dp'))
- grad_encoder: bfloat16 [2, 3584, 32768], P(None, None, ('layer', 'dp'))
- grad_bias: float32 [2, 32768], P(None, ('layer', 'dp'))
- grad_decoder: bfloat16 [5, 32768, 3584], P(None, ('layer', 'dp'))
Inputs may be any that keep to these rules, and one draw needn't show every extreme that they name: Row active[l, n] lists 32 different blocks of layer l, active for tokens n * 32 to (n + 1) * 32 - 1; every block number appears in at least one row of active, counting the rows of all layers together (not necessarily in a row of every layer).
All inputs are finite; a program needn't handle non-finite values.
Results may differ from a plain program's by a relative error of at most 0.0059.
Values may be sent and summed in bfloat16 or wider, within the bound.
No kernel may reach another device: no remote copies, remote signals or barrier semaphores. Data moves between devices by JAX's collectives and lax.ppermute only.
A program may use at most 128 MiB of HBM per device.

v0:
```python
import jax
import jax.numpy as jnp
from jax import lax
from jax.sharding import PartitionSpec as P

FEAT = 16384
BLOCK = 128
LAYERS = 4


def per_device(resid_in, resid_out, encoder, enc_bias, decoder, active):
    tok_dev = resid_in.shape[1]
    model_width = resid_in.shape[2]
    local_width = encoder.shape[2]
    dp_count = lax.axis_size("dp")
    device_rank = lax.axis_index("layer") * dp_count + lax.axis_index("dp")
    first_column = device_rank * local_width
    fold_side = first_column // FEAT
    offset = first_column - fold_side * FEAT
    layer_ids = [fold_side, LAYERS - 1 - fold_side]
    picked = jnp.stack(
        [lax.dynamic_index_in_dim(resid_in, layer_id, 0, keepdims=False) for layer_id in layer_ids]
    )
    inputs = lax.all_gather(picked, "dp", axis=1, tiled=True)
    tokens = inputs.shape[1]
    pre_acts = (
        jnp.einsum("krd,kdf->krf", inputs, encoder, preferred_element_type=jnp.float32)
        + enc_bias[:, None, :]
    )
    block_ids = offset // BLOCK + jnp.arange(local_width // BLOCK, dtype=jnp.int32)
    block_masks = []
    for layer_id in layer_ids:
        listed = lax.dynamic_index_in_dim(active, layer_id, 0, keepdims=False)
        listed_hit = jnp.any(listed[:, :, None] == block_ids[None, None, :], axis=1).astype(
            jnp.float32
        )
        spread = jnp.broadcast_to(
            listed_hit[:, None, :, None], (listed_hit.shape[0], tok_dev, listed_hit.shape[1], BLOCK)
        )
        block_masks.append(spread.reshape(tokens, local_width))
    block_keep = jnp.stack(block_masks)
    positive = jnp.maximum(pre_acts, 0.0)
    feature_codes = (block_keep * positive * positive).astype(jnp.bfloat16)
    pair_table = []
    for pair_slot in range(decoder.shape[0]):
        second = pair_slot >= LAYERS - fold_side
        pair_table.append(
            (second.astype(jnp.int32), jnp.where(second, pair_slot - 1, fold_side + pair_slot))
        )
    decoded = jnp.zeros((LAYERS, tokens, model_width), jnp.float32)
    for pair_slot in range(decoder.shape[0]):
        source_slot, target_layer = pair_table[pair_slot]
        source_codes = lax.dynamic_index_in_dim(feature_codes, source_slot, 0, keepdims=False)
        decoded_part = jnp.dot(source_codes, decoder[pair_slot], preferred_element_type=jnp.float32)
        current = lax.dynamic_index_in_dim(decoded, target_layer, 0, keepdims=False)
        decoded = lax.dynamic_update_index_in_dim(decoded, current + decoded_part, target_layer, 0)
    summed = lax.psum_scatter(decoded, ("layer", "dp"), scatter_dimension=1, tiled=True)
    recon = summed.astype(jnp.bfloat16)
    own_errors = (summed - resid_out.astype(jnp.float32)).astype(jnp.bfloat16)
    errors_all = lax.all_gather(own_errors, ("layer", "dp"), axis=1, tiled=True)
    grad_parts = []
    back_codes = jnp.zeros((2, tokens, local_width), jnp.float32)
    for pair_slot in range(decoder.shape[0]):
        source_slot, target_layer = pair_table[pair_slot]
        source_codes = lax.dynamic_index_in_dim(feature_codes, source_slot, 0, keepdims=False)
        target_errors = lax.dynamic_index_in_dim(errors_all, target_layer, 0, keepdims=False)
        grad_parts.append(
            lax.dot_general(
                source_codes,
                target_errors,
                (((0,), (0,)), ((), ())),
                preferred_element_type=jnp.float32,
            ).astype(jnp.bfloat16)
        )
        pulled = lax.dot_general(
            target_errors,
            decoder[pair_slot],
            (((1,), (1,)), ((), ())),
            preferred_element_type=jnp.float32,
        )
        current = lax.dynamic_index_in_dim(back_codes, source_slot, 0, keepdims=False)
        back_codes = lax.dynamic_update_index_in_dim(back_codes, current + pulled, source_slot, 0)
    grad_decoder = jnp.stack(grad_parts)
    back_pre = (back_codes * block_keep * (2.0 * positive)).astype(jnp.bfloat16)
    grad_encoder = jnp.einsum(
        "krd,krf->kdf", inputs, back_pre, preferred_element_type=jnp.float32
    ).astype(jnp.bfloat16)
    grad_bias = jnp.sum(back_pre.astype(jnp.float32), axis=1)
    return (recon, grad_encoder, grad_bias, grad_decoder)


def solution(mesh):
    in_specs = (
        P(None, "dp", None),
        P(None, ("layer", "dp"), None),
        P(None, None, ("layer", "dp")),
        P(None, ("layer", "dp")),
        P(None, ("layer", "dp"), None),
        P(),
    )
    out_specs = (
        P(None, ("layer", "dp"), None),
        P(None, None, ("layer", "dp")),
        P(None, ("layer", "dp")),
        P(None, ("layer", "dp"), None),
    )
    return jax.shard_map(
        per_device, mesh=mesh, in_specs=in_specs, out_specs=out_specs, check_vma=False
    )
```

profile of v0, /device:TPU:1, one launch (start us, length us, event | category | flops | bytes accessed | tf_op | source)
XLA Modules:
  0.0 637.3 jit_solution(12686391225563851226)
XLA Ops:
  7.2 0.0 all-gather.3.cloned.1.call-start
  7.2 1.1 constant_dynamic-slice_fusion.14
  8.3 0.8 pad_maximum_fusion
  9.1 0.0 all-gather.3.cloned.1.call-update
  9.2 0.0 all-reduce.3.cloned.1.call-start
  9.3 0.7 fusion.118
  10.0 0.2 compare_reduce_fusion
  10.2 0.1 copy.25
  10.3 0.1 broadcast_in_dim.53
  10.5 0.2 stack_reshape.6
  10.7 0.1 copy.26
  10.8 0.1 broadcast_in_dim.54
  10.9 0.2 stack_reshape.7
  11.2 69.9 %all-gather.3.cloned.1.call-done = bf16[2,256,3584]{2,1,0:T(8,128)(2,1)} async-done(((bf16[2,32,3584]{2,1,0:T(8,128)(2,1)}), bf16[2,256,3584]{2,1,0:T(8,128)(2,1)}) %all-gather.3.cloned.1.call-update) | async-done | bytes 3670032 | tf_op jit(solution)/shard_map/all_gather | solution.py:24
  81.2 4.4 fusion.87
  85.6 1.8 broadcast_in_dim.52
  87.5 0.6 fusion.8
  88.1 0.3 constant_dynamic-slice_fusion.12
  88.4 0.7 fusion.1
  89.1 0.3 constant_dynamic-slice_fusion.11
  89.4 0.7 fusion.3
  90.1 0.3 constant_dynamic-slice_fusion.10
  90.3 0.7 fusion.5
  91.0 0.3 constant_dynamic-slice_fusion.9
  91.3 0.7 fusion.7
  92.0 10.9 %copy.27 = f32[4,256,3584]{2,0,1:T(4,128)} copy(f32[4,256,3584]{2,1,0:T(8,128)S(1)} %fusion.7) | data formatting | bytes 29360128 | tf_op jit(solution)/shard_map/jit(dynamic_update_index_in_dim)/dynamic_update_slice | solution.py:56
  102.9 0.0 all-reduce.3.cloned.1.call-update
  102.9 0.2 all-gather.5.cloned.1.call-start
  103.2 171.2 %all-reduce.3.cloned.1.call-done = f32[4,256,3584]{2,0,1:T(4,128)} async-done(((f32[4,256,3584]{2,0,1:T(4,128)}), f32[4,256,3584]{2,0,1:T(4,128)}) %all-reduce.3.cloned.1.call-update) | async-done | bytes 14680080
  274.4 1.6 subtract_convert_fusion
  276.0 0.0 all-gather.5.cloned.1.call-update
  276.0 0.9 dynamic-slice_convert_fusion
  276.9 0.7 copy.34
  277.6 308.9 %all-gather.5.cloned.1.call-done = bf16[4,256,3584]{2,0,1:T(4,128)(2,1)} async-done(((bf16[4,2,3584]{2,0,1:T(4,128)(2,1)}), bf16[4,256,3584]{2,0,1:T(4,128)(2,1)}) %all-gather.5.cloned.1.call-update) | async-done | bytes 7340048 | tf_op jit(solution)/shard_map/all_gather | solution.py:60
  586.5 24.0 %constant_dynamic-slice_fusion = (bf16[1,256,3584]{2,0,1:T(2,128)(2,1)S(1)}, bf16[1,256,3584]{2,0,1:T(2,128)(2,1)S(1)}, bf16[1,256,3584]{2,0,1:T(2,128)(2,1)S(1)...) fusion(bf16[4,256,3584]{2,0,1:T(4,128)(2,1)} %all-gather.5.cloned.1.call-done, s32[]{:T(128)S(6)} %select_n.112, ...), kind=kLoop, calls=%fused_computation.105 | loop fusion | bytes 18350100 | tf_op jit(solution)/shard_map/jit(dynamic_index_in_dim)/dynamic_slice | solution.py:66
  610.5 0.7 fusion.10
  611.2 2.2 fusion.84
  613.4 2.2 fusion.78
  615.6 2.2 fusion.72
  617.9 2.2 fusion.66
  620.1 0.7 fusion.12
  620.8 0.7 fusion.14
  621.4 0.7 fusion.16
  622.1 2.2 fusion.60
  624.3 0.7 fusion.18
  625.0 0.7 convert_reduce_fusion
  625.7 1.6 copy-done
  627.3 3.4 convolution_convert_fusion
  (24 shorter events, 0.2 us)
Async XLA Ops:
  7.2 74.0 %copy-start.2 = (f32[2,256]{1,0:T(2,128)S(1)}, f32[2,256]{1,0:T(2,128)}, u32[]{:S(2)}) copy-start(f32[2,256]{1,0:T(2,128)} %param.9) | copy-start | bytes 6148
  7.2 74.0 %all-gather.3.cloned.1.call-start = ((), (), s32[]{:S(2)}) async-start(), calls=%async_computation | async-start | bytes 4128768 | tf_op jit(solution)/shard_map/all_gather | solution.py:24
  9.2 265.2 %all-reduce.3.cloned.1.call-start = ((), (), s32[]{:S(2)}) async-start(), calls=%async_computation.2 | async-start | bytes 29360128
  81.2 6.3 slice-start
  81.2 6.3 slice-start.1
  85.6 1.9 slice-start.2
  102.9 171.5 %copy-start.1 = (bf16[4,2,3584]{2,1,0:T(2,128)(2,1)S(1)}, bf16[4,2,3584]{2,1,0:T(2,128)(2,1)}, u32[]{:S(2)}) copy-start(bf16[4,2,3584]{2,1,0:T(2,128)(2,1)} %param.7) | copy-start | bytes 172036
  102.9 483.5 %all-gather.5.cloned.1.call-start = ((), (), s32[]{:S(2)}) async-start(), calls=%async_computation.1 | async-start | bytes 7397376 | tf_op jit(solution)/shard_map/all_gather | solution.py:60
  624.3 3.0 copy-start
  625.0 5.8 copy-start.3
Sparse Core Ops, SparseCore 0:
  10.8 70.2 all-gather.2
  103.1 171.3 all-reduce.2
  276.8 309.6 all-gather.4
where the time goes:
time: 638 us; the launch traced here: 637 us
  waiting for transfers between devices  550 us (86%)
  local copies, waits for them, and re-layouts  43.8 us (7%)
  matrix products  25.5 us (4%)
  between operations  14.2 us (2%)
    all_gather x1, waiting for transfers between devices, per_device(): errors_all = lax.all_gather(own_errors, ('layer', 'dp'), axis=1, tiled=True)  309 us
    unnamed x4, waiting for transfers between devices  171 us
    all_gather x1, waiting for transfers between devices, per_device(): inputs = lax.all_gather(picked, 'dp', axis=1, tiled=True)  69.9 us
    dynamic_slice x1, local copies, waits for them, and re-layouts, per_device(): lax.dynamic_index_in_dim(errors_all, target_layer, 0, keepdims=False)  24 us
  transfers between devices with their start and end apart: 3, of which 3 were waited for; matrix products, arithmetic and copies ran while one was open for 1% of the time, Pallas kernels for 0%

commit v1 on v0

v1 whole, which is shorter than its diff:
```python
import functools

import jax
import jax.numpy as jnp
from jax import lax
from jax.experimental import pallas as pl
from jax.experimental.pallas import tpu as pltpu
from jax.sharding import Mesh
from jax.sharding import PartitionSpec as P

FEAT = 16384
BLOCK = 128
LAYERS = 4
D = 3584
W = 256
HALF = 128
TILES = 8
HROW = 16
PAIRS = 5
GRID_AXES = ("y", "x", "zl", "zh")
DP = ("zh", "y")
ALL = ("x", "zl", "core", "zh", "y")
BF = jnp.bfloat16
F32 = jnp.float32
SWAP = [(0, 1), (1, 0)]

SLOT = ((0, 0, 0, 0, 1), (0, 0, 0, 1, 1))
TARGET = ((0, 1, 2, 3, 3), (1, 2, 3, 2, 3))
FIRST = (((0, 1), (1, 1), (2, 1), (3, 1)), ((0, 0), (0, 1), (1, 1), (2, 1)))
SECOND = (((4, 0), (4, 0), (4, 0), (4, 1)), ((3, 0), (3, 0), (3, 1), (4, 1)))


def _tables(side):
    rows = []
    for s in range(2):
        rows.append(
            [p for p, _ in FIRST[s]]
            + [v for _, v in FIRST[s]]
            + [p for p, _ in SECOND[s]]
            + [v for _, v in SECOND[s]]
            + list(SLOT[s])
            + list(TARGET[s])
        )
    return jnp.where(side == 0, jnp.array(rows[0], jnp.int32), jnp.array(rows[1], jnp.int32))


T_FIRST, T_FV, T_SECOND, T_SV, T_SLOT, T_TARGET = 0, 4, 8, 12, 16, 21


def _rows(ref):
    v = ref[...]
    return v.reshape(TILES * HROW, v.shape[-1])


def _encode_kernel(own_ref, oth_ref, enc_ref, bias_ref, keep_ref, codes_ref, slope_ref, acc_ref):
    c = pl.program_id(1)
    x = jnp.concatenate([_rows(own_ref), _rows(oth_ref)], axis=0)
    part = jnp.dot(x, enc_ref[0], preferred_element_type=F32)

    @pl.when(c == 0)
    def _():
        acc_ref[...] = part

    @pl.when(c > 0)
    def _():
        acc_ref[...] += part

    @pl.when(c == pl.num_programs(1) - 1)
    def _():
        positive = jnp.maximum(acc_ref[...] + bias_ref[0], 0.0)
        keep = jnp.broadcast_to(keep_ref[0][:, None, :], (TILES, HROW, W)).reshape(HALF, W)
        keep = jnp.concatenate([keep, keep], axis=0)
        kept = keep * positive
        codes_ref[0] = (kept * positive).astype(BF)
        slope_ref[0] = 2.0 * kept


def _encode(own, oth, encoder, bias, keep):
    chunk = 896
    xspec = pl.BlockSpec((TILES, None, HROW, chunk), lambda k, c: (0, k, 0, c))
    return pl.pallas_call(
        _encode_kernel,
        grid=(2, D // chunk),
        in_specs=[
            xspec,
            xspec,
            pl.BlockSpec((1, chunk, W), lambda k, c: (k, c, 0)),
            pl.BlockSpec((1, 1, W), lambda k, c: (k, 0, 0)),
            pl.BlockSpec((1, TILES, W), lambda k, c: (k, 0, 0)),
        ],
        out_specs=[
            pl.BlockSpec((1, 2 * HALF, W), lambda k, c: (k, 0, 0)),
            pl.BlockSpec((1, 2 * HALF, W), lambda k, c: (k, 0, 0)),
        ],
        out_shape=[
            jax.ShapeDtypeStruct((2, 2 * HALF, W), BF),
            jax.ShapeDtypeStruct((2, 2 * HALF, W), F32),
        ],
        scratch_shapes=[pltpu.VMEM((2 * HALF, W), F32)],
        compiler_params=pltpu.CompilerParams(vmem_limit_bytes=16 << 20),
        cost_estimate=pl.CostEstimate(
            flops=2 * 2 * 256 * D * W, bytes_accessed=2 * D * W * 2 + 2 * 256 * D * 2, transcendentals=0
        ),
        name="encode",
    )(own, oth, encoder, bias[:, None, :], keep)


def _decode_kernel(tab_ref, codes_ref, first_ref, second_ref, own_ref, oth_ref, acc_ref):
    t = pl.program_id(1)
    has_first = tab_ref[T_FV + t] > 0
    has_second = tab_ref[T_SV + t] > 0

    @pl.when(has_first)
    def _():
        acc_ref[...] = jnp.dot(codes_ref[0], first_ref[0], preferred_element_type=F32)

    @pl.when(jnp.logical_not(has_first))
    def _():
        acc_ref[...] = jnp.zeros_like(acc_ref)

    @pl.when(has_second)
    def _():
        acc_ref[...] += jnp.dot(codes_ref[1], second_ref[0], preferred_element_type=F32)

    own_ref[0] = acc_ref[:HALF]
    oth_ref[0] = acc_ref[HALF:].astype(BF)


def _decode(tables, codes, decoder):
    chunk = 1792
    out = pl.BlockSpec((1, HALF, chunk), lambda c, t, tab: (t, 0, c))
    return pl.pallas_call(
        _decode_kernel,
        grid_spec=pltpu.PrefetchScalarGridSpec(
            num_scalar_prefetch=1,
            grid=(D // chunk, LAYERS),
            in_specs=[
                pl.BlockSpec((2, 2 * HALF, W), lambda c, t, tab: (0, 0, 0)),
                pl.BlockSpec((1, W, chunk), lambda c, t, tab: (tab[T_FIRST + t], 0, c)),
                pl.BlockSpec((1, W, chunk), lambda c, t, tab: (tab[T_SECOND + t], 0, c)),
            ],
            out_specs=[out, out],
            scratch_shapes=[pltpu.VMEM((2 * HALF, chunk), F32)],
        ),
        out_shape=[
            jax.ShapeDtypeStruct((LAYERS, HALF, D), F32),
            jax.ShapeDtypeStruct((LAYERS, HALF, D), BF),
        ],
        compiler_params=pltpu.CompilerParams(vmem_limit_bytes=20 << 20),
        cost_estimate=pl.CostEstimate(
            flops=2 * PAIRS * 256 * D * W, bytes_accessed=PAIRS * W * D * 2 + 4 * 128 * D * 6, transcendentals=0
        ),
        name="decode",
    )(tables, codes, decoder, decoder)


def _backward_kernel(
    tab_ref, codes_ref, slope_ref, own_ref, oth_ref, dec_ref, grad_ref, pre_ref, bias_ref, back_ref
):
    p = pl.program_id(0)
    c = pl.program_id(1)
    slot = tab_ref[T_SLOT + p]

    @pl.when(jnp.logical_and(p == 0, c == 0))
    def _():
        back_ref[...] = jnp.zeros_like(back_ref)

    err = jnp.concatenate([own_ref[0], oth_ref[0]], axis=0)
    grad_ref[0] = lax.dot_general(
        codes_ref[slot], err, (((0,), (0,)), ((), ())), preferred_element_type=F32
    ).astype(BF)
    back_ref[slot] += lax.dot_general(
        err, dec_ref[0], (((1,), (1,)), ((), ())), preferred_element_type=F32
    )

    @pl.when(jnp.logical_and(p == pl.num_programs(0) - 1, c == pl.num_programs(1) - 1))
    def _():
        for k in range(2):
            pre = (back_ref[k] * slope_ref[k]).astype(BF)
            pre_ref[k] = pre
            bias_ref[k] = jnp.sum(pre.astype(F32), axis=0, keepdims=True)


def _backward(tables, codes, slope, own, oth, decoder):
    chunk = 1792
    whole = lambda p, c, tab: (0, 0, 0)
    err = pl.BlockSpec((1, HALF, chunk), lambda p, c, tab: (tab[T_TARGET + p], 0, c))
    return pl.pallas_call(
        _backward_kernel,
        grid_spec=pltpu.PrefetchScalarGridSpec(
            num_scalar_prefetch=1,
            grid=(PAIRS, D // chunk),
            in_specs=[
                pl.BlockSpec((2, 2 * HALF, W), whole),
                pl.BlockSpec((2, 2 * HALF, W), whole),
                err,
                err,
                pl.BlockSpec((1, W, chunk), lambda p, c, tab: (p, 0, c)),
            ],
            out_specs=[
                pl.BlockSpec((1, W, chunk), lambda p, c, tab: (p, 0, c)),
                pl.BlockSpec((2, 2 * HALF, W), whole),
                pl.BlockSpec((2, 1, W), whole),
            ],
            scratch_shapes=[pltpu.VMEM((2, 2 * HALF, W), F32)],
        ),
        out_shape=[
            jax.ShapeDtypeStruct((PAIRS, W, D), BF),
            jax.ShapeDtypeStruct((2, 2 * HALF, W), BF),
            jax.ShapeDtypeStruct((2, 1, W), F32),
        ],
        compiler_params=pltpu.CompilerParams(vmem_limit_bytes=20 << 20),
        cost_estimate=pl.CostEstimate(
            flops=4 * PAIRS * 256 * D * W, bytes_accessed=2 * PAIRS * W * D * 2 + 4 * 256 * D * 2, transcendentals=0
        ),
        name="backward",
    )(tables, codes, slope, own, oth, decoder)


def _grad_encoder_kernel(own_ref, oth_ref, pre_ref, out_ref):
    x = jnp.concatenate([_rows(own_ref), _rows(oth_ref)], axis=0)
    out_ref[0] = lax.dot_general(
        x, pre_ref[0], (((0,), (0,)), ((), ())), preferred_element_type=F32
    ).astype(BF)


def _grad_encoder(own, oth, pre):
    chunk = 896
    xspec = pl.BlockSpec((TILES, None, HROW, chunk), lambda k, c: (0, k, 0, c))
    return pl.pallas_call(
        _grad_encoder_kernel,
        grid=(2, D // chunk),
        in_specs=[xspec, xspec, pl.BlockSpec((1, 2 * HALF, W), lambda k, c: (k, 0, 0))],
        out_specs=pl.BlockSpec((1, chunk, W), lambda k, c: (k, c, 0)),
        out_shape=jax.ShapeDtypeStruct((2, D, W), BF),
        compiler_params=pltpu.CompilerParams(vmem_limit_bytes=16 << 20),
        cost_estimate=pl.CostEstimate(
            flops=2 * 2 * 256 * D * W, bytes_accessed=2 * D * W * 2 + 2 * 256 * D * 2, transcendentals=0
        ),
        name="grad_encoder",
    )(own, oth, pre)


def per_device(resid_in, resid_out, encoder, enc_bias, decoder, active):
    x, zl, core = lax.axis_index("x"), lax.axis_index("zl"), lax.axis_index("core")
    zh, y = lax.axis_index("zh"), lax.axis_index("y")
    rank = (((x * 2 + zl) * 2 + core) * 2 + zh) * 4 + y
    side = x // 2
    tables = _tables(side)
    mine = jnp.stack(
        [
            lax.dynamic_slice(resid_in, (layer, core * HROW, 0), (1, HROW, D))[0]
            for layer in (side, LAYERS - 1 - side)
        ]
    )
    own = lax.all_to_all(jnp.broadcast_to(mine[None], (TILES, 2, HROW, D)), DP, 0, 0)
    oth = lax.ppermute(own, "core", SWAP)
    block_ids = (rank * W - side * FEAT) // BLOCK + jnp.arange(W // BLOCK, dtype=jnp.int32)
    listed = jnp.where(side == 0, active[jnp.array([0, 3])], active[jnp.array([1, 2])])
    hit = jnp.any(listed[:, :, :, None] == block_ids, axis=2).astype(F32)
    keep = jnp.repeat(hit, BLOCK, axis=2)
    codes, slope = _encode(own, oth, encoder, enc_bias, keep)
    part_own, part_oth = _decode(tables, codes, decoder)
    part = (part_own + lax.ppermute(part_oth, "core", SWAP).astype(F32)).astype(BF)
    pieces = lax.all_to_all(part.reshape(64, 8, D), GRID_AXES, 0, 0)
    summed = jnp.sum(pieces.astype(F32), axis=0)
    target = lax.all_to_all(resid_out, "y", 0, 0).reshape(8, D)
    errors = (summed - target.astype(F32)).astype(BF)
    recon = lax.all_to_all(summed.astype(BF).reshape(4, 2, D), "y", 0, 0)
    err_own = lax.all_to_all(jnp.broadcast_to(errors[None], (64, 8, D)), GRID_AXES, 0, 0)
    err_own = err_own.reshape(LAYERS, HALF, D)
    err_oth = lax.ppermute(err_own, "core", SWAP)
    grad_decoder, pre, grad_bias = _backward(tables, codes, slope, err_own, err_oth, decoder)
    grad_encoder = _grad_encoder(own, oth, pre)
    return recon, grad_encoder, grad_bias[:, 0, :], grad_decoder


def solution(mesh):
    fine = Mesh(mesh.devices.reshape(4, 2, 2, 2, 4), ALL)
    in_specs = (
        P(None, DP, None),
        P(None, ALL, None),
        P(None, None, ALL),
        P(None, ALL),
        P(None, ALL, None),
        P(),
    )
    out_specs = (P(None, ALL, None), P(None, None, ALL), P(None, ALL), P(None, ALL, None))
    return jax.shard_map(
        per_device, mesh=fine, in_specs=in_specs, out_specs=out_specs, check_vma=False
    )
```

time: 638 us -> 221 us (0.35)
  waiting for transfers between devices: 550 us -> 51.2 us
  blocking collectives: 0 us -> 92.3 us
  Pallas kernels: 0 us -> 34 us
  local copies, waits for them, and re-layouts: 43.8 us -> 16.1 us
  matrix products: 25.5 us -> 0 us
  starting transfers between devices: 0.3 us -> 15.5 us
  between operations: 14.2 us -> 0.88 us
  other arithmetic: 3.33 us -> 9.88 us
    all_gather x2 -> x0, waiting for transfers between devices: 379 us -> none  [the longest x1 309 us: per_device(): errors_all = lax.all_gather(own_errors, ('layer', 'dp'), axis=1, tiled=True)]
    unnamed x4 -> x0, waiting for transfers between devices: 171 us -> none
    all_to_all x0 -> x3, blocking collectives: none -> 92.3 us  [the longest x1 52.6 us: per_device(): lax.all_to_all(jnp.broadcast_to(errors[None], (64, 8, D)), GRID_AXES, 0, 0)]
    all_to_all x0 -> x2, waiting for transfers between devices: none -> 46.1 us  [the longest x1 46.1 us: per_device(): pieces = lax.all_to_all(part.reshape(64, 8, D), GRID_AXES, 0, 0)]
    pallas_call x0 -> x4, Pallas kernels: none -> 34 us  [the longest x1 13.2 us: _backward(): pl.pallas_call(_backward_kernel, grid_spec=pltpu.PrefetchScalarGridSpec(n...]
    dot_general x17 -> x0, matrix products: 25.5 us -> none  [the longest x5 10.9 us: per_device(): lax.dot_general(target_errors, decoder[pair_slot], (((1,), (1,)), ((), ()...]
    dynamic_slice x10 -> x1, local copies, waits for them, and re-layouts: 26.2 us -> 0.98 us  [per_device(): lax.dynamic_slice(resid_in, (layer, core * HROW, 0), (1, HROW, D))[0]]
    unnamed x16 -> x22, local copies, waits for them, and re-layouts: 2.31 us -> 13.5 us
  transfers between devices with their start and end apart: 3 -> 5, of which waited for: 3 -> 3; matrix products, arithmetic and copies ran while one was open for 1% -> 4% of each run, Pallas kernels for 0% -> 0%
where the time goes in v1:
time: 221 us; the launch traced here: 220 us
  blocking collectives  92.3 us (42%)
  waiting for transfers between devices  51.2 us (23%)
  Pallas kernels  34 us (15%)
  local copies, waits for them, and re-layouts  16.1 us (7%)
  starting transfers between devices  15.5 us (7%)
  other arithmetic  9.88 us (4%)
    all_to_all x1, blocking collectives, per_device(): lax.all_to_all(jnp.broadcast_to(errors[None], (64, 8, D)), GRID_AXES, 0, 0)  52.6 us
    all_to_all x1, waiting for transfers between devices, per_device(): pieces = lax.all_to_all(part.reshape(64, 8, D), GRID_AXES, 0, 0)  46.1 us
    all_to_all x1, blocking collectives, per_device(): lax.all_to_all(jnp.broadcast_to(mine[None], (TILES, 2, HROW, D)), DP, 0, 0)  32.9 us
    unnamed x22, local copies, waits for them, and re-layouts  13.5 us
    pallas_call x1, Pallas kernels, _backward(): pl.pallas_call(_backward_kernel, grid_spec=pltpu.PrefetchScalarGridSpec(n...  13.2 us
    pallas_call x1, Pallas kernels, _decode(): pl.pallas_call(_decode_kernel, grid_spec=pltpu.PrefetchScalarGridSpec(num...  7.88 us
    pallas_call x1, Pallas kernels, _grad_encoder(): pl.pallas_call(_grad_encoder_kernel, grid=(2, D // chunk), in_specs=[xspe...  7.12 us
    all_to_all x1, starting transfers between devices, per_device(): pieces = lax.all_to_all(part.reshape(64, 8, D), GRID_AXES, 0, 0)  7.09 us
  transfers between devices with their start and end apart: 5, of which 3 were waited for; matrix products, arithmetic and copies ran while one was open for 4% of the time, Pallas kernels for 0%

profile of v1, /device:TPU:1, one launch (start us, length us, event | category | flops | bytes accessed | tf_op | source)
XLA Modules:
  0.0 219.9 jit_solution(3876856450938248548)
XLA Ops:
  0.6 0.0 copy-start
  0.6 0.0 copy-start.7
  0.7 0.0 copy-start.8
  0.7 0.0 copy-start.9
  0.7 0.0 copy-start.6
  0.7 1.0 constant_dynamic-slice_fusion.1
  1.7 0.2 broadcast_in_dim.12
  1.9 32.9 %all_to_all.25.own_ref = bf16[8,2,16,3584]{3,2,1,0:T(8,128)(2,1)S(1)} all-to-all(bf16[8,2,16,3584]{3,2,1,0:T(8,128)(2,1)S(1)} %broadcast_in_dim.12), channel_id=1, replica_groups=mesh['x'=4,'zl'=2,'core'=2,'zh'=2,'y'=4] {'zh','y'}, dimensions={0} | all-to-all | bytes 3670016 | tf_op jit(solution)/shard_map/all_to_all | solution.py:256
  34.8 1.8 collective-permute-start
  36.6 0.0 copy-done.6
  36.7 0.0 copy-done
  36.7 0.5 gather_fusion
  37.2 0.0 copy-done.7
  37.2 0.5 gather_fusion.1
  37.8 0.2 compare_reduce_fusion
  38.1 0.0 copy-done.8
  38.1 0.0 copy-done.9
  38.1 0.1 broadcast_bitcast_fusion.keep_ref
  38.2 2.0 collective-permute-done.oth_ref
  40.2 0.0 copy-start.5
  40.2 2.0 copy-done.5
  42.2 5.8 %encode.1 = (bf16[2,256,256]{2,1,0:T(8,128)(2,1)S(1)}, f32[2,256,256]{2,1,0:T(8,128)S(1)}) custom-call(bf16[8,2,16,3584]{3,2,1,0:T(8,128)(2,1)S(1)} %all_to_all.25.own_ref, bf16[8,2,16,3584]{3,2,1,0:T(8,128)(2,1)} %collective-permute-done.oth_ref, bf16[2,3584,256]{2,1,0:T(8,128)(2,1)S(1)} %copy-done.5, f32[2,1,256]{2,1,0:T(1,128)S(1)} %broadcast_in_dim.13.bias_ref, ...), custom_call_target="tpu_custom_call" | custom-call | flops 939524096 | bytes 7340032 | tf_op jit(solution)/shard_map/encode/pallas_call | solution.py:81
  48.0 0.0 copy-start.2
  48.0 3.6 %copy-done.2 = bf16[5,256,3584]{2,1,0:T(8,128)(2,1)S(1)} copy-done((bf16[5,256,3584]{2,1,0:T(8,128)(2,1)S(1)}, bf16[5,256,3584]{2,1,0:T(8,128)(2,1)}, u32[]{:S(2)}) %copy-start.2) | copy-done | bytes 9175064
  51.6 7.9 %decode.1 = (f32[4,128,3584]{2,1,0:T(8,128)S(1)}, bf16[4,128,3584]{2,1,0:T(8,128)(2,1)}) custom-call(s32[26]{0:T(128)S(1)} %broadcast_select_fusion.1.tab_ref, bf16[2,256,256]{2,1,0:T(8,128)(2,1)S(1)} %get-tuple-element.11.codes_ref, bf16[5,256,3584]{2,1,0:T(8,128)(2,1)S(1)} %copy-done.2, bf16[5,256,3584]{2,1,0:T(8,128)(2,1)S(1)} %copy-done.2), custom_call_target="tpu_custom_call" | custom-call | flops 2348810240 | bytes 20185088 | tf_op jit(solution)/shard_map/decode/pallas_call | solution.py:132
  59.5 0.0 copy-start.4
  59.5 3.0 %copy-done.4 = f32[4,128,3584]{2,1,0:T(8,128)} copy-done((f32[4,128,3584]{2,1,0:T(8,128)}, f32[4,128,3584]{2,1,0:T(8,128)S(1)}, u32[]{:S(2)}) %copy-start.4) | copy-done | bytes 7340056
  62.6 0.4 collective-permute-start.1
  62.9 3.3 %all-to-all-start.3 = ((bf16[4,2,3584]{2,1,0:T(2,128)(2,1)}), bf16[4,2,3584]{2,1,0:T(2,128)(2,1)S(1)}, u32[]{:S(2)}, u32[]{:S(2)}) async-start(bf16[4,2,3584]{2,1,0:T(2,128)(2,1)} %param.11), calls=%async_computation.3 | async-start | bytes 114688 | tf_op jit(solution)/shard_map/all_to_all | solution.py:267
  66.2 3.1 %collective-permute-done.1 = bf16[4,128,3584]{2,1,0:T(8,128)(2,1)} collective-permute-done((bf16[4,128,3584]{2,1,0:T(8,128)(2,1)}, bf16[4,128,3584]{2,1,0:T(8,128)(2,1)}, u32[]{:S(2)}, u32[]{:S(2)}) %collective-permute-start.1) | collective-permute-done | bytes 3670048 | tf_op jit(solution)/shard_map/ppermute | solution.py:264
  69.3 7.0 %add_convert_fusion = bf16[4,128,3584]{2,1,0:T(8,128)(2,1)} fusion(f32[4,128,3584]{2,1,0:T(8,128)} %copy-done.4, bf16[4,128,3584]{2,1,0:T(8,128)(2,1)} %collective-permute-done.1), kind=kLoop, calls=%fused_computation.3 | loop fusion | flops 5505024 | bytes 14680064 | tf_op jit(solution)/shard_map/convert_element_type | solution.py:264
  76.4 0.0 all-to-all-done.3
  76.4 7.1 %all-to-all-start.1 = ((bf16[64,8,3584]{2,1,0:T(8,128)(2,1)}), bf16[64,8,3584]{2,1,0:T(8,128)(2,1)}, u32[]{:S(2)}, u32[]{:S(2)}) async-start(bf16[64,8,3584]{2,1,0:T(8,128)(2,1)} %bitcast.7), calls=%async_computation.1 | async-start | bytes 7340032 | tf_op jit(solution)/shard_map/all_to_all | solution.py:265
  83.5 46.1 %all-to-all-done.1 = bf16[64,8,3584]{2,1,0:T(8,128)(2,1)} async-done(((bf16[64,8,3584]{2,1,0:T(8,128)(2,1)}), bf16[64,8,3584]{2,1,0:T(8,128)(2,1)}, u32[]{:S(2)}, u32[]{:S(2)}) %all-to-all-start.1) | async-done | bytes 3670048 | tf_op jit(solution)/shard_map/all_to_all | solution.py:265
  129.5 2.6 %convert_reduce_fusion = f32[8,3584]{1,0:T(8,128)S(1)} fusion(bf16[64,8,3584]{2,1,0:T(8,128)(2,1)} %all-to-all-done.1), kind=kLoop, calls=%fused_computation.2 | loop fusion | flops 3641344 | bytes 3784704 | tf_op jit(solution)/shard_map/reduce_sum | solution.py:266
  132.1 0.2 broadcast_in_dim.31
  132.4 52.6 %all_to_all.26 = bf16[64,8,3584]{2,1,0:T(8,128)(2,1)} all-to-all(bf16[64,8,3584]{2,1,0:T(8,128)(2,1)S(1)} %broadcast_in_dim.31), channel_id=1, replica_groups=mesh['x'=4,'zl'=2,'core'=2,'zh'=2,'y'=4] {'y','x','zl','zh'}, dimensions={0} | all-to-all | bytes 7340032 | tf_op jit(solution)/shard_map/all_to_all | solution.py:270
  185.0 3.0 %collective-permute-start.2 = (bf16[4,128,3584]{2,1,0:T(8,128)(2,1)}, bf16[4,128,3584]{2,1,0:T(8,128)(2,1)}, u32[]{:S(2)}, u32[]{:S(2)}) collective-permute-start(bf16[4,128,3584]{2,1,0:T(8,128)(2,1)} %bitcast.2.own_ref), channel_id=1, source_target_pairs={{0,8},{8,0},{1,9},{9,1},{2,10},{10,2},{3,11},{11,3},{4,12},{12,4},... | collective-permute-start | bytes 11010056 | tf_op jit(solution)/shard_map/ppermute | solution.py:272
  188.0 6.8 %all_to_all.27 = bf16[4,2,3584]{2,1,0:T(2,128)(2,1)S(1)} all-to-all(bf16[4,2,3584]{2,1,0:T(2,128)(2,1)S(1)} %convert_element_type.41), channel_id=1, replica_groups=mesh['x'=4,'zl'=2,'core'=2,'zh'=2,'y'=4] {'y'}, dimensions={0} | all-to-all | bytes 114688 | tf_op jit(solution)/shard_map/all_to_all | solution.py:269
  194.8 0.0 collective-permute-done.2.oth_ref
  194.8 0.0 copy-start.3
  194.8 3.6 %copy-done.3 = bf16[5,256,3584]{2,1,0:T(8,128)(2,1)S(1)} copy-done((bf16[5,256,3584]{2,1,0:T(8,128)(2,1)S(1)}, bf16[5,256,3584]{2,1,0:T(8,128)(2,1)}, u32[]{:S(2)}) %copy-start.3) | copy-done | bytes 9175064
  198.4 13.2 %backward.1 = (bf16[5,256,3584]{2,1,0:T(8,128)(2,1)}, bf16[2,256,256]{2,1,0:T(8,128)(2,1)S(1)}, f32[2,1,256]{2,1,0:T(1,128)S(1)}) custom-call(s32[26]{0:T(128)S(1)} %broadcast_select_fusion.1.tab_ref, bf16[2,256,256]{2,1,0:T(8,128)(2,1)S(1)} %get-tuple-element.11.codes_ref, f32[2,256,256]{2,1,0:T(8,128)S(1)} %get-tuple-element.14.slope_ref, ...), custom_call_target="tpu_custom_call" | custom-call | flops 4697620480 | bytes 25690112 | tf_op jit(solution)/shard_map/backward/pallas_call | solution.py:188
  211.6 0.6 copy.16
  212.2 0.0 copy-start.1
  212.2 7.1 %grad_encoder.1 = bf16[2,3584,256]{2,1,0:T(8,128)(2,1)} custom-call(bf16[8,2,16,3584]{3,2,1,0:T(8,128)(2,1)S(1)} %all_to_all.25.own_ref, bf16[8,2,16,3584]{3,2,1,0:T(8,128)(2,1)} %collective-permute-done.oth_ref, bf16[2,256,256]{2,1,0:T(8,128)(2,1)S(1)} %get-tuple-element.15.pre_ref), custom_call_target="tpu_custom_call" | custom-call | flops 939524096 | bytes 7340032 | tf_op jit(solution)/shard_map/grad_encoder/pallas_call | solution.py:230
  219.3 0.6 copy.18
  219.9 0.0 copy-done.1
  (12 shorter events, 0.1 us)
Async XLA Ops:
  0.6 36.0 %copy-start = (s32[4,8,32]{2,1,0:T(8,128)S(1)}, s32[4,8,32]{2,1,0:T(8,128)}, u32[]{:S(2)}) copy-start(s32[4,8,32]{2,1,0:T(8,128)} %param.15) | copy-start | bytes 12292
  0.6 36.6 %copy-start.7 = (s32[2]{0:T(128)S(1)}, s32[2]{0:T(128)}, u32[]{:S(2)}) copy-start(s32[2]{0:T(128)} %constant.84) | copy-start | bytes 28
  0.7 37.4 %copy-start.8 = (s32[26]{0:T(128)S(1)}, s32[26]{0:T(128)}, u32[]{:S(2)}) copy-start(s32[26]{0:T(128)} %constant.76.clone) | copy-start | bytes 316
  0.7 37.4 %copy-start.9 = (s32[26]{0:T(128)S(1)}, s32[26]{0:T(128)}, u32[]{:S(2)}) copy-start(s32[26]{0:T(128)} %constant.75.clone) | copy-start | bytes 316
  0.7 35.9 %copy-start.6 = (f32[2,256]{1,0:T(2,128)S(1)}, f32[2,256]{1,0:T(2,128)}, u32[]{:S(2)}) copy-start(f32[2,256]{1,0:T(2,128)} %param.13) | copy-start | bytes 6148
  34.8 5.4 %collective-permute-start = (bf16[8,2,16,3584]{3,2,1,0:T(8,128)(2,1)S(1)}, bf16[8,2,16,3584]{3,2,1,0:T(8,128)(2,1)}, u32[]{:S(2)}, u32[]{:S(2)}) collective-permute-start(bf16[8,2,16,3584]{3,2,1,0:T(8,128)(2,1)S(1)} %all_to_all.25.own_ref), channel_id=1, source_target_pairs={{0,8},{8,0},{1,9},{9,1},{2,10},{10,2},{3,11},{11,3},{4,12},{12,4},... | collective-permute-start | bytes 5505032 | tf_op jit(solution)/shard_map/ppermute | solution.py:257
  40.2 2.0 copy-start.5
  48.0 3.6 %copy-start.2 = (bf16[5,256,3584]{2,1,0:T(8,128)(2,1)S(1)}, bf16[5,256,3584]{2,1,0:T(8,128)(2,1)}, u32[]{:S(2)}) copy-start(bf16[5,256,3584]{2,1,0:T(8,128)(2,1)} %dec_ref.1) | copy-start | bytes 27525124
  59.5 3.0 %copy-start.4 = (f32[4,128,3584]{2,1,0:T(8,128)}, f32[4,128,3584]{2,1,0:T(8,128)S(1)}, u32[]{:S(2)}) copy-start(f32[4,128,3584]{2,1,0:T(8,128)S(1)} %get-tuple-element.12) | copy-start | bytes 22020100
  62.6 6.8 %collective-permute-start.1 = (bf16[4,128,3584]{2,1,0:T(8,128)(2,1)}, bf16[4,128,3584]{2,1,0:T(8,128)(2,1)}, u32[]{:S(2)}, u32[]{:S(2)}) collective-permute-start(bf16[4,128,3584]{2,1,0:T(8,128)(2,1)} %get-tuple-element.13), channel_id=1, source_target_pairs={{0,8},{8,0},{1,9},{9,1},{2,10},{10,2},{3,11},{11,3},{4,12},{12,4},... | collective-permute-start | bytes 11010056 | tf_op jit(solution)/shard_map/ppermute | solution.py:264
  62.9 13.4 %all-to-all-start.3 = ((bf16[4,2,3584]{2,1,0:T(2,128)(2,1)}), bf16[4,2,3584]{2,1,0:T(2,128)(2,1)S(1)}, u32[]{:S(2)}, u32[]{:S(2)}) async-start(bf16[4,2,3584]{2,1,0:T(2,128)(2,1)} %param.11), calls=%async_computation.3 | async-start | bytes 114688 | tf_op jit(solution)/shard_map/all_to_all | solution.py:267
  76.4 53.2 %all-to-all-start.1 = ((bf16[64,8,3584]{2,1,0:T(8,128)(2,1)}), bf16[64,8,3584]{2,1,0:T(8,128)(2,1)}, u32[]{:S(2)}, u32[]{:S(2)}) async-start(bf16[64,8,3584]{2,1,0:T(8,128)(2,1)} %bitcast.7), calls=%async_computation.1 | async-start | bytes 7340032 | tf_op jit(solution)/shard_map/all_to_all | solution.py:265
  185.0 9.8 %collective-permute-start.2 = (bf16[4,128,3584]{2,1,0:T(8,128)(2,1)}, bf16[4,128,3584]{2,1,0:T(8,128)(2,1)}, u32[]{:S(2)}, u32[]{:S(2)}) collective-permute-start(bf16[4,128,3584]{2,1,0:T(8,128)(2,1)} %bitcast.2.own_ref), channel_id=1, source_target_pairs={{0,8},{8,0},{1,9},{9,1},{2,10},{10,2},{3,11},{11,3},{4,12},{12,4},... | collective-permute-start | bytes 11010056 | tf_op jit(solution)/shard_map/ppermute | solution.py:272
  194.8 3.6 %copy-start.3 = (bf16[5,256,3584]{2,1,0:T(8,128)(2,1)S(1)}, bf16[5,256,3584]{2,1,0:T(8,128)(2,1)}, u32[]{:S(2)}) copy-start(bf16[5,256,3584]{2,1,0:T(8,128)(2,1)} %dec_ref.1) | copy-start | bytes 27525124
  212.2 7.7 %copy-start.1 = (s32[4,8,32]{2,1,0:T(8,128)S(1)}, s32[4,8,32]{2,1,0:T(8,128)}, u32[]{:S(2)}) copy-start(s32[4,8,32]{2,1,0:T(8,128)} %param.15) | copy-start | bytes 12292

commit v2 on v1

v2 whole, which is shorter than its diff:
```python
import jax
import jax.numpy as jnp
from jax import lax
from jax.experimental import pallas as pl
from jax.experimental.pallas import tpu as pltpu
from jax.sharding import Mesh
from jax.sharding import PartitionSpec as P

FEAT = 16384
BLOCK = 128
LAYERS = 4
D = 3584
W = 256
HALF = 128
TILES = 8
HROW = 16
PAIRS = 5
GRID_AXES = ("y", "x", "zl", "zh")
DP = ("zh", "y")
ALL = ("x", "zl", "core", "zh", "y")
BF = jnp.bfloat16
F32 = jnp.float32
SWAP = [(0, 1), (1, 0)]

SLOT = ((0, 0, 0, 0, 1), (0, 0, 0, 1, 1))
TARGET = ((0, 1, 2, 3, 3), (1, 2, 3, 2, 3))
FIRST = (((0, 1), (1, 1), (2, 1), (3, 1)), ((0, 0), (0, 1), (1, 1), (2, 1)))
SECOND = (((4, 0), (4, 0), (4, 0), (4, 1)), ((3, 0), (3, 0), (3, 1), (4, 1)))


def _tables(side):
    rows = []
    for s in range(2):
        rows.append(
            [p for p, _ in FIRST[s]]
            + [v for _, v in FIRST[s]]
            + [p for p, _ in SECOND[s]]
            + [v for _, v in SECOND[s]]
            + list(SLOT[s])
            + list(TARGET[s])
        )
    return jnp.where(side == 0, jnp.array(rows[0], jnp.int32), jnp.array(rows[1], jnp.int32))


T_FIRST, T_FV, T_SECOND, T_SV, T_SLOT, T_TARGET = 0, 4, 8, 12, 16, 21


def _tokens(own_ref, oth_ref, k):
    own = own_ref[:, k].reshape(HALF, D)
    oth = oth_ref[:, k].reshape(HALF, D)
    return own, oth


VMEM = pltpu.MemorySpace.VMEM
WHOLE = pl.BlockSpec(memory_space=VMEM)
CHUNK = 512


def _encode_kernel(own_ref, oth_ref, enc_ref, bias_ref, keep_ref, codes_ref, turned_ref, slope_ref):
    k = pl.program_id(0)
    x = jnp.concatenate(_tokens(own_ref, oth_ref, k), axis=0)
    pre = jnp.dot(x, enc_ref[0], preferred_element_type=F32) + bias_ref[0]
    positive = jnp.maximum(pre, 0.0)
    keep = jnp.broadcast_to(keep_ref[0][:, None, :], (TILES, HROW, W)).reshape(HALF, W)
    keep = jnp.concatenate([keep, keep], axis=0)
    kept = keep * positive
    codes = kept * positive
    codes_ref[0] = codes.astype(BF)
    turned_ref[0] = codes.T.astype(BF)
    slope_ref[0] = 2.0 * kept


def _encode(own, oth, encoder, bias, keep):
    out = pl.BlockSpec((1, 2 * HALF, W), lambda k: (k, 0, 0))
    return pl.pallas_call(
        _encode_kernel,
        grid=(2,),
        in_specs=[
            WHOLE,
            WHOLE,
            pl.BlockSpec((1, D, W), lambda k: (k, 0, 0)),
            pl.BlockSpec((1, 1, W), lambda k: (k, 0, 0)),
            pl.BlockSpec((1, TILES, W), lambda k: (k, 0, 0)),
        ],
        out_specs=[out, out, out],
        out_shape=[
            jax.ShapeDtypeStruct((2, 2 * HALF, W), BF),
            jax.ShapeDtypeStruct((2, W, 2 * HALF), BF),
            jax.ShapeDtypeStruct((2, 2 * HALF, W), F32),
        ],
        compiler_params=pltpu.CompilerParams(vmem_limit_bytes=24 << 20),
        cost_estimate=pl.CostEstimate(
            flops=2 * 2 * 256 * D * W, bytes_accessed=2 * D * W * 2, transcendentals=0
        ),
        name="encode",
    )(own, oth, encoder, bias[:, None, :], keep)


def _decode_kernel(tab_ref, codes_ref, first_ref, second_ref, own_ref, oth_ref):
    t = pl.program_id(0)
    has_first = tab_ref[T_FV + t] > 0
    has_second = tab_ref[T_SV + t] > 0

    def write(cols, value):
        own_ref[0, :, cols] = value[:HALF].astype(BF)
        oth_ref[0, :, cols] = value[HALF:].astype(BF)

    def sweep(part):
        for c in range(D // CHUNK):
            cols = slice(c * CHUNK, (c + 1) * CHUNK)
            write(cols, part(cols))

    def first(cols):
        return jnp.dot(codes_ref[0], first_ref[0, :, cols], preferred_element_type=F32)

    def both(cols):
        return first(cols) + jnp.dot(codes_ref[1], second_ref[0, :, cols], preferred_element_type=F32)

    @pl.when(has_second)
    def _():
        sweep(both)

    @pl.when(jnp.logical_and(has_first, jnp.logical_not(has_second)))
    def _():
        sweep(first)

    @pl.when(jnp.logical_not(has_first))
    def _():
        own_ref[...] = jnp.zeros_like(own_ref)
        oth_ref[...] = jnp.zeros_like(oth_ref)


def _decode(tables, codes, decoder):
    out = pl.BlockSpec((1, HALF, D), lambda t, tab: (t, 0, 0))
    return pl.pallas_call(
        _decode_kernel,
        grid_spec=pltpu.PrefetchScalarGridSpec(
            num_scalar_prefetch=1,
            grid=(LAYERS,),
            in_specs=[
                pl.BlockSpec((2, 2 * HALF, W), lambda t, tab: (0, 0, 0)),
                pl.BlockSpec((1, W, D), lambda t, tab: (tab[T_FIRST + t], 0, 0)),
                pl.BlockSpec((1, W, D), lambda t, tab: (tab[T_SECOND + t], 0, 0)),
            ],
            out_specs=[out, out],
        ),
        out_shape=[
            jax.ShapeDtypeStruct((LAYERS, HALF, D), BF),
            jax.ShapeDtypeStruct((LAYERS, HALF, D), BF),
        ],
        compiler_params=pltpu.CompilerParams(vmem_limit_bytes=24 << 20),
        cost_estimate=pl.CostEstimate(
            flops=2 * PAIRS * 256 * D * W, bytes_accessed=PAIRS * W * D * 2 + 4 * 128 * D * 4, transcendentals=0
        ),
        name="decode",
    )(tables, codes, decoder, decoder)


def _turn_kernel(own_ref, oth_ref, out_ref):
    k = pl.program_id(0)
    own, oth = _tokens(own_ref, oth_ref, k)
    for c in range(D // CHUNK):
        cols = slice(c * CHUNK, (c + 1) * CHUNK)
        out_ref[0, cols, :HALF] = own[:, cols].T
        out_ref[0, cols, HALF:] = oth[:, cols].T


def _turn(own, oth):
    return pl.pallas_call(
        _turn_kernel,
        grid=(2,),
        in_specs=[WHOLE, WHOLE],
        out_specs=pl.BlockSpec((1, D, 2 * HALF), lambda k: (k, 0, 0)),
        out_shape=jax.ShapeDtypeStruct((2, D, 2 * HALF), BF),
        compiler_params=pltpu.CompilerParams(vmem_limit_bytes=20 << 20),
        cost_estimate=pl.CostEstimate(flops=2 * 256 * D * 300, bytes_accessed=4 * 256 * D * 2, transcendentals=0),
        name="turn",
    )(own, oth)


def _backward_kernel(
    tab_ref, turned_ref, slope_ref, own_ref, oth_ref, xt_ref, dec_ref, grad_ref, genc_ref, bias_ref, back_ref, pre_ref
):
    p = pl.program_id(0)

    @pl.when(p == 0)
    def _():
        back_ref[...] = jnp.zeros_like(back_ref)

    @pl.when(p < PAIRS)
    def _():
        pair = jnp.minimum(p, PAIRS - 1)
        slot = tab_ref[T_SLOT + pair]
        target = tab_ref[T_TARGET + pair]
        err = jnp.concatenate([own_ref[target], oth_ref[target]], axis=0)
        back_ref[slot] += lax.dot_general(
            err, dec_ref[0], (((1,), (1,)), ((), ())), preferred_element_type=F32
        )
        turned = turned_ref[slot]
        for c in range(D // CHUNK):
            cols = slice(c * CHUNK, (c + 1) * CHUNK)
            grad_ref[0, :, cols] = jnp.dot(
                turned, err[:, cols], preferred_element_type=F32
            ).astype(BF)

    @pl.when(p == PAIRS)
    def _():
        for k in range(2):
            pre = (back_ref[k] * slope_ref[k]).astype(BF)
            pre_ref[k] = pre
            bias_ref[k] = jnp.sum(pre.astype(F32), axis=0, keepdims=True)

    @pl.when(p >= PAIRS)
    def _():
        k = jnp.maximum(p - PAIRS, 0)
        genc_ref[0] = jnp.dot(xt_ref[0], pre_ref[k], preferred_element_type=F32).astype(BF)


def _backward(tables, turned, slope, own, oth, xt, decoder):
    pair = lambda p, tab: (jnp.minimum(p, PAIRS - 1), 0, 0)
    enc = lambda p, tab: (jnp.maximum(p - PAIRS, 0), 0, 0)
    return pl.pallas_call(
        _backward_kernel,
        grid_spec=pltpu.PrefetchScalarGridSpec(
            num_scalar_prefetch=1,
            grid=(PAIRS + 2,),
            in_specs=[WHOLE, WHOLE, WHOLE, WHOLE, pl.BlockSpec((1, D, 2 * HALF), enc), pl.BlockSpec((1, W, D), pair)],
            out_specs=[
                pl.BlockSpec((1, W, D), pair),
                pl.BlockSpec((1, D, W), enc),
                pl.BlockSpec((2, 1, W), lambda p, tab: (0, 0, 0)),
            ],
            scratch_shapes=[pltpu.VMEM((2, 2 * HALF, W), F32), pltpu.VMEM((2, 2 * HALF, W), BF)],
        ),
        out_shape=[
            jax.ShapeDtypeStruct((PAIRS, W, D), BF),
            jax.ShapeDtypeStruct((2, D, W), BF),
            jax.ShapeDtypeStruct((2, 1, W), F32),
        ],
        compiler_params=pltpu.CompilerParams(vmem_limit_bytes=32 << 20),
        cost_estimate=pl.CostEstimate(
            flops=4 * PAIRS * 256 * D * W + 4 * 256 * D * W,
            bytes_accessed=2 * PAIRS * W * D * 2 + 2 * D * W * 2,
            transcendentals=0,
        ),
        name="backward",
    )(tables, turned, slope, own, oth, xt, decoder)


def _hbm(x):
    return pltpu.with_memory_space_constraint(x, pltpu.MemorySpace.HBM)


def _vmem(x):
    return pltpu.with_memory_space_constraint(x, VMEM)


def per_device(resid_in, resid_out, encoder, enc_bias, decoder, active):
    x, zl, core = lax.axis_index("x"), lax.axis_index("zl"), lax.axis_index("core")
    zh, y = lax.axis_index("zh"), lax.axis_index("y")
    rank = (((x * 2 + zl) * 2 + core) * 2 + zh) * 4 + y
    side = x // 2
    tables = _tables(side)
    mine = jnp.stack(
        [
            lax.dynamic_slice(resid_in, (layer, core * HROW, 0), (1, HROW, D))[0]
            for layer in (side, LAYERS - 1 - side)
        ]
    )
    own = lax.all_to_all(jnp.broadcast_to(mine[None], (TILES, 2, HROW, D)), DP, 0, 0)
    oth = lax.ppermute(own, "core", SWAP)
    block_ids = (rank * W - side * FEAT) // BLOCK + jnp.arange(W // BLOCK, dtype=jnp.int32)
    listed = jnp.where(side == 0, active[jnp.array([0, 3])], active[jnp.array([1, 2])])
    hit = jnp.any(listed[:, :, :, None] == block_ids, axis=2).astype(F32)
    keep = jnp.repeat(hit, BLOCK, axis=2)
    codes, turned, slope = _encode(own, oth, _hbm(encoder), enc_bias, keep)
    part_own, part_oth = _decode(tables, codes, _hbm(decoder))
    swapped = lax.ppermute(part_oth, "core", SWAP)
    part = (part_own.astype(F32) + swapped.astype(F32)).astype(BF)
    pieces = lax.all_to_all(part.reshape(64, 8, D), GRID_AXES, 0, 0)
    summed = jnp.sum(pieces.astype(F32), axis=0)
    target = lax.all_to_all(resid_out, "y", 0, 0).reshape(8, D)
    errors = (summed - target.astype(F32)).astype(BF)
    xt = _turn(own, oth)
    errors, xt = lax.optimization_barrier((errors, xt))
    recon = lax.all_to_all(summed.astype(BF).reshape(4, 2, D), "y", 0, 0)
    err_own = lax.all_to_all(jnp.broadcast_to(errors[None], (64, 8, D)), GRID_AXES, 0, 0)
    err_own = err_own.reshape(LAYERS, HALF, D)
    err_oth = lax.ppermute(err_own, "core", SWAP)
    grad_decoder, grad_encoder, grad_bias = _backward(
        tables, turned, slope, _vmem(err_own), _vmem(err_oth), _hbm(xt), _hbm(decoder)
    )
    return recon, grad_encoder, grad_bias[:, 0, :], grad_decoder


def solution(mesh):
    fine = Mesh(mesh.devices.reshape(4, 2, 2, 2, 4), ALL)
    in_specs = (
        P(None, DP, None),
        P(None, ALL, None),
        P(None, None, ALL),
        P(None, ALL),
        P(None, ALL, None),
        P(),
    )
    out_specs = (P(None, ALL, None), P(None, None, ALL), P(None, ALL), P(None, ALL, None))
    return jax.shard_map(
        per_device, mesh=fine, in_specs=in_specs, out_specs=out_specs, check_vma=False
    )
```

time: 221 us -> 203 us (0.919)
  local copies, waits for them, and re-layouts: 16.1 us -> 7.47 us
  waiting for transfers between devices: 51.2 us -> 46.8 us
  Pallas kernels: 34 us -> 31 us
    unnamed x22 -> x18, local copies, waits for them, and re-layouts: 13.5 us -> 4.87 us
    pallas_call x2, Pallas kernels: 12.9 us -> 6.1 us  [the longest x1 3.52 us: _encode(): pl.pallas_call(_encode_kernel, grid=(2,), in_specs=[WHOLE, WHOLE, pl.Bloc...]
    all_to_all x1, waiting for transfers between devices: 46.1 us -> 41.7 us  [per_device(): pieces = lax.all_to_all(part.reshape(64, 8, D), GRID_AXES, 0, 0)]
    pallas_call x1, Pallas kernels: 13.2 us -> 16.7 us  [_backward(): pl.pallas_call(_backward_kernel, grid_spec=pltpu.PrefetchScalarGridSpec(n...]
  transfers between devices with their start and end apart: 5 -> 5, of which waited for: 3 -> 3; matrix products, arithmetic and copies ran while one was open for 4% -> 4% of each run, Pallas kernels for 0% -> 1%
where the time goes in v2:
time: 203 us; the launch traced here: 202 us
  blocking collectives  92.3 us (45%)
  waiting for transfers between devices  46.8 us (23%)
  Pallas kernels  31 us (15%)
  starting transfers between devices  14.9 us (7%)
  other arithmetic  8.74 us (4%)
  local copies, waits for them, and re-layouts  7.47 us (4%)
    all_to_all x1, blocking collectives, per_device(): lax.all_to_all(jnp.broadcast_to(errors[None], (64, 8, D)), GRID_AXES, 0, 0)  52.6 us
    all_to_all x1, waiting for transfers between devices, per_device(): pieces = lax.all_to_all(part.reshape(64, 8, D), GRID_AXES, 0, 0)  41.7 us
    all_to_all x1, blocking collectives, per_device(): lax.all_to_all(jnp.broadcast_to(mine[None], (TILES, 2, HROW, D)), DP, 0, 0)  32.9 us
    pallas_call x1, Pallas kernels, _backward(): pl.pallas_call(_backward_kernel, grid_spec=pltpu.PrefetchScalarGridSpec(n...  16.7 us
    pallas_call x1, Pallas kernels, _decode(): pl.pallas_call(_decode_kernel, grid_spec=pltpu.PrefetchScalarGridSpec(num...  8.18 us
    all_to_all x1, blocking collectives, per_device(): recon = lax.all_to_all(summed.astype(BF).reshape(4, 2, D), 'y', 0, 0)  6.8 us
    all_to_all x1, starting transfers between devices, per_device(): pieces = lax.all_to_all(part.reshape(64, 8, D), GRID_AXES, 0, 0)  6.49 us
    convert_element_type x1, other arithmetic, per_device(): part = (part_own.astype(F32) + swapped.astype(F32)).astype(BF)  5.89 us
  transfers between devices with their start and end apart: 5, of which 3 were waited for; matrix products, arithmetic and copies ran while one was open for 4% of the time, Pallas kernels for 1%

profile of v2, /device:TPU:1, one launch (start us, length us, event | category | flops | bytes accessed | tf_op | source)
XLA Modules:
  0.0 202.1 jit_solution(10479442014645487202)
XLA Ops:
  0.6 0.0 copy-start
  0.6 0.0 copy-start.5
  0.7 0.0 copy-start.6
  0.7 0.0 copy-start.7
  0.7 0.0 copy-start.4
  0.7 1.0 constant_dynamic-slice_fusion.1
  1.7 0.2 broadcast_in_dim.12
  1.9 32.9 %all_to_all.25.own_ref = bf16[8,2,16,3584]{3,2,1,0:T(8,128)(2,1)S(1)} all-to-all(bf16[8,2,16,3584]{3,2,1,0:T(8,128)(2,1)S(1)} %broadcast_in_dim.12), channel_id=1, replica_groups=mesh['x'=4,'zl'=2,'core'=2,'zh'=2,'y'=4] {'zh','y'}, dimensions={0} | all-to-all | bytes 3670016 | tf_op jit(solution)/shard_map/all_to_all | solution.py:270
  34.8 1.8 collective-permute-start
  36.6 0.0 copy-done.4
  36.7 0.0 copy-done
  36.7 0.5 gather_fusion
  37.2 0.0 copy-done.5
  37.2 0.5 gather_fusion.1
  37.8 0.2 compare_reduce_fusion
  38.1 0.0 copy-done.6
  38.1 0.0 copy-done.7
  38.1 0.1 broadcast_bitcast_fusion.keep_ref
  38.2 2.0 collective-permute-done.oth_ref
  40.2 3.5 %encode.1 = (bf16[2,256,256]{2,1,0:T(8,128)(2,1)S(1)}, bf16[2,256,256]{2,1,0:T(8,128)(2,1)S(1)}, f32[2,256,256]{2,1,0:T(8,128)S(1)}) custom-call(bf16[8,2,16,3584]{3,2,1,0:T(8,128)(2,1)S(1)} %all_to_all.25.own_ref, bf16[8,2,16,3584]{3,2,1,0:T(8,128)(2,1)} %collective-permute-done.oth_ref, bf16[2,3584,256]{2,1,0:T(8,128)(2,1)} %enc_ref.1, ...), custom_call_target="tpu_custom_call" | custom-call | flops 939524096 | bytes 3670016 | tf_op jit(solution)/shard_map/encode/pallas_call | solution.py:75
  43.7 8.2 %decode.1 = (bf16[4,128,3584]{2,1,0:T(8,128)(2,1)S(1)}, bf16[4,128,3584]{2,1,0:T(8,128)(2,1)}) custom-call(s32[26]{0:T(128)S(1)} %broadcast_select_fusion.1.tab_ref, bf16[2,256,256]{2,1,0:T(8,128)(2,1)S(1)} %get-tuple-element.14.codes_ref, bf16[5,256,3584]{2,1,0:T(8,128)(2,1)} %dec_ref.1, bf16[5,256,3584]{2,1,0:T(8,128)(2,1)} %dec_ref.1), custom_call_target="tpu_custom_call" | custom-call | flops 2348810240 | bytes 16515072 | tf_op jit(solution)/shard_map/decode/pallas_call | solution.py:135
  51.9 0.0 copy-start.3
  51.9 1.8 copy-done.3
  53.7 0.4 collective-permute-start.1
  54.1 3.3 %all-to-all-start.3 = ((bf16[4,2,3584]{2,1,0:T(2,128)(2,1)}), bf16[4,2,3584]{2,1,0:T(2,128)(2,1)S(1)}, u32[]{:S(2)}, u32[]{:S(2)}) async-start(bf16[4,2,3584]{2,1,0:T(2,128)(2,1)} %param.11), calls=%async_computation.3 | async-start | bytes 114688 | tf_op jit(solution)/shard_map/all_to_all | solution.py:282
  57.4 3.1 %collective-permute-done.1 = bf16[4,128,3584]{2,1,0:T(8,128)(2,1)} collective-permute-done((bf16[4,128,3584]{2,1,0:T(8,128)(2,1)}, bf16[4,128,3584]{2,1,0:T(8,128)(2,1)}, u32[]{:S(2)}, u32[]{:S(2)}) %collective-permute-start.1) | collective-permute-done | bytes 3670048 | tf_op jit(solution)/shard_map/ppermute | solution.py:278
  60.5 5.9 %add_convert_fusion = bf16[4,128,3584]{2,1,0:T(8,128)(2,1)} fusion(bf16[4,128,3584]{2,1,0:T(8,128)(2,1)} %collective-permute-done.1, bf16[4,128,3584]{2,1,0:T(8,128)(2,1)} %copy-done.3), kind=kLoop, calls=%fused_computation.3 | loop fusion | flops 7340032 | bytes 11010048 | tf_op jit(solution)/shard_map/convert_element_type | solution.py:279
  66.4 0.0 all-to-all-done.3
  66.4 6.5 %all-to-all-start.1 = ((bf16[64,8,3584]{2,1,0:T(8,128)(2,1)}), bf16[64,8,3584]{2,1,0:T(8,128)(2,1)}, u32[]{:S(2)}, u32[]{:S(2)}) async-start(bf16[64,8,3584]{2,1,0:T(8,128)(2,1)} %bitcast.7), calls=%async_computation.1 | async-start | bytes 7340032 | tf_op jit(solution)/shard_map/all_to_all | solution.py:280
  72.9 2.6 %turn.1.xt_ref = bf16[2,3584,256]{2,1,0:T(8,128)(2,1)S(1)} custom-call(bf16[8,2,16,3584]{3,2,1,0:T(8,128)(2,1)S(1)} %all_to_all.25.own_ref, bf16[8,2,16,3584]{3,2,1,0:T(8,128)(2,1)} %collective-permute-done.oth_ref), custom_call_target="tpu_custom_call" | custom-call | flops 550502400 | bytes 7340032 | tf_op jit(solution)/shard_map/turn/pallas_call | solution.py:169
  75.5 0.0 copy-start.2
  75.5 1.8 copy-done.2
  77.3 41.7 %all-to-all-done.1 = bf16[64,8,3584]{2,1,0:T(8,128)(2,1)} async-done(((bf16[64,8,3584]{2,1,0:T(8,128)(2,1)}), bf16[64,8,3584]{2,1,0:T(8,128)(2,1)}, u32[]{:S(2)}, u32[]{:S(2)}) %all-to-all-start.1) | async-done | bytes 3670048 | tf_op jit(solution)/shard_map/all_to_all | solution.py:280
  119.0 2.6 %convert_reduce_fusion = f32[8,3584]{1,0:T(8,128)S(1)} fusion(bf16[64,8,3584]{2,1,0:T(8,128)(2,1)} %all-to-all-done.1), kind=kLoop, calls=%fused_computation.2 | loop fusion | flops 3641344 | bytes 3784704 | tf_op jit(solution)/shard_map/reduce_sum | solution.py:281
  121.5 0.2 broadcast_in_dim.31
  121.8 52.6 %all_to_all.26 = bf16[64,8,3584]{2,1,0:T(8,128)(2,1)} all-to-all(bf16[64,8,3584]{2,1,0:T(8,128)(2,1)S(1)} %broadcast_in_dim.31), channel_id=1, replica_groups=mesh['x'=4,'zl'=2,'core'=2,'zh'=2,'y'=4] {'y','x','zl','zh'}, dimensions={0} | all-to-all | bytes 7340032 | tf_op jit(solution)/shard_map/all_to_all | solution.py:287
  174.4 3.0 %collective-permute-start.2 = (bf16[4,128,3584]{2,1,0:T(8,128)(2,1)}, bf16[4,128,3584]{2,1,0:T(8,128)(2,1)}, u32[]{:S(2)}, u32[]{:S(2)}) collective-permute-start(bf16[4,128,3584]{2,1,0:T(8,128)(2,1)} %bitcast.2.own_ref), channel_id=1, source_target_pairs={{0,8},{8,0},{1,9},{9,1},{2,10},{10,2},{3,11},{11,3},{4,12},{12,4},... | collective-permute-start | bytes 11010056 | tf_op jit(solution)/shard_map/ppermute | solution.py:289
  177.4 6.8 %all_to_all.27 = bf16[4,2,3584]{2,1,0:T(2,128)(2,1)S(1)} all-to-all(bf16[4,2,3584]{2,1,0:T(2,128)(2,1)S(1)} %convert_element_type.37), channel_id=1, replica_groups=mesh['x'=4,'zl'=2,'core'=2,'zh'=2,'y'=4] {'y'}, dimensions={0} | all-to-all | bytes 114688 | tf_op jit(solution)/shard_map/all_to_all | solution.py:286
  184.2 0.0 collective-permute-done.2.oth_ref
  184.2 0.0 copy-start.1
  184.2 16.7 %backward.1 = (bf16[5,256,3584]{2,1,0:T(8,128)(2,1)}, bf16[2,3584,256]{2,1,0:T(8,128)(2,1)}, f32[2,1,256]{2,1,0:T(1,128)S(1)}) custom-call(s32[26]{0:T(128)S(1)} %broadcast_select_fusion.1.tab_ref, bf16[2,256,256]{2,1,0:T(8,128)(2,1)S(1)} %get-tuple-element.17.turned_ref, f32[2,256,256]{2,1,0:T(8,128)S(1)} %get-tuple-element.18.slope_ref, ...), custom_call_target="tpu_custom_call" | custom-call | flops 5637144576 | bytes 22020096 | tf_op jit(solution)/shard_map/backward/pallas_call | solution.py:222
  200.9 0.6 copy.16
  201.5 0.6 copy.18
  202.1 0.0 copy-done.1
  (12 shorter events, 0.1 us)
Async XLA Ops:
  0.6 36.0 %copy-start = (s32[4,8,32]{2,1,0:T(8,128)S(1)}, s32[4,8,32]{2,1,0:T(8,128)}, u32[]{:S(2)}) copy-start(s32[4,8,32]{2,1,0:T(8,128)} %param.15) | copy-start | bytes 12292
  0.6 36.6 %copy-start.5 = (s32[2]{0:T(128)S(1)}, s32[2]{0:T(128)}, u32[]{:S(2)}) copy-start(s32[2]{0:T(128)} %constant.84) | copy-start | bytes 28
  0.7 37.4 %copy-start.6 = (s32[26]{0:T(128)S(1)}, s32[26]{0:T(128)}, u32[]{:S(2)}) copy-start(s32[26]{0:T(128)} %constant.76.clone) | copy-start | bytes 316
  0.7 37.4 %copy-start.7 = (s32[26]{0:T(128)S(1)}, s32[26]{0:T(128)}, u32[]{:S(2)}) copy-start(s32[26]{0:T(128)} %constant.75.clone) | copy-start | bytes 316
  0.7 35.9 %copy-start.4 = (f32[2,256]{1,0:T(2,128)S(1)}, f32[2,256]{1,0:T(2,128)}, u32[]{:S(2)}) copy-start(f32[2,256]{1,0:T(2,128)} %param.13) | copy-start | bytes 6148
  34.8 5.4 %collective-permute-start = (bf16[8,2,16,3584]{3,2,1,0:T(8,128)(2,1)S(1)}, bf16[8,2,16,3584]{3,2,1,0:T(8,128)(2,1)}, u32[]{:S(2)}, u32[]{:S(2)}) collective-permute-start(bf16[8,2,16,3584]{3,2,1,0:T(8,128)(2,1)S(1)} %all_to_all.25.own_ref), channel_id=1, source_target_pairs={{0,8},{8,0},{1,9},{9,1},{2,10},{10,2},{3,11},{11,3},{4,12},{12,4},... | collective-permute-start | bytes 5505032 | tf_op jit(solution)/shard_map/ppermute | solution.py:271
  51.9 1.8 copy-start.3
  53.7 6.8 %collective-permute-start.1 = (bf16[4,128,3584]{2,1,0:T(8,128)(2,1)}, bf16[4,128,3584]{2,1,0:T(8,128)(2,1)}, u32[]{:S(2)}, u32[]{:S(2)}) collective-permute-start(bf16[4,128,3584]{2,1,0:T(8,128)(2,1)} %get-tuple-element.16), channel_id=1, source_target_pairs={{0,8},{8,0},{1,9},{9,1},{2,10},{10,2},{3,11},{11,3},{4,12},{12,4},... | collective-permute-start | bytes 11010056 | tf_op jit(solution)/shard_map/ppermute | solution.py:278
  54.1 12.3 %all-to-all-start.3 = ((bf16[4,2,3584]{2,1,0:T(2,128)(2,1)}), bf16[4,2,3584]{2,1,0:T(2,128)(2,1)S(1)}, u32[]{:S(2)}, u32[]{:S(2)}) async-start(bf16[4,2,3584]{2,1,0:T(2,128)(2,1)} %param.11), calls=%async_computation.3 | async-start | bytes 114688 | tf_op jit(solution)/shard_map/all_to_all | solution.py:282
  66.4 52.6 %all-to-all-start.1 = ((bf16[64,8,3584]{2,1,0:T(8,128)(2,1)}), bf16[64,8,3584]{2,1,0:T(8,128)(2,1)}, u32[]{:S(2)}, u32[]{:S(2)}) async-start(bf16[64,8,3584]{2,1,0:T(8,128)(2,1)} %bitcast.7), calls=%async_computation.1 | async-start | bytes 7340032 | tf_op jit(solution)/shard_map/all_to_all | solution.py:280
  75.5 1.8 copy-start.2
  174.4 9.8 %collective-permute-start.2 = (bf16[4,128,3584]{2,1,0:T(8,128)(2,1)}, bf16[4,128,3584]{2,1,0:T(8,128)(2,1)}, u32[]{:S(2)}, u32[]{:S(2)}) collective-permute-start(bf16[4,128,3584]{2,1,0:T(8,128)(2,1)} %bitcast.2.own_ref), channel_id=1, source_target_pairs={{0,8},{8,0},{1,9},{9,1},{2,10},{10,2},{3,11},{11,3},{4,12},{12,4},... | collective-permute-start | bytes 11010056 | tf_op jit(solution)/shard_map/ppermute | solution.py:289
  184.2 17.9 %copy-start.1 = (s32[4,8,32]{2,1,0:T(8,128)S(1)}, s32[4,8,32]{2,1,0:T(8,128)}, u32[]{:S(2)}) copy-start(s32[4,8,32]{2,1,0:T(8,128)} %param.15) | copy-start | bytes 12292

commit v3 on v2

v3 whole, which is shorter than its diff:
```python
import jax
import jax.numpy as jnp
from jax import lax
from jax.experimental import pallas as pl
from jax.experimental.pallas import tpu as pltpu
from jax.sharding import Mesh
from jax.sharding import PartitionSpec as P

FEAT = 16384
BLOCK = 128
LAYERS = 4
D = 3584
W = 256
HALF = 128
TILES = 8
HROW = 16
PAIRS = 5
GRID_AXES = ("y", "x", "zl", "zh")
DP = ("zh", "y")
ALL = ("x", "zl", "core", "zh", "y")
BF = jnp.bfloat16
F32 = jnp.float32
SWAP = [(0, 1), (1, 0)]

SLOT = ((0, 0, 0, 0, 1), (0, 0, 0, 1, 1))
TARGET = ((0, 1, 2, 3, 3), (1, 2, 3, 2, 3))
FIRST = (((0, 1), (1, 1), (2, 1), (3, 1)), ((0, 0), (0, 1), (1, 1), (2, 1)))
SECOND = (((4, 0), (4, 0), (4, 0), (4, 1)), ((3, 0), (3, 0), (3, 1), (4, 1)))


def _tables(side):
    rows = []
    for s in range(2):
        rows.append(
            [p for p, _ in FIRST[s]]
            + [v for _, v in FIRST[s]]
            + [p for p, _ in SECOND[s]]
            + [v for _, v in SECOND[s]]
            + list(SLOT[s])
            + list(TARGET[s])
        )
    return jnp.where(side == 0, jnp.array(rows[0], jnp.int32), jnp.array(rows[1], jnp.int32))


T_FIRST, T_FV, T_SECOND, T_SV, T_SLOT, T_TARGET = 0, 4, 8, 12, 16, 21


VMEM = pltpu.MemorySpace.VMEM
HBM = pltpu.MemorySpace.HBM
WHOLE = pl.BlockSpec(memory_space=VMEM)
CHUNK = 512
CHUNKS = [slice(c, c + CHUNK) for c in range(0, D, CHUNK)]


def _hbm(x):
    return pltpu.with_memory_space_constraint(x, HBM)


def _vmem(x):
    return pltpu.with_memory_space_constraint(x, VMEM)


def _params(mib):
    return pltpu.CompilerParams(vmem_limit_bytes=mib << 20)


def _tokens(own_ref, oth_ref, k):
    return own_ref[:, k].reshape(HALF, D), oth_ref[:, k].reshape(HALF, D)


def _forward_kernel(
    tab_ref, own_ref, oth_ref, enc_hbm, dec_hbm, bias_ref, keep_ref,
    part_own_ref, part_oth_ref, turned_ref, slope_ref, dec_ref, enc_ref, codes_ref, enc_sem, dec_sem,
):
    enc_copies = [
        pltpu.make_async_copy(enc_hbm.at[k], enc_ref.at[k], enc_sem.at[k]) for k in range(2)
    ]
    dec_copies = [
        pltpu.make_async_copy(dec_hbm.at[p], dec_ref.at[p], dec_sem.at[p]) for p in range(PAIRS)
    ]
    for copy in enc_copies + dec_copies:
        copy.start()
    for k in range(2):
        x = jnp.concatenate(_tokens(own_ref, oth_ref, k), axis=0)
        enc_copies[k].wait()
        pre = jnp.dot(x, enc_ref[k], preferred_element_type=F32) + bias_ref[k : k + 1]
        positive = jnp.maximum(pre, 0.0)
        keep = jnp.broadcast_to(keep_ref[k][:, None, :], (TILES, HROW, W)).reshape(HALF, W)
        keep = jnp.concatenate([keep, keep], axis=0)
        kept = keep * positive
        codes = kept * positive
        codes_ref[k] = codes.astype(BF)
        turned_ref[k] = codes.T.astype(BF)
        slope_ref[k] = 2.0 * kept

    def sweep(t, part):
        for cols in CHUNKS:
            value = part(cols).astype(BF)
            part_own_ref[t, :, cols] = value[:HALF]
            part_oth_ref[t, :, cols] = value[HALF:]

    needed = ((0,), (1,), (2, 3), (4,))
    for t in range(LAYERS):
        for p in needed[t]:
            dec_copies[p].wait()
        has_first = tab_ref[T_FV + t] > 0
        has_second = tab_ref[T_SV + t] > 0
        one = tab_ref[T_FIRST + t]
        two = tab_ref[T_SECOND + t]

        def first(cols, one=one):
            return jnp.dot(codes_ref[0], dec_ref[one, :, cols], preferred_element_type=F32)

        def both(cols, first=first, two=two):
            return first(cols) + jnp.dot(
                codes_ref[1], dec_ref[two, :, cols], preferred_element_type=F32
            )

        @pl.when(has_second)
        def _():
            sweep(t, both)

        @pl.when(jnp.logical_and(has_first, jnp.logical_not(has_second)))
        def _():
            sweep(t, first)

        @pl.when(jnp.logical_not(has_first))
        def _():
            part_own_ref[t] = jnp.zeros((HALF, D), BF)
            part_oth_ref[t] = jnp.zeros((HALF, D), BF)


def _forward(tables, own, oth, encoder, decoder, bias, keep):
    smem = pl.BlockSpec(memory_space=pltpu.MemorySpace.SMEM)
    hbm = pl.BlockSpec(memory_space=HBM)
    return pl.pallas_call(
        _forward_kernel,
        in_specs=[smem, WHOLE, WHOLE, hbm, hbm, WHOLE, WHOLE],
        out_specs=[WHOLE] * 5,
        out_shape=[
            jax.ShapeDtypeStruct((LAYERS, HALF, D), BF),
            jax.ShapeDtypeStruct((LAYERS, HALF, D), BF),
            jax.ShapeDtypeStruct((2, W, 2 * HALF), BF),
            jax.ShapeDtypeStruct((2, 2 * HALF, W), F32),
            jax.ShapeDtypeStruct((PAIRS, W, D), BF),
        ],
        scratch_shapes=[
            pltpu.VMEM((2, D, W), BF),
            pltpu.VMEM((2, 2 * HALF, W), BF),
            pltpu.SemaphoreType.DMA((2,)),
            pltpu.SemaphoreType.DMA((PAIRS,)),
        ],
        compiler_params=_params(18),
        cost_estimate=pl.CostEstimate(
            flops=2 * (PAIRS + 2) * 256 * D * W,
            bytes_accessed=(2 * D * W + PAIRS * W * D) * 2,
            transcendentals=0,
        ),
        name="forward",
    )(tables, own, oth, encoder, decoder, bias, keep)


def _join_kernel(own_ref, got_ref, out_ref):
    out_ref[...] = (own_ref[...].astype(F32) + got_ref[...].astype(F32)).astype(BF)


def _join(own, got):
    return pl.pallas_call(
        _join_kernel,
        grid=(LAYERS,),
        in_specs=[pl.BlockSpec((1, HALF, D), lambda t: (t, 0, 0))] * 2,
        out_specs=pl.BlockSpec((1, HALF, D), lambda t: (t, 0, 0)),
        out_shape=jax.ShapeDtypeStruct((LAYERS, HALF, D), BF),
        compiler_params=_params(8),
        cost_estimate=pl.CostEstimate(
            flops=4 * HALF * D, bytes_accessed=3 * 4 * HALF * D * 2, transcendentals=0
        ),
        name="join",
    )(own, got)


def _settle_kernel(pieces_ref, target_ref, errors_ref, recon_ref, rows_ref):
    summed = lax.fori_loop(
        0, 64, lambda i, acc: acc + pieces_ref[i].astype(F32), jnp.zeros((8, D), F32), unroll=8
    )
    for j in range(4):
        rows_ref[2 * j : 2 * j + 2] = target_ref[j].astype(F32)
    errors = (summed - rows_ref[...]).astype(BF)
    rows_ref[...] = summed
    for j in range(4):
        recon_ref[j] = rows_ref[2 * j : 2 * j + 2].astype(BF)

    def spread(i, carry):
        errors_ref[i] = errors
        return carry

    lax.fori_loop(0, 64, spread, 0, unroll=8)


def _settle(pieces, target):
    return pl.pallas_call(
        _settle_kernel,
        in_specs=[WHOLE, WHOLE],
        out_specs=[WHOLE, WHOLE],
        out_shape=[
            jax.ShapeDtypeStruct((64, 8, D), BF),
            jax.ShapeDtypeStruct((4, 2, D), BF),
        ],
        scratch_shapes=[pltpu.VMEM((8, D), F32)],
        compiler_params=_params(4),
        cost_estimate=pl.CostEstimate(
            flops=64 * 8 * D, bytes_accessed=2 * 64 * 8 * D * 2, transcendentals=0
        ),
        name="settle",
    )(pieces, target)


def _backward_kernel(
    tab_ref, turned_ref, slope_ref, own_ref, oth_ref, x_own_ref, x_oth_ref, dec_ref, grad_ref, genc_ref, bias_ref, back_ref, pre_ref
):
    p = pl.program_id(0)

    @pl.when(p == 0)
    def _():
        back_ref[...] = jnp.zeros_like(back_ref)

    @pl.when(p < PAIRS)
    def _():
        pair = jnp.minimum(p, PAIRS - 1)
        slot = tab_ref[T_SLOT + pair]
        target = tab_ref[T_TARGET + pair]
        err = jnp.concatenate([own_ref[target], oth_ref[target]], axis=0)
        back_ref[slot] += lax.dot_general(
            err, dec_ref[pair], (((1,), (1,)), ((), ())), preferred_element_type=F32
        )
        turned = turned_ref[slot]
        for cols in CHUNKS:
            err = jnp.concatenate([own_ref[target, :, cols], oth_ref[target, :, cols]], axis=0)
            grad_ref[0, :, cols] = jnp.dot(turned, err, preferred_element_type=F32).astype(BF)

    @pl.when(p == PAIRS)
    def _():
        for k in range(2):
            pre = (back_ref[k] * slope_ref[k]).astype(BF)
            pre_ref[k] = pre
            bias_ref[k : k + 1] = jnp.sum(pre.astype(F32), axis=0, keepdims=True)

    @pl.when(p >= PAIRS)
    def _():
        k = jnp.maximum(p - PAIRS, 0)
        own, oth = _tokens(x_own_ref, x_oth_ref, k)
        for rows in CHUNKS:
            x = jnp.concatenate([own[:, rows], oth[:, rows]], axis=0)
            genc_ref[0, rows] = lax.dot_general(
                x, pre_ref[k], (((0,), (0,)), ((), ())), preferred_element_type=F32
            ).astype(BF)


def _backward(tables, turned, slope, own, oth, x_own, x_oth, decoder):
    pair = lambda p, tab: (jnp.minimum(p, PAIRS - 1), 0, 0)
    enc = lambda p, tab: (jnp.maximum(p - PAIRS, 0), 0, 0)
    return pl.pallas_call(
        _backward_kernel,
        grid_spec=pltpu.PrefetchScalarGridSpec(
            num_scalar_prefetch=1,
            grid=(PAIRS + 2,),
            in_specs=[WHOLE] * 7,
            out_specs=[
                pl.BlockSpec((1, W, D), pair),
                pl.BlockSpec((1, D, W), enc),
                pl.BlockSpec((2, W), lambda p, tab: (0, 0)),
            ],
            scratch_shapes=[pltpu.VMEM((2, 2 * HALF, W), F32), pltpu.VMEM((2, 2 * HALF, W), BF)],
        ),
        out_shape=[
            jax.ShapeDtypeStruct((PAIRS, W, D), BF),
            jax.ShapeDtypeStruct((2, D, W), BF),
            jax.ShapeDtypeStruct((2, W), F32),
        ],
        compiler_params=_params(18),
        cost_estimate=pl.CostEstimate(
            flops=4 * PAIRS * 256 * D * W + 4 * 256 * D * W,
            bytes_accessed=PAIRS * W * D * 2 + 2 * D * W * 2,
            transcendentals=0,
        ),
        name="backward",
    )(tables, turned, slope, own, oth, x_own, x_oth, decoder)


def per_device(resid_in, resid_out, encoder, enc_bias, decoder, active):
    x, zl, core = lax.axis_index("x"), lax.axis_index("zl"), lax.axis_index("core")
    zh, y = lax.axis_index("zh"), lax.axis_index("y")
    rank = (((x * 2 + zl) * 2 + core) * 2 + zh) * 4 + y
    side = x // 2
    tables = _tables(side)
    block_ids = (rank * W - side * FEAT) // BLOCK + jnp.arange(W // BLOCK, dtype=jnp.int32)
    outer = jnp.concatenate([active[:1], active[3:]], axis=0)
    listed = jnp.where(side == 0, outer, active[1:3])
    hit = jnp.any(listed[:, :, :, None] == block_ids, axis=2).astype(F32)
    keep = jnp.repeat(hit, BLOCK, axis=2)
    mine = jnp.stack(
        [
            lax.dynamic_slice(resid_in, (layer, core * HROW, 0), (1, HROW, D))[0]
            for layer in (side, LAYERS - 1 - side)
        ]
    )
    mine, tables, keep = lax.optimization_barrier((mine, tables, keep))
    own = lax.all_to_all(jnp.broadcast_to(mine[None], (TILES, 2, HROW, D)), DP, 0, 0)
    oth = lax.ppermute(own, "core", SWAP)
    part_own, part_oth, turned, slope, dec = _forward(
        tables, own, oth, _hbm(encoder), _hbm(decoder), enc_bias, keep
    )
    swapped = lax.ppermute(part_oth, "core", SWAP)
    resid_out, part_own = lax.optimization_barrier((resid_out, part_own))
    target = lax.all_to_all(resid_out, "y", 0, 0)
    swapped, target = lax.optimization_barrier((swapped, target))
    part = _join(part_own, swapped)
    pieces = lax.all_to_all(part.reshape(64, 8, D), GRID_AXES, 0, 0)
    errors, recon = _settle(pieces, target)
    err_own = lax.all_to_all(errors, GRID_AXES, 0, 0).reshape(LAYERS, HALF, D)
    err_oth = lax.ppermute(err_own, "core", SWAP)
    recon, err_own = lax.optimization_barrier((recon, err_own))
    recon = lax.all_to_all(recon, "y", 0, 0)
    err_oth, recon = lax.optimization_barrier((err_oth, recon))
    grad_decoder, grad_encoder, grad_bias = _backward(
        tables, turned, slope, err_own, err_oth, own, oth, dec
    )
    return recon, grad_encoder, grad_bias, grad_decoder


def solution(mesh):
    fine = Mesh(mesh.devices.reshape(4, 2, 2, 2, 4), ALL)
    in_specs = (
        P(None, DP, None),
        P(None, ALL, None),
        P(None, None, ALL),
        P(None, ALL),
        P(None, ALL, None),
        P(),
    )
    out_specs = (P(None, ALL, None), P(None, None, ALL), P(None, ALL), P(None, ALL, None))
    return jax.shard_map(
        per_device, mesh=fine, in_specs=in_specs, out_specs=out_specs, check_vma=False
    )
```

time: 203 us -> 183 us (0.901)
  blocking collectives: 92.3 us -> 147 us
  waiting for transfers between devices: 46.8 us -> 3.42 us
  Pallas kernels: 31 us -> 21.1 us
  starting transfers between devices: 14.9 us -> 5.72 us
  other arithmetic: 8.74 us -> 1.62 us
  local copies, waits for them, and re-layouts: 7.47 us -> 2.56 us
    all_to_all x2 -> x4, blocking collectives: 59.4 us -> 114 us  [the longest x1 51.3 us: per_device(): pieces = lax.all_to_all(part.reshape(64, 8, D), GRID_AXES, 0, 0)]
    all_to_all x2 -> x0, waiting for transfers between devices: 41.7 us -> none  [the longest x1 41.7 us: per_device(): pieces = lax.all_to_all(part.reshape(64, 8, D), GRID_AXES, 0, 0)]
    all_to_all x2 -> x0, starting transfers between devices: 9.77 us -> none  [the longest x1 6.49 us: per_device(): pieces = lax.all_to_all(part.reshape(64, 8, D), GRID_AXES, 0, 0)]
    pallas_call x1, Pallas kernels: 16.7 us -> 10 us  [_backward(): pl.pallas_call(_backward_kernel, grid_spec=pltpu.PrefetchScalarGridSpec(n...]
    convert_element_type x2 -> x0, other arithmetic: 5.9 us -> none  [the longest x1 5.89 us: per_device(): part = (part_own.astype(F32) + swapped.astype(F32)).astype(BF)]
    unnamed x18 -> x5, local copies, waits for them, and re-layouts: 4.87 us -> 0.63 us
    pallas_call x3, Pallas kernels: 14.3 us -> 11.1 us  [the longest x1 9.29 us: _forward(): pl.pallas_call(_forward_kernel, in_specs=[smem, WHOLE, WHOLE, hbm, hbm, W...]
    ppermute x1, waiting for transfers between devices: 3.09 us -> 0.01 us  [per_device(): swapped = lax.ppermute(part_oth, 'core', SWAP)]
  transfers between devices with their start and end apart: 5 -> 3, of which waited for: 3 -> 1; matrix products, arithmetic and copies ran while one was open for 4% -> 0% of each run, Pallas kernels for 1% -> 0%
where the time goes in v3:
time: 183 us; the launch traced here: 182 us
  blocking collectives  147 us (80%)
  Pallas kernels  21.1 us (12%)
  starting transfers between devices  5.72 us (3%)
  waiting for transfers between devices  3.42 us (2%)
  local copies, waits for them, and re-layouts  2.56 us (1%)
    all_to_all x1, blocking collectives, per_device(): pieces = lax.all_to_all(part.reshape(64, 8, D), GRID_AXES, 0, 0)  51.3 us
    all_to_all x1, blocking collectives, per_device(): err_own = lax.all_to_all(errors, GRID_AXES, 0, 0).reshape(LAYERS, HALF, D)  49.3 us
    all_to_all x1, blocking collectives, per_device(): lax.all_to_all(jnp.broadcast_to(mine[None], (TILES, 2, HROW, D)), DP, 0, 0)  32.9 us
    pallas_call x1, Pallas kernels, _backward(): pl.pallas_call(_backward_kernel, grid_spec=pltpu.PrefetchScalarGridSpec(n...  10 us
    pallas_call x1, Pallas kernels, _forward(): pl.pallas_call(_forward_kernel, in_specs=[smem, WHOLE, WHOLE, hbm, hbm, W...  9.29 us
    all_to_all x1, blocking collectives, per_device(): recon = lax.all_to_all(recon, 'y', 0, 0)  6.79 us
    all_to_all x1, blocking collectives, per_device(): target = lax.all_to_all(resid_out, 'y', 0, 0)  6.78 us
  transfers between devices with their start and end apart: 3, of which 1 were waited for; matrix products, arithmetic and copies ran while one was open for 0% of the time, Pallas kernels for 0%

profile of v3, /device:TPU:1, one launch (start us, length us, event | category | flops | bytes accessed | tf_op | source)
XLA Modules:
  0.0 182.2 jit_solution(12379065100811208563)
XLA Ops:
  0.6 0.0 copy-start
  0.7 0.7 fusion
  1.4 0.7 add_select_fusion
  2.1 0.2 compare_reduce_fusion
  2.3 0.1 broadcast_bitcast_fusion.keep_ref
  2.4 1.0 constant_dynamic-slice_fusion.1
  3.4 0.7 broadcast_select_fusion.tab_ref
  4.1 0.2 broadcast_in_dim.5
  4.3 32.9 %all_to_all.25.own_ref.x_own_ref = bf16[8,2,16,3584]{3,2,1,0:T(8,128)(2,1)S(1)} all-to-all(bf16[8,2,16,3584]{3,2,1,0:T(8,128)(2,1)S(1)} %broadcast_in_dim.5), channel_id=1, replica_groups=mesh['x'=4,'zl'=2,'core'=2,'zh'=2,'y'=4] {'zh','y'}, dimensions={0} | all-to-all | bytes 3670016 | tf_op jit(solution)/shard_map/all_to_all | solution.py:308
  37.2 0.0 copy-start.1
  37.2 1.8 collective-permute-start
  39.0 3.4 %collective-permute-done.oth_ref.x_oth_ref = bf16[8,2,16,3584]{3,2,1,0:T(8,128)(2,1)S(1)} collective-permute-done((bf16[8,2,16,3584]{3,2,1,0:T(8,128)(2,1)S(1)}, bf16[8,2,16,3584]{3,2,1,0:T(8,128)(2,1)S(1)}, u32[]{:S(2)}, u32[]{:S(2)}) %collective-permute-start) | collective-permute-done | bytes 1835040 | tf_op jit(solution)/shard_map/ppermute | solution.py:309
  42.4 0.0 copy-done
  42.4 9.3 %forward.1 = (bf16[4,128,3584]{2,1,0:T(8,128)(2,1)S(1)}, bf16[4,128,3584]{2,1,0:T(8,128)(2,1)S(1)}, bf16[2,256,256]{2,1,0:T(8,128)(2,1)S(1)}, f32[2,256,256]{2,1,0:T(8,128)S(1)}, bf16[5,256,3584]{2,1,0:T(8,128)(2,1)S(1)}) custom-call(s32[26]{0:T(128)S(1)} %broadcast_select_fusion.tab_ref, bf16[8,2,16,3584]{3,2,1,0:T(8,128)(2,1)S(1)} %all_to_all.25.own_ref.x_own_ref, ...), custom_call_target="tpu_custom_call" | custom-call | flops 3288334336 | bytes 12845056 | tf_op jit(solution)/shard_map/forward/pallas_call | solution.py:136
  51.7 0.5 collective-permute-start.1
  52.1 0.0 copy-done.1
  52.1 6.8 %all_to_all.26.target_ref = bf16[4,2,3584]{2,1,0:T(2,128)(2,1)S(1)} all-to-all(bf16[4,2,3584]{2,1,0:T(2,128)(2,1)S(1)} %copy-done.1), channel_id=1, replica_groups=mesh['x'=4,'zl'=2,'core'=2,'zh'=2,'y'=4] {'y'}, dimensions={0} | all-to-all | bytes 114688 | tf_op jit(solution)/shard_map/all_to_all | solution.py:315
  58.9 0.0 collective-permute-done.1.got_ref
  58.9 0.9 join.1
  59.8 51.3 %all_to_all.27.pieces_ref = bf16[64,8,3584]{2,1,0:T(8,128)(2,1)S(1)} all-to-all(bf16[64,8,3584]{2,1,0:T(8,128)(2,1)S(1)} %bitcast.6), channel_id=1, replica_groups=mesh['x'=4,'zl'=2,'core'=2,'zh'=2,'y'=4] {'y','x','zl','zh'}, dimensions={0} | all-to-all | bytes 7340032 | tf_op jit(solution)/shard_map/all_to_all | solution.py:318
  111.1 0.9 settle.1
  112.0 49.3 %all_to_all.28 = bf16[64,8,3584]{2,1,0:T(8,128)(2,1)S(1)} all-to-all(bf16[64,8,3584]{2,1,0:T(8,128)(2,1)S(1)} %get-tuple-element.34), channel_id=1, replica_groups=mesh['x'=4,'zl'=2,'core'=2,'zh'=2,'y'=4] {'y','x','zl','zh'}, dimensions={0} | all-to-all | bytes 7340032 | tf_op jit(solution)/shard_map/all_to_all | solution.py:320
  161.3 3.5 %collective-permute-start.2 = (bf16[4,128,3584]{2,1,0:T(8,128)(2,1)S(1)}, bf16[4,128,3584]{2,1,0:T(8,128)(2,1)S(1)}, u32[]{:S(2)}, u32[]{:S(2)}) collective-permute-start(bf16[4,128,3584]{2,1,0:T(8,128)(2,1)S(1)} %bitcast.4), channel_id=1, source_target_pairs={{0,8},{8,0},{1,9},{9,1},{2,10},{10,2},{3,11},{11,3},{4,12},{12,4},... | collective-permute-start | bytes 11010056 | tf_op jit(solution)/shard_map/ppermute | solution.py:321
  164.8 6.8 %all_to_all.29 = bf16[4,2,3584]{2,1,0:T(2,128)(2,1)S(1)} all-to-all(bf16[4,2,3584]{2,1,0:T(2,128)(2,1)S(1)} %get-tuple-element.36), channel_id=1, replica_groups=mesh['x'=4,'zl'=2,'core'=2,'zh'=2,'y'=4] {'y'}, dimensions={0} | all-to-all | bytes 114688 | tf_op jit(solution)/shard_map/all_to_all | solution.py:323
  171.6 0.0 collective-permute-done.2.oth_ref
  171.6 10.0 %backward.1 = (bf16[5,256,3584]{2,1,0:T(8,128)(2,1)}, bf16[2,3584,256]{2,1,0:T(8,128)(2,1)}, f32[2,256]{1,0:T(2,128)}) custom-call(s32[26]{0:T(128)S(1)} %broadcast_select_fusion.tab_ref, bf16[2,256,256]{2,1,0:T(8,128)(2,1)S(1)} %get-tuple-element.38.turned_ref, f32[2,256,256]{2,1,0:T(8,128)S(1)} %get-tuple-element.39.slope_ref, ...), custom_call_target="tpu_custom_call" | custom-call | flops 5637144576 | bytes 12845056 | tf_op jit(solution)/shard_map/backward/pallas_call | solution.py:262
  181.6 0.6 copy.13
  (3 shorter events, 0.0 us)
Async XLA Ops:
  0.6 41.8 %copy-start = (f32[2,256]{1,0:T(2,128)S(1)}, f32[2,256]{1,0:T(2,128)}, u32[]{:S(2)}) copy-start(f32[2,256]{1,0:T(2,128)} %bias_ref.1) | copy-start | bytes 6148
  37.2 15.0 %copy-start.1 = (bf16[4,2,3584]{2,1,0:T(2,128)(2,1)S(1)}, bf16[4,2,3584]{2,1,0:T(2,128)(2,1)}, u32[]{:S(2)}) copy-start(bf16[4,2,3584]{2,1,0:T(2,128)(2,1)} %param.9) | copy-start | bytes 172036
  37.2 5.2 %collective-permute-start = (bf16[8,2,16,3584]{3,2,1,0:T(8,128)(2,1)S(1)}, bf16[8,2,16,3584]{3,2,1,0:T(8,128)(2,1)S(1)}, u32[]{:S(2)}, u32[]{:S(2)}) collective-permute-start(bf16[8,2,16,3584]{3,2,1,0:T(8,128)(2,1)S(1)} %all_to_all.25.own_ref.x_own_ref), channel_id=1, source_target_pairs={{0,8},{8,0},{1,9},{9,1},{2,10},{10,2},{3,11},{11,3},{4,12},{12,4},... | collective-permute-start | bytes 5505032 | tf_op jit(solution)/shard_map/ppermute | solution.py:309
  51.7 7.2 %collective-permute-start.1 = (bf16[4,128,3584]{2,1,0:T(8,128)(2,1)S(1)}, bf16[4,128,3584]{2,1,0:T(8,128)(2,1)S(1)}, u32[]{:S(2)}, u32[]{:S(2)}) collective-permute-start(bf16[4,128,3584]{2,1,0:T(8,128)(2,1)S(1)} %get-tuple-element.30), channel_id=1, source_target_pairs={{0,8},{8,0},{1,9},{9,1},{2,10},{10,2},{3,11},{11,3},{4,12},{12,4},... | collective-permute-start | bytes 11010056 | tf_op jit(solution)/shard_map/ppermute | solution.py:313
  161.3 10.2 %collective-permute-start.2 = (bf16[4,128,3584]{2,1,0:T(8,128)(2,1)S(1)}, bf16[4,128,3584]{2,1,0:T(8,128)(2,1)S(1)}, u32[]{:S(2)}, u32[]{:S(2)}) collective-permute-start(bf16[4,128,3584]{2,1,0:T(8,128)(2,1)S(1)} %bitcast.4), channel_id=1, source_target_pairs={{0,8},{8,0},{1,9},{9,1},{2,10},{10,2},{3,11},{11,3},{4,12},{12,4},... | collective-permute-start | bytes 11010056 | tf_op jit(solution)/shard_map/ppermute | solution.py:321

commit v4 on v3

v4 whole, which is shorter than its diff:
```python
import jax
import jax.numpy as jnp
from jax import lax
from jax.experimental import pallas as pl
from jax.experimental.pallas import tpu as pltpu
from jax.sharding import Mesh
from jax.sharding import PartitionSpec as P

FEAT = 16384
BLOCK = 128
LAYERS = 4
D = 3584
W = 256
HALF = 128
TILES = 8
HROW = 16
PAIRS = 5
GRID_AXES = ("y", "x", "zl", "zh")
DP = ("zh", "y")
ALL = ("x", "zl", "core", "zh", "y")
BF = jnp.bfloat16
F32 = jnp.float32
SWAP = [(0, 1), (1, 0)]

VMEM = pltpu.MemorySpace.VMEM
HBM = pltpu.MemorySpace.HBM
WHOLE = pl.BlockSpec(memory_space=VMEM)
CHUNK = 512
CHUNKS = [slice(c, c + CHUNK) for c in range(0, D, CHUNK)]


def _hbm(x):
    return pltpu.with_memory_space_constraint(x, HBM)


def _vmem(x):
    return pltpu.with_memory_space_constraint(x, VMEM)


def _params(mib):
    return pltpu.CompilerParams(vmem_limit_bytes=mib << 20)


def _tokens(own_ref, oth_ref, k):
    return own_ref[:, k].reshape(HALF, D), oth_ref[:, k].reshape(HALF, D)


def _side():
    return lax.axis_index("x") // 2


def _prepare_kernel(in_hbm, out_ref, spread_ref, *rest):
    piece_refs, sem = rest[:4], rest[4]
    side, core, y = _side(), lax.axis_index("core"), lax.axis_index("y")
    copies = []
    for k, layer in enumerate((side, LAYERS - 1 - side)):
        for i in range(TILES):
            copies.append(
                pltpu.make_async_copy(
                    in_hbm.at[layer, pl.ds(pl.multiple_of(core * HROW, HROW), HROW)],
                    spread_ref.at[i, k],
                    sem.at[k * TILES + i],
                )
            )
    for copy in copies:
        copy.start()
    for j in range(4):
        piece_refs[j][...] = out_ref[lax.rem(y + j, 4)]
    for copy in copies:
        copy.wait()


def _prepare(resid_in, resid_out):
    return pl.pallas_call(
        _prepare_kernel,
        in_specs=[pl.BlockSpec(memory_space=HBM), WHOLE],
        out_specs=[WHOLE] * 5,
        out_shape=[jax.ShapeDtypeStruct((TILES, 2, HROW, D), BF)]
        + [jax.ShapeDtypeStruct((2, D), BF)] * 4,
        scratch_shapes=[pltpu.SemaphoreType.DMA((2 * TILES,))],
        compiler_params=_params(2),
        name="prepare",
    )(_hbm(resid_in), resid_out)


def _decode(t, side, codes_ref, dec_ref, own_ref, oth_ref, at):
    has_first = t >= side
    has_second = t + 1 >= LAYERS - side
    one = jnp.maximum(t - side, 0)

    def sweep(part):
        for cols in CHUNKS:
            value = part(cols).astype(BF)
            own_ref[at, :, cols] = value[:HALF]
            oth_ref[at, :, cols] = value[HALF:]

    def first(cols):
        return jnp.dot(codes_ref[0], dec_ref[one, :, cols], preferred_element_type=F32)

    def both(cols):
        return first(cols) + jnp.dot(
            codes_ref[1], dec_ref[t + 1, :, cols], preferred_element_type=F32
        )

    @pl.when(has_second)
    def _():
        sweep(both)

    @pl.when(jnp.logical_and(has_first, jnp.logical_not(has_second)))
    def _():
        sweep(first)

    @pl.when(jnp.logical_not(has_first))
    def _():
        own_ref[at] = jnp.zeros((HALF, D), BF)
        oth_ref[at] = jnp.zeros((HALF, D), BF)


def _forward_kernel(
    own_ref, oth_ref, enc_hbm, dec_hbm, bias_ref, active_ref,
    part_own_ref, part_oth_ref, codes_ref, turned_ref, slope_ref, dec_ref, enc_ref, enc_sem, dec_sem,
):
    enc_copies = [
        pltpu.make_async_copy(enc_hbm.at[k], enc_ref.at[k], enc_sem.at[k]) for k in range(2)
    ]
    dec_copies = [
        pltpu.make_async_copy(dec_hbm.at[p], dec_ref.at[p], dec_sem.at[p]) for p in range(PAIRS)
    ]
    for copy in enc_copies + dec_copies[::-1]:
        copy.start()
    x, zl, core = lax.axis_index("x"), lax.axis_index("zl"), lax.axis_index("core")
    zh, y = lax.axis_index("zh"), lax.axis_index("y")
    side = _side()
    rank = (((x * 2 + zl) * 2 + core) * 2 + zh) * 4 + y
    block = rank * (W // BLOCK) - side * (FEAT // BLOCK)
    for k, layer in enumerate((side, LAYERS - 1 - side)):
        rows = jnp.concatenate(_tokens(own_ref, oth_ref, k), axis=0)
        listed = active_ref[layer]
        keep = [
            jnp.broadcast_to(
                jnp.max((listed == block + b).astype(F32), axis=1, keepdims=True), (TILES, BLOCK)
            )
            for b in range(W // BLOCK)
        ]
        keep = jnp.concatenate(keep, axis=1)
        keep = jnp.broadcast_to(keep[:, None, :], (TILES, HROW, W)).reshape(HALF, W)
        keep = jnp.concatenate([keep, keep], axis=0)
        enc_copies[k].wait()
        pre = jnp.dot(rows, enc_ref[k], preferred_element_type=F32) + bias_ref[k : k + 1]
        positive = jnp.maximum(pre, 0.0)
        kept = keep * positive
        codes = kept * positive
        codes_ref[k] = codes.astype(BF)
        turned_ref[k] = codes.T.astype(BF)
        slope_ref[k] = 2.0 * kept
    for p in (4, 3, 2):
        dec_copies[p].wait()
    _decode(3, side, codes_ref, dec_ref, part_own_ref, part_oth_ref, 1)
    dec_copies[1].wait()
    _decode(2, side, codes_ref, dec_ref, part_own_ref, part_oth_ref, 0)
    dec_copies[0].wait()


def _forward(own, oth, encoder, decoder, bias, active):
    hbm = pl.BlockSpec(memory_space=HBM)
    return pl.pallas_call(
        _forward_kernel,
        in_specs=[WHOLE, WHOLE, hbm, hbm, WHOLE, WHOLE],
        out_specs=[WHOLE] * 6,
        out_shape=[
            jax.ShapeDtypeStruct((2, HALF, D), BF),
            jax.ShapeDtypeStruct((2, HALF, D), BF),
            jax.ShapeDtypeStruct((2, 2 * HALF, W), BF),
            jax.ShapeDtypeStruct((2, W, 2 * HALF), BF),
            jax.ShapeDtypeStruct((2, 2 * HALF, W), F32),
            jax.ShapeDtypeStruct((PAIRS, W, D), BF),
        ],
        scratch_shapes=[
            pltpu.VMEM((2, D, W), BF),
            pltpu.SemaphoreType.DMA((2,)),
            pltpu.SemaphoreType.DMA((PAIRS,)),
        ],
        compiler_params=_params(10),
        cost_estimate=pl.CostEstimate(
            flops=2 * 5 * 256 * D * W,
            bytes_accessed=(2 * D * W + PAIRS * W * D) * 2,
            transcendentals=0,
        ),
        name="forward",
    )(own, oth, _hbm(encoder), _hbm(decoder), bias, active)


def _forward_low_kernel(codes_ref, dec_ref, part_own_ref, part_oth_ref):
    for t in (1, 0):
        _decode(t, _side(), codes_ref, dec_ref, part_own_ref, part_oth_ref, t)


def _forward_low(codes, dec):
    return pl.pallas_call(
        _forward_low_kernel,
        in_specs=[WHOLE, WHOLE],
        out_specs=[WHOLE, WHOLE],
        out_shape=[jax.ShapeDtypeStruct((2, HALF, D), BF)] * 2,
        compiler_params=_params(4),
        cost_estimate=pl.CostEstimate(
            flops=2 * 2 * 256 * D * W, bytes_accessed=2 * 256 * D * 2, transcendentals=0
        ),
        name="forward_low",
    )(codes, dec)


def _join_kernel(own_low_ref, own_ref, got_low_ref, got_ref, out_ref):
    for t in range(2):
        out_ref[t] = (own_low_ref[t].astype(F32) + got_low_ref[t].astype(F32)).astype(BF)
        out_ref[2 + t] = (own_ref[t].astype(F32) + got_ref[t].astype(F32)).astype(BF)


def _join(*parts):
    return pl.pallas_call(
        _join_kernel,
        in_specs=[WHOLE] * 4,
        out_specs=WHOLE,
        out_shape=jax.ShapeDtypeStruct((LAYERS, HALF, D), BF),
        compiler_params=_params(4),
        cost_estimate=pl.CostEstimate(
            flops=4 * HALF * D, bytes_accessed=3 * 4 * HALF * D * 2, transcendentals=0
        ),
        name="join",
    )(*parts)


def _settle_kernel(pieces_ref, *rest):
    target_refs, errors_ref, recon_refs, rows_ref, turn_ref = (
        rest[:4], rest[4], rest[5:9], rest[9], rest[10]
    )
    y = lax.axis_index("y")
    for j in range(4):
        turn_ref[lax.rem(y + 4 - j, 4)] = target_refs[j][...].astype(F32)
    for j in range(4):
        rows_ref[2 * j : 2 * j + 2] = turn_ref[j]
    summed = lax.fori_loop(
        0, 64, lambda i, acc: acc + pieces_ref[i].astype(F32), jnp.zeros((8, D), F32), unroll=8
    )
    errors = (summed - rows_ref[...]).astype(BF)
    rows_ref[...] = summed
    for j in range(4):
        turn_ref[j] = rows_ref[2 * j : 2 * j + 2]
    for j in range(4):
        recon_refs[j][...] = turn_ref[lax.rem(y + j, 4)].astype(BF)

    def spread(i, carry):
        errors_ref[i] = errors
        return carry

    lax.fori_loop(0, 64, spread, 0, unroll=8)


def _settle(pieces, targets):
    return pl.pallas_call(
        _settle_kernel,
        in_specs=[WHOLE] * 5,
        out_specs=[WHOLE] * 5,
        out_shape=[jax.ShapeDtypeStruct((64, 8, D), BF)]
        + [jax.ShapeDtypeStruct((2, D), BF)] * 4,
        scratch_shapes=[pltpu.VMEM((8, D), F32), pltpu.VMEM((4, 2, D), F32)],
        compiler_params=_params(4),
        cost_estimate=pl.CostEstimate(
            flops=64 * 8 * D, bytes_accessed=2 * 64 * 8 * D * 2, transcendentals=0
        ),
        name="settle",
    )(pieces, *targets)


def _backward_kernel(
    turned_ref, slope_ref, own_ref, oth_ref, x_own_ref, x_oth_ref, dec_ref, *rest
):
    piece_refs = rest[:4]
    grad_ref, genc_ref, bias_ref, recon_ref, back_ref, pre_ref = rest[4:]
    side, y = _side(), lax.axis_index("y")
    p = pl.program_id(0)

    @pl.when(p == 0)
    def _():
        back_ref[...] = jnp.zeros_like(back_ref)
        for j in range(4):
            recon_ref[lax.rem(y + 4 - j, 4)] = piece_refs[j][...]

    @pl.when(p < PAIRS)
    def _():
        pair = jnp.minimum(p, PAIRS - 1)
        slot = (pair >= LAYERS - side).astype(jnp.int32)
        target = jnp.where(slot > 0, pair - 1, side + pair)
        err = jnp.concatenate([own_ref[target], oth_ref[target]], axis=0)
        back_ref[slot] += lax.dot_general(
            err, dec_ref[pair], (((1,), (1,)), ((), ())), preferred_element_type=F32
        )
        turned = turned_ref[slot]
        for cols in CHUNKS:
            err = jnp.concatenate([own_ref[target, :, cols], oth_ref[target, :, cols]], axis=0)
            grad_ref[0, :, cols] = jnp.dot(turned, err, preferred_element_type=F32).astype(BF)

    @pl.when(p == PAIRS)
    def _():
        for k in range(2):
            pre = (back_ref[k] * slope_ref[k]).astype(BF)
            pre_ref[k] = pre
            bias_ref[k : k + 1] = jnp.sum(pre.astype(F32), axis=0, keepdims=True)

    @pl.when(p >= PAIRS)
    def _():
        k = jnp.maximum(p - PAIRS, 0)
        own, oth = _tokens(x_own_ref, x_oth_ref, k)
        for rows in CHUNKS:
            x = jnp.concatenate([own[:, rows], oth[:, rows]], axis=0)
            genc_ref[0, rows] = lax.dot_general(
                x, pre_ref[k], (((0,), (0,)), ((), ())), preferred_element_type=F32
            ).astype(BF)


def _backward(turned, slope, own, oth, x_own, x_oth, decoder, pieces):
    return pl.pallas_call(
        _backward_kernel,
        grid=(PAIRS + 2,),
        in_specs=[WHOLE] * 11,
        out_specs=[
            pl.BlockSpec((1, W, D), lambda p: (jnp.minimum(p, PAIRS - 1), 0, 0)),
            pl.BlockSpec((1, D, W), lambda p: (jnp.maximum(p - PAIRS, 0), 0, 0)),
            pl.BlockSpec((2, W), lambda p: (0, 0)),
            pl.BlockSpec((4, 2, D), lambda p: (0, 0, 0)),
        ],
        scratch_shapes=[pltpu.VMEM((2, 2 * HALF, W), F32), pltpu.VMEM((2, 2 * HALF, W), BF)],
        out_shape=[
            jax.ShapeDtypeStruct((PAIRS, W, D), BF),
            jax.ShapeDtypeStruct((2, D, W), BF),
            jax.ShapeDtypeStruct((2, W), F32),
            jax.ShapeDtypeStruct((4, 2, D), BF),
        ],
        compiler_params=_params(12),
        cost_estimate=pl.CostEstimate(
            flops=4 * PAIRS * 256 * D * W + 4 * 256 * D * W,
            bytes_accessed=PAIRS * W * D * 2 + 2 * D * W * 2,
            transcendentals=0,
        ),
        name="backward",
    )(turned, slope, own, oth, x_own, x_oth, decoder, *pieces)


def _around_y(pieces):
    return [pieces[0]] + [
        lax.ppermute(pieces[j], "y", [(i, (i + j) % 4) for i in range(4)]) for j in (1, 2, 3)
    ]


def per_device(resid_in, resid_out, encoder, enc_bias, decoder, active):
    spread, *targets = _prepare(resid_in, resid_out)
    own = lax.all_to_all(spread, DP, 0, 0)
    oth = lax.ppermute(own, "core", SWAP)
    targets[1:], own = lax.optimization_barrier((targets[1:], own))
    targets = _around_y(targets)
    part_own, part_oth, codes, turned, slope, dec = _forward(
        own, oth, encoder, decoder, enc_bias, active
    )
    got = lax.ppermute(part_oth, "core", SWAP)
    low_own, low_oth = _forward_low(codes, dec)
    got_low = lax.ppermute(low_oth, "core", SWAP)
    part = _join(low_own, part_own, got_low, got)
    part, targets = lax.optimization_barrier((part, targets))
    pieces = lax.all_to_all(part.reshape(64, 8, D), GRID_AXES, 0, 0)
    errors, *recon = _settle(pieces, targets)
    err_own = lax.all_to_all(errors, GRID_AXES, 0, 0).reshape(LAYERS, HALF, D)
    err_oth = lax.ppermute(err_own, "core", SWAP)
    recon, err_own = lax.optimization_barrier((recon, err_own))
    recon = _around_y(recon)
    grad_decoder, grad_encoder, grad_bias, recon = _backward(
        turned, slope, err_own, err_oth, own, oth, dec, recon
    )
    return recon, grad_encoder, grad_bias, grad_decoder


def solution(mesh):
    fine = Mesh(mesh.devices.reshape(4, 2, 2, 2, 4), ALL)
    in_specs = (
        P(None, DP, None),
        P(None, ALL, None),
        P(None, None, ALL),
        P(None, ALL),
        P(None, ALL, None),
        P(),
    )
    out_specs = (P(None, ALL, None), P(None, None, ALL), P(None, ALL), P(None, ALL, None))
    return jax.shard_map(
        per_device, mesh=fine, in_specs=in_specs, out_specs=out_specs, check_vma=False
    )
```

time: 183 us -> 178 us (0.973)
  blocking collectives: 147 us -> 134 us
  starting transfers between devices: 5.72 us -> 12.3 us
  waiting for transfers between devices: 3.42 us -> 8.14 us
    all_to_all x3 -> x1, blocking collectives: 46.5 us -> 32.4 us  [per_device(): own = lax.all_to_all(spread, DP, 0, 0)]
    ppermute x1 -> x8, starting transfers between devices: 0.45 us -> 6.51 us  [the longest x6 5.84 us: _around_y(): lax.ppermute(pieces[j], 'y', [(i, (i + j) % 4) for i in range(4)])]
    ppermute x1 -> x8, waiting for transfers between devices: 0.01 us -> 3.51 us  [the longest x6 2.04 us: _around_y(): lax.ppermute(pieces[j], 'y', [(i, (i + j) % 4) for i in range(4)])]
    pallas_call x4 -> x6, Pallas kernels: 21.1 us -> 22.2 us  [the longest x1 9.6 us: _backward(): pl.pallas_call(_backward_kernel, grid=(PAIRS + 2,), in_specs=[WHOLE] * 11...]
  transfers between devices with their start and end apart: 3 -> 10, of which waited for: 1 -> 6; matrix products, arithmetic and copies ran while one was open for 0% -> 0% of each run, Pallas kernels for 0% -> 1%
where the time goes in v4:
time: 178 us
  blocking collectives  134 us (75%)
  Pallas kernels  22.2 us (12%)
  starting transfers between devices  12.3 us (7%)
  waiting for transfers between devices  8.14 us (5%)
    all_to_all x1, blocking collectives, per_device(): pieces = lax.all_to_all(part.reshape(64, 8, D), GRID_AXES, 0, 0)  51.7 us
    all_to_all x1, blocking collectives, per_device(): err_own = lax.all_to_all(errors, GRID_AXES, 0, 0).reshape(LAYERS, HALF, D)  49.5 us
    all_to_all x1, blocking collectives, per_device(): own = lax.all_to_all(spread, DP, 0, 0)  32.4 us
    pallas_call x1, Pallas kernels, _backward(): pl.pallas_call(_backward_kernel, grid=(PAIRS + 2,), in_specs=[WHOLE] * 11...  9.6 us
    pallas_call x1, Pallas kernels, _forward(): pl.pallas_call(_forward_kernel, in_specs=[WHOLE, WHOLE, hbm, hbm, WHOLE,...  7.5 us
    ppermute x6, starting transfers between devices, _around_y(): lax.ppermute(pieces[j], 'y', [(i, (i + j) % 4) for i in range(4)])  5.84 us
  transfers between devices with their start and end apart: 10, of which 6 were waited for; matrix products, arithmetic and copies ran while one was open for 0% of the time, Pallas kernels for 1%

profile of v4, /device:TPU:1, one launch (start us, length us, event | category | flops | bytes accessed | tf_op | source)
XLA Modules:
  0.0 177.7 jit_solution(17334837981018612447)
XLA Ops:
  0.6 0.0 copy-start
  0.6 0.8 copy-done
  1.5 0.0 copy-start.1
  1.5 0.0 copy-start.2
  1.5 2.0 %prepare.1 = (bf16[8,2,16,3584]{3,2,1,0:T(8,128)(2,1)S(1)}, bf16[2,3584]{1,0:T(2,128)(2,1)S(1)}, bf16[2,3584]{1,0:T(2,128)(2,1)S(1)}, bf16[2,3584]{1,0:T(2,128)(2,1)S(1)}, bf16[2,3584]{1,0:T(2,128)(2,1)S(1)}) custom-call(bf16[4,32,3584]{2,1,0:T(8,128)(2,1)} %in_hbm.1, bf16[4,2,3584]{2,1,0:T(2,128)(2,1)S(1)} %copy-done), custom_call_target="tpu_custom_call" | custom-call | tf_op jit(solution)/shard_map/prepare/pallas_call | solution.py:74
  3.4 32.4 %all_to_all.15.own_ref.x_own_ref = bf16[8,2,16,3584]{3,2,1,0:T(8,128)(2,1)S(1)} all-to-all(bf16[8,2,16,3584]{3,2,1,0:T(8,128)(2,1)S(1)} %get-tuple-element.43), channel_id=1, replica_groups=mesh['x'=4,'zl'=2,'core'=2,'zh'=2,'y'=4] {'zh','y'}, dimensions={0} | all-to-all | bytes 3670016 | tf_op jit(solution)/shard_map/all_to_all | solution.py:356
  35.8 2.3 %collective-permute-start = (bf16[8,2,16,3584]{3,2,1,0:T(8,128)(2,1)S(1)}, bf16[8,2,16,3584]{3,2,1,0:T(8,128)(2,1)S(1)}, u32[]{:S(2)}, u32[]{:S(2)}) collective-permute-start(bf16[8,2,16,3584]{3,2,1,0:T(8,128)(2,1)S(1)} %all_to_all.15.own_ref.x_own_ref), channel_id=1, source_target_pairs={{0,8},{8,0},{1,9},{9,1},{2,10},{10,2},{3,11},{11,3},{4,12},{12,4},... | collective-permute-start | bytes 5505032 | tf_op jit(solution)/shard_map/ppermute | solution.py:357
  38.2 3.4 %collective-permute-done.oth_ref.x_oth_ref = bf16[8,2,16,3584]{3,2,1,0:T(8,128)(2,1)S(1)} collective-permute-done((bf16[8,2,16,3584]{3,2,1,0:T(8,128)(2,1)S(1)}, bf16[8,2,16,3584]{3,2,1,0:T(8,128)(2,1)S(1)}, u32[]{:S(2)}, u32[]{:S(2)}) %collective-permute-start) | collective-permute-done | bytes 1835040 | tf_op jit(solution)/shard_map/ppermute | solution.py:357
  41.6 0.0 copy-done.1
  41.6 0.0 copy-done.2
  41.6 7.5 %forward.1 = (bf16[2,128,3584]{2,1,0:T(8,128)(2,1)S(1)}, bf16[2,128,3584]{2,1,0:T(8,128)(2,1)S(1)}, bf16[2,256,256]{2,1,0:T(8,128)(2,1)S(1)}, bf16[2,256,256]{2,...) custom-call(bf16[8,2,16,3584]{3,2,1,0:T(8,128)(2,1)S(1)} %all_to_all.15.own_ref.x_own_ref, ...), custom_call_target="tpu_custom_call" | custom-call | flops 2348810240 | bytes 12845056 | tf_op jit(solution)/shard_map/forward/pallas_call | solution.py:166
  49.1 0.5 collective-permute-start.2
  49.5 1.3 forward_low.1
  50.8 0.2 collective-permute-start.1
  51.1 0.6 collective-permute-start.3
  51.7 1.4 collective-permute-start.4
  53.1 1.0 collective-permute-start.5
  54.1 0.0 collective-permute-done.2.got_ref
  54.1 1.5 collective-permute-done.1.got_low_ref
  55.6 0.8 join.1
  56.4 0.0 collective-permute-done.3.rest_1_
  56.4 0.0 collective-permute-done.4.rest_2_
  56.4 0.0 collective-permute-done.5.rest_3_
  56.4 51.7 %all_to_all.16.pieces_ref = bf16[64,8,3584]{2,1,0:T(8,128)(2,1)S(1)} all-to-all(bf16[64,8,3584]{2,1,0:T(8,128)(2,1)S(1)} %bitcast.4), channel_id=1, replica_groups=mesh['x'=4,'zl'=2,'core'=2,'zh'=2,'y'=4] {'y','x','zl','zh'}, dimensions={0} | all-to-all | bytes 7340032 | tf_op jit(solution)/shard_map/all_to_all | solution.py:368
  108.2 1.0 settle.1
  109.2 49.5 %all_to_all.17 = bf16[64,8,3584]{2,1,0:T(8,128)(2,1)S(1)} all-to-all(bf16[64,8,3584]{2,1,0:T(8,128)(2,1)S(1)} %get-tuple-element.66), channel_id=1, replica_groups=mesh['x'=4,'zl'=2,'core'=2,'zh'=2,'y'=4] {'y','x','zl','zh'}, dimensions={0} | all-to-all | bytes 7340032 | tf_op jit(solution)/shard_map/all_to_all | solution.py:370
  158.7 3.5 %collective-permute-start.6 = (bf16[4,128,3584]{2,1,0:T(8,128)(2,1)S(1)}, bf16[4,128,3584]{2,1,0:T(8,128)(2,1)S(1)}, u32[]{:S(2)}, u32[]{:S(2)}) collective-permute-start(bf16[4,128,3584]{2,1,0:T(8,128)(2,1)S(1)} %bitcast.2), channel_id=1, source_target_pairs={{0,8},{8,0},{1,9},{9,1},{2,10},{10,2},{3,11},{11,3},{4,12},{12,4},... | collective-permute-start | bytes 11010056 | tf_op jit(solution)/shard_map/ppermute | solution.py:371
  162.1 0.4 collective-permute-start.7
  162.5 1.6 collective-permute-start.8
  164.1 0.8 collective-permute-start.9
  164.9 1.0 collective-permute-done.7.rest_1_
  165.9 0.7 collective-permute-done.8.rest_2_
  166.6 0.4 collective-permute-done.9.rest_3_
  166.9 1.2 collective-permute-done.6.oth_ref
  168.1 9.6 %backward.1 = (bf16[5,256,3584]{2,1,0:T(8,128)(2,1)}, bf16[2,3584,256]{2,1,0:T(8,128)(2,1)}, f32[2,256]{1,0:T(2,128)}, bf16[4,2,3584]{2,1,0:T(2,128)(2,1)}) custom-call(bf16[2,256,256]{2,1,0:T(8,128)(2,1)S(1)} %get-tuple-element.45.turned_ref, f32[2,256,256]{2,1,0:T(8,128)S(1)} %get-tuple-element.46.slope_ref, bf16[4,128,3584]{2,1,0:T(8,128)(2,1)S(1)} %bitcast.3, ...), custom_call_target="tpu_custom_call" | custom-call | flops 5637144576 | bytes 12845056 | tf_op jit(solution)/shard_map/backward/pallas_call | solution.py:321
Async XLA Ops:
  0.6 0.8 copy-start
  1.5 40.1 %copy-start.1 = (s32[4,8,32]{2,1,0:T(8,128)S(1)}, s32[4,8,32]{2,1,0:T(8,128)}, u32[]{:S(2)}) copy-start(s32[4,8,32]{2,1,0:T(8,128)} %active_ref.1) | copy-start | bytes 12292
  1.5 40.1 %copy-start.2 = (f32[2,256]{1,0:T(2,128)S(1)}, f32[2,256]{1,0:T(2,128)}, u32[]{:S(2)}) copy-start(f32[2,256]{1,0:T(2,128)} %bias_ref.1) | copy-start | bytes 6148
  35.8 5.7 %collective-permute-start = (bf16[8,2,16,3584]{3,2,1,0:T(8,128)(2,1)S(1)}, bf16[8,2,16,3584]{3,2,1,0:T(8,128)(2,1)S(1)}, u32[]{:S(2)}, u32[]{:S(2)}) collective-permute-start(bf16[8,2,16,3584]{3,2,1,0:T(8,128)(2,1)S(1)} %all_to_all.15.own_ref.x_own_ref), channel_id=1, source_target_pairs={{0,8},{8,0},{1,9},{9,1},{2,10},{10,2},{3,11},{11,3},{4,12},{12,4},... | collective-permute-start | bytes 5505032 | tf_op jit(solution)/shard_map/ppermute | solution.py:357
  49.1 5.0 %collective-permute-start.2 = (bf16[2,128,3584]{2,1,0:T(8,128)(2,1)S(1)}, bf16[2,128,3584]{2,1,0:T(8,128)(2,1)S(1)}, u32[]{:S(2)}, u32[]{:S(2)}) collective-permute-start(bf16[2,128,3584]{2,1,0:T(8,128)(2,1)S(1)} %get-tuple-element.52), channel_id=1, source_target_pairs={{0,8},{8,0},{1,9},{9,1},{2,10},{10,2},{3,11},{11,3},{4,12},{12,4},... | collective-permute-start | bytes 5505032 | tf_op jit(solution)/shard_map/ppermute | solution.py:363
  50.8 4.7 %collective-permute-start.1 = (bf16[2,128,3584]{2,1,0:T(8,128)(2,1)S(1)}, bf16[2,128,3584]{2,1,0:T(8,128)(2,1)S(1)}, u32[]{:S(2)}, u32[]{:S(2)}) collective-permute-start(bf16[2,128,3584]{2,1,0:T(8,128)(2,1)S(1)} %get-tuple-element.51), channel_id=1, source_target_pairs={{0,8},{8,0},{1,9},{9,1},{2,10},{10,2},{3,11},{11,3},{4,12},{12,4},... | collective-permute-start | bytes 5505032 | tf_op jit(solution)/shard_map/ppermute | solution.py:365
  51.1 5.4 %collective-permute-start.3 = (bf16[2,3584]{1,0:T(2,128)(2,1)S(1)}, bf16[2,3584]{1,0:T(2,128)(2,1)S(1)}, u32[]{:S(2)}, u32[]{:S(2)}) collective-permute-start(bf16[2,3584]{1,0:T(2,128)(2,1)S(1)} %get-tuple-element.54), channel_id=1, source_target_pairs={{0,1},{1,2},{2,3},{3,0},{4,5},{5,6},{6,7},{7,4},{8,9},{9,10},{10,1... | collective-permute-start | bytes 43016 | tf_op jit(solution)/shard_map/ppermute | solution.py:350
  51.7 4.7 %collective-permute-start.4 = (bf16[2,3584]{1,0:T(2,128)(2,1)S(1)}, bf16[2,3584]{1,0:T(2,128)(2,1)S(1)}, u32[]{:S(2)}, u32[]{:S(2)}) collective-permute-start(bf16[2,3584]{1,0:T(2,128)(2,1)S(1)} %get-tuple-element.55), channel_id=1, source_target_pairs={{0,2},{1,3},{2,0},{3,1},{4,6},{5,7},{6,4},{7,5},{8,10},{9,11},{10,... | collective-permute-start | bytes 43016 | tf_op jit(solution)/shard_map/ppermute | solution.py:350
  53.1 3.4 %collective-permute-start.5 = (bf16[2,3584]{1,0:T(2,128)(2,1)S(1)}, bf16[2,3584]{1,0:T(2,128)(2,1)S(1)}, u32[]{:S(2)}, u32[]{:S(2)}) collective-permute-start(bf16[2,3584]{1,0:T(2,128)(2,1)S(1)} %get-tuple-element.56), channel_id=1, source_target_pairs={{0,3},{1,0},{2,1},{3,2},{4,7},{5,4},{6,5},{7,6},{8,11},{9,8},{10,9... | collective-permute-start | bytes 43016 | tf_op jit(solution)/shard_map/ppermute | solution.py:350
  158.7 9.5 %collective-permute-start.6 = (bf16[4,128,3584]{2,1,0:T(8,128)(2,1)S(1)}, bf16[4,128,3584]{2,1,0:T(8,128)(2,1)S(1)}, u32[]{:S(2)}, u32[]{:S(2)}) collective-permute-start(bf16[4,128,3584]{2,1,0:T(8,128)(2,1)S(1)} %bitcast.2), channel_id=1, source_target_pairs={{0,8},{8,0},{1,9},{9,1},{2,10},{10,2},{3,11},{11,3},{4,12},{12,4},... | collective-permute-start | bytes 11010056 | tf_op jit(solution)/shard_map/ppermute | solution.py:371
  162.1 3.8 %collective-permute-start.7 = (bf16[2,3584]{1,0:T(2,128)(2,1)S(1)}, bf16[2,3584]{1,0:T(2,128)(2,1)S(1)}, u32[]{:S(2)}, u32[]{:S(2)}) collective-permute-start(bf16[2,3584]{1,0:T(2,128)(2,1)S(1)} %get-tuple-element.69), channel_id=1, source_target_pairs={{0,1},{1,2},{2,3},{3,0},{4,5},{5,6},{6,7},{7,4},{8,9},{9,10},{10,1... | collective-permute-start | bytes 43016 | tf_op jit(solution)/shard_map/ppermute | solution.py:350
  162.5 4.1 %collective-permute-start.8 = (bf16[2,3584]{1,0:T(2,128)(2,1)S(1)}, bf16[2,3584]{1,0:T(2,128)(2,1)S(1)}, u32[]{:S(2)}, u32[]{:S(2)}) collective-permute-start(bf16[2,3584]{1,0:T(2,128)(2,1)S(1)} %get-tuple-element.70), channel_id=1, source_target_pairs={{0,2},{1,3},{2,0},{3,1},{4,6},{5,7},{6,4},{7,5},{8,10},{9,11},{10,... | collective-permute-start | bytes 43016 | tf_op jit(solution)/shard_map/ppermute | solution.py:350
  164.1 2.9 %collective-permute-start.9 = (bf16[2,3584]{1,0:T(2,128)(2,1)S(1)}, bf16[2,3584]{1,0:T(2,128)(2,1)S(1)}, u32[]{:S(2)}, u32[]{:S(2)}) collective-permute-start(bf16[2,3584]{1,0:T(2,128)(2,1)S(1)} %get-tuple-element.71), channel_id=1, source_target_pairs={{0,3},{1,0},{2,1},{3,2},{4,7},{5,4},{6,5},{7,6},{8,11},{9,8},{10,9... | collective-permute-start | bytes 43016 | tf_op jit(solution)/shard_map/ppermute | solution.py:350

commit v5 on v4

--- a/solution.py
+++ b/solution.py
@@ -49,7 +49,7 @@
     return lax.axis_index("x") // 2
 
 
-def _prepare_kernel(in_hbm, out_ref, spread_ref, *rest):
+def _prepare_kernel(in_hbm, out_hbm, spread_ref, *rest):
     piece_refs, sem = rest[:4], rest[4]
     side, core, y = _side(), lax.axis_index("core"), lax.axis_index("y")
     copies = []
@@ -62,10 +62,14 @@
                     sem.at[k * TILES + i],
                 )
             )
+    for j in range(4):
+        copies.append(
+            pltpu.make_async_copy(
+                out_hbm.at[lax.rem(y + j, 4)], piece_refs[j], sem.at[2 * TILES + j]
+            )
+        )
     for copy in copies:
         copy.start()
-    for j in range(4):
-        piece_refs[j][...] = out_ref[lax.rem(y + j, 4)]
     for copy in copies:
         copy.wait()
 
@@ -73,14 +77,14 @@
 def _prepare(resid_in, resid_out):
     return pl.pallas_call(
         _prepare_kernel,
-        in_specs=[pl.BlockSpec(memory_space=HBM), WHOLE],
+        in_specs=[pl.BlockSpec(memory_space=HBM)] * 2,
         out_specs=[WHOLE] * 5,
         out_shape=[jax.ShapeDtypeStruct((TILES, 2, HROW, D), BF)]
         + [jax.ShapeDtypeStruct((2, D), BF)] * 4,
-        scratch_shapes=[pltpu.SemaphoreType.DMA((2 * TILES,))],
+        scratch_shapes=[pltpu.SemaphoreType.DMA((2 * TILES + 4,))],
         compiler_params=_params(2),
         name="prepare",
-    )(_hbm(resid_in), resid_out)
+    )(_hbm(resid_in), _hbm(resid_out))
 
 
 def _decode(t, side, codes_ref, dec_ref, own_ref, oth_ref, at):
@@ -117,17 +121,9 @@
 
 
 def _forward_kernel(
-    own_ref, oth_ref, enc_hbm, dec_hbm, bias_ref, active_ref,
-    part_own_ref, part_oth_ref, codes_ref, turned_ref, slope_ref, dec_ref, enc_ref, enc_sem, dec_sem,
+    own_ref, oth_ref, enc_ref, dec_ref, bias_ref, active_ref,
+    part_own_ref, part_oth_ref, codes_ref, turned_ref, slope_ref,
 ):
-    enc_copies = [
-        pltpu.make_async_copy(enc_hbm.at[k], enc_ref.at[k], enc_sem.at[k]) for k in range(2)
-    ]
-    dec_copies = [
-        pltpu.make_async_copy(dec_hbm.at[p], dec_ref.at[p], dec_sem.at[p]) for p in range(PAIRS)
-    ]
-    for copy in enc_copies + dec_copies[::-1]:
-        copy.start()
     x, zl, core = lax.axis_index("x"), lax.axis_index("zl"), lax.axis_index("core")
     zh, y = lax.axis_index("zh"), lax.axis_index("y")
     side = _side()
@@ -145,7 +141,6 @@
         keep = jnp.concatenate(keep, axis=1)
         keep = jnp.broadcast_to(keep[:, None, :], (TILES, HROW, W)).reshape(HALF, W)
         keep = jnp.concatenate([keep, keep], axis=0)
-        enc_copies[k].wait()
         pre = jnp.dot(rows, enc_ref[k], preferred_element_type=F32) + bias_ref[k : k + 1]
         positive = jnp.maximum(pre, 0.0)
         kept = keep * positive
@@ -153,41 +148,28 @@
         codes_ref[k] = codes.astype(BF)
         turned_ref[k] = codes.T.astype(BF)
         slope_ref[k] = 2.0 * kept
-    for p in (4, 3, 2):
-        dec_copies[p].wait()
     _decode(3, side, codes_ref, dec_ref, part_own_ref, part_oth_ref, 1)
-    dec_copies[1].wait()
     _decode(2, side, codes_ref, dec_ref, part_own_ref, part_oth_ref, 0)
-    dec_copies[0].wait()
 
 
 def _forward(own, oth, encoder, decoder, bias, active):
-    hbm = pl.BlockSpec(memory_space=HBM)
     return pl.pallas_call(
         _forward_kernel,
-        in_specs=[WHOLE, WHOLE, hbm, hbm, WHOLE, WHOLE],
-        out_specs=[WHOLE] * 6,
+        in_specs=[WHOLE] * 6,
+        out_specs=[WHOLE] * 5,
         out_shape=[
             jax.ShapeDtypeStruct((2, HALF, D), BF),
             jax.ShapeDtypeStruct((2, HALF, D), BF),
             jax.ShapeDtypeStruct((2, 2 * HALF, W), BF),
             jax.ShapeDtypeStruct((2, W, 2 * HALF), BF),
             jax.ShapeDtypeStruct((2, 2 * HALF, W), F32),
-            jax.ShapeDtypeStruct((PAIRS, W, D), BF),
         ],
-        scratch_shapes=[
-            pltpu.VMEM((2, D, W), BF),
-            pltpu.SemaphoreType.DMA((2,)),
-            pltpu.SemaphoreType.DMA((PAIRS,)),
-        ],
-        compiler_params=_params(10),
-        cost_estimate=pl.CostEstimate(
-            flops=2 * 5 * 256 * D * W,
-            bytes_accessed=(2 * D * W + PAIRS * W * D) * 2,
-            transcendentals=0,
+        compiler_params=_params(6),
+        cost_estimate=pl.CostEstimate(
+            flops=2 * 5 * 256 * D * W, bytes_accessed=2 * 256 * D * 2, transcendentals=0
         ),
         name="forward",
-    )(own, oth, _hbm(encoder), _hbm(decoder), bias, active)
+    )(own, oth, encoder, decoder, bias, active)
 
 
 def _forward_low_kernel(codes_ref, dec_ref, part_own_ref, part_oth_ref):
@@ -352,14 +334,14 @@
 
 
 def per_device(resid_in, resid_out, encoder, enc_bias, decoder, active):
+    enc, dec = (lax.ppermute(w, "core", [(0, 0), (1, 1)]) for w in (encoder, decoder))
     spread, *targets = _prepare(resid_in, resid_out)
     own = lax.all_to_all(spread, DP, 0, 0)
     oth = lax.ppermute(own, "core", SWAP)
     targets[1:], own = lax.optimization_barrier((targets[1:], own))
     targets = _around_y(targets)
-    part_own, part_oth, codes, turned, slope, dec = _forward(
-        own, oth, encoder, decoder, enc_bias, active
-    )
+    oth, targets, enc, dec = lax.optimization_barrier((oth, targets, enc, dec))
+    part_own, part_oth, codes, turned, slope = _forward(own, oth, enc, dec, enc_bias, active)
     got = lax.ppermute(part_oth, "core", SWAP)
     low_own, low_oth = _forward_low(codes, dec)
     got_low = lax.ppermute(low_oth, "core", SWAP)

time: 178 us -> 184 us (1.034)
  starting transfers between devices: 12.3 us -> 18.1 us
  Pallas kernels: 22.2 us -> 17.7 us
  waiting for transfers between devices: 8.14 us -> 12.2 us
    ppermute x0 -> x2, starting transfers between devices: none -> 5.66 us  [per_device(): lax.ppermute(w, 'core', [(0, 0), (1, 1)])]
    pallas_call x2, Pallas kernels: 9.49 us -> 5.05 us  [the longest x1 3.02 us: _forward(): pl.pallas_call(_forward_kernel, in_specs=[WHOLE] * 6, out_specs=[WHOLE] *...]
    ppermute x6, waiting for transfers between devices: 2.04 us -> 6.36 us  [_around_y(): lax.ppermute(pieces[j], 'y', [(i, (i + j) % 4) for i in range(4)])]
    ppermute x1, waiting for transfers between devices: 3.41 us -> 0.01 us  [per_device(): oth = lax.ppermute(own, 'core', SWAP)]
    ppermute x1, waiting for transfers between devices: 0.01 us -> 2 us  [per_device(): got = lax.ppermute(part_oth, 'core', SWAP)]
    ppermute x1, starting transfers between devices: 0.45 us -> 2.38 us  [per_device(): got = lax.ppermute(part_oth, 'core', SWAP)]
  transfers between devices with their start and end apart: 10 -> 12, of which waited for: 6 -> 9; matrix products, arithmetic and copies ran while one was open for 0% -> 0% of each run, Pallas kernels for 1% -> 2%
where the time goes in v5:
time: 184 us
  blocking collectives  135 us (73%)
  starting transfers between devices  18.1 us (10%)
  Pallas kernels  17.7 us (10%)
  waiting for transfers between devices  12.2 us (7%)
    all_to_all x1, blocking collectives, per_device(): pieces = lax.all_to_all(part.reshape(64, 8, D), GRID_AXES, 0, 0)  52.5 us
    all_to_all x1, blocking collectives, per_device(): err_own = lax.all_to_all(errors, GRID_AXES, 0, 0).reshape(LAYERS, HALF, D)  50 us
    all_to_all x1, blocking collectives, per_device(): own = lax.all_to_all(spread, DP, 0, 0)  32.4 us
    pallas_call x1, Pallas kernels, _backward(): pl.pallas_call(_backward_kernel, grid=(PAIRS + 2,), in_specs=[WHOLE] * 11...  9.55 us
    ppermute x6, waiting for transfers between devices, _around_y(): lax.ppermute(pieces[j], 'y', [(i, (i + j) % 4) for i in range(4)])  6.36 us
    ppermute x2, starting transfers between devices, per_device(): lax.ppermute(w, 'core', [(0, 0), (1, 1)])  5.66 us
    ppermute x6, starting transfers between devices, _around_y(): lax.ppermute(pieces[j], 'y', [(i, (i + j) % 4) for i in range(4)])  4.8 us
  transfers between devices with their start and end apart: 12, of which 9 were waited for; matrix products, arithmetic and copies ran while one was open for 0% of the time, Pallas kernels for 2%

profile of v5, /device:TPU:1, one launch (start us, length us, event | category | flops | bytes accessed | tf_op | source)
XLA Modules:
  0.0 183.7 jit_solution(1817551134430084304)
XLA Ops:
  0.6 0.0 copy-start
  0.6 0.0 copy-start.1
  0.7 3.6 %collective-permute-start.5 = (bf16[5,256,3584]{2,1,0:T(8,128)(2,1)}, bf16[5,256,3584]{2,1,0:T(8,128)(2,1)S(1)}, u32[]{:S(2)}, u32[]{:S(2)}) collective-permute-start(bf16[5,256,3584]{2,1,0:T(8,128)(2,1)} %param.10), channel_id=1, source_target_pairs={{0,0},{8,8},{1,1},{9,9},{2,2},{10,10},{3,3},{11,11},{4,4},{12,12},... | collective-permute-start | bytes 27525128 | tf_op jit(solution)/shard_map/ppermute | solution.py:337
  4.3 2.0 %collective-permute-start.4 = (bf16[2,3584,256]{2,1,0:T(8,128)(2,1)}, bf16[2,3584,256]{2,1,0:T(8,128)(2,1)S(1)}, u32[]{:S(2)}, u32[]{:S(2)}) collective-permute-start(bf16[2,3584,256]{2,1,0:T(8,128)(2,1)} %param.8), channel_id=1, source_target_pairs={{0,0},{8,8},{1,1},{9,9},{2,2},{10,10},{3,3},{11,11},{4,4},{12,12},... | collective-permute-start | bytes 11010056 | tf_op jit(solution)/shard_map/ppermute | solution.py:337
  6.3 2.0 %prepare.1 = (bf16[8,2,16,3584]{3,2,1,0:T(8,128)(2,1)S(1)}, bf16[2,3584]{1,0:T(2,128)(2,1)S(1)}, bf16[2,3584]{1,0:T(2,128)(2,1)S(1)}, bf16[2,3584]{1,0:T(2,128)(2,1)S(1)}, bf16[2,3584]{1,0:T(2,128)(2,1)S(1)}) custom-call(bf16[4,32,3584]{2,1,0:T(8,128)(2,1)} %in_hbm.1, bf16[4,2,3584]{2,1,0:T(2,128)(2,1)} %out_hbm.1), custom_call_target="tpu_custom_call" | custom-call | tf_op jit(solution)/shard_map/prepare/pallas_call | solution.py:78
  8.4 32.4 %all_to_all.15.own_ref.x_own_ref = bf16[8,2,16,3584]{3,2,1,0:T(8,128)(2,1)S(1)} all-to-all(bf16[8,2,16,3584]{3,2,1,0:T(8,128)(2,1)S(1)} %get-tuple-element.49), channel_id=1, replica_groups=mesh['x'=4,'zl'=2,'core'=2,'zh'=2,'y'=4] {'zh','y'}, dimensions={0} | all-to-all | bytes 3670016 | tf_op jit(solution)/shard_map/all_to_all | solution.py:339
  40.7 2.3 %collective-permute-start = (bf16[8,2,16,3584]{3,2,1,0:T(8,128)(2,1)S(1)}, bf16[8,2,16,3584]{3,2,1,0:T(8,128)(2,1)S(1)}, u32[]{:S(2)}, u32[]{:S(2)}) collective-permute-start(bf16[8,2,16,3584]{3,2,1,0:T(8,128)(2,1)S(1)} %all_to_all.15.own_ref.x_own_ref), channel_id=1, source_target_pairs={{0,8},{8,0},{1,9},{9,1},{2,10},{10,2},{3,11},{11,3},{4,12},{12,4},... | collective-permute-start | bytes 5505032 | tf_op jit(solution)/shard_map/ppermute | solution.py:340
  43.1 0.6 collective-permute-start.1
  43.7 1.4 collective-permute-start.2
  45.1 1.8 collective-permute-done.1.rest_1_
  46.9 0.0 collective-permute-start.3
  46.9 0.9 collective-permute-done.2.rest_2_
  47.8 1.7 collective-permute-done.3.rest_3_
  49.4 0.0 collective-permute-done.oth_ref.x_oth_ref
  49.4 0.0 collective-permute-done.4.enc_ref
  49.4 0.0 collective-permute-done.5.dec_ref
  49.4 0.0 copy-done
  49.4 0.0 copy-done.1
  49.5 3.0 %forward.1 = (bf16[2,128,3584]{2,1,0:T(8,128)(2,1)S(1)}, bf16[2,128,3584]{2,1,0:T(8,128)(2,1)S(1)}, bf16[2,256,256]{2,1,0:T(8,128)(2,1)S(1)}, bf16[2,256,256]{2,1,0:T(8,128)(2,1)S(1)}, f32[2,256,256]{2,1,0:T(8,128)S(1)}) custom-call(bf16[8,2,16,3584]{3,2,1,0:T(8,128)(2,1)S(1)} %all_to_all.15.own_ref.x_own_ref, ...), custom_call_target="tpu_custom_call" | custom-call | flops 2348810240 | bytes 3670016 | tf_op jit(solution)/shard_map/forward/pallas_call | solution.py:156
  52.5 2.4 %collective-permute-start.7 = (bf16[2,128,3584]{2,1,0:T(8,128)(2,1)S(1)}, bf16[2,128,3584]{2,1,0:T(8,128)(2,1)S(1)}, u32[]{:S(2)}, u32[]{:S(2)}) collective-permute-start(bf16[2,128,3584]{2,1,0:T(8,128)(2,1)S(1)} %get-tuple-element.64), channel_id=1, source_target_pairs={{0,8},{8,0},{1,9},{9,1},{2,10},{10,2},{3,11},{11,3},{4,12},{12,4},... | collective-permute-start | bytes 5505032 | tf_op jit(solution)/shard_map/ppermute | solution.py:345
  54.9 1.3 forward_low.1
  56.2 0.1 collective-permute-start.6
  56.3 2.0 %collective-permute-done.7.got_ref = bf16[2,128,3584]{2,1,0:T(8,128)(2,1)S(1)} collective-permute-done((bf16[2,128,3584]{2,1,0:T(8,128)(2,1)S(1)}, bf16[2,128,3584]{2,1,0:T(8,128)(2,1)S(1)}, u32[]{:S(2)}, u32[]{:S(2)}) %collective-permute-start.7) | collective-permute-done | bytes 1835040 | tf_op jit(solution)/shard_map/ppermute | solution.py:345
  58.3 2.6 %collective-permute-done.6.got_low_ref = bf16[2,128,3584]{2,1,0:T(8,128)(2,1)S(1)} collective-permute-done((bf16[2,128,3584]{2,1,0:T(8,128)(2,1)S(1)}, bf16[2,128,3584]{2,1,0:T(8,128)(2,1)S(1)}, u32[]{:S(2)}, u32[]{:S(2)}) %collective-permute-start.6) | collective-permute-done | bytes 1835040 | tf_op jit(solution)/shard_map/ppermute | solution.py:347
  60.9 0.8 join.1
  61.7 52.5 %all_to_all.16.pieces_ref = bf16[64,8,3584]{2,1,0:T(8,128)(2,1)S(1)} all-to-all(bf16[64,8,3584]{2,1,0:T(8,128)(2,1)S(1)} %bitcast.4), channel_id=1, replica_groups=mesh['x'=4,'zl'=2,'core'=2,'zh'=2,'y'=4] {'y','x','zl','zh'}, dimensions={0} | all-to-all | bytes 7340032 | tf_op jit(solution)/shard_map/all_to_all | solution.py:350
  114.3 1.0 settle.1
  115.2 50.0 %all_to_all.17 = bf16[64,8,3584]{2,1,0:T(8,128)(2,1)S(1)} all-to-all(bf16[64,8,3584]{2,1,0:T(8,128)(2,1)S(1)} %get-tuple-element.78), channel_id=1, replica_groups=mesh['x'=4,'zl'=2,'core'=2,'zh'=2,'y'=4] {'y','x','zl','zh'}, dimensions={0} | all-to-all | bytes 7340032 | tf_op jit(solution)/shard_map/all_to_all | solution.py:352
  165.3 2.8 %collective-permute-start.8 = (bf16[4,128,3584]{2,1,0:T(8,128)(2,1)S(1)}, bf16[4,128,3584]{2,1,0:T(8,128)(2,1)S(1)}, u32[]{:S(2)}, u32[]{:S(2)}) collective-permute-start(bf16[4,128,3584]{2,1,0:T(8,128)(2,1)S(1)} %bitcast.2), channel_id=1, source_target_pairs={{0,8},{8,0},{1,9},{9,1},{2,10},{10,2},{3,11},{11,3},{4,12},{12,4},... | collective-permute-start | bytes 11010056 | tf_op jit(solution)/shard_map/ppermute | solution.py:353
  168.1 0.4 collective-permute-start.9
  168.5 1.6 collective-permute-start.10
  170.1 0.8 collective-permute-start.11
  170.9 1.0 collective-permute-done.9.rest_1_
  171.9 0.7 collective-permute-done.10.rest_2_
  172.6 0.4 collective-permute-done.11.rest_3_
  172.9 1.2 collective-permute-done.8.oth_ref
  174.1 9.5 %backward.1 = (bf16[5,256,3584]{2,1,0:T(8,128)(2,1)}, bf16[2,3584,256]{2,1,0:T(8,128)(2,1)}, f32[2,256]{1,0:T(2,128)}, bf16[4,2,3584]{2,1,0:T(2,128)(2,1)}) custom-call(bf16[2,256,256]{2,1,0:T(8,128)(2,1)S(1)} %get-tuple-element.58.turned_ref, f32[2,256,256]{2,1,0:T(8,128)S(1)} %get-tuple-element.59.slope_ref, bf16[4,128,3584]{2,1,0:T(8,128)(2,1)S(1)} %bitcast.3, ...), custom_call_target="tpu_custom_call" | custom-call | flops 5637144576 | bytes 12845056 | tf_op jit(solution)/shard_map/backward/pallas_call | solution.py:303
Async XLA Ops:
  0.6 48.8 %copy-start = (s32[4,8,32]{2,1,0:T(8,128)S(1)}, s32[4,8,32]{2,1,0:T(8,128)}, u32[]{:S(2)}) copy-start(s32[4,8,32]{2,1,0:T(8,128)} %active_ref.1) | copy-start | bytes 12292
  0.6 48.8 %copy-start.1 = (f32[2,256]{1,0:T(2,128)S(1)}, f32[2,256]{1,0:T(2,128)}, u32[]{:S(2)}) copy-start(f32[2,256]{1,0:T(2,128)} %bias_ref.1) | copy-start | bytes 6148
  0.7 48.8 %collective-permute-start.5 = (bf16[5,256,3584]{2,1,0:T(8,128)(2,1)}, bf16[5,256,3584]{2,1,0:T(8,128)(2,1)S(1)}, u32[]{:S(2)}, u32[]{:S(2)}) collective-permute-start(bf16[5,256,3584]{2,1,0:T(8,128)(2,1)} %param.10), channel_id=1, source_target_pairs={{0,0},{8,8},{1,1},{9,9},{2,2},{10,10},{3,3},{11,11},{4,4},{12,12},... | collective-permute-start | bytes 27525128 | tf_op jit(solution)/shard_map/ppermute | solution.py:337
  4.3 45.2 %collective-permute-start.4 = (bf16[2,3584,256]{2,1,0:T(8,128)(2,1)}, bf16[2,3584,256]{2,1,0:T(8,128)(2,1)S(1)}, u32[]{:S(2)}, u32[]{:S(2)}) collective-permute-start(bf16[2,3584,256]{2,1,0:T(8,128)(2,1)} %param.8), channel_id=1, source_target_pairs={{0,0},{8,8},{1,1},{9,9},{2,2},{10,10},{3,3},{11,11},{4,4},{12,12},... | collective-permute-start | bytes 11010056 | tf_op jit(solution)/shard_map/ppermute | solution.py:337
  40.7 8.7 %collective-permute-start = (bf16[8,2,16,3584]{3,2,1,0:T(8,128)(2,1)S(1)}, bf16[8,2,16,3584]{3,2,1,0:T(8,128)(2,1)S(1)}, u32[]{:S(2)}, u32[]{:S(2)}) collective-permute-start(bf16[8,2,16,3584]{3,2,1,0:T(8,128)(2,1)S(1)} %all_to_all.15.own_ref.x_own_ref), channel_id=1, source_target_pairs={{0,8},{8,0},{1,9},{9,1},{2,10},{10,2},{3,11},{11,3},{4,12},{12,4},... | collective-permute-start | bytes 5505032 | tf_op jit(solution)/shard_map/ppermute | solution.py:340
  43.1 3.8 %collective-permute-start.1 = (bf16[2,3584]{1,0:T(2,128)(2,1)S(1)}, bf16[2,3584]{1,0:T(2,128)(2,1)S(1)}, u32[]{:S(2)}, u32[]{:S(2)}) collective-permute-start(bf16[2,3584]{1,0:T(2,128)(2,1)S(1)} %get-tuple-element.52), channel_id=1, source_target_pairs={{0,1},{1,2},{2,3},{3,0},{4,5},{5,6},{6,7},{7,4},{8,9},{9,10},{10,1... | collective-permute-start | bytes 43016 | tf_op jit(solution)/shard_map/ppermute | solution.py:332
  43.7 4.1 %collective-permute-start.2 = (bf16[2,3584]{1,0:T(2,128)(2,1)S(1)}, bf16[2,3584]{1,0:T(2,128)(2,1)S(1)}, u32[]{:S(2)}, u32[]{:S(2)}) collective-permute-start(bf16[2,3584]{1,0:T(2,128)(2,1)S(1)} %get-tuple-element.53), channel_id=1, source_target_pairs={{0,2},{1,3},{2,0},{3,1},{4,6},{5,7},{6,4},{7,5},{8,10},{9,11},{10,... | collective-permute-start | bytes 43016 | tf_op jit(solution)/shard_map/ppermute | solution.py:332
  46.9 2.6 %collective-permute-start.3 = (bf16[2,3584]{1,0:T(2,128)(2,1)S(1)}, bf16[2,3584]{1,0:T(2,128)(2,1)S(1)}, u32[]{:S(2)}, u32[]{:S(2)}) collective-permute-start(bf16[2,3584]{1,0:T(2,128)(2,1)S(1)} %get-tuple-element.54), channel_id=1, source_target_pairs={{0,3},{1,0},{2,1},{3,2},{4,7},{5,4},{6,5},{7,6},{8,11},{9,8},{10,9... | collective-permute-start | bytes 43016 | tf_op jit(solution)/shard_map/ppermute | solution.py:332
  52.5 5.8 %collective-permute-start.7 = (bf16[2,128,3584]{2,1,0:T(8,128)(2,1)S(1)}, bf16[2,128,3584]{2,1,0:T(8,128)(2,1)S(1)}, u32[]{:S(2)}, u32[]{:S(2)}) collective-permute-start(bf16[2,128,3584]{2,1,0:T(8,128)(2,1)S(1)} %get-tuple-element.64), channel_id=1, source_target_pairs={{0,8},{8,0},{1,9},{9,1},{2,10},{10,2},{3,11},{11,3},{4,12},{12,4},... | collective-permute-start | bytes 5505032 | tf_op jit(solution)/shard_map/ppermute | solution.py:345
  56.2 4.7 %collective-permute-start.6 = (bf16[2,128,3584]{2,1,0:T(8,128)(2,1)S(1)}, bf16[2,128,3584]{2,1,0:T(8,128)(2,1)S(1)}, u32[]{:S(2)}, u32[]{:S(2)}) collective-permute-start(bf16[2,128,3584]{2,1,0:T(8,128)(2,1)S(1)} %get-tuple-element.63), channel_id=1, source_target_pairs={{0,8},{8,0},{1,9},{9,1},{2,10},{10,2},{3,11},{11,3},{4,12},{12,4},... | collective-permute-start | bytes 5505032 | tf_op jit(solution)/shard_map/ppermute | solution.py:347
  165.3 8.8 %collective-permute-start.8 = (bf16[4,128,3584]{2,1,0:T(8,128)(2,1)S(1)}, bf16[4,128,3584]{2,1,0:T(8,128)(2,1)S(1)}, u32[]{:S(2)}, u32[]{:S(2)}) collective-permute-start(bf16[4,128,3584]{2,1,0:T(8,128)(2,1)S(1)} %bitcast.2), channel_id=1, source_target_pairs={{0,8},{8,0},{1,9},{9,1},{2,10},{10,2},{3,11},{11,3},{4,12},{12,4},... | collective-permute-start | bytes 11010056 | tf_op jit(solution)/shard_map/ppermute | solution.py:353
  168.1 3.8 %collective-permute-start.9 = (bf16[2,3584]{1,0:T(2,128)(2,1)S(1)}, bf16[2,3584]{1,0:T(2,128)(2,1)S(1)}, u32[]{:S(2)}, u32[]{:S(2)}) collective-permute-start(bf16[2,3584]{1,0:T(2,128)(2,1)S(1)} %get-tuple-element.81), channel_id=1, source_target_pairs={{0,1},{1,2},{2,3},{3,0},{4,5},{5,6},{6,7},{7,4},{8,9},{9,10},{10,1... | collective-permute-start | bytes 43016 | tf_op jit(solution)/shard_map/ppermute | solution.py:332
  168.5 4.1 %collective-permute-start.10 = (bf16[2,3584]{1,0:T(2,128)(2,1)S(1)}, bf16[2,3584]{1,0:T(2,128)(2,1)S(1)}, u32[]{:S(2)}, u32[]{:S(2)}) collective-permute-start(bf16[2,3584]{1,0:T(2,128)(2,1)S(1)} %get-tuple-element.82), channel_id=1, source_target_pairs={{0,2},{1,3},{2,0},{3,1},{4,6},{5,7},{6,4},{7,5},{8,10},{9,11},{10,... | collective-permute-start | bytes 43016 | tf_op jit(solution)/shard_map/ppermute | solution.py:332
  170.1 2.9 %collective-permute-start.11 = (bf16[2,3584]{1,0:T(2,128)(2,1)S(1)}, bf16[2,3584]{1,0:T(2,128)(2,1)S(1)}, u32[]{:S(2)}, u32[]{:S(2)}) collective-permute-start(bf16[2,3584]{1,0:T(2,128)(2,1)S(1)} %get-tuple-element.83), channel_id=1, source_target_pairs={{0,3},{1,0},{2,1},{3,2},{4,7},{5,4},{6,5},{7,6},{8,11},{9,8},{10,9... | collective-permute-start | bytes 43016 | tf_op jit(solution)/shard_map/ppermute | solution.py:332

commit v6 on v4

--- a/solution.py
+++ b/solution.py
@@ -1,3 +1,5 @@
+import functools
+
 import jax
 import jax.numpy as jnp
 from jax import lax
@@ -15,12 +17,46 @@
 TILES = 8
 HROW = 16
 PAIRS = 5
-GRID_AXES = ("y", "x", "zl", "zh")
 DP = ("zh", "y")
 ALL = ("x", "zl", "core", "zh", "y")
 BF = jnp.bfloat16
 F32 = jnp.float32
 SWAP = [(0, 1), (1, 0)]
+QUARTER = 128
+BOX = 32
+
+
+def _rank(x, zl, core, zh, y):
+    return (((x * 2 + zl) * 2 + core) * 2 + zh) * 4 + y
+
+
+def _pairs(move):
+    return [
+        (_rank(x, zl, core, zh, y), _rank(*move(x, zl, core, zh, y)))
+        for x in range(4)
+        for zl in range(2)
+        for core in range(2)
+        for zh in range(2)
+        for y in range(4)
+    ]
+
+
+def _ring(flip):
+    return _pairs(
+        lambda x, zl, core, zh, y: (x ^ (flip * core), zl, core, zh, y ^ (flip * (1 - core)))
+    )
+
+
+RING = {flip: _ring(flip) for flip in (1, 3)}
+ALONG_Y = {
+    flip: _pairs(lambda x, zl, core, zh, y, flip=flip: (x, zl, core, zh, y ^ flip)) for flip in (1, 3)
+}
+ACROSS = _pairs(lambda x, zl, core, zh, y: (x, zl, core, zh ^ 1, y))
+GROUPS = [
+    [_rank(x, zl, 0, zh, y) for x in range(4) for zl in range(2) for zh in range(2)] for y in range(4)
+] + [
+    [_rank(x, zl, 1, zh, y) for y in range(4) for zl in range(2) for zh in range(2)] for x in range(4)
+]
 
 VMEM = pltpu.MemorySpace.VMEM
 HBM = pltpu.MemorySpace.HBM
@@ -49,23 +85,19 @@
     return lax.axis_index("x") // 2
 
 
-def _prepare_kernel(in_hbm, out_ref, spread_ref, *rest):
+def _prepare_kernel(in_hbm, out_hbm, mine_ref, *rest):
     piece_refs, sem = rest[:4], rest[4]
     side, core, y = _side(), lax.axis_index("core"), lax.axis_index("y")
-    copies = []
-    for k, layer in enumerate((side, LAYERS - 1 - side)):
-        for i in range(TILES):
-            copies.append(
-                pltpu.make_async_copy(
-                    in_hbm.at[layer, pl.ds(pl.multiple_of(core * HROW, HROW), HROW)],
-                    spread_ref.at[i, k],
-                    sem.at[k * TILES + i],
-                )
-            )
+    rows = pl.ds(pl.multiple_of(core * HROW, HROW), HROW)
+    copies = [
+        pltpu.make_async_copy(in_hbm.at[layer, rows], mine_ref.at[k], sem.at[k])
+        for k, layer in enumerate((side, LAYERS - 1 - side))
+    ] + [
+        pltpu.make_async_copy(out_hbm.at[lax.rem(y + j, 4)], piece_refs[j], sem.at[2 + j])
+        for j in range(4)
+    ]
     for copy in copies:
         copy.start()
-    for j in range(4):
-        piece_refs[j][...] = out_ref[lax.rem(y + j, 4)]
     for copy in copies:
         copy.wait()
 
@@ -73,14 +105,59 @@
 def _prepare(resid_in, resid_out):
     return pl.pallas_call(
         _prepare_kernel,
-        in_specs=[pl.BlockSpec(memory_space=HBM), WHOLE],
+        in_specs=[pl.BlockSpec(memory_space=HBM)] * 2,
         out_specs=[WHOLE] * 5,
-        out_shape=[jax.ShapeDtypeStruct((TILES, 2, HROW, D), BF)]
-        + [jax.ShapeDtypeStruct((2, D), BF)] * 4,
-        scratch_shapes=[pltpu.SemaphoreType.DMA((2 * TILES,))],
+        out_shape=[jax.ShapeDtypeStruct((2, HROW, D), BF)] + [jax.ShapeDtypeStruct((2, D), BF)] * 4,
+        scratch_shapes=[pltpu.SemaphoreType.DMA((6,))],
         compiler_params=_params(2),
         name="prepare",
-    )(_hbm(resid_in), resid_out)
+    )(_hbm(resid_in), _hbm(resid_out))
+
+
+def _plain(kernel, out_shape, name, *operands, scratch=(), alias=None):
+    return pl.pallas_call(
+        kernel,
+        in_specs=[WHOLE] * len(operands),
+        out_specs=jax.tree.map(lambda _: WHOLE, out_shape),
+        out_shape=out_shape,
+        scratch_shapes=scratch,
+        input_output_aliases=alias or {},
+        compiler_params=_params(4),
+        name=name,
+    )(*operands)
+
+
+TILE_FROM = ((0, 0), (0, 1), (0, 3), (0, 2), (1, 0), (1, 1), (1, 3), (1, 2))
+
+
+def _arrange_kernel(*refs):
+    zh, y = lax.axis_index("zh"), lax.axis_index("y")
+    for piece_ref, (across, flip) in zip(refs[:TILES], TILE_FROM):
+        tile = lax.rem(zh + across, 2) * 4 + lax.bitwise_xor(y, flip)
+        refs[TILES][tile] = piece_ref[...]
+
+
+def _gather_inputs(mine):
+    far = lax.ppermute(mine, ALL, ACROSS)
+    mine_1, mine_3 = (lax.ppermute(mine, ALL, ALONG_Y[flip]) for flip in (1, 3))
+    far_3, far_1 = (lax.ppermute(far, ALL, ALONG_Y[flip]) for flip in (3, 1))
+    mine_2 = lax.ppermute(mine_1, ALL, ALONG_Y[3])
+    far_2 = lax.ppermute(far_3, ALL, ALONG_Y[1])
+    return _plain(
+        _arrange_kernel,
+        jax.ShapeDtypeStruct((TILES, 2, HROW, D), BF),
+        "arrange",
+        mine, mine_1, mine_3, mine_2, far, far_1, far_3, far_2,
+    )
+
+
+def _place(quarter, i):
+    core = lax.axis_index("core")
+    return jnp.where(core == 0, quarter, i), jnp.where(core == 0, i, quarter)
+
+
+def _me():
+    return jnp.where(lax.axis_index("core") == 0, lax.axis_index("y"), lax.axis_index("x"))
 
 
 def _decode(t, side, codes_ref, dec_ref, own_ref, oth_ref, at):
@@ -209,24 +286,89 @@
     )(codes, dec)
 
 
-def _join_kernel(own_low_ref, own_ref, got_low_ref, got_ref, out_ref):
-    for t in range(2):
-        out_ref[t] = (own_low_ref[t].astype(F32) + got_low_ref[t].astype(F32)).astype(BF)
-        out_ref[2 + t] = (own_ref[t].astype(F32) + got_ref[t].astype(F32)).astype(BF)
-
-
-def _join(*parts):
-    return pl.pallas_call(
+def _join_kernel(
+    own_low_ref, own_ref, got_low_ref, got_ref, mine_ref, to1_ref, to3_ref, far1_ref, far3_ref
+):
+    outs = {0: (mine_ref, mine_ref), 1: (to1_ref, to1_ref), 3: (to3_ref, to3_ref), 2: (far1_ref, far3_ref)}
+    for flip, (first_ref, second_ref) in outs.items():
+        for i in range(4):
+            t, x = _place(lax.bitwise_xor(_me(), flip), i)
+            rows = pl.ds(pl.multiple_of(x * BOX, BOX), BOX)
+            out_ref = first_ref if i < 2 else second_ref
+            at = (i % 2 if flip == 2 else i) * BOX
+
+            def add(one_ref, two_ref, index, out_ref=out_ref, at=at, rows=rows):
+                value = one_ref[index, rows].astype(F32) + two_ref[index, rows].astype(F32)
+                out_ref[at : at + BOX] = value.astype(out_ref.dtype)
+
+            @pl.when(t < 2)
+            def _(add=add, t=t):
+                add(own_low_ref, got_low_ref, jnp.minimum(t, 1))
+
+            @pl.when(t >= 2)
+            def _(add=add, t=t):
+                add(own_ref, got_ref, jnp.maximum(t - 2, 0))
+
+
+def _fold_kernel(at, quarter_ref, got_ref, out_ref):
+    rows = slice(at, at + QUARTER // 2)
+    out_ref[rows] = (quarter_ref[rows].astype(F32) + got_ref[...].astype(F32)).astype(BF)
+
+
+def _total_kernel(mine_ref, one_ref, three_ref, out_ref):
+    out_ref[...] = (
+        mine_ref[...] + one_ref[...].astype(F32) + three_ref[...].astype(F32)
+    ).astype(BF)
+
+
+def _reduce_ring(parts):
+    quarter = jax.ShapeDtypeStruct((QUARTER, D), BF)
+    half = jax.ShapeDtypeStruct((QUARTER // 2, D), BF)
+    mine, to1, to3, far1, far3 = _plain(
         _join_kernel,
-        in_specs=[WHOLE] * 4,
-        out_specs=WHOLE,
-        out_shape=jax.ShapeDtypeStruct((LAYERS, HALF, D), BF),
-        compiler_params=_params(4),
-        cost_estimate=pl.CostEstimate(
-            flops=4 * HALF * D, bytes_accessed=3 * 4 * HALF * D * 2, transcendentals=0
-        ),
-        name="join",
-    )(*parts)
+        [jax.ShapeDtypeStruct((QUARTER, D), F32), quarter, quarter, half, half],
+        "join",
+        *parts,
+    )
+    got1 = lax.ppermute(far1, ALL, RING[1])
+    got3 = lax.ppermute(far3, ALL, RING[3])
+    to3 = _plain(functools.partial(_fold_kernel, 0), quarter, "fold_low", to3, got1, alias={0: 0})
+    from3 = lax.ppermute(to3, ALL, RING[3])
+    to1 = _plain(
+        functools.partial(_fold_kernel, QUARTER // 2), quarter, "fold_high", to1, got3, alias={0: 0}
+    )
+    from1 = lax.ppermute(to1, ALL, RING[1])
+    return _plain(_total_kernel, quarter, "total", mine, from1, from3)
+
+
+def _half_kernel(at, quarter_ref, out_ref):
+    out_ref[...] = quarter_ref[at : at + QUARTER // 2]
+
+
+def _assemble_kernel(mine_ref, one_ref, three_ref, far1_ref, far3_ref, out_ref):
+    refs = {0: (mine_ref, mine_ref), 1: (one_ref, one_ref), 3: (three_ref, three_ref), 2: (far1_ref, far3_ref)}
+    for flip, (first_ref, second_ref) in refs.items():
+        for i in range(4):
+            t, x = _place(lax.bitwise_xor(_me(), flip), i)
+            in_ref = first_ref if i < 2 else second_ref
+            at = (i % 2 if flip == 2 else i) * BOX
+            out_ref[t, pl.ds(pl.multiple_of(x * BOX, BOX), BOX)] = in_ref[at : at + BOX]
+
+
+def _gather_ring(quarter):
+    half = jax.ShapeDtypeStruct((QUARTER // 2, D), BF)
+    one = lax.ppermute(quarter, ALL, RING[1])
+    three = lax.ppermute(quarter, ALL, RING[3])
+    pass3 = _plain(functools.partial(_half_kernel, 0), half, "half_low", one)
+    far1 = lax.ppermute(pass3, ALL, RING[3])
+    pass1 = _plain(functools.partial(_half_kernel, QUARTER // 2), half, "half_high", three)
+    far3 = lax.ppermute(pass1, ALL, RING[1])
+    return _plain(
+        _assemble_kernel,
+        jax.ShapeDtypeStruct((LAYERS, HALF, D), BF),
+        "assemble",
+        quarter, one, three, far1, far3,
+    )
 
 
 def _settle_kernel(pieces_ref, *rest):
@@ -239,7 +381,7 @@
     for j in range(4):
         rows_ref[2 * j : 2 * j + 2] = turn_ref[j]
     summed = lax.fori_loop(
-        0, 64, lambda i, acc: acc + pieces_ref[i].astype(F32), jnp.zeros((8, D), F32), unroll=8
+        0, 16, lambda i, acc: acc + pieces_ref[i].astype(F32), jnp.zeros((8, D), F32), unroll=8
     )
     errors = (summed - rows_ref[...]).astype(BF)
     rows_ref[...] = summed
@@ -252,7 +394,7 @@
         errors_ref[i] = errors
         return carry
 
-    lax.fori_loop(0, 64, spread, 0, unroll=8)
+    lax.fori_loop(0, 16, spread, 0, unroll=8)
 
 
 def _settle(pieces, targets):
@@ -260,12 +402,12 @@
         _settle_kernel,
         in_specs=[WHOLE] * 5,
         out_specs=[WHOLE] * 5,
-        out_shape=[jax.ShapeDtypeStruct((64, 8, D), BF)]
+        out_shape=[jax.ShapeDtypeStruct((16, 8, D), BF)]
         + [jax.ShapeDtypeStruct((2, D), BF)] * 4,
         scratch_shapes=[pltpu.VMEM((8, D), F32), pltpu.VMEM((4, 2, D), F32)],
         compiler_params=_params(4),
         cost_estimate=pl.CostEstimate(
-            flops=64 * 8 * D, bytes_accessed=2 * 64 * 8 * D * 2, transcendentals=0
+            flops=16 * 8 * D, bytes_accessed=2 * 16 * 8 * D * 2, transcendentals=0
         ),
         name="settle",
     )(pieces, *targets)
@@ -352,8 +494,8 @@
 
 
 def per_device(resid_in, resid_out, encoder, enc_bias, decoder, active):
-    spread, *targets = _prepare(resid_in, resid_out)
-    own = lax.all_to_all(spread, DP, 0, 0)
+    mine, *targets = _prepare(resid_in, resid_out)
+    own = _gather_inputs(mine)
     oth = lax.ppermute(own, "core", SWAP)
     targets[1:], own = lax.optimization_barrier((targets[1:], own))
     targets = _around_y(targets)
@@ -363,11 +505,13 @@
     got = lax.ppermute(part_oth, "core", SWAP)
     low_own, low_oth = _forward_low(codes, dec)
     got_low = lax.ppermute(low_oth, "core", SWAP)
-    part = _join(low_own, part_own, got_low, got)
-    part, targets = lax.optimization_barrier((part, targets))
-    pieces = lax.all_to_all(part.reshape(64, 8, D), GRID_AXES, 0, 0)
+    quarter = _reduce_ring((low_own, part_own, got_low, got))
+    quarter, targets = lax.optimization_barrier((quarter, targets))
+    pieces = lax.all_to_all(quarter.reshape(16, 8, D), ALL, 0, 0, axis_index_groups=GROUPS)
     errors, *recon = _settle(pieces, targets)
-    err_own = lax.all_to_all(errors, GRID_AXES, 0, 0).reshape(LAYERS, HALF, D)
+    quarter = lax.all_to_all(errors, ALL, 0, 0, axis_index_groups=GROUPS).reshape(QUARTER, D)
+    quarter, recon = lax.optimization_barrier((quarter, recon))
+    err_own = _gather_ring(quarter)
     err_oth = lax.ppermute(err_own, "core", SWAP)
     recon, err_own = lax.optimization_barrier((recon, err_own))
     recon = _around_y(recon)

time: 178 us -> 154 us (0.87)
  blocking collectives: 134 us -> 36.6 us
  waiting for transfers between devices: 8.14 us -> 59 us
  starting transfers between devices: 12.3 us -> 35.3 us
    all_to_all x3 -> x2, blocking collectives: 134 us -> 36.6 us  [the longest x1 18.6 us: per_device(): lax.all_to_all(quarter.reshape(16, 8, D), ALL, 0, 0, axis_index_groups=GR...]
    ppermute x0 -> x15, waiting for transfers between devices: none -> 48.4 us  [the longest x1 12.5 us: _gather_ring(): three = lax.ppermute(quarter, ALL, RING[3])]
    ppermute x0 -> x15, starting transfers between devices: none -> 20.6 us  [the longest x1 4.51 us: _gather_inputs(): far = lax.ppermute(mine, ALL, ACROSS)]
    ppermute x1, waiting for transfers between devices: 0.01 us -> 1.9 us  [per_device(): got = lax.ppermute(part_oth, 'core', SWAP)]
    pallas_call x2 -> x9, Pallas kernels: 2.81 us -> 3.76 us  [the longest x8 2.72 us: _plain(): pl.pallas_call(kernel, in_specs=[WHOLE] * len(operands), out_specs=jax.tr...]
  transfers between devices with their start and end apart: 10 -> 25, of which waited for: 6 -> 17; matrix products, arithmetic and copies ran while one was open for 0% -> 0% of each run, Pallas kernels for 1% -> 2%
where the time goes in v6:
time: 154 us
  waiting for transfers between devices  59 us (38%)
  blocking collectives  36.6 us (24%)
  starting transfers between devices  35.3 us (23%)
  Pallas kernels  22.5 us (15%)
    all_to_all x1, blocking collectives, per_device(): lax.all_to_all(quarter.reshape(16, 8, D), ALL, 0, 0, axis_index_groups=GR...  18.6 us
    all_to_all x1, blocking collectives, per_device(): lax.all_to_all(errors, ALL, 0, 0, axis_index_groups=GROUPS)  17.9 us
    ppermute x1, waiting for transfers between devices, _gather_ring(): three = lax.ppermute(quarter, ALL, RING[3])  12.5 us
    pallas_call x1, Pallas kernels, _backward(): pl.pallas_call(_backward_kernel, grid=(PAIRS + 2,), in_specs=[WHOLE] * 11...  9.6 us
    pallas_call x1, Pallas kernels, _forward(): pl.pallas_call(_forward_kernel, in_specs=[WHOLE, WHOLE, hbm, hbm, WHOLE,...  7.5 us
    ppermute x6, starting transfers between devices, _around_y(): lax.ppermute(pieces[j], 'y', [(i, (i + j) % 4) for i in range(4)])  7.31 us
    ppermute x1, waiting for transfers between devices, _reduce_ring(): from3 = lax.ppermute(to3, ALL, RING[3])  6.7 us
    ppermute x1, waiting for transfers between devices, _gather_ring(): far3 = lax.ppermute(pass1, ALL, RING[1])  6.16 us
  transfers between devices with their start and end apart: 25, of which 17 were waited for; matrix products, arithmetic and copies ran while one was open for 0% of the time, Pallas kernels for 2%

profile of v6, /device:TPU:1, one launch (start us, length us, event | category | flops | bytes accessed | tf_op | source)
XLA Modules:
  0.0 154.1 jit_solution(5457421821632389680)
XLA Ops:
  0.6 1.0 prepare.1
  1.7 4.5 %collective-permute-start.3 = (bf16[2,16,3584]{2,1,0:T(8,128)(2,1)S(1)}, bf16[2,16,3584]{2,1,0:T(8,128)(2,1)S(1)}, u32[]{:S(2)}, u32[]{:S(2)}) collective-permute-start(bf16[2,16,3584]{2,1,0:T(8,128)(2,1)S(1)} %get-tuple-element.53.refs_0_), channel_id=1, source_target_pairs={{0,4},{1,5},{2,6},{3,7},{4,0},{5,1},{6,2},{7,3},{8,12},{9,13},{10,... | collective-permute-start | bytes 688136 | tf_op jit(solution)/shard_map/ppermute | solution.py:141
  6.2 1.3 collective-permute-start
  7.5 4.0 %collective-permute-done.3.refs_4_ = bf16[2,16,3584]{2,1,0:T(8,128)(2,1)S(1)} collective-permute-done((bf16[2,16,3584]{2,1,0:T(8,128)(2,1)S(1)}, bf16[2,16,3584]{2,1,0:T(8,128)(2,1)S(1)}, u32[]{:S(2)}, u32[]{:S(2)}) %collective-permute-start.3) | collective-permute-done | bytes 229408 | tf_op jit(solution)/shard_map/ppermute | solution.py:141
  11.5 2.7 %collective-permute-start.5 = (bf16[2,16,3584]{2,1,0:T(8,128)(2,1)S(1)}, bf16[2,16,3584]{2,1,0:T(8,128)(2,1)S(1)}, u32[]{:S(2)}, u32[]{:S(2)}) collective-permute-start(bf16[2,16,3584]{2,1,0:T(8,128)(2,1)S(1)} %collective-permute-done.3.refs_4_), channel_id=1, source_target_pairs={{0,3},{1,2},{2,1},{3,0},{4,7},{5,6},{6,5},{7,4},{8,11},{9,10},{10,... | collective-permute-start | bytes 688136 | tf_op jit(solution)/shard_map/ppermute | solution.py:143
  14.3 2.6 %collective-permute-start.2 = (bf16[2,16,3584]{2,1,0:T(8,128)(2,1)S(1)}, bf16[2,16,3584]{2,1,0:T(8,128)(2,1)S(1)}, u32[]{:S(2)}, u32[]{:S(2)}) collective-permute-start(bf16[2,16,3584]{2,1,0:T(8,128)(2,1)S(1)} %collective-permute-done.refs_1_), channel_id=1, source_target_pairs={{0,3},{1,2},{2,1},{3,0},{4,7},{5,6},{6,5},{7,4},{8,11},{9,10},{10,... | collective-permute-start | bytes 688136 | tf_op jit(solution)/shard_map/ppermute | solution.py:144
  17.0 1.8 %collective-permute-done.5.refs_6_ = bf16[2,16,3584]{2,1,0:T(8,128)(2,1)S(1)} collective-permute-done((bf16[2,16,3584]{2,1,0:T(8,128)(2,1)S(1)}, bf16[2,16,3584]{2,1,0:T(8,128)(2,1)S(1)}, u32[]{:S(2)}, u32[]{:S(2)}) %collective-permute-start.5) | collective-permute-done | bytes 229408 | tf_op jit(solution)/shard_map/ppermute | solution.py:143
  18.7 4.9 %collective-permute-done.1.refs_2_ = bf16[2,16,3584]{2,1,0:T(8,128)(2,1)S(1)} collective-permute-done((bf16[2,16,3584]{2,1,0:T(8,128)(2,1)S(1)}, bf16[2,16,3584]{2,1,0:T(8,128)(2,1)S(1)}, u32[]{:S(2)}, u32[]{:S(2)}) %collective-permute-start.1) | collective-permute-done | bytes 229408 | tf_op jit(solution)/shard_map/ppermute | solution.py:142
  23.7 4.9 %collective-permute-done.2.refs_3_ = bf16[2,16,3584]{2,1,0:T(8,128)(2,1)S(1)} collective-permute-done((bf16[2,16,3584]{2,1,0:T(8,128)(2,1)S(1)}, bf16[2,16,3584]{2,1,0:T(8,128)(2,1)S(1)}, u32[]{:S(2)}, u32[]{:S(2)}) %collective-permute-start.2) | collective-permute-done | bytes 229408 | tf_op jit(solution)/shard_map/ppermute | solution.py:144
  28.6 0.1 arrange.1.own_ref.x_own_ref
  28.7 2.2 %collective-permute-start.7 = (bf16[8,2,16,3584]{3,2,1,0:T(8,128)(2,1)S(1)}, bf16[8,2,16,3584]{3,2,1,0:T(8,128)(2,1)S(1)}, u32[]{:S(2)}, u32[]{:S(2)}) collective-permute-start(bf16[8,2,16,3584]{3,2,1,0:T(8,128)(2,1)S(1)} %arrange.1.own_ref.x_own_ref), channel_id=1, source_target_pairs={{0,8},{8,0},{1,9},{9,1},{2,10},{10,2},{3,11},{11,3},{4,12},{12,4},... | collective-permute-start | bytes 5505032 | tf_op jit(solution)/shard_map/ppermute | solution.py:499
  30.9 3.4 %collective-permute-done.7.oth_ref.x_oth_ref = bf16[8,2,16,3584]{3,2,1,0:T(8,128)(2,1)S(1)} collective-permute-done((bf16[8,2,16,3584]{3,2,1,0:T(8,128)(2,1)S(1)}, bf16[8,2,16,3584]{3,2,1,0:T(8,128)(2,1)S(1)}, u32[]{:S(2)}, u32[]{:S(2)}) %collective-permute-start.7) | collective-permute-done | bytes 1835040 | tf_op jit(solution)/shard_map/ppermute | solution.py:499
  34.3 7.5 %forward.1 = (bf16[2,128,3584]{2,1,0:T(8,128)(2,1)S(1)}, bf16[2,128,3584]{2,1,0:T(8,128)(2,1)S(1)}, bf16[2,256,256]{2,1,0:T(8,128)(2,1)S(1)}, bf16[2,256,256]{2,...) custom-call(bf16[8,2,16,3584]{3,2,1,0:T(8,128)(2,1)S(1)} %arrange.1.own_ref.x_own_ref, ...), custom_call_target="tpu_custom_call" | custom-call | flops 2348810240 | bytes 12845056 | tf_op jit(solution)/shard_map/forward/pallas_call | solution.py:243
  41.8 0.5 collective-permute-start.9
  42.3 1.3 forward_low.1
  43.6 0.2 collective-permute-start.8
  43.8 1.9 %collective-permute-done.9.got_ref = bf16[2,128,3584]{2,1,0:T(8,128)(2,1)S(1)} collective-permute-done((bf16[2,128,3584]{2,1,0:T(8,128)(2,1)S(1)}, bf16[2,128,3584]{2,1,0:T(8,128)(2,1)S(1)}, u32[]{:S(2)}, u32[]{:S(2)}) %collective-permute-start.9) | collective-permute-done | bytes 1835040 | tf_op jit(solution)/shard_map/ppermute | solution.py:505
  45.7 2.6 %collective-permute-done.8.got_low_ref = bf16[2,128,3584]{2,1,0:T(8,128)(2,1)S(1)} collective-permute-done((bf16[2,128,3584]{2,1,0:T(8,128)(2,1)S(1)}, bf16[2,128,3584]{2,1,0:T(8,128)(2,1)S(1)}, u32[]{:S(2)}, u32[]{:S(2)}) %collective-permute-start.8) | collective-permute-done | bytes 1835040 | tf_op jit(solution)/shard_map/ppermute | solution.py:507
  48.3 1.2 join.1
  49.5 1.3 collective-permute-start.12
  50.8 2.3 %collective-permute-start.10 = (bf16[64,3584]{1,0:T(8,128)(2,1)S(1)}, bf16[64,3584]{1,0:T(8,128)(2,1)S(1)}, u32[]{:S(2)}, u32[]{:S(2)}) collective-permute-start(bf16[64,3584]{1,0:T(8,128)(2,1)S(1)} %get-tuple-element.65), channel_id=1, source_target_pairs={{0,3},{1,2},{2,1},{3,0},{4,7},{5,6},{6,5},{7,4},{8,104},{9,105},{1... | collective-permute-start | bytes 1376264 | tf_op jit(solution)/shard_map/ppermute | solution.py:334
  53.1 4.1 %collective-permute-done.12.got_ref = bf16[64,3584]{1,0:T(8,128)(2,1)S(1)} collective-permute-done((bf16[64,3584]{1,0:T(8,128)(2,1)S(1)}, bf16[64,3584]{1,0:T(8,128)(2,1)S(1)}, u32[]{:S(2)}, u32[]{:S(2)}) %collective-permute-start.12) | collective-permute-done | bytes 458784 | tf_op jit(solution)/shard_map/ppermute | solution.py:333
  57.2 0.4 fold_low.1
  57.6 3.0 %collective-permute-start.13 = (bf16[128,3584]{1,0:T(8,128)(2,1)S(1)}, bf16[128,3584]{1,0:T(8,128)(2,1)S(1)}, u32[]{:S(2)}, u32[]{:S(2)}) collective-permute-start(bf16[128,3584]{1,0:T(8,128)(2,1)S(1)} %fold_low.1), channel_id=1, source_target_pairs={{0,3},{1,2},{2,1},{3,0},{4,7},{5,6},{6,5},{7,4},{8,104},{9,105},{1... | collective-permute-start | bytes 2752520 | tf_op jit(solution)/shard_map/ppermute | solution.py:336
  60.6 0.4 fold_high.1
  61.1 0.1 collective-permute-start.14
  61.1 3.8 %collective-permute-start.15 = (bf16[2,3584]{1,0:T(2,128)(2,1)S(1)}, bf16[2,3584]{1,0:T(2,128)(2,1)S(1)}, u32[]{:S(2)}, u32[]{:S(2)}) collective-permute-start(bf16[2,3584]{1,0:T(2,128)(2,1)S(1)} %get-tuple-element.70), channel_id=1, source_target_pairs={{0,2},{1,3},{2,0},{3,1},{4,6},{5,7},{6,4},{7,5},{8,10},{9,11},{10,... | collective-permute-start | bytes 43016 | tf_op jit(solution)/shard_map/ppermute | solution.py:492
  65.0 6.7 %collective-permute-done.13.three_ref = bf16[128,3584]{1,0:T(8,128)(2,1)S(1)} collective-permute-done((bf16[128,3584]{1,0:T(8,128)(2,1)S(1)}, bf16[128,3584]{1,0:T(8,128)(2,1)S(1)}, u32[]{:S(2)}, u32[]{:S(2)}) %collective-permute-start.13) | collective-permute-done | bytes 917536 | tf_op jit(solution)/shard_map/ppermute | solution.py:336
  71.7 1.9 %collective-permute-done.11.one_ref = bf16[128,3584]{1,0:T(8,128)(2,1)S(1)} collective-permute-done((bf16[128,3584]{1,0:T(8,128)(2,1)S(1)}, bf16[128,3584]{1,0:T(8,128)(2,1)S(1)}, u32[]{:S(2)}, u32[]{:S(2)}) %collective-permute-start.11) | collective-permute-done | bytes 917536 | tf_op jit(solution)/shard_map/ppermute | solution.py:340
  73.6 0.4 total.1
  74.0 18.6 %all_to_all.10.pieces_ref = bf16[16,8,3584]{2,1,0:T(8,128)(2,1)S(1)} all-to-all(bf16[16,8,3584]{2,1,0:T(8,128)(2,1)S(1)} %bitcast.5), channel_id=1, replica_groups={{0,4,16,20,32,36,48,52,64,68,80,84,96,100,112,116},{1,5,17,21,33,37,49,..., dimensions={0} | all-to-all | bytes 1835008 | tf_op jit(solution)/shard_map/all_to_all | solution.py:510
  92.6 0.3 settle.1
  92.9 17.9 %all_to_all.11 = bf16[16,8,3584]{2,1,0:T(8,128)(2,1)S(1)} all-to-all(bf16[16,8,3584]{2,1,0:T(8,128)(2,1)S(1)} %get-tuple-element.77), channel_id=1, replica_groups={{0,4,16,20,32,36,48,52,64,68,80,84,96,100,112,116},{1,5,17,21,33,37,49,..., dimensions={0} | all-to-all | bytes 1835008 | tf_op jit(solution)/shard_map/all_to_all | solution.py:512
  110.9 1.2 collective-permute-start.18
  112.1 12.5 %collective-permute-done.18.quarter_ref.three_ref = bf16[128,3584]{1,0:T(8,128)(2,1)S(1)} collective-permute-done((bf16[128,3584]{1,0:T(8,128)(2,1)S(1)}, bf16[128,3584]{1,0:T(8,128)(2,1)S(1)}, u32[]{:S(2)}, u32[]{:S(2)}) %collective-permute-start.18) | collective-permute-done | bytes 917536 | tf_op jit(solution)/shard_map/ppermute | solution.py:361
  124.8 1.4 collective-permute-start.19
  126.2 6.2 %collective-permute-done.20.far3_ref = bf16[64,3584]{1,0:T(8,128)(2,1)S(1)} collective-permute-done((bf16[64,3584]{1,0:T(8,128)(2,1)S(1)}, bf16[64,3584]{1,0:T(8,128)(2,1)S(1)}, u32[]{:S(2)}, u32[]{:S(2)}) %collective-permute-start.20) | collective-permute-done | bytes 458784 | tf_op jit(solution)/shard_map/ppermute | solution.py:365
  132.4 1.4 collective-permute-done.19.far1_ref
  133.7 0.2 assemble.1.own_ref
  134.0 4.5 %collective-permute-start.21 = (bf16[4,128,3584]{2,1,0:T(8,128)(2,1)S(1)}, bf16[4,128,3584]{2,1,0:T(8,128)(2,1)S(1)}, u32[]{:S(2)}, u32[]{:S(2)}) collective-permute-start(bf16[4,128,3584]{2,1,0:T(8,128)(2,1)S(1)} %assemble.1.own_ref), channel_id=1, source_target_pairs={{0,8},{8,0},{1,9},{9,1},{2,10},{10,2},{3,11},{11,3},{4,12},{12,4},... | collective-permute-start | bytes 11010056 | tf_op jit(solution)/shard_map/ppermute | solution.py:515
  138.5 0.4 collective-permute-start.22
  138.9 2.3 %collective-permute-start.23 = (bf16[2,3584]{1,0:T(2,128)(2,1)S(1)}, bf16[2,3584]{1,0:T(2,128)(2,1)S(1)}, u32[]{:S(2)}, u32[]{:S(2)}) collective-permute-start(bf16[2,3584]{1,0:T(2,128)(2,1)S(1)} %get-tuple-element.90), channel_id=1, source_target_pairs={{0,2},{1,3},{2,0},{3,1},{4,6},{5,7},{6,4},{7,5},{8,10},{9,11},{10,... | collective-permute-start | bytes 43016 | tf_op jit(solution)/shard_map/ppermute | solution.py:492
  141.1 0.7 collective-permute-start.24
  141.8 0.4 collective-permute-done.22.rest_1_
  142.2 0.7 collective-permute-done.23.rest_2_
  142.9 1.1 collective-permute-done.24.rest_3_
  144.0 0.5 collective-permute-done.21.oth_ref
  144.5 9.6 %backward.1 = (bf16[5,256,3584]{2,1,0:T(8,128)(2,1)}, bf16[2,3584,256]{2,1,0:T(8,128)(2,1)}, f32[2,256]{1,0:T(2,128)}, bf16[4,2,3584]{2,1,0:T(2,128)(2,1)}) custom-call(bf16[2,256,256]{2,1,0:T(8,128)(2,1)S(1)} %get-tuple-element.55.turned_ref, f32[2,256,256]{2,1,0:T(8,128)S(1)} %get-tuple-element.56.slope_ref, bf16[4,128,3584]{2,1,0:T(8,128)(2,1)S(1)} %assemble.1.own_ref, ...), custom_call_target="tpu_custom_call" | custom-call | flops 5637144576 | bytes 12845056 | tf_op jit(solution)/shard_map/backward/pallas_call | solution.py:463
  (21 shorter events, 0.3 us)
Async XLA Ops:
  1.7 32.6 %copy-start = (s32[4,8,32]{2,1,0:T(8,128)S(1)}, s32[4,8,32]{2,1,0:T(8,128)}, u32[]{:S(2)}) copy-start(s32[4,8,32]{2,1,0:T(8,128)} %active_ref.1) | copy-start | bytes 12292
  1.7 32.6 %copy-start.1 = (f32[2,256]{1,0:T(2,128)S(1)}, f32[2,256]{1,0:T(2,128)}, u32[]{:S(2)}) copy-start(f32[2,256]{1,0:T(2,128)} %bias_ref.1) | copy-start | bytes 6148
  1.7 9.8 %collective-permute-start.3 = (bf16[2,16,3584]{2,1,0:T(8,128)(2,1)S(1)}, bf16[2,16,3584]{2,1,0:T(8,128)(2,1)S(1)}, u32[]{:S(2)}, u32[]{:S(2)}) collective-permute-start(bf16[2,16,3584]{2,1,0:T(8,128)(2,1)S(1)} %get-tuple-element.53.refs_0_), channel_id=1, source_target_pairs={{0,4},{1,5},{2,6},{3,7},{4,0},{5,1},{6,2},{7,3},{8,12},{9,13},{10,... | collective-permute-start | bytes 688136 | tf_op jit(solution)/shard_map/ppermute | solution.py:141
  6.2 8.1 %collective-permute-start = (bf16[2,16,3584]{2,1,0:T(8,128)(2,1)S(1)}, bf16[2,16,3584]{2,1,0:T(8,128)(2,1)S(1)}, u32[]{:S(2)}, u32[]{:S(2)}) collective-permute-start(bf16[2,16,3584]{2,1,0:T(8,128)(2,1)S(1)} %get-tuple-element.53.refs_0_), channel_id=1, source_target_pairs={{0,1},{1,0},{2,3},{3,2},{4,5},{5,4},{6,7},{7,6},{8,9},{9,8},{10,11... | collective-permute-start | bytes 688136 | tf_op jit(solution)/shard_map/ppermute | solution.py:142
  11.5 7.2 %collective-permute-start.5 = (bf16[2,16,3584]{2,1,0:T(8,128)(2,1)S(1)}, bf16[2,16,3584]{2,1,0:T(8,128)(2,1)S(1)}, u32[]{:S(2)}, u32[]{:S(2)}) collective-permute-start(bf16[2,16,3584]{2,1,0:T(8,128)(2,1)S(1)} %collective-permute-done.3.refs_4_), channel_id=1, source_target_pairs={{0,3},{1,2},{2,1},{3,0},{4,7},{5,6},{6,5},{7,4},{8,11},{9,10},{10,... | collective-permute-start | bytes 688136 | tf_op jit(solution)/shard_map/ppermute | solution.py:143
  14.3 9.4 %collective-permute-start.1 = (bf16[2,16,3584]{2,1,0:T(8,128)(2,1)S(1)}, bf16[2,16,3584]{2,1,0:T(8,128)(2,1)S(1)}, u32[]{:S(2)}, u32[]{:S(2)}) collective-permute-start(bf16[2,16,3584]{2,1,0:T(8,128)(2,1)S(1)} %get-tuple-element.53.refs_0_), channel_id=1, source_target_pairs={{0,3},{1,2},{2,1},{3,0},{4,7},{5,6},{6,5},{7,4},{8,11},{9,10},{10,... | collective-permute-start | bytes 688136 | tf_op jit(solution)/shard_map/ppermute | solution.py:142
  14.3 9.4 %collective-permute-start.4 = (bf16[2,16,3584]{2,1,0:T(8,128)(2,1)S(1)}, bf16[2,16,3584]{2,1,0:T(8,128)(2,1)S(1)}, u32[]{:S(2)}, u32[]{:S(2)}) collective-permute-start(bf16[2,16,3584]{2,1,0:T(8,128)(2,1)S(1)} %collective-permute-done.3.refs_4_), channel_id=1, source_target_pairs={{0,1},{1,0},{2,3},{3,2},{4,5},{5,4},{6,7},{7,6},{8,9},{9,8},{10,11... | collective-permute-start | bytes 688136 | tf_op jit(solution)/shard_map/ppermute | solution.py:143
  14.3 14.3 %collective-permute-start.2 = (bf16[2,16,3584]{2,1,0:T(8,128)(2,1)S(1)}, bf16[2,16,3584]{2,1,0:T(8,128)(2,1)S(1)}, u32[]{:S(2)}, u32[]{:S(2)}) collective-permute-start(bf16[2,16,3584]{2,1,0:T(8,128)(2,1)S(1)} %collective-permute-done.refs_1_), channel_id=1, source_target_pairs={{0,3},{1,2},{2,1},{3,0},{4,7},{5,6},{6,5},{7,4},{8,11},{9,10},{10,... | collective-permute-start | bytes 688136 | tf_op jit(solution)/shard_map/ppermute | solution.py:144
  18.7 9.8 %collective-permute-start.6 = (bf16[2,16,3584]{2,1,0:T(8,128)(2,1)S(1)}, bf16[2,16,3584]{2,1,0:T(8,128)(2,1)S(1)}, u32[]{:S(2)}, u32[]{:S(2)}) collective-permute-start(bf16[2,16,3584]{2,1,0:T(8,128)(2,1)S(1)} %collective-permute-done.5.refs_6_), channel_id=1, source_target_pairs={{0,1},{1,0},{2,3},{3,2},{4,5},{5,4},{6,7},{7,6},{8,9},{9,8},{10,11... | collective-permute-start | bytes 688136 | tf_op jit(solution)/shard_map/ppermute | solution.py:145
  28.7 5.6 %collective-permute-start.7 = (bf16[8,2,16,3584]{3,2,1,0:T(8,128)(2,1)S(1)}, bf16[8,2,16,3584]{3,2,1,0:T(8,128)(2,1)S(1)}, u32[]{:S(2)}, u32[]{:S(2)}) collective-permute-start(bf16[8,2,16,3584]{3,2,1,0:T(8,128)(2,1)S(1)} %arrange.1.own_ref.x_own_ref), channel_id=1, source_target_pairs={{0,8},{8,0},{1,9},{9,1},{2,10},{10,2},{3,11},{11,3},{4,12},{12,4},... | collective-permute-start | bytes 5505032 | tf_op jit(solution)/shard_map/ppermute | solution.py:499
  41.8 3.9 %collective-permute-start.9 = (bf16[2,128,3584]{2,1,0:T(8,128)(2,1)S(1)}, bf16[2,128,3584]{2,1,0:T(8,128)(2,1)S(1)}, u32[]{:S(2)}, u32[]{:S(2)}) collective-permute-start(bf16[2,128,3584]{2,1,0:T(8,128)(2,1)S(1)} %get-tuple-element.62), channel_id=1, source_target_pairs={{0,8},{8,0},{1,9},{9,1},{2,10},{10,2},{3,11},{11,3},{4,12},{12,4},... | collective-permute-start | bytes 5505032 | tf_op jit(solution)/shard_map/ppermute | solution.py:505
  43.6 4.7 %collective-permute-start.8 = (bf16[2,128,3584]{2,1,0:T(8,128)(2,1)S(1)}, bf16[2,128,3584]{2,1,0:T(8,128)(2,1)S(1)}, u32[]{:S(2)}, u32[]{:S(2)}) collective-permute-start(bf16[2,128,3584]{2,1,0:T(8,128)(2,1)S(1)} %get-tuple-element.61), channel_id=1, source_target_pairs={{0,8},{8,0},{1,9},{9,1},{2,10},{10,2},{3,11},{11,3},{4,12},{12,4},... | collective-permute-start | bytes 5505032 | tf_op jit(solution)/shard_map/ppermute | solution.py:507
  49.5 7.7 %collective-permute-start.12 = (bf16[64,3584]{1,0:T(8,128)(2,1)S(1)}, bf16[64,3584]{1,0:T(8,128)(2,1)S(1)}, u32[]{:S(2)}, u32[]{:S(2)}) collective-permute-start(bf16[64,3584]{1,0:T(8,128)(2,1)S(1)} %get-tuple-element.67), channel_id=1, source_target_pairs={{0,1},{1,0},{2,3},{3,2},{4,5},{5,4},{6,7},{7,6},{8,40},{9,41},{10,... | collective-permute-start | bytes 1376264 | tf_op jit(solution)/shard_map/ppermute | solution.py:333
  50.8 9.8 %collective-permute-start.10 = (bf16[64,3584]{1,0:T(8,128)(2,1)S(1)}, bf16[64,3584]{1,0:T(8,128)(2,1)S(1)}, u32[]{:S(2)}, u32[]{:S(2)}) collective-permute-start(bf16[64,3584]{1,0:T(8,128)(2,1)S(1)} %get-tuple-element.65), channel_id=1, source_target_pairs={{0,3},{1,2},{2,1},{3,0},{4,7},{5,6},{6,5},{7,4},{8,104},{9,105},{1... | collective-permute-start | bytes 1376264 | tf_op jit(solution)/shard_map/ppermute | solution.py:334
  57.6 14.1 %collective-permute-start.13 = (bf16[128,3584]{1,0:T(8,128)(2,1)S(1)}, bf16[128,3584]{1,0:T(8,128)(2,1)S(1)}, u32[]{:S(2)}, u32[]{:S(2)}) collective-permute-start(bf16[128,3584]{1,0:T(8,128)(2,1)S(1)} %fold_low.1), channel_id=1, source_target_pairs={{0,3},{1,2},{2,1},{3,0},{4,7},{5,6},{6,5},{7,4},{8,104},{9,105},{1... | collective-permute-start | bytes 2752520 | tf_op jit(solution)/shard_map/ppermute | solution.py:336
  61.0 12.6 %collective-permute-start.11 = (bf16[128,3584]{1,0:T(8,128)(2,1)S(1)}, bf16[128,3584]{1,0:T(8,128)(2,1)S(1)}, u32[]{:S(2)}, u32[]{:S(2)}) collective-permute-start(bf16[128,3584]{1,0:T(8,128)(2,1)S(1)} %fold_high.1), channel_id=1, source_target_pairs={{0,1},{1,0},{2,3},{3,2},{4,5},{5,4},{6,7},{7,6},{8,40},{9,41},{10,... | collective-permute-start | bytes 2752520 | tf_op jit(solution)/shard_map/ppermute | solution.py:340
  61.1 12.9 %collective-permute-start.14 = (bf16[2,3584]{1,0:T(2,128)(2,1)S(1)}, bf16[2,3584]{1,0:T(2,128)(2,1)S(1)}, u32[]{:S(2)}, u32[]{:S(2)}) collective-permute-start(bf16[2,3584]{1,0:T(2,128)(2,1)S(1)} %get-tuple-element.69), channel_id=1, source_target_pairs={{0,1},{1,2},{2,3},{3,0},{4,5},{5,6},{6,7},{7,4},{8,9},{9,10},{10,1... | collective-permute-start | bytes 43016 | tf_op jit(solution)/shard_map/ppermute | solution.py:492
  61.1 12.8 %collective-permute-start.15 = (bf16[2,3584]{1,0:T(2,128)(2,1)S(1)}, bf16[2,3584]{1,0:T(2,128)(2,1)S(1)}, u32[]{:S(2)}, u32[]{:S(2)}) collective-permute-start(bf16[2,3584]{1,0:T(2,128)(2,1)S(1)} %get-tuple-element.70), channel_id=1, source_target_pairs={{0,2},{1,3},{2,0},{3,1},{4,6},{5,7},{6,4},{7,5},{8,10},{9,11},{10,... | collective-permute-start | bytes 43016 | tf_op jit(solution)/shard_map/ppermute | solution.py:492
  65.0 9.0 %collective-permute-start.16 = (bf16[2,3584]{1,0:T(2,128)(2,1)S(1)}, bf16[2,3584]{1,0:T(2,128)(2,1)S(1)}, u32[]{:S(2)}, u32[]{:S(2)}) collective-permute-start(bf16[2,3584]{1,0:T(2,128)(2,1)S(1)} %get-tuple-element.71), channel_id=1, source_target_pairs={{0,3},{1,0},{2,1},{3,2},{4,7},{5,4},{6,5},{7,6},{8,11},{9,8},{10,9... | collective-permute-start | bytes 43016 | tf_op jit(solution)/shard_map/ppermute | solution.py:492
  110.9 13.8 %collective-permute-start.18 = (bf16[128,3584]{1,0:T(8,128)(2,1)S(1)}, bf16[128,3584]{1,0:T(8,128)(2,1)S(1)}, u32[]{:S(2)}, u32[]{:S(2)}) collective-permute-start(bf16[128,3584]{1,0:T(8,128)(2,1)S(1)} %bitcast.2), channel_id=1, source_target_pairs={{0,3},{1,2},{2,1},{3,0},{4,7},{5,6},{6,5},{7,4},{8,104},{9,105},{1... | collective-permute-start | bytes 2752520 | tf_op jit(solution)/shard_map/ppermute | solution.py:361
  112.1 12.6 %collective-permute-start.17 = (bf16[128,3584]{1,0:T(8,128)(2,1)S(1)}, bf16[128,3584]{1,0:T(8,128)(2,1)S(1)}, u32[]{:S(2)}, u32[]{:S(2)}) collective-permute-start(bf16[128,3584]{1,0:T(8,128)(2,1)S(1)} %bitcast.3), channel_id=1, source_target_pairs={{0,1},{1,0},{2,3},{3,2},{4,5},{5,4},{6,7},{7,6},{8,40},{9,41},{10,... | collective-permute-start | bytes 2752520 | tf_op jit(solution)/shard_map/ppermute | solution.py:360
  124.7 7.7 %collective-permute-start.20 = (bf16[64,3584]{1,0:T(8,128)(2,1)S(1)}, bf16[64,3584]{1,0:T(8,128)(2,1)S(1)}, u32[]{:S(2)}, u32[]{:S(2)}) collective-permute-start(bf16[64,3584]{1,0:T(8,128)(2,1)S(1)} %half_high.1), channel_id=1, source_target_pairs={{0,1},{1,0},{2,3},{3,2},{4,5},{5,4},{6,7},{7,6},{8,40},{9,41},{10,... | collective-permute-start | bytes 1376264 | tf_op jit(solution)/shard_map/ppermute | solution.py:365
  124.8 8.9 %collective-permute-start.19 = (bf16[64,3584]{1,0:T(8,128)(2,1)S(1)}, bf16[64,3584]{1,0:T(8,128)(2,1)S(1)}, u32[]{:S(2)}, u32[]{:S(2)}) collective-permute-start(bf16[64,3584]{1,0:T(8,128)(2,1)S(1)} %half_low.1), channel_id=1, source_target_pairs={{0,3},{1,2},{2,1},{3,0},{4,7},{5,6},{6,5},{7,4},{8,104},{9,105},{1... | collective-permute-start | bytes 1376264 | tf_op jit(solution)/shard_map/ppermute | solution.py:363
  134.0 10.5 %collective-permute-start.21 = (bf16[4,128,3584]{2,1,0:T(8,128)(2,1)S(1)}, bf16[4,128,3584]{2,1,0:T(8,128)(2,1)S(1)}, u32[]{:S(2)}, u32[]{:S(2)}) collective-permute-start(bf16[4,128,3584]{2,1,0:T(8,128)(2,1)S(1)} %assemble.1.own_ref), channel_id=1, source_target_pairs={{0,8},{8,0},{1,9},{9,1},{2,10},{10,2},{3,11},{11,3},{4,12},{12,4},... | collective-permute-start | bytes 11010056 | tf_op jit(solution)/shard_map/ppermute | solution.py:515
  138.5 3.8 %collective-permute-start.22 = (bf16[2,3584]{1,0:T(2,128)(2,1)S(1)}, bf16[2,3584]{1,0:T(2,128)(2,1)S(1)}, u32[]{:S(2)}, u32[]{:S(2)}) collective-permute-start(bf16[2,3584]{1,0:T(2,128)(2,1)S(1)} %get-tuple-element.89), channel_id=1, source_target_pairs={{0,1},{1,2},{2,3},{3,0},{4,5},{5,6},{6,7},{7,4},{8,9},{9,10},{10,1... | collective-permute-start | bytes 43016 | tf_op jit(solution)/shard_map/ppermute | solution.py:492
  138.9 4.1 %collective-permute-start.23 = (bf16[2,3584]{1,0:T(2,128)(2,1)S(1)}, bf16[2,3584]{1,0:T(2,128)(2,1)S(1)}, u32[]{:S(2)}, u32[]{:S(2)}) collective-permute-start(bf16[2,3584]{1,0:T(2,128)(2,1)S(1)} %get-tuple-element.90), channel_id=1, source_target_pairs={{0,2},{1,3},{2,0},{3,1},{4,6},{5,7},{6,4},{7,5},{8,10},{9,11},{10,... | collective-permute-start | bytes 43016 | tf_op jit(solution)/shard_map/ppermute | solution.py:492
  141.1 2.9 %collective-permute-start.24 = (bf16[2,3584]{1,0:T(2,128)(2,1)S(1)}, bf16[2,3584]{1,0:T(2,128)(2,1)S(1)}, u32[]{:S(2)}, u32[]{:S(2)}) collective-permute-start(bf16[2,3584]{1,0:T(2,128)(2,1)S(1)} %get-tuple-element.91), channel_id=1, source_target_pairs={{0,3},{1,0},{2,1},{3,2},{4,7},{5,4},{6,5},{7,6},{8,11},{9,8},{10,9... | collective-permute-start | bytes 43016 | tf_op jit(solution)/shard_map/ppermute | solution.py:492

commit v7 on v6

--- a/solution.py
+++ b/solution.py
@@ -137,27 +137,28 @@
         refs[TILES][tile] = piece_ref[...]
 
 
-def _gather_inputs(mine):
+def _gather_inputs(mine, staged):
     far = lax.ppermute(mine, ALL, ACROSS)
     mine_1, mine_3 = (lax.ppermute(mine, ALL, ALONG_Y[flip]) for flip in (1, 3))
+    far, staged = lax.optimization_barrier((far, staged))
     far_3, far_1 = (lax.ppermute(far, ALL, ALONG_Y[flip]) for flip in (3, 1))
     mine_2 = lax.ppermute(mine_1, ALL, ALONG_Y[3])
     far_2 = lax.ppermute(far_3, ALL, ALONG_Y[1])
-    return _plain(
+    own = _plain(
         _arrange_kernel,
         jax.ShapeDtypeStruct((TILES, 2, HROW, D), BF),
         "arrange",
         mine, mine_1, mine_3, mine_2, far, far_1, far_3, far_2,
     )
-
-
-def _place(quarter, i):
-    core = lax.axis_index("core")
+    return own, staged
+
+
+def _place(core, quarter, i):
     return jnp.where(core == 0, quarter, i), jnp.where(core == 0, i, quarter)
 
 
-def _me():
-    return jnp.where(lax.axis_index("core") == 0, lax.axis_index("y"), lax.axis_index("x"))
+def _me(core):
+    return jnp.where(core == 0, lax.axis_index("y"), lax.axis_index("x"))
 
 
 def _decode(t, side, codes_ref, dec_ref, own_ref, oth_ref, at):
@@ -193,18 +194,39 @@
         oth_ref[at] = jnp.zeros((HALF, D), BF)
 
 
+def _stage_kernel(enc_hbm, dec_hbm, enc_ref, dec_ref, sem):
+    copies = [
+        pltpu.make_async_copy(enc_hbm, enc_ref, sem.at[0]),
+        pltpu.make_async_copy(dec_hbm, dec_ref, sem.at[1]),
+    ]
+    for copy in copies:
+        copy.start()
+    for copy in copies:
+        copy.wait()
+
+
+def _stage(encoder, decoder):
+    return pl.pallas_call(
+        _stage_kernel,
+        in_specs=[pl.BlockSpec(memory_space=HBM)] * 2,
+        out_specs=[WHOLE, WHOLE],
+        out_shape=[
+            jax.ShapeDtypeStruct((2, D, W), BF),
+            jax.ShapeDtypeStruct((PAIRS, W, D), BF),
+        ],
+        scratch_shapes=[pltpu.SemaphoreType.DMA((2,))],
+        compiler_params=_params(1),
+        cost_estimate=pl.CostEstimate(
+            flops=0, bytes_accessed=2 * (2 * D * W + PAIRS * W * D) * 2, transcendentals=0
+        ),
+        name="stage",
+    )(_hbm(encoder), _hbm(decoder))
+
+
 def _forward_kernel(
-    own_ref, oth_ref, enc_hbm, dec_hbm, bias_ref, active_ref,
-    part_own_ref, part_oth_ref, codes_ref, turned_ref, slope_ref, dec_ref, enc_ref, enc_sem, dec_sem,
+    own_ref, oth_ref, enc_ref, dec_ref, bias_ref, active_ref,
+    part_own_ref, part_oth_ref, codes_ref, turned_ref, slope_ref,
 ):
-    enc_copies = [
-        pltpu.make_async_copy(enc_hbm.at[k], enc_ref.at[k], enc_sem.at[k]) for k in range(2)
-    ]
-    dec_copies = [
-        pltpu.make_async_copy(dec_hbm.at[p], dec_ref.at[p], dec_sem.at[p]) for p in range(PAIRS)
-    ]
-    for copy in enc_copies + dec_copies[::-1]:
-        copy.start()
     x, zl, core = lax.axis_index("x"), lax.axis_index("zl"), lax.axis_index("core")
     zh, y = lax.axis_index("zh"), lax.axis_index("y")
     side = _side()
@@ -222,7 +244,6 @@
         keep = jnp.concatenate(keep, axis=1)
         keep = jnp.broadcast_to(keep[:, None, :], (TILES, HROW, W)).reshape(HALF, W)
         keep = jnp.concatenate([keep, keep], axis=0)
-        enc_copies[k].wait()
         pre = jnp.dot(rows, enc_ref[k], preferred_element_type=F32) + bias_ref[k : k + 1]
         positive = jnp.maximum(pre, 0.0)
         kept = keep * positive
@@ -230,59 +251,46 @@
         codes_ref[k] = codes.astype(BF)
         turned_ref[k] = codes.T.astype(BF)
         slope_ref[k] = 2.0 * kept
-    for p in (4, 3, 2):
-        dec_copies[p].wait()
-    _decode(3, side, codes_ref, dec_ref, part_own_ref, part_oth_ref, 1)
-    dec_copies[1].wait()
-    _decode(2, side, codes_ref, dec_ref, part_own_ref, part_oth_ref, 0)
-    dec_copies[0].wait()
+    for t in (0, 1):
+        _decode(t, side, codes_ref, dec_ref, part_own_ref, part_oth_ref, t)
 
 
 def _forward(own, oth, encoder, decoder, bias, active):
-    hbm = pl.BlockSpec(memory_space=HBM)
     return pl.pallas_call(
         _forward_kernel,
-        in_specs=[WHOLE, WHOLE, hbm, hbm, WHOLE, WHOLE],
-        out_specs=[WHOLE] * 6,
+        in_specs=[WHOLE] * 6,
+        out_specs=[WHOLE] * 5,
         out_shape=[
             jax.ShapeDtypeStruct((2, HALF, D), BF),
             jax.ShapeDtypeStruct((2, HALF, D), BF),
             jax.ShapeDtypeStruct((2, 2 * HALF, W), BF),
             jax.ShapeDtypeStruct((2, W, 2 * HALF), BF),
             jax.ShapeDtypeStruct((2, 2 * HALF, W), F32),
-            jax.ShapeDtypeStruct((PAIRS, W, D), BF),
         ],
-        scratch_shapes=[
-            pltpu.VMEM((2, D, W), BF),
-            pltpu.SemaphoreType.DMA((2,)),
-            pltpu.SemaphoreType.DMA((PAIRS,)),
-        ],
-        compiler_params=_params(10),
+        compiler_params=_params(6),
         cost_estimate=pl.CostEstimate(
-            flops=2 * 5 * 256 * D * W,
-            bytes_accessed=(2 * D * W + PAIRS * W * D) * 2,
-            transcendentals=0,
+            flops=2 * 4 * 256 * D * W, bytes_accessed=2 * 256 * D * 2, transcendentals=0
         ),
         name="forward",
-    )(own, oth, _hbm(encoder), _hbm(decoder), bias, active)
-
-
-def _forward_low_kernel(codes_ref, dec_ref, part_own_ref, part_oth_ref):
-    for t in (1, 0):
-        _decode(t, _side(), codes_ref, dec_ref, part_own_ref, part_oth_ref, t)
-
-
-def _forward_low(codes, dec):
-    return pl.pallas_call(
-        _forward_low_kernel,
+    )(own, oth, encoder, decoder, bias, active)
+
+
+def _forward_high_kernel(codes_ref, dec_ref, part_own_ref, part_oth_ref):
+    for t in (2, 3):
+        _decode(t, _side(), codes_ref, dec_ref, part_own_ref, part_oth_ref, t - 2)
+
+
+def _forward_high(codes, dec):
+    return pl.pallas_call(
+        _forward_high_kernel,
         in_specs=[WHOLE, WHOLE],
         out_specs=[WHOLE, WHOLE],
         out_shape=[jax.ShapeDtypeStruct((2, HALF, D), BF)] * 2,
         compiler_params=_params(4),
         cost_estimate=pl.CostEstimate(
-            flops=2 * 2 * 256 * D * W, bytes_accessed=2 * 256 * D * 2, transcendentals=0
+            flops=2 * 3 * 256 * D * W, bytes_accessed=2 * 256 * D * 2, transcendentals=0
         ),
-        name="forward_low",
+        name="forward_high",
     )(codes, dec)
 
 
@@ -290,9 +298,10 @@
     own_low_ref, own_ref, got_low_ref, got_ref, mine_ref, to1_ref, to3_ref, far1_ref, far3_ref
 ):
     outs = {0: (mine_ref, mine_ref), 1: (to1_ref, to1_ref), 3: (to3_ref, to3_ref), 2: (far1_ref, far3_ref)}
+    core = lax.axis_index("core")
     for flip, (first_ref, second_ref) in outs.items():
         for i in range(4):
-            t, x = _place(lax.bitwise_xor(_me(), flip), i)
+            t, x = _place(core, lax.bitwise_xor(_me(core), flip), i)
             rows = pl.ds(pl.multiple_of(x * BOX, BOX), BOX)
             out_ref = first_ref if i < 2 else second_ref
             at = (i % 2 if flip == 2 else i) * BOX
@@ -345,11 +354,13 @@
     out_ref[...] = quarter_ref[at : at + QUARTER // 2]
 
 
-def _assemble_kernel(mine_ref, one_ref, three_ref, far1_ref, far3_ref, out_ref):
+def _assemble_kernel(other, mine_ref, one_ref, three_ref, far1_ref, far3_ref, out_ref):
     refs = {0: (mine_ref, mine_ref), 1: (one_ref, one_ref), 3: (three_ref, three_ref), 2: (far1_ref, far3_ref)}
+    core = lax.axis_index("core")
+    core = 1 - core if other else core
     for flip, (first_ref, second_ref) in refs.items():
         for i in range(4):
-            t, x = _place(lax.bitwise_xor(_me(), flip), i)
+            t, x = _place(core, lax.bitwise_xor(_me(core), flip), i)
             in_ref = first_ref if i < 2 else second_ref
             at = (i % 2 if flip == 2 else i) * BOX
             out_ref[t, pl.ds(pl.multiple_of(x * BOX, BOX), BOX)] = in_ref[at : at + BOX]
@@ -363,12 +374,12 @@
     far1 = lax.ppermute(pass3, ALL, RING[3])
     pass1 = _plain(functools.partial(_half_kernel, QUARTER // 2), half, "half_high", three)
     far3 = lax.ppermute(pass1, ALL, RING[1])
-    return _plain(
-        _assemble_kernel,
-        jax.ShapeDtypeStruct((LAYERS, HALF, D), BF),
-        "assemble",
-        quarter, one, three, far1, far3,
-    )
+    pieces = (quarter, one, three, far1, far3)
+    others = [lax.ppermute(piece, "core", SWAP) for piece in pieces]
+    whole = jax.ShapeDtypeStruct((LAYERS, HALF, D), BF)
+    own = _plain(functools.partial(_assemble_kernel, False), whole, "assemble_own", *pieces)
+    oth = _plain(functools.partial(_assemble_kernel, True), whole, "assemble_oth", *others)
+    return own, oth
 
 
 def _settle_kernel(pieces_ref, *rest):
@@ -495,25 +506,22 @@
 
 def per_device(resid_in, resid_out, encoder, enc_bias, decoder, active):
     mine, *targets = _prepare(resid_in, resid_out)
-    own = _gather_inputs(mine)
+    encoder, decoder, mine = lax.optimization_barrier((encoder, decoder, mine))
+    own, (enc, dec) = _gather_inputs(mine, _stage(encoder, decoder))
+    targets[1:], own = lax.optimization_barrier((targets[1:], own))
     oth = lax.ppermute(own, "core", SWAP)
-    targets[1:], own = lax.optimization_barrier((targets[1:], own))
     targets = _around_y(targets)
-    part_own, part_oth, codes, turned, slope, dec = _forward(
-        own, oth, encoder, decoder, enc_bias, active
-    )
+    low_own, low_oth, codes, turned, slope = _forward(own, oth, enc, dec, enc_bias, active)
+    got_low = lax.ppermute(low_oth, "core", SWAP)
+    part_own, part_oth = _forward_high(codes, dec)
     got = lax.ppermute(part_oth, "core", SWAP)
-    low_own, low_oth = _forward_low(codes, dec)
-    got_low = lax.ppermute(low_oth, "core", SWAP)
     quarter = _reduce_ring((low_own, part_own, got_low, got))
     quarter, targets = lax.optimization_barrier((quarter, targets))
     pieces = lax.all_to_all(quarter.reshape(16, 8, D), ALL, 0, 0, axis_index_groups=GROUPS)
     errors, *recon = _settle(pieces, targets)
     quarter = lax.all_to_all(errors, ALL, 0, 0, axis_index_groups=GROUPS).reshape(QUARTER, D)
     quarter, recon = lax.optimization_barrier((quarter, recon))
-    err_own = _gather_ring(quarter)
-    err_oth = lax.ppermute(err_own, "core", SWAP)
-    recon, err_own = lax.optimization_barrier((recon, err_own))
+    err_own, err_oth = _gather_ring(quarter)
     recon = _around_y(recon)
     grad_decoder, grad_encoder, grad_bias, recon = _backward(
         turned, slope, err_own, err_oth, own, oth, dec, recon

time: 154 us -> 147 us (0.955)
  waiting for transfers between devices: 59 us -> 47.3 us
  starting transfers between devices: 35.3 us -> 40.8 us
    ppermute x1 -> x5, starting transfers between devices: 4.48 us -> 12.5 us  [_gather_ring(): others = [lax.ppermute(piece, 'core', SWAP) for piece in pieces]]
    ppermute x1, waiting for transfers between devices: 6.16 us -> 2.07 us  [_gather_ring(): far3 = lax.ppermute(pass1, ALL, RING[1])]
    ppermute x1, waiting for transfers between devices: 4.03 us -> 0.01 us  [_gather_inputs(): far = lax.ppermute(mine, ALL, ACROSS)]
    ppermute x1, waiting for transfers between devices: 12.5 us -> 9.28 us  [_gather_ring(): three = lax.ppermute(quarter, ALL, RING[3])]
    pallas_call x2 -> x3, Pallas kernels: 8.79 us -> 9.06 us  [the longest x1 4.74 us: _stage(): pl.pallas_call(_stage_kernel, in_specs=[pl.BlockSpec(memory_space=HBM)] *...]
  transfers between devices with their start and end apart: 25 -> 29, of which waited for: 17 -> 14; matrix products, arithmetic and copies ran while one was open for 0% -> 0% of each run, Pallas kernels for 2% -> 5%
where the time goes in v7:
time: 147 us
  waiting for transfers between devices  47.3 us (32%)
  starting transfers between devices  40.8 us (28%)
  blocking collectives  35.7 us (24%)
  Pallas kernels  22.7 us (15%)
    all_to_all x1, blocking collectives, per_device(): lax.all_to_all(errors, ALL, 0, 0, axis_index_groups=GROUPS)  17.9 us
    all_to_all x1, blocking collectives, per_device(): lax.all_to_all(quarter.reshape(16, 8, D), ALL, 0, 0, axis_index_groups=GR...  17.8 us
    ppermute x5, starting transfers between devices, _gather_ring(): others = [lax.ppermute(piece, 'core', SWAP) for piece in pieces]  12.5 us
    pallas_call x1, Pallas kernels, _backward(): pl.pallas_call(_backward_kernel, grid=(PAIRS + 2,), in_specs=[WHOLE] * 11...  9.53 us
    ppermute x1, waiting for transfers between devices, _gather_ring(): three = lax.ppermute(quarter, ALL, RING[3])  9.28 us
    ppermute x1, waiting for transfers between devices, _reduce_ring(): from3 = lax.ppermute(to3, ALL, RING[3])  7.71 us
    ppermute x6, starting transfers between devices, _around_y(): lax.ppermute(pieces[j], 'y', [(i, (i + j) % 4) for i in range(4)])  6.98 us
    ppermute x1, waiting for transfers between devices, _reduce_ring(): got1 = lax.ppermute(far1, ALL, RING[1])  5.04 us
  transfers between devices with their start and end apart: 29, of which 14 were waited for; matrix products, arithmetic and copies ran while one was open for 0% of the time, Pallas kernels for 5%

profile of v7, /device:TPU:1, one launch (start us, length us, event | category | flops | bytes accessed | tf_op | source)
XLA Modules:
  0.0 147.2 jit_solution(18134674999112446643)
XLA Ops:
  0.6 1.0 prepare.1
  1.7 4.5 %collective-permute-start.3 = (bf16[2,16,3584]{2,1,0:T(8,128)(2,1)S(1)}, bf16[2,16,3584]{2,1,0:T(8,128)(2,1)S(1)}, u32[]{:S(2)}, u32[]{:S(2)}) collective-permute-start(bf16[2,16,3584]{2,1,0:T(8,128)(2,1)S(1)} %get-tuple-element.56.refs_0_), channel_id=1, source_target_pairs={{0,4},{1,5},{2,6},{3,7},{4,0},{5,1},{6,2},{7,3},{8,12},{9,13},{10,... | collective-permute-start | bytes 688136 | tf_op jit(solution)/shard_map/ppermute | solution.py:141
  6.2 1.3 collective-permute-start
  7.5 4.7 %stage.1 = (bf16[2,3584,256]{2,1,0:T(8,128)(2,1)S(1)}, bf16[5,256,3584]{2,1,0:T(8,128)(2,1)S(1)}) custom-call(bf16[2,3584,256]{2,1,0:T(8,128)(2,1)} %enc_hbm, bf16[5,256,3584]{2,1,0:T(8,128)(2,1)} %dec_hbm), custom_call_target="tpu_custom_call" | custom-call | bytes 25690112 | tf_op jit(solution)/shard_map/stage/pallas_call | solution.py:209
  12.3 2.0 %collective-permute-start.5 = (bf16[2,16,3584]{2,1,0:T(8,128)(2,1)S(1)}, bf16[2,16,3584]{2,1,0:T(8,128)(2,1)S(1)}, u32[]{:S(2)}, u32[]{:S(2)}) collective-permute-start(bf16[2,16,3584]{2,1,0:T(8,128)(2,1)S(1)} %collective-permute-done.3.refs_4_), channel_id=1, source_target_pairs={{0,3},{1,2},{2,1},{3,0},{4,7},{5,6},{6,5},{7,4},{8,11},{9,10},{10,... | collective-permute-start | bytes 688136 | tf_op jit(solution)/shard_map/ppermute | solution.py:144
  14.2 0.8 collective-permute-start.1
  15.0 1.9 %collective-permute-start.2 = (bf16[2,16,3584]{2,1,0:T(8,128)(2,1)S(1)}, bf16[2,16,3584]{2,1,0:T(8,128)(2,1)S(1)}, u32[]{:S(2)}, u32[]{:S(2)}) collective-permute-start(bf16[2,16,3584]{2,1,0:T(8,128)(2,1)S(1)} %collective-permute-done.refs_1_), channel_id=1, source_target_pairs={{0,3},{1,2},{2,1},{3,0},{4,7},{5,6},{6,5},{7,4},{8,11},{9,10},{10,... | collective-permute-start | bytes 688136 | tf_op jit(solution)/shard_map/ppermute | solution.py:145
  16.9 2.5 %collective-permute-done.5.refs_6_ = bf16[2,16,3584]{2,1,0:T(8,128)(2,1)S(1)} collective-permute-done((bf16[2,16,3584]{2,1,0:T(8,128)(2,1)S(1)}, bf16[2,16,3584]{2,1,0:T(8,128)(2,1)S(1)}, u32[]{:S(2)}, u32[]{:S(2)}) %collective-permute-start.5) | collective-permute-done | bytes 229408 | tf_op jit(solution)/shard_map/ppermute | solution.py:144
  19.4 4.9 %collective-permute-done.1.refs_2_ = bf16[2,16,3584]{2,1,0:T(8,128)(2,1)S(1)} collective-permute-done((bf16[2,16,3584]{2,1,0:T(8,128)(2,1)S(1)}, bf16[2,16,3584]{2,1,0:T(8,128)(2,1)S(1)}, u32[]{:S(2)}, u32[]{:S(2)}) %collective-permute-start.1) | collective-permute-done | bytes 229408 | tf_op jit(solution)/shard_map/ppermute | solution.py:142
  24.3 4.9 %collective-permute-done.2.refs_3_ = bf16[2,16,3584]{2,1,0:T(8,128)(2,1)S(1)} collective-permute-done((bf16[2,16,3584]{2,1,0:T(8,128)(2,1)S(1)}, bf16[2,16,3584]{2,1,0:T(8,128)(2,1)S(1)}, u32[]{:S(2)}, u32[]{:S(2)}) %collective-permute-start.2) | collective-permute-done | bytes 229408 | tf_op jit(solution)/shard_map/ppermute | solution.py:145
  29.4 2.2 %collective-permute-start.7 = (bf16[8,2,16,3584]{3,2,1,0:T(8,128)(2,1)S(1)}, bf16[8,2,16,3584]{3,2,1,0:T(8,128)(2,1)S(1)}, u32[]{:S(2)}, u32[]{:S(2)}) collective-permute-start(bf16[8,2,16,3584]{3,2,1,0:T(8,128)(2,1)S(1)} %arrange.1.own_ref.x_own_ref), channel_id=1, source_target_pairs={{0,8},{8,0},{1,9},{9,1},{2,10},{10,2},{3,11},{11,3},{4,12},{12,4},... | collective-permute-start | bytes 5505032 | tf_op jit(solution)/shard_map/ppermute | solution.py:512
  31.6 3.4 %collective-permute-done.7.oth_ref.x_oth_ref = bf16[8,2,16,3584]{3,2,1,0:T(8,128)(2,1)S(1)} collective-permute-done((bf16[8,2,16,3584]{3,2,1,0:T(8,128)(2,1)S(1)}, bf16[8,2,16,3584]{3,2,1,0:T(8,128)(2,1)S(1)}, u32[]{:S(2)}, u32[]{:S(2)}) %collective-permute-start.7) | collective-permute-done | bytes 1835040 | tf_op jit(solution)/shard_map/ppermute | solution.py:512
  35.0 2.5 %forward.1 = (bf16[2,128,3584]{2,1,0:T(8,128)(2,1)S(1)}, bf16[2,128,3584]{2,1,0:T(8,128)(2,1)S(1)}, bf16[2,256,256]{2,1,0:T(8,128)(2,1)S(1)}, bf16[2,256,256]{2,1,0:T(8,128)(2,1)S(1)}, f32[2,256,256]{2,1,0:T(8,128)S(1)}) custom-call(bf16[8,2,16,3584]{3,2,1,0:T(8,128)(2,1)S(1)} %arrange.1.own_ref.x_own_ref, ...), custom_call_target="tpu_custom_call" | custom-call | flops 1879048192 | bytes 3670016 | tf_op jit(solution)/shard_map/forward/pallas_call | solution.py:259
  37.6 0.5 collective-permute-start.8
  38.1 1.8 %forward_high.1 = (bf16[2,128,3584]{2,1,0:T(8,128)(2,1)S(1)}, bf16[2,128,3584]{2,1,0:T(8,128)(2,1)S(1)}) custom-call(bf16[2,256,256]{2,1,0:T(8,128)(2,1)S(1)} %get-tuple-element.68.codes_ref, bf16[5,256,3584]{2,1,0:T(8,128)(2,1)S(1)} %get-tuple-element.64.dec_ref), custom_call_target="tpu_custom_call" | custom-call | flops 1409286144 | bytes 3670016 | tf_op jit(solution)/shard_map/forward_high/pallas_call | solution.py:284
  40.0 1.4 collective-permute-done.8.got_low_ref
  41.5 2.6 %collective-permute-done.9.got_ref = bf16[2,128,3584]{2,1,0:T(8,128)(2,1)S(1)} collective-permute-done((bf16[2,128,3584]{2,1,0:T(8,128)(2,1)S(1)}, bf16[2,128,3584]{2,1,0:T(8,128)(2,1)S(1)}, u32[]{:S(2)}, u32[]{:S(2)}) %collective-permute-start.9) | collective-permute-done | bytes 1835040 | tf_op jit(solution)/shard_map/ppermute | solution.py:517
  44.1 1.0 join.1
  45.1 1.5 collective-permute-start.12
  46.6 1.4 collective-permute-start.10
  48.0 5.0 %collective-permute-done.12.got_ref = bf16[64,3584]{1,0:T(8,128)(2,1)S(1)} collective-permute-done((bf16[64,3584]{1,0:T(8,128)(2,1)S(1)}, bf16[64,3584]{1,0:T(8,128)(2,1)S(1)}, u32[]{:S(2)}, u32[]{:S(2)}) %collective-permute-start.12) | collective-permute-done | bytes 458784 | tf_op jit(solution)/shard_map/ppermute | solution.py:342
  53.0 0.4 fold_low.1
  53.4 2.1 %collective-permute-start.13 = (bf16[128,3584]{1,0:T(8,128)(2,1)S(1)}, bf16[128,3584]{1,0:T(8,128)(2,1)S(1)}, u32[]{:S(2)}, u32[]{:S(2)}) collective-permute-start(bf16[128,3584]{1,0:T(8,128)(2,1)S(1)} %fold_low.1), channel_id=1, source_target_pairs={{0,3},{1,2},{2,1},{3,0},{4,7},{5,6},{6,5},{7,4},{8,104},{9,105},{1... | collective-permute-start | bytes 2752520 | tf_op jit(solution)/shard_map/ppermute | solution.py:345
  55.5 0.4 fold_high.1
  56.0 3.1 %collective-permute-start.15 = (bf16[2,3584]{1,0:T(2,128)(2,1)S(1)}, bf16[2,3584]{1,0:T(2,128)(2,1)S(1)}, u32[]{:S(2)}, u32[]{:S(2)}) collective-permute-start(bf16[2,3584]{1,0:T(2,128)(2,1)S(1)} %get-tuple-element.79), channel_id=1, source_target_pairs={{0,2},{1,3},{2,0},{3,1},{4,6},{5,7},{6,4},{7,5},{8,10},{9,11},{10,... | collective-permute-start | bytes 43016 | tf_op jit(solution)/shard_map/ppermute | solution.py:503
  59.1 0.4 collective-permute-start.16
  59.5 7.7 %collective-permute-done.13.three_ref = bf16[128,3584]{1,0:T(8,128)(2,1)S(1)} collective-permute-done((bf16[128,3584]{1,0:T(8,128)(2,1)S(1)}, bf16[128,3584]{1,0:T(8,128)(2,1)S(1)}, u32[]{:S(2)}, u32[]{:S(2)}) %collective-permute-start.13) | collective-permute-done | bytes 917536 | tf_op jit(solution)/shard_map/ppermute | solution.py:345
  67.2 1.3 collective-permute-done.11.one_ref
  68.5 0.3 total.1
  68.8 17.8 %all_to_all.10.pieces_ref = bf16[16,8,3584]{2,1,0:T(8,128)(2,1)S(1)} all-to-all(bf16[16,8,3584]{2,1,0:T(8,128)(2,1)S(1)} %bitcast.6), channel_id=1, replica_groups={{0,4,16,20,32,36,48,52,64,68,80,84,96,100,112,116},{1,5,17,21,33,37,49,..., dimensions={0} | all-to-all | bytes 1835008 | tf_op jit(solution)/shard_map/all_to_all | solution.py:520
  86.5 0.3 settle.1
  86.9 17.9 %all_to_all.11 = bf16[16,8,3584]{2,1,0:T(8,128)(2,1)S(1)} all-to-all(bf16[16,8,3584]{2,1,0:T(8,128)(2,1)S(1)} %get-tuple-element.86), channel_id=1, replica_groups={{0,4,16,20,32,36,48,52,64,68,80,84,96,100,112,116},{1,5,17,21,33,37,49,..., dimensions={0} | all-to-all | bytes 1835008 | tf_op jit(solution)/shard_map/all_to_all | solution.py:522
  104.8 1.4 collective-permute-start.18
  106.2 3.1 %collective-permute-start.21 = (bf16[128,3584]{1,0:T(8,128)(2,1)S(1)}, bf16[128,3584]{1,0:T(8,128)(2,1)S(1)}, u32[]{:S(2)}, u32[]{:S(2)}) collective-permute-start(bf16[128,3584]{1,0:T(8,128)(2,1)S(1)} %bitcast.4), channel_id=1, source_target_pairs={{0,8},{8,0},{1,9},{9,1},{2,10},{10,2},{3,11},{11,3},{4,12},{12,4},... | collective-permute-start | bytes 2752520 | tf_op jit(solution)/shard_map/ppermute | solution.py:378
  109.3 9.3 %collective-permute-done.18.quarter_ref.three_ref = bf16[128,3584]{1,0:T(8,128)(2,1)S(1)} collective-permute-done((bf16[128,3584]{1,0:T(8,128)(2,1)S(1)}, bf16[128,3584]{1,0:T(8,128)(2,1)S(1)}, u32[]{:S(2)}, u32[]{:S(2)}) %collective-permute-start.18) | collective-permute-done | bytes 917536 | tf_op jit(solution)/shard_map/ppermute | solution.py:372
  118.7 3.6 %collective-permute-start.23 = (bf16[128,3584]{1,0:T(8,128)(2,1)S(1)}, bf16[128,3584]{1,0:T(8,128)(2,1)S(1)}, u32[]{:S(2)}, u32[]{:S(2)}) collective-permute-start(bf16[128,3584]{1,0:T(8,128)(2,1)S(1)} %collective-permute-done.18.quarter_ref.three_ref), channel_id=1, source_target_pairs={{0,8},{8,0},{1,9},{9,1},{2,10},{10,2},{3,11},{11,3},{4,12},{12,4},... | collective-permute-start | bytes 2752520 | tf_op jit(solution)/shard_map/ppermute | solution.py:378
  122.3 1.3 collective-permute-start.19
  123.7 0.6 collective-permute-start.22
  124.2 2.1 %collective-permute-done.20.far3_ref = bf16[64,3584]{1,0:T(8,128)(2,1)S(1)} collective-permute-done((bf16[64,3584]{1,0:T(8,128)(2,1)S(1)}, bf16[64,3584]{1,0:T(8,128)(2,1)S(1)}, u32[]{:S(2)}, u32[]{:S(2)}) %collective-permute-start.20) | collective-permute-done | bytes 458784 | tf_op jit(solution)/shard_map/ppermute | solution.py:376
  126.3 4.4 %collective-permute-start.25 = (bf16[64,3584]{1,0:T(8,128)(2,1)S(1)}, bf16[64,3584]{1,0:T(8,128)(2,1)S(1)}, u32[]{:S(2)}, u32[]{:S(2)}) collective-permute-start(bf16[64,3584]{1,0:T(8,128)(2,1)S(1)} %collective-permute-done.20.far3_ref), channel_id=1, source_target_pairs={{0,8},{8,0},{1,9},{9,1},{2,10},{10,2},{3,11},{11,3},{4,12},{12,4},... | collective-permute-start | bytes 1376264 | tf_op jit(solution)/shard_map/ppermute | solution.py:378
  130.7 0.6 collective-permute-done.19.far1_ref
  131.2 0.9 collective-permute-start.24
  132.1 0.5 collective-permute-start.26
  132.6 2.2 %collective-permute-start.27 = (bf16[2,3584]{1,0:T(2,128)(2,1)S(1)}, bf16[2,3584]{1,0:T(2,128)(2,1)S(1)}, u32[]{:S(2)}, u32[]{:S(2)}) collective-permute-start(bf16[2,3584]{1,0:T(2,128)(2,1)S(1)} %get-tuple-element.94), channel_id=1, source_target_pairs={{0,2},{1,3},{2,0},{3,1},{4,6},{5,7},{6,4},{7,5},{8,10},{9,11},{10,... | collective-permute-start | bytes 43016 | tf_op jit(solution)/shard_map/ppermute | solution.py:503
  134.8 0.8 collective-permute-start.28
  136.1 0.5 collective-permute-done.27.rest_2_
  136.7 1.0 collective-permute-done.28.rest_3_
  137.7 9.5 %backward.1 = (bf16[5,256,3584]{2,1,0:T(8,128)(2,1)}, bf16[2,3584,256]{2,1,0:T(8,128)(2,1)}, f32[2,256]{1,0:T(2,128)}, bf16[4,2,3584]{2,1,0:T(2,128)(2,1)}) custom-call(bf16[2,256,256]{2,1,0:T(8,128)(2,1)S(1)} %get-tuple-element.65.turned_ref, f32[2,256,256]{2,1,0:T(8,128)S(1)} %get-tuple-element.66.slope_ref, ...), custom_call_target="tpu_custom_call" | custom-call | flops 5637144576 | bytes 12845056 | tf_op jit(solution)/shard_map/backward/pallas_call | solution.py:474
  (31 shorter events, 1.2 us)
Async XLA Ops:
  1.7 10.6 %collective-permute-start.3 = (bf16[2,16,3584]{2,1,0:T(8,128)(2,1)S(1)}, bf16[2,16,3584]{2,1,0:T(8,128)(2,1)S(1)}, u32[]{:S(2)}, u32[]{:S(2)}) collective-permute-start(bf16[2,16,3584]{2,1,0:T(8,128)(2,1)S(1)} %get-tuple-element.56.refs_0_), channel_id=1, source_target_pairs={{0,4},{1,5},{2,6},{3,7},{4,0},{5,1},{6,2},{7,3},{8,12},{9,13},{10,... | collective-permute-start | bytes 688136 | tf_op jit(solution)/shard_map/ppermute | solution.py:141
  6.2 8.8 %collective-permute-start = (bf16[2,16,3584]{2,1,0:T(8,128)(2,1)S(1)}, bf16[2,16,3584]{2,1,0:T(8,128)(2,1)S(1)}, u32[]{:S(2)}, u32[]{:S(2)}) collective-permute-start(bf16[2,16,3584]{2,1,0:T(8,128)(2,1)S(1)} %get-tuple-element.56.refs_0_), channel_id=1, source_target_pairs={{0,1},{1,0},{2,3},{3,2},{4,5},{5,4},{6,7},{7,6},{8,9},{9,8},{10,11... | collective-permute-start | bytes 688136 | tf_op jit(solution)/shard_map/ppermute | solution.py:142
  12.2 22.8 %copy-start = (s32[4,8,32]{2,1,0:T(8,128)S(1)}, s32[4,8,32]{2,1,0:T(8,128)}, u32[]{:S(2)}) copy-start(s32[4,8,32]{2,1,0:T(8,128)} %active_ref.1) | copy-start | bytes 12292
  12.2 22.8 %copy-start.1 = (f32[2,256]{1,0:T(2,128)S(1)}, f32[2,256]{1,0:T(2,128)}, u32[]{:S(2)}) copy-start(f32[2,256]{1,0:T(2,128)} %bias_ref.1) | copy-start | bytes 6148
  12.3 7.1 %collective-permute-start.5 = (bf16[2,16,3584]{2,1,0:T(8,128)(2,1)S(1)}, bf16[2,16,3584]{2,1,0:T(8,128)(2,1)S(1)}, u32[]{:S(2)}, u32[]{:S(2)}) collective-permute-start(bf16[2,16,3584]{2,1,0:T(8,128)(2,1)S(1)} %collective-permute-done.3.refs_4_), channel_id=1, source_target_pairs={{0,3},{1,2},{2,1},{3,0},{4,7},{5,6},{6,5},{7,4},{8,11},{9,10},{10,... | collective-permute-start | bytes 688136 | tf_op jit(solution)/shard_map/ppermute | solution.py:144
  14.2 10.1 %collective-permute-start.1 = (bf16[2,16,3584]{2,1,0:T(8,128)(2,1)S(1)}, bf16[2,16,3584]{2,1,0:T(8,128)(2,1)S(1)}, u32[]{:S(2)}, u32[]{:S(2)}) collective-permute-start(bf16[2,16,3584]{2,1,0:T(8,128)(2,1)S(1)} %get-tuple-element.56.refs_0_), channel_id=1, source_target_pairs={{0,3},{1,2},{2,1},{3,0},{4,7},{5,6},{6,5},{7,4},{8,11},{9,10},{10,... | collective-permute-start | bytes 688136 | tf_op jit(solution)/shard_map/ppermute | solution.py:142
  15.0 14.2 %collective-permute-start.4 = (bf16[2,16,3584]{2,1,0:T(8,128)(2,1)S(1)}, bf16[2,16,3584]{2,1,0:T(8,128)(2,1)S(1)}, u32[]{:S(2)}, u32[]{:S(2)}) collective-permute-start(bf16[2,16,3584]{2,1,0:T(8,128)(2,1)S(1)} %collective-permute-done.3.refs_4_), channel_id=1, source_target_pairs={{0,1},{1,0},{2,3},{3,2},{4,5},{5,4},{6,7},{7,6},{8,9},{9,8},{10,11... | collective-permute-start | bytes 688136 | tf_op jit(solution)/shard_map/ppermute | solution.py:144
  15.0 14.2 %collective-permute-start.2 = (bf16[2,16,3584]{2,1,0:T(8,128)(2,1)S(1)}, bf16[2,16,3584]{2,1,0:T(8,128)(2,1)S(1)}, u32[]{:S(2)}, u32[]{:S(2)}) collective-permute-start(bf16[2,16,3584]{2,1,0:T(8,128)(2,1)S(1)} %collective-permute-done.refs_1_), channel_id=1, source_target_pairs={{0,3},{1,2},{2,1},{3,0},{4,7},{5,6},{6,5},{7,4},{8,11},{9,10},{10,... | collective-permute-start | bytes 688136 | tf_op jit(solution)/shard_map/ppermute | solution.py:145
  19.4 9.8 %collective-permute-start.6 = (bf16[2,16,3584]{2,1,0:T(8,128)(2,1)S(1)}, bf16[2,16,3584]{2,1,0:T(8,128)(2,1)S(1)}, u32[]{:S(2)}, u32[]{:S(2)}) collective-permute-start(bf16[2,16,3584]{2,1,0:T(8,128)(2,1)S(1)} %collective-permute-done.5.refs_6_), channel_id=1, source_target_pairs={{0,1},{1,0},{2,3},{3,2},{4,5},{5,4},{6,7},{7,6},{8,9},{9,8},{10,11... | collective-permute-start | bytes 688136 | tf_op jit(solution)/shard_map/ppermute | solution.py:146
  29.4 5.7 %collective-permute-start.7 = (bf16[8,2,16,3584]{3,2,1,0:T(8,128)(2,1)S(1)}, bf16[8,2,16,3584]{3,2,1,0:T(8,128)(2,1)S(1)}, u32[]{:S(2)}, u32[]{:S(2)}) collective-permute-start(bf16[8,2,16,3584]{3,2,1,0:T(8,128)(2,1)S(1)} %arrange.1.own_ref.x_own_ref), channel_id=1, source_target_pairs={{0,8},{8,0},{1,9},{9,1},{2,10},{10,2},{3,11},{11,3},{4,12},{12,4},... | collective-permute-start | bytes 5505032 | tf_op jit(solution)/shard_map/ppermute | solution.py:512
  37.6 3.9 %collective-permute-start.8 = (bf16[2,128,3584]{2,1,0:T(8,128)(2,1)S(1)}, bf16[2,128,3584]{2,1,0:T(8,128)(2,1)S(1)}, u32[]{:S(2)}, u32[]{:S(2)}) collective-permute-start(bf16[2,128,3584]{2,1,0:T(8,128)(2,1)S(1)} %get-tuple-element.70), channel_id=1, source_target_pairs={{0,8},{8,0},{1,9},{9,1},{2,10},{10,2},{3,11},{11,3},{4,12},{12,4},... | collective-permute-start | bytes 5505032 | tf_op jit(solution)/shard_map/ppermute | solution.py:515
  39.8 4.3 %collective-permute-start.9 = (bf16[2,128,3584]{2,1,0:T(8,128)(2,1)S(1)}, bf16[2,128,3584]{2,1,0:T(8,128)(2,1)S(1)}, u32[]{:S(2)}, u32[]{:S(2)}) collective-permute-start(bf16[2,128,3584]{2,1,0:T(8,128)(2,1)S(1)} %get-tuple-element.71), channel_id=1, source_target_pairs={{0,8},{8,0},{1,9},{9,1},{2,10},{10,2},{3,11},{11,3},{4,12},{12,4},... | collective-permute-start | bytes 5505032 | tf_op jit(solution)/shard_map/ppermute | solution.py:517
  45.1 7.9 %collective-permute-start.12 = (bf16[64,3584]{1,0:T(8,128)(2,1)S(1)}, bf16[64,3584]{1,0:T(8,128)(2,1)S(1)}, u32[]{:S(2)}, u32[]{:S(2)}) collective-permute-start(bf16[64,3584]{1,0:T(8,128)(2,1)S(1)} %get-tuple-element.76), channel_id=1, source_target_pairs={{0,1},{1,0},{2,3},{3,2},{4,5},{5,4},{6,7},{7,6},{8,40},{9,41},{10,... | collective-permute-start | bytes 1376264 | tf_op jit(solution)/shard_map/ppermute | solution.py:342
  46.6 8.9 %collective-permute-start.10 = (bf16[64,3584]{1,0:T(8,128)(2,1)S(1)}, bf16[64,3584]{1,0:T(8,128)(2,1)S(1)}, u32[]{:S(2)}, u32[]{:S(2)}) collective-permute-start(bf16[64,3584]{1,0:T(8,128)(2,1)S(1)} %get-tuple-element.74), channel_id=1, source_target_pairs={{0,3},{1,2},{2,1},{3,0},{4,7},{5,6},{6,5},{7,4},{8,104},{9,105},{1... | collective-permute-start | bytes 1376264 | tf_op jit(solution)/shard_map/ppermute | solution.py:343
  53.4 13.8 %collective-permute-start.13 = (bf16[128,3584]{1,0:T(8,128)(2,1)S(1)}, bf16[128,3584]{1,0:T(8,128)(2,1)S(1)}, u32[]{:S(2)}, u32[]{:S(2)}) collective-permute-start(bf16[128,3584]{1,0:T(8,128)(2,1)S(1)} %fold_low.1), channel_id=1, source_target_pairs={{0,3},{1,2},{2,1},{3,0},{4,7},{5,6},{6,5},{7,4},{8,104},{9,105},{1... | collective-permute-start | bytes 2752520 | tf_op jit(solution)/shard_map/ppermute | solution.py:345
  55.8 12.6 %collective-permute-start.11 = (bf16[128,3584]{1,0:T(8,128)(2,1)S(1)}, bf16[128,3584]{1,0:T(8,128)(2,1)S(1)}, u32[]{:S(2)}, u32[]{:S(2)}) collective-permute-start(bf16[128,3584]{1,0:T(8,128)(2,1)S(1)} %fold_high.1), channel_id=1, source_target_pairs={{0,1},{1,0},{2,3},{3,2},{4,5},{5,4},{6,7},{7,6},{8,40},{9,41},{10,... | collective-permute-start | bytes 2752520 | tf_op jit(solution)/shard_map/ppermute | solution.py:349
  55.9 12.8 %collective-permute-start.14 = (bf16[2,3584]{1,0:T(2,128)(2,1)S(1)}, bf16[2,3584]{1,0:T(2,128)(2,1)S(1)}, u32[]{:S(2)}, u32[]{:S(2)}) collective-permute-start(bf16[2,3584]{1,0:T(2,128)(2,1)S(1)} %get-tuple-element.78), channel_id=1, source_target_pairs={{0,1},{1,2},{2,3},{3,0},{4,5},{5,6},{6,7},{7,4},{8,9},{9,10},{10,1... | collective-permute-start | bytes 43016 | tf_op jit(solution)/shard_map/ppermute | solution.py:503
  56.0 12.7 %collective-permute-start.15 = (bf16[2,3584]{1,0:T(2,128)(2,1)S(1)}, bf16[2,3584]{1,0:T(2,128)(2,1)S(1)}, u32[]{:S(2)}, u32[]{:S(2)}) collective-permute-start(bf16[2,3584]{1,0:T(2,128)(2,1)S(1)} %get-tuple-element.79), channel_id=1, source_target_pairs={{0,2},{1,3},{2,0},{3,1},{4,6},{5,7},{6,4},{7,5},{8,10},{9,11},{10,... | collective-permute-start | bytes 43016 | tf_op jit(solution)/shard_map/ppermute | solution.py:503
  59.1 9.7 %collective-permute-start.16 = (bf16[2,3584]{1,0:T(2,128)(2,1)S(1)}, bf16[2,3584]{1,0:T(2,128)(2,1)S(1)}, u32[]{:S(2)}, u32[]{:S(2)}) collective-permute-start(bf16[2,3584]{1,0:T(2,128)(2,1)S(1)} %get-tuple-element.80), channel_id=1, source_target_pairs={{0,3},{1,0},{2,1},{3,2},{4,7},{5,4},{6,5},{7,6},{8,11},{9,8},{10,9... | collective-permute-start | bytes 43016 | tf_op jit(solution)/shard_map/ppermute | solution.py:503
  104.8 13.8 %collective-permute-start.18 = (bf16[128,3584]{1,0:T(8,128)(2,1)S(1)}, bf16[128,3584]{1,0:T(8,128)(2,1)S(1)}, u32[]{:S(2)}, u32[]{:S(2)}) collective-permute-start(bf16[128,3584]{1,0:T(8,128)(2,1)S(1)} %bitcast.2), channel_id=1, source_target_pairs={{0,3},{1,2},{2,1},{3,0},{4,7},{5,6},{6,5},{7,4},{8,104},{9,105},{1... | collective-permute-start | bytes 2752520 | tf_op jit(solution)/shard_map/ppermute | solution.py:372
  106.2 16.1 %collective-permute-start.17 = (bf16[128,3584]{1,0:T(8,128)(2,1)S(1)}, bf16[128,3584]{1,0:T(8,128)(2,1)S(1)}, u32[]{:S(2)}, u32[]{:S(2)}) collective-permute-start(bf16[128,3584]{1,0:T(8,128)(2,1)S(1)} %bitcast.3), channel_id=1, source_target_pairs={{0,1},{1,0},{2,3},{3,2},{4,5},{5,4},{6,7},{7,6},{8,40},{9,41},{10,... | collective-permute-start | bytes 2752520 | tf_op jit(solution)/shard_map/ppermute | solution.py:371
  106.2 26.0 %collective-permute-start.21 = (bf16[128,3584]{1,0:T(8,128)(2,1)S(1)}, bf16[128,3584]{1,0:T(8,128)(2,1)S(1)}, u32[]{:S(2)}, u32[]{:S(2)}) collective-permute-start(bf16[128,3584]{1,0:T(8,128)(2,1)S(1)} %bitcast.4), channel_id=1, source_target_pairs={{0,8},{8,0},{1,9},{9,1},{2,10},{10,2},{3,11},{11,3},{4,12},{12,4},... | collective-permute-start | bytes 2752520 | tf_op jit(solution)/shard_map/ppermute | solution.py:378
  118.6 7.7 %collective-permute-start.20 = (bf16[64,3584]{1,0:T(8,128)(2,1)S(1)}, bf16[64,3584]{1,0:T(8,128)(2,1)S(1)}, u32[]{:S(2)}, u32[]{:S(2)}) collective-permute-start(bf16[64,3584]{1,0:T(8,128)(2,1)S(1)} %half_high.1), channel_id=1, source_target_pairs={{0,1},{1,0},{2,3},{3,2},{4,5},{5,4},{6,7},{7,6},{8,40},{9,41},{10,... | collective-permute-start | bytes 1376264 | tf_op jit(solution)/shard_map/ppermute | solution.py:376
  118.7 16.1 %collective-permute-start.23 = (bf16[128,3584]{1,0:T(8,128)(2,1)S(1)}, bf16[128,3584]{1,0:T(8,128)(2,1)S(1)}, u32[]{:S(2)}, u32[]{:S(2)}) collective-permute-start(bf16[128,3584]{1,0:T(8,128)(2,1)S(1)} %collective-permute-done.18.quarter_ref.three_ref), channel_id=1, source_target_pairs={{0,8},{8,0},{1,9},{9,1},{2,10},{10,2},{3,11},{11,3},{4,12},{12,4},... | collective-permute-start | bytes 2752520 | tf_op jit(solution)/shard_map/ppermute | solution.py:378
  122.3 8.9 %collective-permute-start.19 = (bf16[64,3584]{1,0:T(8,128)(2,1)S(1)}, bf16[64,3584]{1,0:T(8,128)(2,1)S(1)}, u32[]{:S(2)}, u32[]{:S(2)}) collective-permute-start(bf16[64,3584]{1,0:T(8,128)(2,1)S(1)} %half_low.1), channel_id=1, source_target_pairs={{0,3},{1,2},{2,1},{3,0},{4,7},{5,6},{6,5},{7,4},{8,104},{9,105},{1... | collective-permute-start | bytes 1376264 | tf_op jit(solution)/shard_map/ppermute | solution.py:374
  123.7 12.2 %collective-permute-start.22 = (bf16[128,3584]{1,0:T(8,128)(2,1)S(1)}, bf16[128,3584]{1,0:T(8,128)(2,1)S(1)}, u32[]{:S(2)}, u32[]{:S(2)}) collective-permute-start(bf16[128,3584]{1,0:T(8,128)(2,1)S(1)} %collective-permute-done.17.quarter_ref.one_ref), channel_id=1, source_target_pairs={{0,8},{8,0},{1,9},{9,1},{2,10},{10,2},{3,11},{11,3},{4,12},{12,4},... | collective-permute-start | bytes 2752520 | tf_op jit(solution)/shard_map/ppermute | solution.py:378
  126.3 6.3 %collective-permute-start.25 = (bf16[64,3584]{1,0:T(8,128)(2,1)S(1)}, bf16[64,3584]{1,0:T(8,128)(2,1)S(1)}, u32[]{:S(2)}, u32[]{:S(2)}) collective-permute-start(bf16[64,3584]{1,0:T(8,128)(2,1)S(1)} %collective-permute-done.20.far3_ref), channel_id=1, source_target_pairs={{0,8},{8,0},{1,9},{9,1},{2,10},{10,2},{3,11},{11,3},{4,12},{12,4},... | collective-permute-start | bytes 1376264 | tf_op jit(solution)/shard_map/ppermute | solution.py:378
  131.2 4.6 %collective-permute-start.24 = (bf16[64,3584]{1,0:T(8,128)(2,1)S(1)}, bf16[64,3584]{1,0:T(8,128)(2,1)S(1)}, u32[]{:S(2)}, u32[]{:S(2)}) collective-permute-start(bf16[64,3584]{1,0:T(8,128)(2,1)S(1)} %collective-permute-done.19.far1_ref), channel_id=1, source_target_pairs={{0,8},{8,0},{1,9},{9,1},{2,10},{10,2},{3,11},{11,3},{4,12},{12,4},... | collective-permute-start | bytes 1376264 | tf_op jit(solution)/shard_map/ppermute | solution.py:378
  132.1 4.0 %collective-permute-start.26 = (bf16[2,3584]{1,0:T(2,128)(2,1)S(1)}, bf16[2,3584]{1,0:T(2,128)(2,1)S(1)}, u32[]{:S(2)}, u32[]{:S(2)}) collective-permute-start(bf16[2,3584]{1,0:T(2,128)(2,1)S(1)} %get-tuple-element.93), channel_id=1, source_target_pairs={{0,1},{1,2},{2,3},{3,0},{4,5},{5,6},{6,7},{7,4},{8,9},{9,10},{10,1... | collective-permute-start | bytes 43016 | tf_op jit(solution)/shard_map/ppermute | solution.py:503
  132.6 4.1 %collective-permute-start.27 = (bf16[2,3584]{1,0:T(2,128)(2,1)S(1)}, bf16[2,3584]{1,0:T(2,128)(2,1)S(1)}, u32[]{:S(2)}, u32[]{:S(2)}) collective-permute-start(bf16[2,3584]{1,0:T(2,128)(2,1)S(1)} %get-tuple-element.94), channel_id=1, source_target_pairs={{0,2},{1,3},{2,0},{3,1},{4,6},{5,7},{6,4},{7,5},{8,10},{9,11},{10,... | collective-permute-start | bytes 43016 | tf_op jit(solution)/shard_map/ppermute | solution.py:503
  134.8 2.9 %collective-permute-start.28 = (bf16[2,3584]{1,0:T(2,128)(2,1)S(1)}, bf16[2,3584]{1,0:T(2,128)(2,1)S(1)}, u32[]{:S(2)}, u32[]{:S(2)}) collective-permute-start(bf16[2,3584]{1,0:T(2,128)(2,1)S(1)} %get-tuple-element.95), channel_id=1, source_target_pairs={{0,3},{1,0},{2,1},{3,2},{4,7},{5,4},{6,5},{7,6},{8,11},{9,8},{10,9... | collective-permute-start | bytes 43016 | tf_op jit(solution)/shard_map/ppermute | solution.py:503

commit v8 on v7

--- a/solution.py
+++ b/solution.py
@@ -366,10 +366,11 @@
             out_ref[t, pl.ds(pl.multiple_of(x * BOX, BOX), BOX)] = in_ref[at : at + BOX]
 
 
-def _gather_ring(quarter):
+def _gather_ring(quarter, recon):
     half = jax.ShapeDtypeStruct((QUARTER // 2, D), BF)
     one = lax.ppermute(quarter, ALL, RING[1])
     three = lax.ppermute(quarter, ALL, RING[3])
+    one, three, recon = lax.optimization_barrier((one, three, _around_y(recon)))
     pass3 = _plain(functools.partial(_half_kernel, 0), half, "half_low", one)
     far1 = lax.ppermute(pass3, ALL, RING[3])
     pass1 = _plain(functools.partial(_half_kernel, QUARTER // 2), half, "half_high", three)
@@ -379,7 +380,7 @@
     whole = jax.ShapeDtypeStruct((LAYERS, HALF, D), BF)
     own = _plain(functools.partial(_assemble_kernel, False), whole, "assemble_own", *pieces)
     oth = _plain(functools.partial(_assemble_kernel, True), whole, "assemble_oth", *others)
-    return own, oth
+    return own, oth, recon
 
 
 def _settle_kernel(pieces_ref, *rest):
@@ -521,8 +522,7 @@
     errors, *recon = _settle(pieces, targets)
     quarter = lax.all_to_all(errors, ALL, 0, 0, axis_index_groups=GROUPS).reshape(QUARTER, D)
     quarter, recon = lax.optimization_barrier((quarter, recon))
-    err_own, err_oth = _gather_ring(quarter)
-    recon = _around_y(recon)
+    err_own, err_oth, recon = _gather_ring(quarter, recon)
     grad_decoder, grad_encoder, grad_bias, recon = _backward(
         turned, slope, err_own, err_oth, own, oth, dec, recon
     )

time: 147 us -> 145 us (0.986)
  waiting for transfers between devices: 47.3 us -> 39.4 us
  starting transfers between devices: 40.8 us -> 46.5 us
    ppermute x1, waiting for transfers between devices: 9.28 us -> 0.01 us  [_gather_ring(): three = lax.ppermute(quarter, ALL, RING[3])]
    ppermute x5, starting transfers between devices: 12.5 us -> 17.3 us  [_gather_ring(): others = [lax.ppermute(piece, 'core', SWAP) for piece in pieces]]
    ppermute x1, waiting for transfers between devices: 2.07 us -> 4.4 us  [_gather_ring(): far3 = lax.ppermute(pass1, ALL, RING[1])]
    ppermute x6, waiting for transfers between devices: 1.57 us -> 0.02 us  [_around_y(): lax.ppermute(pieces[j], 'y', [(i, (i + j) % 4) for i in range(4)])]
  transfers between devices with their start and end apart: 29 -> 29, of which waited for: 14 -> 11; matrix products, arithmetic and copies ran while one was open for 0% -> 0% of each run, Pallas kernels for 5% -> 5%
where the time goes in v8:
time: 145 us
  starting transfers between devices  46.5 us (32%)
  waiting for transfers between devices  39.4 us (27%)
  blocking collectives  35.7 us (25%)
  Pallas kernels  22.7 us (16%)
    all_to_all x1, blocking collectives, per_device(): lax.all_to_all(errors, ALL, 0, 0, axis_index_groups=GROUPS)  17.9 us
    all_to_all x1, blocking collectives, per_device(): lax.all_to_all(quarter.reshape(16, 8, D), ALL, 0, 0, axis_index_groups=GR...  17.8 us
    ppermute x5, starting transfers between devices, _gather_ring(): others = [lax.ppermute(piece, 'core', SWAP) for piece in pieces]  17.3 us
    pallas_call x1, Pallas kernels, _backward(): pl.pallas_call(_backward_kernel, grid=(PAIRS + 2,), in_specs=[WHOLE] * 11...  9.6 us
    ppermute x6, starting transfers between devices, _around_y(): lax.ppermute(pieces[j], 'y', [(i, (i + j) % 4) for i in range(4)])  7.91 us
    ppermute x1, waiting for transfers between devices, _reduce_ring(): from3 = lax.ppermute(to3, ALL, RING[3])  7.71 us
    ppermute x1, waiting for transfers between devices, _reduce_ring(): got1 = lax.ppermute(far1, ALL, RING[1])  5.04 us
    ppermute x1, waiting for transfers between devices, _gather_inputs(): mine_2 = lax.ppermute(mine_1, ALL, ALONG_Y[3])  4.91 us
  transfers between devices with their start and end apart: 29, of which 11 were waited for; matrix products, arithmetic and copies ran while one was open for 0% of the time, Pallas kernels for 5%

profile of v8, /device:TPU:1, one launch (start us, length us, event | category | flops | bytes accessed | tf_op | source)
XLA Modules:
  0.0 145.1 jit_solution(7330236318610711538)
XLA Ops:
  0.6 1.0 prepare.1
  1.7 4.5 %collective-permute-start.3 = (bf16[2,16,3584]{2,1,0:T(8,128)(2,1)S(1)}, bf16[2,16,3584]{2,1,0:T(8,128)(2,1)S(1)}, u32[]{:S(2)}, u32[]{:S(2)}) collective-permute-start(bf16[2,16,3584]{2,1,0:T(8,128)(2,1)S(1)} %get-tuple-element.62.refs_0_), channel_id=1, source_target_pairs={{0,4},{1,5},{2,6},{3,7},{4,0},{5,1},{6,2},{7,3},{8,12},{9,13},{10,... | collective-permute-start | bytes 688136 | tf_op jit(solution)/shard_map/ppermute | solution.py:141
  6.2 1.3 collective-permute-start
  7.5 4.7 %stage.1 = (bf16[2,3584,256]{2,1,0:T(8,128)(2,1)S(1)}, bf16[5,256,3584]{2,1,0:T(8,128)(2,1)S(1)}) custom-call(bf16[2,3584,256]{2,1,0:T(8,128)(2,1)} %enc_hbm, bf16[5,256,3584]{2,1,0:T(8,128)(2,1)} %dec_hbm), custom_call_target="tpu_custom_call" | custom-call | bytes 25690112 | tf_op jit(solution)/shard_map/stage/pallas_call | solution.py:209
  12.3 2.0 %collective-permute-start.5 = (bf16[2,16,3584]{2,1,0:T(8,128)(2,1)S(1)}, bf16[2,16,3584]{2,1,0:T(8,128)(2,1)S(1)}, u32[]{:S(2)}, u32[]{:S(2)}) collective-permute-start(bf16[2,16,3584]{2,1,0:T(8,128)(2,1)S(1)} %collective-permute-done.3.refs_4_), channel_id=1, source_target_pairs={{0,3},{1,2},{2,1},{3,0},{4,7},{5,6},{6,5},{7,4},{8,11},{9,10},{10,... | collective-permute-start | bytes 688136 | tf_op jit(solution)/shard_map/ppermute | solution.py:144
  14.2 0.8 collective-permute-start.1
  15.0 1.9 %collective-permute-start.2 = (bf16[2,16,3584]{2,1,0:T(8,128)(2,1)S(1)}, bf16[2,16,3584]{2,1,0:T(8,128)(2,1)S(1)}, u32[]{:S(2)}, u32[]{:S(2)}) collective-permute-start(bf16[2,16,3584]{2,1,0:T(8,128)(2,1)S(1)} %collective-permute-done.refs_1_), channel_id=1, source_target_pairs={{0,3},{1,2},{2,1},{3,0},{4,7},{5,6},{6,5},{7,4},{8,11},{9,10},{10,... | collective-permute-start | bytes 688136 | tf_op jit(solution)/shard_map/ppermute | solution.py:145
  16.9 2.5 %collective-permute-done.5.refs_6_ = bf16[2,16,3584]{2,1,0:T(8,128)(2,1)S(1)} collective-permute-done((bf16[2,16,3584]{2,1,0:T(8,128)(2,1)S(1)}, bf16[2,16,3584]{2,1,0:T(8,128)(2,1)S(1)}, u32[]{:S(2)}, u32[]{:S(2)}) %collective-permute-start.5) | collective-permute-done | bytes 229408 | tf_op jit(solution)/shard_map/ppermute | solution.py:144
  19.4 4.9 %collective-permute-done.1.refs_2_ = bf16[2,16,3584]{2,1,0:T(8,128)(2,1)S(1)} collective-permute-done((bf16[2,16,3584]{2,1,0:T(8,128)(2,1)S(1)}, bf16[2,16,3584]{2,1,0:T(8,128)(2,1)S(1)}, u32[]{:S(2)}, u32[]{:S(2)}) %collective-permute-start.1) | collective-permute-done | bytes 229408 | tf_op jit(solution)/shard_map/ppermute | solution.py:142
  24.3 4.9 %collective-permute-done.2.refs_3_ = bf16[2,16,3584]{2,1,0:T(8,128)(2,1)S(1)} collective-permute-done((bf16[2,16,3584]{2,1,0:T(8,128)(2,1)S(1)}, bf16[2,16,3584]{2,1,0:T(8,128)(2,1)S(1)}, u32[]{:S(2)}, u32[]{:S(2)}) %collective-permute-start.2) | collective-permute-done | bytes 229408 | tf_op jit(solution)/shard_map/ppermute | solution.py:145
  29.2 0.1 arrange.1.own_ref.x_own_ref
  29.4 2.2 %collective-permute-start.7 = (bf16[8,2,16,3584]{3,2,1,0:T(8,128)(2,1)S(1)}, bf16[8,2,16,3584]{3,2,1,0:T(8,128)(2,1)S(1)}, u32[]{:S(2)}, u32[]{:S(2)}) collective-permute-start(bf16[8,2,16,3584]{3,2,1,0:T(8,128)(2,1)S(1)} %arrange.1.own_ref.x_own_ref), channel_id=1, source_target_pairs={{0,8},{8,0},{1,9},{9,1},{2,10},{10,2},{3,11},{11,3},{4,12},{12,4},... | collective-permute-start | bytes 5505032 | tf_op jit(solution)/shard_map/ppermute | solution.py:513
  31.6 3.4 %collective-permute-done.7.oth_ref.x_oth_ref = bf16[8,2,16,3584]{3,2,1,0:T(8,128)(2,1)S(1)} collective-permute-done((bf16[8,2,16,3584]{3,2,1,0:T(8,128)(2,1)S(1)}, bf16[8,2,16,3584]{3,2,1,0:T(8,128)(2,1)S(1)}, u32[]{:S(2)}, u32[]{:S(2)}) %collective-permute-start.7) | collective-permute-done | bytes 1835040 | tf_op jit(solution)/shard_map/ppermute | solution.py:513
  35.0 2.5 %forward.1 = (bf16[2,128,3584]{2,1,0:T(8,128)(2,1)S(1)}, bf16[2,128,3584]{2,1,0:T(8,128)(2,1)S(1)}, bf16[2,256,256]{2,1,0:T(8,128)(2,1)S(1)}, bf16[2,256,256]{2,1,0:T(8,128)(2,1)S(1)}, f32[2,256,256]{2,1,0:T(8,128)S(1)}) custom-call(bf16[8,2,16,3584]{3,2,1,0:T(8,128)(2,1)S(1)} %arrange.1.own_ref.x_own_ref, ...), custom_call_target="tpu_custom_call" | custom-call | flops 1879048192 | bytes 3670016 | tf_op jit(solution)/shard_map/forward/pallas_call | solution.py:259
  37.6 0.5 collective-permute-start.8
  38.1 1.8 %forward_high.1 = (bf16[2,128,3584]{2,1,0:T(8,128)(2,1)S(1)}, bf16[2,128,3584]{2,1,0:T(8,128)(2,1)S(1)}) custom-call(bf16[2,256,256]{2,1,0:T(8,128)(2,1)S(1)} %get-tuple-element.74.codes_ref, bf16[5,256,3584]{2,1,0:T(8,128)(2,1)S(1)} %get-tuple-element.70.dec_ref), custom_call_target="tpu_custom_call" | custom-call | flops 1409286144 | bytes 3670016 | tf_op jit(solution)/shard_map/forward_high/pallas_call | solution.py:284
  39.8 0.2 collective-permute-start.9
  40.0 1.4 collective-permute-done.8.got_low_ref
  41.5 2.6 %collective-permute-done.9.got_ref = bf16[2,128,3584]{2,1,0:T(8,128)(2,1)S(1)} collective-permute-done((bf16[2,128,3584]{2,1,0:T(8,128)(2,1)S(1)}, bf16[2,128,3584]{2,1,0:T(8,128)(2,1)S(1)}, u32[]{:S(2)}, u32[]{:S(2)}) %collective-permute-start.9) | collective-permute-done | bytes 1835040 | tf_op jit(solution)/shard_map/ppermute | solution.py:518
  44.1 1.0 join.1
  45.1 1.5 %collective-permute-start.12 = (bf16[64,3584]{1,0:T(8,128)(2,1)S(1)}, bf16[64,3584]{1,0:T(8,128)(2,1)S(1)}, u32[]{:S(2)}, u32[]{:S(2)}) collective-permute-start(bf16[64,3584]{1,0:T(8,128)(2,1)S(1)} %get-tuple-element.82), channel_id=1, source_target_pairs={{0,1},{1,0},{2,3},{3,2},{4,5},{5,4},{6,7},{7,6},{8,40},{9,41},{10,... | collective-permute-start | bytes 1376264 | tf_op jit(solution)/shard_map/ppermute | solution.py:342
  46.6 1.4 collective-permute-start.10
  48.0 5.0 %collective-permute-done.12.got_ref = bf16[64,3584]{1,0:T(8,128)(2,1)S(1)} collective-permute-done((bf16[64,3584]{1,0:T(8,128)(2,1)S(1)}, bf16[64,3584]{1,0:T(8,128)(2,1)S(1)}, u32[]{:S(2)}, u32[]{:S(2)}) %collective-permute-start.12) | collective-permute-done | bytes 458784 | tf_op jit(solution)/shard_map/ppermute | solution.py:342
  53.0 0.4 fold_low.1
  53.4 2.1 %collective-permute-start.13 = (bf16[128,3584]{1,0:T(8,128)(2,1)S(1)}, bf16[128,3584]{1,0:T(8,128)(2,1)S(1)}, u32[]{:S(2)}, u32[]{:S(2)}) collective-permute-start(bf16[128,3584]{1,0:T(8,128)(2,1)S(1)} %fold_low.1), channel_id=1, source_target_pairs={{0,3},{1,2},{2,1},{3,0},{4,7},{5,6},{6,5},{7,4},{8,104},{9,105},{1... | collective-permute-start | bytes 2752520 | tf_op jit(solution)/shard_map/ppermute | solution.py:345
  55.5 0.4 fold_high.1
  56.0 3.1 %collective-permute-start.15 = (bf16[2,3584]{1,0:T(2,128)(2,1)S(1)}, bf16[2,3584]{1,0:T(2,128)(2,1)S(1)}, u32[]{:S(2)}, u32[]{:S(2)}) collective-permute-start(bf16[2,3584]{1,0:T(2,128)(2,1)S(1)} %get-tuple-element.85), channel_id=1, source_target_pairs={{0,2},{1,3},{2,0},{3,1},{4,6},{5,7},{6,4},{7,5},{8,10},{9,11},{10,... | collective-permute-start | bytes 43016 | tf_op jit(solution)/shard_map/ppermute | solution.py:504
  59.1 0.4 collective-permute-start.16
  59.5 7.7 %collective-permute-done.13.three_ref = bf16[128,3584]{1,0:T(8,128)(2,1)S(1)} collective-permute-done((bf16[128,3584]{1,0:T(8,128)(2,1)S(1)}, bf16[128,3584]{1,0:T(8,128)(2,1)S(1)}, u32[]{:S(2)}, u32[]{:S(2)}) %collective-permute-start.13) | collective-permute-done | bytes 917536 | tf_op jit(solution)/shard_map/ppermute | solution.py:345
  67.2 1.3 collective-permute-done.11.one_ref
  68.5 0.3 total.1
  68.8 17.8 %all_to_all.10.pieces_ref = bf16[16,8,3584]{2,1,0:T(8,128)(2,1)S(1)} all-to-all(bf16[16,8,3584]{2,1,0:T(8,128)(2,1)S(1)} %bitcast.6), channel_id=1, replica_groups={{0,4,16,20,32,36,48,52,64,68,80,84,96,100,112,116},{1,5,17,21,33,37,49,..., dimensions={0} | all-to-all | bytes 1835008 | tf_op jit(solution)/shard_map/all_to_all | solution.py:521
  86.5 0.3 settle.1
  86.9 17.9 %all_to_all.11 = bf16[16,8,3584]{2,1,0:T(8,128)(2,1)S(1)} all-to-all(bf16[16,8,3584]{2,1,0:T(8,128)(2,1)S(1)} %get-tuple-element.92), channel_id=1, replica_groups={{0,4,16,20,32,36,48,52,64,68,80,84,96,100,112,116},{1,5,17,21,33,37,49,..., dimensions={0} | all-to-all | bytes 1835008 | tf_op jit(solution)/shard_map/all_to_all | solution.py:523
  104.8 1.4 collective-permute-start.18
  106.2 3.3 %collective-permute-start.20 = (bf16[2,3584]{1,0:T(2,128)(2,1)S(1)}, bf16[2,3584]{1,0:T(2,128)(2,1)S(1)}, u32[]{:S(2)}, u32[]{:S(2)}) collective-permute-start(bf16[2,3584]{1,0:T(2,128)(2,1)S(1)} %get-tuple-element.100), channel_id=1, source_target_pairs={{0,2},{1,3},{2,0},{3,1},{4,6},{5,7},{6,4},{7,5},{8,10},{9,11},{10,... | collective-permute-start | bytes 43016 | tf_op jit(solution)/shard_map/ppermute | solution.py:504
  109.5 1.0 collective-permute-start.21
  110.5 11.7 %collective-permute-start.24 = (bf16[128,3584]{1,0:T(8,128)(2,1)S(1)}, bf16[128,3584]{1,0:T(8,128)(2,1)S(1)}, u32[]{:S(2)}, u32[]{:S(2)}) collective-permute-start(bf16[128,3584]{1,0:T(8,128)(2,1)S(1)} %bitcast.4), channel_id=1, source_target_pairs={{0,8},{8,0},{1,9},{9,1},{2,10},{10,2},{3,11},{11,3},{4,12},{12,4},... | collective-permute-start | bytes 2752520 | tf_op jit(solution)/shard_map/ppermute | solution.py:379
  122.3 0.2 collective-permute-start.23
  122.5 1.3 collective-permute-start.22
  123.8 1.8 %collective-permute-start.25 = (bf16[128,3584]{1,0:T(8,128)(2,1)S(1)}, bf16[128,3584]{1,0:T(8,128)(2,1)S(1)}, u32[]{:S(2)}, u32[]{:S(2)}) collective-permute-start(bf16[128,3584]{1,0:T(8,128)(2,1)S(1)} %collective-permute-done.17.quarter_ref.one_ref), channel_id=1, source_target_pairs={{0,8},{8,0},{1,9},{9,1},{2,10},{10,2},{3,11},{11,3},{4,12},{12,4},... | collective-permute-start | bytes 2752520 | tf_op jit(solution)/shard_map/ppermute | solution.py:379
  125.6 4.4 %collective-permute-done.23.far3_ref = bf16[64,3584]{1,0:T(8,128)(2,1)S(1)} collective-permute-done((bf16[64,3584]{1,0:T(8,128)(2,1)S(1)}, bf16[64,3584]{1,0:T(8,128)(2,1)S(1)}, u32[]{:S(2)}, u32[]{:S(2)}) %collective-permute-start.23) | collective-permute-done | bytes 458784 | tf_op jit(solution)/shard_map/ppermute | solution.py:377
  130.0 2.5 %collective-permute-start.28 = (bf16[64,3584]{1,0:T(8,128)(2,1)S(1)}, bf16[64,3584]{1,0:T(8,128)(2,1)S(1)}, u32[]{:S(2)}, u32[]{:S(2)}) collective-permute-start(bf16[64,3584]{1,0:T(8,128)(2,1)S(1)} %collective-permute-done.23.far3_ref), channel_id=1, source_target_pairs={{0,8},{8,0},{1,9},{9,1},{2,10},{10,2},{3,11},{11,3},{4,12},{12,4},... | collective-permute-start | bytes 1376264 | tf_op jit(solution)/shard_map/ppermute | solution.py:379
  132.5 1.3 collective-permute-start.27
  133.8 0.2 assemble_own.1.own_ref
  134.1 1.2 collective-permute-done.27.far1_ref
  135.2 0.3 assemble_oth.1.oth_ref
  135.5 9.6 %backward.1 = (bf16[5,256,3584]{2,1,0:T(8,128)(2,1)}, bf16[2,3584,256]{2,1,0:T(8,128)(2,1)}, f32[2,256]{1,0:T(2,128)}, bf16[4,2,3584]{2,1,0:T(2,128)(2,1)}) custom-call(bf16[2,256,256]{2,1,0:T(8,128)(2,1)S(1)} %get-tuple-element.71.turned_ref, f32[2,256,256]{2,1,0:T(8,128)S(1)} %get-tuple-element.72.slope_ref, ...), custom_call_target="tpu_custom_call" | custom-call | flops 5637144576 | bytes 12845056 | tf_op jit(solution)/shard_map/backward/pallas_call | solution.py:475
  (31 shorter events, 0.3 us)
Async XLA Ops:
  1.7 10.6 %collective-permute-start.3 = (bf16[2,16,3584]{2,1,0:T(8,128)(2,1)S(1)}, bf16[2,16,3584]{2,1,0:T(8,128)(2,1)S(1)}, u32[]{:S(2)}, u32[]{:S(2)}) collective-permute-start(bf16[2,16,3584]{2,1,0:T(8,128)(2,1)S(1)} %get-tuple-element.62.refs_0_), channel_id=1, source_target_pairs={{0,4},{1,5},{2,6},{3,7},{4,0},{5,1},{6,2},{7,3},{8,12},{9,13},{10,... | collective-permute-start | bytes 688136 | tf_op jit(solution)/shard_map/ppermute | solution.py:141
  6.2 8.8 %collective-permute-start = (bf16[2,16,3584]{2,1,0:T(8,128)(2,1)S(1)}, bf16[2,16,3584]{2,1,0:T(8,128)(2,1)S(1)}, u32[]{:S(2)}, u32[]{:S(2)}) collective-permute-start(bf16[2,16,3584]{2,1,0:T(8,128)(2,1)S(1)} %get-tuple-element.62.refs_0_), channel_id=1, source_target_pairs={{0,1},{1,0},{2,3},{3,2},{4,5},{5,4},{6,7},{7,6},{8,9},{9,8},{10,11... | collective-permute-start | bytes 688136 | tf_op jit(solution)/shard_map/ppermute | solution.py:142
  12.2 22.8 %copy-start = (s32[4,8,32]{2,1,0:T(8,128)S(1)}, s32[4,8,32]{2,1,0:T(8,128)}, u32[]{:S(2)}) copy-start(s32[4,8,32]{2,1,0:T(8,128)} %active_ref.1) | copy-start | bytes 12292
  12.2 22.8 %copy-start.1 = (f32[2,256]{1,0:T(2,128)S(1)}, f32[2,256]{1,0:T(2,128)}, u32[]{:S(2)}) copy-start(f32[2,256]{1,0:T(2,128)} %bias_ref.1) | copy-start | bytes 6148
  12.3 7.1 %collective-permute-start.5 = (bf16[2,16,3584]{2,1,0:T(8,128)(2,1)S(1)}, bf16[2,16,3584]{2,1,0:T(8,128)(2,1)S(1)}, u32[]{:S(2)}, u32[]{:S(2)}) collective-permute-start(bf16[2,16,3584]{2,1,0:T(8,128)(2,1)S(1)} %collective-permute-done.3.refs_4_), channel_id=1, source_target_pairs={{0,3},{1,2},{2,1},{3,0},{4,7},{5,6},{6,5},{7,4},{8,11},{9,10},{10,... | collective-permute-start | bytes 688136 | tf_op jit(solution)/shard_map/ppermute | solution.py:144
  14.2 10.1 %collective-permute-start.1 = (bf16[2,16,3584]{2,1,0:T(8,128)(2,1)S(1)}, bf16[2,16,3584]{2,1,0:T(8,128)(2,1)S(1)}, u32[]{:S(2)}, u32[]{:S(2)}) collective-permute-start(bf16[2,16,3584]{2,1,0:T(8,128)(2,1)S(1)} %get-tuple-element.62.refs_0_), channel_id=1, source_target_pairs={{0,3},{1,2},{2,1},{3,0},{4,7},{5,6},{6,5},{7,4},{8,11},{9,10},{10,... | collective-permute-start | bytes 688136 | tf_op jit(solution)/shard_map/ppermute | solution.py:142
  15.0 14.2 %collective-permute-start.4 = (bf16[2,16,3584]{2,1,0:T(8,128)(2,1)S(1)}, bf16[2,16,3584]{2,1,0:T(8,128)(2,1)S(1)}, u32[]{:S(2)}, u32[]{:S(2)}) collective-permute-start(bf16[2,16,3584]{2,1,0:T(8,128)(2,1)S(1)} %collective-permute-done.3.refs_4_), channel_id=1, source_target_pairs={{0,1},{1,0},{2,3},{3,2},{4,5},{5,4},{6,7},{7,6},{8,9},{9,8},{10,11... | collective-permute-start | bytes 688136 | tf_op jit(solution)/shard_map/ppermute | solution.py:144
  15.0 14.2 %collective-permute-start.2 = (bf16[2,16,3584]{2,1,0:T(8,128)(2,1)S(1)}, bf16[2,16,3584]{2,1,0:T(8,128)(2,1)S(1)}, u32[]{:S(2)}, u32[]{:S(2)}) collective-permute-start(bf16[2,16,3584]{2,1,0:T(8,128)(2,1)S(1)} %collective-permute-done.refs_1_), channel_id=1, source_target_pairs={{0,3},{1,2},{2,1},{3,0},{4,7},{5,6},{6,5},{7,4},{8,11},{9,10},{10,... | collective-permute-start | bytes 688136 | tf_op jit(solution)/shard_map/ppermute | solution.py:145
  19.4 9.8 %collective-permute-start.6 = (bf16[2,16,3584]{2,1,0:T(8,128)(2,1)S(1)}, bf16[2,16,3584]{2,1,0:T(8,128)(2,1)S(1)}, u32[]{:S(2)}, u32[]{:S(2)}) collective-permute-start(bf16[2,16,3584]{2,1,0:T(8,128)(2,1)S(1)} %collective-permute-done.5.refs_6_), channel_id=1, source_target_pairs={{0,1},{1,0},{2,3},{3,2},{4,5},{5,4},{6,7},{7,6},{8,9},{9,8},{10,11... | collective-permute-start | bytes 688136 | tf_op jit(solution)/shard_map/ppermute | solution.py:146
  29.4 5.7 %collective-permute-start.7 = (bf16[8,2,16,3584]{3,2,1,0:T(8,128)(2,1)S(1)}, bf16[8,2,16,3584]{3,2,1,0:T(8,128)(2,1)S(1)}, u32[]{:S(2)}, u32[]{:S(2)}) collective-permute-start(bf16[8,2,16,3584]{3,2,1,0:T(8,128)(2,1)S(1)} %arrange.1.own_ref.x_own_ref), channel_id=1, source_target_pairs={{0,8},{8,0},{1,9},{9,1},{2,10},{10,2},{3,11},{11,3},{4,12},{12,4},... | collective-permute-start | bytes 5505032 | tf_op jit(solution)/shard_map/ppermute | solution.py:513
  37.6 3.9 %collective-permute-start.8 = (bf16[2,128,3584]{2,1,0:T(8,128)(2,1)S(1)}, bf16[2,128,3584]{2,1,0:T(8,128)(2,1)S(1)}, u32[]{:S(2)}, u32[]{:S(2)}) collective-permute-start(bf16[2,128,3584]{2,1,0:T(8,128)(2,1)S(1)} %get-tuple-element.76), channel_id=1, source_target_pairs={{0,8},{8,0},{1,9},{9,1},{2,10},{10,2},{3,11},{11,3},{4,12},{12,4},... | collective-permute-start | bytes 5505032 | tf_op jit(solution)/shard_map/ppermute | solution.py:516
  39.8 4.3 %collective-permute-start.9 = (bf16[2,128,3584]{2,1,0:T(8,128)(2,1)S(1)}, bf16[2,128,3584]{2,1,0:T(8,128)(2,1)S(1)}, u32[]{:S(2)}, u32[]{:S(2)}) collective-permute-start(bf16[2,128,3584]{2,1,0:T(8,128)(2,1)S(1)} %get-tuple-element.77), channel_id=1, source_target_pairs={{0,8},{8,0},{1,9},{9,1},{2,10},{10,2},{3,11},{11,3},{4,12},{12,4},... | collective-permute-start | bytes 5505032 | tf_op jit(solution)/shard_map/ppermute | solution.py:518
  45.1 7.9 %collective-permute-start.12 = (bf16[64,3584]{1,0:T(8,128)(2,1)S(1)}, bf16[64,3584]{1,0:T(8,128)(2,1)S(1)}, u32[]{:S(2)}, u32[]{:S(2)}) collective-permute-start(bf16[64,3584]{1,0:T(8,128)(2,1)S(1)} %get-tuple-element.82), channel_id=1, source_target_pairs={{0,1},{1,0},{2,3},{3,2},{4,5},{5,4},{6,7},{7,6},{8,40},{9,41},{10,... | collective-permute-start | bytes 1376264 | tf_op jit(solution)/shard_map/ppermute | solution.py:342
  46.6 8.9 %collective-permute-start.10 = (bf16[64,3584]{1,0:T(8,128)(2,1)S(1)}, bf16[64,3584]{1,0:T(8,128)(2,1)S(1)}, u32[]{:S(2)}, u32[]{:S(2)}) collective-permute-start(bf16[64,3584]{1,0:T(8,128)(2,1)S(1)} %get-tuple-element.80), channel_id=1, source_target_pairs={{0,3},{1,2},{2,1},{3,0},{4,7},{5,6},{6,5},{7,4},{8,104},{9,105},{1... | collective-permute-start | bytes 1376264 | tf_op jit(solution)/shard_map/ppermute | solution.py:343
  53.4 13.8 %collective-permute-start.13 = (bf16[128,3584]{1,0:T(8,128)(2,1)S(1)}, bf16[128,3584]{1,0:T(8,128)(2,1)S(1)}, u32[]{:S(2)}, u32[]{:S(2)}) collective-permute-start(bf16[128,3584]{1,0:T(8,128)(2,1)S(1)} %fold_low.1), channel_id=1, source_target_pairs={{0,3},{1,2},{2,1},{3,0},{4,7},{5,6},{6,5},{7,4},{8,104},{9,105},{1... | collective-permute-start | bytes 2752520 | tf_op jit(solution)/shard_map/ppermute | solution.py:345
  55.8 12.6 %collective-permute-start.11 = (bf16[128,3584]{1,0:T(8,128)(2,1)S(1)}, bf16[128,3584]{1,0:T(8,128)(2,1)S(1)}, u32[]{:S(2)}, u32[]{:S(2)}) collective-permute-start(bf16[128,3584]{1,0:T(8,128)(2,1)S(1)} %fold_high.1), channel_id=1, source_target_pairs={{0,1},{1,0},{2,3},{3,2},{4,5},{5,4},{6,7},{7,6},{8,40},{9,41},{10,... | collective-permute-start | bytes 2752520 | tf_op jit(solution)/shard_map/ppermute | solution.py:349
  55.9 12.8 %collective-permute-start.14 = (bf16[2,3584]{1,0:T(2,128)(2,1)S(1)}, bf16[2,3584]{1,0:T(2,128)(2,1)S(1)}, u32[]{:S(2)}, u32[]{:S(2)}) collective-permute-start(bf16[2,3584]{1,0:T(2,128)(2,1)S(1)} %get-tuple-element.84), channel_id=1, source_target_pairs={{0,1},{1,2},{2,3},{3,0},{4,5},{5,6},{6,7},{7,4},{8,9},{9,10},{10,1... | collective-permute-start | bytes 43016 | tf_op jit(solution)/shard_map/ppermute | solution.py:504
  56.0 12.7 %collective-permute-start.15 = (bf16[2,3584]{1,0:T(2,128)(2,1)S(1)}, bf16[2,3584]{1,0:T(2,128)(2,1)S(1)}, u32[]{:S(2)}, u32[]{:S(2)}) collective-permute-start(bf16[2,3584]{1,0:T(2,128)(2,1)S(1)} %get-tuple-element.85), channel_id=1, source_target_pairs={{0,2},{1,3},{2,0},{3,1},{4,6},{5,7},{6,4},{7,5},{8,10},{9,11},{10,... | collective-permute-start | bytes 43016 | tf_op jit(solution)/shard_map/ppermute | solution.py:504
  59.1 9.7 %collective-permute-start.16 = (bf16[2,3584]{1,0:T(2,128)(2,1)S(1)}, bf16[2,3584]{1,0:T(2,128)(2,1)S(1)}, u32[]{:S(2)}, u32[]{:S(2)}) collective-permute-start(bf16[2,3584]{1,0:T(2,128)(2,1)S(1)} %get-tuple-element.86), channel_id=1, source_target_pairs={{0,3},{1,0},{2,1},{3,2},{4,7},{5,4},{6,5},{7,6},{8,11},{9,8},{10,9... | collective-permute-start | bytes 43016 | tf_op jit(solution)/shard_map/ppermute | solution.py:504
  104.8 17.4 %collective-permute-start.18 = (bf16[128,3584]{1,0:T(8,128)(2,1)S(1)}, bf16[128,3584]{1,0:T(8,128)(2,1)S(1)}, u32[]{:S(2)}, u32[]{:S(2)}) collective-permute-start(bf16[128,3584]{1,0:T(8,128)(2,1)S(1)} %bitcast.2), channel_id=1, source_target_pairs={{0,3},{1,2},{2,1},{3,0},{4,7},{5,6},{6,5},{7,4},{8,104},{9,105},{1... | collective-permute-start | bytes 2752520 | tf_op jit(solution)/shard_map/ppermute | solution.py:372
  106.2 16.1 %collective-permute-start.17 = (bf16[128,3584]{1,0:T(8,128)(2,1)S(1)}, bf16[128,3584]{1,0:T(8,128)(2,1)S(1)}, u32[]{:S(2)}, u32[]{:S(2)}) collective-permute-start(bf16[128,3584]{1,0:T(8,128)(2,1)S(1)} %bitcast.3), channel_id=1, source_target_pairs={{0,1},{1,0},{2,3},{3,2},{4,5},{5,4},{6,7},{7,6},{8,40},{9,41},{10,... | collective-permute-start | bytes 2752520 | tf_op jit(solution)/shard_map/ppermute | solution.py:371
  106.2 4.4 %collective-permute-start.19 = (bf16[2,3584]{1,0:T(2,128)(2,1)S(1)}, bf16[2,3584]{1,0:T(2,128)(2,1)S(1)}, u32[]{:S(2)}, u32[]{:S(2)}) collective-permute-start(bf16[2,3584]{1,0:T(2,128)(2,1)S(1)} %get-tuple-element.99), channel_id=1, source_target_pairs={{0,1},{1,2},{2,3},{3,0},{4,5},{5,6},{6,7},{7,4},{8,9},{9,10},{10,1... | collective-permute-start | bytes 43016 | tf_op jit(solution)/shard_map/ppermute | solution.py:504
  106.2 16.0 %collective-permute-start.20 = (bf16[2,3584]{1,0:T(2,128)(2,1)S(1)}, bf16[2,3584]{1,0:T(2,128)(2,1)S(1)}, u32[]{:S(2)}, u32[]{:S(2)}) collective-permute-start(bf16[2,3584]{1,0:T(2,128)(2,1)S(1)} %get-tuple-element.100), channel_id=1, source_target_pairs={{0,2},{1,3},{2,0},{3,1},{4,6},{5,7},{6,4},{7,5},{8,10},{9,11},{10,... | collective-permute-start | bytes 43016 | tf_op jit(solution)/shard_map/ppermute | solution.py:504
  109.5 12.7 %collective-permute-start.21 = (bf16[2,3584]{1,0:T(2,128)(2,1)S(1)}, bf16[2,3584]{1,0:T(2,128)(2,1)S(1)}, u32[]{:S(2)}, u32[]{:S(2)}) collective-permute-start(bf16[2,3584]{1,0:T(2,128)(2,1)S(1)} %get-tuple-element.101), channel_id=1, source_target_pairs={{0,3},{1,0},{2,1},{3,2},{4,7},{5,4},{6,5},{7,6},{8,11},{9,8},{10,9... | collective-permute-start | bytes 43016 | tf_op jit(solution)/shard_map/ppermute | solution.py:504
  110.5 23.5 %collective-permute-start.24 = (bf16[128,3584]{1,0:T(8,128)(2,1)S(1)}, bf16[128,3584]{1,0:T(8,128)(2,1)S(1)}, u32[]{:S(2)}, u32[]{:S(2)}) collective-permute-start(bf16[128,3584]{1,0:T(8,128)(2,1)S(1)} %bitcast.4), channel_id=1, source_target_pairs={{0,8},{8,0},{1,9},{9,1},{2,10},{10,2},{3,11},{11,3},{4,12},{12,4},... | collective-permute-start | bytes 2752520 | tf_op jit(solution)/shard_map/ppermute | solution.py:379
  122.3 7.7 %collective-permute-start.23 = (bf16[64,3584]{1,0:T(8,128)(2,1)S(1)}, bf16[64,3584]{1,0:T(8,128)(2,1)S(1)}, u32[]{:S(2)}, u32[]{:S(2)}) collective-permute-start(bf16[64,3584]{1,0:T(8,128)(2,1)S(1)} %half_high.1), channel_id=1, source_target_pairs={{0,1},{1,0},{2,3},{3,2},{4,5},{5,4},{6,7},{7,6},{8,40},{9,41},{10,... | collective-permute-start | bytes 1376264 | tf_op jit(solution)/shard_map/ppermute | solution.py:377
  122.5 10.0 %collective-permute-start.22 = (bf16[64,3584]{1,0:T(8,128)(2,1)S(1)}, bf16[64,3584]{1,0:T(8,128)(2,1)S(1)}, u32[]{:S(2)}, u32[]{:S(2)}) collective-permute-start(bf16[64,3584]{1,0:T(8,128)(2,1)S(1)} %half_low.1), channel_id=1, source_target_pairs={{0,3},{1,2},{2,1},{3,0},{4,7},{5,6},{6,5},{7,4},{8,104},{9,105},{1... | collective-permute-start | bytes 1376264 | tf_op jit(solution)/shard_map/ppermute | solution.py:375
  123.8 11.5 %collective-permute-start.25 = (bf16[128,3584]{1,0:T(8,128)(2,1)S(1)}, bf16[128,3584]{1,0:T(8,128)(2,1)S(1)}, u32[]{:S(2)}, u32[]{:S(2)}) collective-permute-start(bf16[128,3584]{1,0:T(8,128)(2,1)S(1)} %collective-permute-done.17.quarter_ref.one_ref), channel_id=1, source_target_pairs={{0,8},{8,0},{1,9},{9,1},{2,10},{10,2},{3,11},{11,3},{4,12},{12,4},... | collective-permute-start | bytes 2752520 | tf_op jit(solution)/shard_map/ppermute | solution.py:379
  125.6 9.7 %collective-permute-start.26 = (bf16[128,3584]{1,0:T(8,128)(2,1)S(1)}, bf16[128,3584]{1,0:T(8,128)(2,1)S(1)}, u32[]{:S(2)}, u32[]{:S(2)}) collective-permute-start(bf16[128,3584]{1,0:T(8,128)(2,1)S(1)} %collective-permute-done.18.quarter_ref.three_ref), channel_id=1, source_target_pairs={{0,8},{8,0},{1,9},{9,1},{2,10},{10,2},{3,11},{11,3},{4,12},{12,4},... | collective-permute-start | bytes 2752520 | tf_op jit(solution)/shard_map/ppermute | solution.py:379
  130.0 4.1 %collective-permute-start.28 = (bf16[64,3584]{1,0:T(8,128)(2,1)S(1)}, bf16[64,3584]{1,0:T(8,128)(2,1)S(1)}, u32[]{:S(2)}, u32[]{:S(2)}) collective-permute-start(bf16[64,3584]{1,0:T(8,128)(2,1)S(1)} %collective-permute-done.23.far3_ref), channel_id=1, source_target_pairs={{0,8},{8,0},{1,9},{9,1},{2,10},{10,2},{3,11},{11,3},{4,12},{12,4},... | collective-permute-start | bytes 1376264 | tf_op jit(solution)/shard_map/ppermute | solution.py:379
  132.5 2.8 %collective-permute-start.27 = (bf16[64,3584]{1,0:T(8,128)(2,1)S(1)}, bf16[64,3584]{1,0:T(8,128)(2,1)S(1)}, u32[]{:S(2)}, u32[]{:S(2)}) collective-permute-start(bf16[64,3584]{1,0:T(8,128)(2,1)S(1)} %collective-permute-done.22.far1_ref), channel_id=1, source_target_pairs={{0,8},{8,0},{1,9},{9,1},{2,10},{10,2},{3,11},{11,3},{4,12},{12,4},... | collective-permute-start | bytes 1376264 | tf_op jit(solution)/shard_map/ppermute | solution.py:379

commit v9 on v8

--- a/solution.py
+++ b/solution.py
@@ -51,7 +51,7 @@
 ALONG_Y = {
     flip: _pairs(lambda x, zl, core, zh, y, flip=flip: (x, zl, core, zh, y ^ flip)) for flip in (1, 3)
 }
-ACROSS = _pairs(lambda x, zl, core, zh, y: (x, zl, core, zh ^ 1, y))
+ACROSS = _pairs(lambda x, zl, core, zh, y: (x, zl ^ 1, core, zh ^ 1, y))
 GROUPS = [
     [_rank(x, zl, 0, zh, y) for x in range(4) for zl in range(2) for zh in range(2)] for y in range(4)
 ] + [
@@ -140,7 +140,7 @@
 def _gather_inputs(mine, staged):
     far = lax.ppermute(mine, ALL, ACROSS)
     mine_1, mine_3 = (lax.ppermute(mine, ALL, ALONG_Y[flip]) for flip in (1, 3))
-    far, staged = lax.optimization_barrier((far, staged))
+    far, mine_1, mine_3, staged = lax.optimization_barrier((far, mine_1, mine_3, staged))
     far_3, far_1 = (lax.ppermute(far, ALL, ALONG_Y[flip]) for flip in (3, 1))
     mine_2 = lax.ppermute(mine_1, ALL, ALONG_Y[3])
     far_2 = lax.ppermute(far_3, ALL, ALONG_Y[1])
@@ -294,10 +294,11 @@
     )(codes, dec)
 
 
-def _join_kernel(
-    own_low_ref, own_ref, got_low_ref, got_ref, mine_ref, to1_ref, to3_ref, far1_ref, far3_ref
-):
-    outs = {0: (mine_ref, mine_ref), 1: (to1_ref, to1_ref), 3: (to3_ref, to3_ref), 2: (far1_ref, far3_ref)}
+def _join_kernel(flips, own_low_ref, own_ref, got_low_ref, got_ref, *out_refs):
+    if flips == (2,):
+        outs = {2: out_refs}
+    else:
+        outs = {flip: (out_ref, out_ref) for flip, out_ref in zip(flips, out_refs)}
     core = lax.axis_index("core")
     for flip, (first_ref, second_ref) in outs.items():
         for i in range(4):
@@ -333,9 +334,10 @@
 def _reduce_ring(parts):
     quarter = jax.ShapeDtypeStruct((QUARTER, D), BF)
     half = jax.ShapeDtypeStruct((QUARTER // 2, D), BF)
-    mine, to1, to3, far1, far3 = _plain(
-        _join_kernel,
-        [jax.ShapeDtypeStruct((QUARTER, D), F32), quarter, quarter, half, half],
+    far1, far3 = _plain(functools.partial(_join_kernel, (2,)), [half, half], "join_far", *parts)
+    mine, to1, to3 = _plain(
+        functools.partial(_join_kernel, (0, 1, 3)),
+        [jax.ShapeDtypeStruct((QUARTER, D), F32), quarter, quarter],
         "join",
         *parts,
     )

time: 145 us -> 143 us (0.986)
  starting transfers between devices: 46.5 us -> 52.5 us
  blocking collectives: 35.7 us -> 30.1 us
  waiting for transfers between devices: 39.4 us -> 36.5 us
    ppermute x2, waiting for transfers between devices: 4.91 us -> 0.01 us  [_gather_inputs(): mine_1, mine_3 = (lax.ppermute(mine, ALL, ALONG_Y[flip]) for flip in (1, 3))]
    ppermute x5, starting transfers between devices: 17.3 us -> 21.3 us  [_gather_ring(): others = [lax.ppermute(piece, 'core', SWAP) for piece in pieces]]
    ppermute x1, starting transfers between devices: 2.24 us -> 5.79 us  [per_device(): oth = lax.ppermute(own, 'core', SWAP)]
    all_to_all x1, blocking collectives: 17.9 us -> 15.1 us  [per_device(): lax.all_to_all(errors, ALL, 0, 0, axis_index_groups=GROUPS)]
    all_to_all x1, blocking collectives: 17.8 us -> 15.1 us  [per_device(): lax.all_to_all(quarter.reshape(16, 8, D), ALL, 0, 0, axis_index_groups=GR...]
    ppermute x6, starting transfers between devices: 7.91 us -> 5.83 us  [_around_y(): lax.ppermute(pieces[j], 'y', [(i, (i + j) % 4) for i in range(4)])]
    ppermute x2, starting transfers between devices: 2.06 us -> 3.65 us  [_gather_inputs(): mine_1, mine_3 = (lax.ppermute(mine, ALL, ALONG_Y[flip]) for flip in (1, 3))]
  transfers between devices with their start and end apart: 29 -> 29, of which waited for: 11 -> 13; matrix products, arithmetic and copies ran while one was open for 0% -> 0% of each run, Pallas kernels for 5% -> 6%
where the time goes in v9:
time: 143 us
  starting transfers between devices  52.5 us (37%)
  waiting for transfers between devices  36.5 us (26%)
  blocking collectives  30.1 us (21%)
  Pallas kernels  22.9 us (16%)
    ppermute x5, starting transfers between devices, _gather_ring(): others = [lax.ppermute(piece, 'core', SWAP) for piece in pieces]  21.3 us
    all_to_all x1, blocking collectives, per_device(): lax.all_to_all(errors, ALL, 0, 0, axis_index_groups=GROUPS)  15.1 us
    all_to_all x1, blocking collectives, per_device(): lax.all_to_all(quarter.reshape(16, 8, D), ALL, 0, 0, axis_index_groups=GR...  15.1 us
    pallas_call x1, Pallas kernels, _backward(): pl.pallas_call(_backward_kernel, grid=(PAIRS + 2,), in_specs=[WHOLE] * 11...  9.59 us
    ppermute x1, waiting for transfers between devices, _reduce_ring(): from3 = lax.ppermute(to3, ALL, RING[3])  8.48 us
    ppermute x6, starting transfers between devices, _around_y(): lax.ppermute(pieces[j], 'y', [(i, (i + j) % 4) for i in range(4)])  5.83 us
    ppermute x1, starting transfers between devices, per_device(): oth = lax.ppermute(own, 'core', SWAP)  5.79 us
    ppermute x1, waiting for transfers between devices, _gather_ring(): far3 = lax.ppermute(pass1, ALL, RING[1])  4.94 us
  transfers between devices with their start and end apart: 29, of which 13 were waited for; matrix products, arithmetic and copies ran while one was open for 0% of the time, Pallas kernels for 6%

profile of v9, /device:TPU:1, one launch (start us, length us, event | category | flops | bytes accessed | tf_op | source)
XLA Modules:
  0.0 142.8 jit_solution(1933601505902237729)
XLA Ops:
  0.6 1.0 prepare.1
  1.7 3.6 %collective-permute-start.2 = (bf16[2,16,3584]{2,1,0:T(8,128)(2,1)S(1)}, bf16[2,16,3584]{2,1,0:T(8,128)(2,1)S(1)}, u32[]{:S(2)}, u32[]{:S(2)}) collective-permute-start(bf16[2,16,3584]{2,1,0:T(8,128)(2,1)S(1)} %get-tuple-element.64.refs_0_), channel_id=1, source_target_pairs={{0,3},{1,2},{2,1},{3,0},{4,7},{5,6},{6,5},{7,4},{8,11},{9,10},{10,... | collective-permute-start | bytes 688136 | tf_op jit(solution)/shard_map/ppermute | solution.py:142
  5.3 3.8 %collective-permute-start = (bf16[2,16,3584]{2,1,0:T(8,128)(2,1)S(1)}, bf16[2,16,3584]{2,1,0:T(8,128)(2,1)S(1)}, u32[]{:S(2)}, u32[]{:S(2)}) collective-permute-start(bf16[2,16,3584]{2,1,0:T(8,128)(2,1)S(1)} %get-tuple-element.64.refs_0_), channel_id=1, source_target_pairs={{0,20},{1,21},{2,22},{3,23},{4,16},{5,17},{6,18},{7,19},{8,28},{9,... | collective-permute-start | bytes 688136 | tf_op jit(solution)/shard_map/ppermute | solution.py:141
  9.1 4.7 %stage.1 = (bf16[2,3584,256]{2,1,0:T(8,128)(2,1)S(1)}, bf16[5,256,3584]{2,1,0:T(8,128)(2,1)S(1)}) custom-call(bf16[2,3584,256]{2,1,0:T(8,128)(2,1)} %enc_hbm, bf16[5,256,3584]{2,1,0:T(8,128)(2,1)} %dec_hbm), custom_call_target="tpu_custom_call" | custom-call | bytes 25690112 | tf_op jit(solution)/shard_map/stage/pallas_call | solution.py:209
  13.9 0.7 collective-permute-start.5
  14.6 0.9 collective-permute-start.4
  15.5 2.0 %collective-permute-start.3 = (bf16[2,16,3584]{2,1,0:T(8,128)(2,1)S(1)}, bf16[2,16,3584]{2,1,0:T(8,128)(2,1)S(1)}, u32[]{:S(2)}, u32[]{:S(2)}) collective-permute-start(bf16[2,16,3584]{2,1,0:T(8,128)(2,1)S(1)} %collective-permute-done.1.refs_1_), channel_id=1, source_target_pairs={{0,3},{1,2},{2,1},{3,0},{4,7},{5,6},{6,5},{7,4},{8,11},{9,10},{10,... | collective-permute-start | bytes 688136 | tf_op jit(solution)/shard_map/ppermute | solution.py:145
  17.5 3.1 %collective-permute-done.5.refs_6_ = bf16[2,16,3584]{2,1,0:T(8,128)(2,1)S(1)} collective-permute-done((bf16[2,16,3584]{2,1,0:T(8,128)(2,1)S(1)}, bf16[2,16,3584]{2,1,0:T(8,128)(2,1)S(1)}, u32[]{:S(2)}, u32[]{:S(2)}) %collective-permute-start.5) | collective-permute-done | bytes 229408 | tf_op jit(solution)/shard_map/ppermute | solution.py:144
  20.6 0.3 collective-permute-start.6
  20.8 4.6 %collective-permute-done.3.refs_3_ = bf16[2,16,3584]{2,1,0:T(8,128)(2,1)S(1)} collective-permute-done((bf16[2,16,3584]{2,1,0:T(8,128)(2,1)S(1)}, bf16[2,16,3584]{2,1,0:T(8,128)(2,1)S(1)}, u32[]{:S(2)}, u32[]{:S(2)}) %collective-permute-start.3) | collective-permute-done | bytes 229408 | tf_op jit(solution)/shard_map/ppermute | solution.py:145
  25.9 5.8 %collective-permute-start.7 = (bf16[8,2,16,3584]{3,2,1,0:T(8,128)(2,1)S(1)}, bf16[8,2,16,3584]{3,2,1,0:T(8,128)(2,1)S(1)}, u32[]{:S(2)}, u32[]{:S(2)}) collective-permute-start(bf16[8,2,16,3584]{3,2,1,0:T(8,128)(2,1)S(1)} %arrange.1.own_ref.x_own_ref), channel_id=1, source_target_pairs={{0,8},{8,0},{1,9},{9,1},{2,10},{10,2},{3,11},{11,3},{4,12},{12,4},... | collective-permute-start | bytes 5505032 | tf_op jit(solution)/shard_map/ppermute | solution.py:515
  31.7 3.4 %collective-permute-done.7.oth_ref.x_oth_ref = bf16[8,2,16,3584]{3,2,1,0:T(8,128)(2,1)S(1)} collective-permute-done((bf16[8,2,16,3584]{3,2,1,0:T(8,128)(2,1)S(1)}, bf16[8,2,16,3584]{3,2,1,0:T(8,128)(2,1)S(1)}, u32[]{:S(2)}, u32[]{:S(2)}) %collective-permute-start.7) | collective-permute-done | bytes 1835040 | tf_op jit(solution)/shard_map/ppermute | solution.py:515
  35.1 2.5 %forward.1 = (bf16[2,128,3584]{2,1,0:T(8,128)(2,1)S(1)}, bf16[2,128,3584]{2,1,0:T(8,128)(2,1)S(1)}, bf16[2,256,256]{2,1,0:T(8,128)(2,1)S(1)}, bf16[2,256,256]{2,1,0:T(8,128)(2,1)S(1)}, f32[2,256,256]{2,1,0:T(8,128)S(1)}) custom-call(bf16[8,2,16,3584]{3,2,1,0:T(8,128)(2,1)S(1)} %arrange.1.own_ref.x_own_ref, ...), custom_call_target="tpu_custom_call" | custom-call | flops 1879048192 | bytes 3670016 | tf_op jit(solution)/shard_map/forward/pallas_call | solution.py:259
  37.6 0.5 collective-permute-start.8
  38.1 1.8 %forward_high.1 = (bf16[2,128,3584]{2,1,0:T(8,128)(2,1)S(1)}, bf16[2,128,3584]{2,1,0:T(8,128)(2,1)S(1)}) custom-call(bf16[2,256,256]{2,1,0:T(8,128)(2,1)S(1)} %get-tuple-element.78.codes_ref, bf16[5,256,3584]{2,1,0:T(8,128)(2,1)S(1)} %get-tuple-element.74.dec_ref), custom_call_target="tpu_custom_call" | custom-call | flops 1409286144 | bytes 3670016 | tf_op jit(solution)/shard_map/forward_high/pallas_call | solution.py:284
  40.1 1.4 collective-permute-done.8.got_low_ref
  41.5 2.6 %collective-permute-done.9.got_ref = bf16[2,128,3584]{2,1,0:T(8,128)(2,1)S(1)} collective-permute-done((bf16[2,128,3584]{2,1,0:T(8,128)(2,1)S(1)}, bf16[2,128,3584]{2,1,0:T(8,128)(2,1)S(1)}, u32[]{:S(2)}, u32[]{:S(2)}) %collective-permute-start.9) | collective-permute-done | bytes 1835040 | tf_op jit(solution)/shard_map/ppermute | solution.py:520
  44.1 0.3 join_far.1
  44.4 1.3 collective-permute-start.12
  45.7 1.4 collective-permute-start.10
  47.0 0.9 join.1
  48.0 4.1 %collective-permute-done.12.got_ref = bf16[64,3584]{1,0:T(8,128)(2,1)S(1)} collective-permute-done((bf16[64,3584]{1,0:T(8,128)(2,1)S(1)}, bf16[64,3584]{1,0:T(8,128)(2,1)S(1)}, u32[]{:S(2)}, u32[]{:S(2)}) %collective-permute-start.12) | collective-permute-done | bytes 458784 | tf_op jit(solution)/shard_map/ppermute | solution.py:344
  52.1 0.4 fold_low.1
  52.4 2.1 %collective-permute-start.13 = (bf16[128,3584]{1,0:T(8,128)(2,1)S(1)}, bf16[128,3584]{1,0:T(8,128)(2,1)S(1)}, u32[]{:S(2)}, u32[]{:S(2)}) collective-permute-start(bf16[128,3584]{1,0:T(8,128)(2,1)S(1)} %fold_low.1), channel_id=1, source_target_pairs={{0,3},{1,2},{2,1},{3,0},{4,7},{5,6},{6,5},{7,4},{8,104},{9,105},{1... | collective-permute-start | bytes 2752520 | tf_op jit(solution)/shard_map/ppermute | solution.py:347
  54.6 0.4 fold_high.1
  55.0 0.3 collective-permute-start.14
  55.3 1.4 collective-permute-start.15
  56.7 1.1 collective-permute-start.16
  57.8 8.5 %collective-permute-done.13.three_ref = bf16[128,3584]{1,0:T(8,128)(2,1)S(1)} collective-permute-done((bf16[128,3584]{1,0:T(8,128)(2,1)S(1)}, bf16[128,3584]{1,0:T(8,128)(2,1)S(1)}, u32[]{:S(2)}, u32[]{:S(2)}) %collective-permute-start.13) | collective-permute-done | bytes 917536 | tf_op jit(solution)/shard_map/ppermute | solution.py:347
  66.3 1.3 collective-permute-done.11.one_ref
  67.5 0.3 total.1
  67.8 15.1 %all_to_all.10.pieces_ref = bf16[16,8,3584]{2,1,0:T(8,128)(2,1)S(1)} all-to-all(bf16[16,8,3584]{2,1,0:T(8,128)(2,1)S(1)} %bitcast.6), channel_id=1, replica_groups={{0,4,16,20,32,36,48,52,64,68,80,84,96,100,112,116},{1,5,17,21,33,37,49,..., dimensions={0} | all-to-all | bytes 1835008 | tf_op jit(solution)/shard_map/all_to_all | solution.py:523
  82.9 0.3 settle.1
  83.2 15.1 %all_to_all.11 = bf16[16,8,3584]{2,1,0:T(8,128)(2,1)S(1)} all-to-all(bf16[16,8,3584]{2,1,0:T(8,128)(2,1)S(1)} %get-tuple-element.96), channel_id=1, replica_groups={{0,4,16,20,32,36,48,52,64,68,80,84,96,100,112,116},{1,5,17,21,33,37,49,..., dimensions={0} | all-to-all | bytes 1835008 | tf_op jit(solution)/shard_map/all_to_all | solution.py:525
  98.3 0.5 collective-permute-start.18
  98.8 1.6 %collective-permute-start.20 = (bf16[2,3584]{1,0:T(2,128)(2,1)S(1)}, bf16[2,3584]{1,0:T(2,128)(2,1)S(1)}, u32[]{:S(2)}, u32[]{:S(2)}) collective-permute-start(bf16[2,3584]{1,0:T(2,128)(2,1)S(1)} %get-tuple-element.104), channel_id=1, source_target_pairs={{0,2},{1,3},{2,0},{3,1},{4,6},{5,7},{6,4},{7,5},{8,10},{9,11},{10,... | collective-permute-start | bytes 43016 | tf_op jit(solution)/shard_map/ppermute | solution.py:506
  100.4 1.5 %collective-permute-start.21 = (bf16[2,3584]{1,0:T(2,128)(2,1)S(1)}, bf16[2,3584]{1,0:T(2,128)(2,1)S(1)}, u32[]{:S(2)}, u32[]{:S(2)}) collective-permute-start(bf16[2,3584]{1,0:T(2,128)(2,1)S(1)} %get-tuple-element.105), channel_id=1, source_target_pairs={{0,3},{1,0},{2,1},{3,2},{4,7},{5,4},{6,5},{7,6},{8,11},{9,8},{10,9... | collective-permute-start | bytes 43016 | tf_op jit(solution)/shard_map/ppermute | solution.py:506
  101.9 1.0 collective-permute-done.19.rest_1_
  102.9 17.0 %collective-permute-start.24 = (bf16[128,3584]{1,0:T(8,128)(2,1)S(1)}, bf16[128,3584]{1,0:T(8,128)(2,1)S(1)}, u32[]{:S(2)}, u32[]{:S(2)}) collective-permute-start(bf16[128,3584]{1,0:T(8,128)(2,1)S(1)} %bitcast.4), channel_id=1, source_target_pairs={{0,8},{8,0},{1,9},{9,1},{2,10},{10,2},{3,11},{11,3},{4,12},{12,4},... | collective-permute-start | bytes 2752520 | tf_op jit(solution)/shard_map/ppermute | solution.py:381
  120.0 0.5 collective-permute-start.23
  120.5 1.7 %collective-permute-start.22 = (bf16[64,3584]{1,0:T(8,128)(2,1)S(1)}, bf16[64,3584]{1,0:T(8,128)(2,1)S(1)}, u32[]{:S(2)}, u32[]{:S(2)}) collective-permute-start(bf16[64,3584]{1,0:T(8,128)(2,1)S(1)} %half_low.1), channel_id=1, source_target_pairs={{0,3},{1,2},{2,1},{3,0},{4,7},{5,6},{6,5},{7,4},{8,104},{9,105},{1... | collective-permute-start | bytes 1376264 | tf_op jit(solution)/shard_map/ppermute | solution.py:377
  122.3 0.5 collective-permute-start.25
  122.8 4.9 %collective-permute-done.23.far3_ref = bf16[64,3584]{1,0:T(8,128)(2,1)S(1)} collective-permute-done((bf16[64,3584]{1,0:T(8,128)(2,1)S(1)}, bf16[64,3584]{1,0:T(8,128)(2,1)S(1)}, u32[]{:S(2)}, u32[]{:S(2)}) %collective-permute-start.23) | collective-permute-done | bytes 458784 | tf_op jit(solution)/shard_map/ppermute | solution.py:379
  127.7 2.5 %collective-permute-start.28 = (bf16[64,3584]{1,0:T(8,128)(2,1)S(1)}, bf16[64,3584]{1,0:T(8,128)(2,1)S(1)}, u32[]{:S(2)}, u32[]{:S(2)}) collective-permute-start(bf16[64,3584]{1,0:T(8,128)(2,1)S(1)} %collective-permute-done.23.far3_ref), channel_id=1, source_target_pairs={{0,8},{8,0},{1,9},{9,1},{2,10},{10,2},{3,11},{11,3},{4,12},{12,4},... | collective-permute-start | bytes 1376264 | tf_op jit(solution)/shard_map/ppermute | solution.py:381
  130.2 1.3 collective-permute-start.27
  131.8 1.2 collective-permute-done.27.far1_ref
  133.0 0.3 assemble_oth.1.oth_ref
  133.2 9.6 %backward.1 = (bf16[5,256,3584]{2,1,0:T(8,128)(2,1)}, bf16[2,3584,256]{2,1,0:T(8,128)(2,1)}, f32[2,256]{1,0:T(2,128)}, bf16[4,2,3584]{2,1,0:T(2,128)(2,1)}) custom-call(bf16[2,256,256]{2,1,0:T(8,128)(2,1)S(1)} %get-tuple-element.75.turned_ref, f32[2,256,256]{2,1,0:T(8,128)S(1)} %get-tuple-element.76.slope_ref, ...), custom_call_target="tpu_custom_call" | custom-call | flops 5637144576 | bytes 12845056 | tf_op jit(solution)/shard_map/backward/pallas_call | solution.py:477
  (32 shorter events, 1.2 us)
Async XLA Ops:
  1.7 12.2 %collective-permute-start.2 = (bf16[2,16,3584]{2,1,0:T(8,128)(2,1)S(1)}, bf16[2,16,3584]{2,1,0:T(8,128)(2,1)S(1)}, u32[]{:S(2)}, u32[]{:S(2)}) collective-permute-start(bf16[2,16,3584]{2,1,0:T(8,128)(2,1)S(1)} %get-tuple-element.64.refs_0_), channel_id=1, source_target_pairs={{0,3},{1,2},{2,1},{3,0},{4,7},{5,6},{6,5},{7,4},{8,11},{9,10},{10,... | collective-permute-start | bytes 688136 | tf_op jit(solution)/shard_map/ppermute | solution.py:142
  5.3 8.5 %collective-permute-start.1 = (bf16[2,16,3584]{2,1,0:T(8,128)(2,1)S(1)}, bf16[2,16,3584]{2,1,0:T(8,128)(2,1)S(1)}, u32[]{:S(2)}, u32[]{:S(2)}) collective-permute-start(bf16[2,16,3584]{2,1,0:T(8,128)(2,1)S(1)} %get-tuple-element.64.refs_0_), channel_id=1, source_target_pairs={{0,1},{1,0},{2,3},{3,2},{4,5},{5,4},{6,7},{7,6},{8,9},{9,8},{10,11... | collective-permute-start | bytes 688136 | tf_op jit(solution)/shard_map/ppermute | solution.py:142
  5.3 8.6 %collective-permute-start = (bf16[2,16,3584]{2,1,0:T(8,128)(2,1)S(1)}, bf16[2,16,3584]{2,1,0:T(8,128)(2,1)S(1)}, u32[]{:S(2)}, u32[]{:S(2)}) collective-permute-start(bf16[2,16,3584]{2,1,0:T(8,128)(2,1)S(1)} %get-tuple-element.64.refs_0_), channel_id=1, source_target_pairs={{0,20},{1,21},{2,22},{3,23},{4,16},{5,17},{6,18},{7,19},{8,28},{9,... | collective-permute-start | bytes 688136 | tf_op jit(solution)/shard_map/ppermute | solution.py:141
  13.9 21.1 %copy-start = (s32[4,8,32]{2,1,0:T(8,128)S(1)}, s32[4,8,32]{2,1,0:T(8,128)}, u32[]{:S(2)}) copy-start(s32[4,8,32]{2,1,0:T(8,128)} %active_ref.1) | copy-start | bytes 12292
  13.9 21.1 %copy-start.1 = (f32[2,256]{1,0:T(2,128)S(1)}, f32[2,256]{1,0:T(2,128)}, u32[]{:S(2)}) copy-start(f32[2,256]{1,0:T(2,128)} %bias_ref.1) | copy-start | bytes 6148
  13.9 6.6 %collective-permute-start.5 = (bf16[2,16,3584]{2,1,0:T(8,128)(2,1)S(1)}, bf16[2,16,3584]{2,1,0:T(8,128)(2,1)S(1)}, u32[]{:S(2)}, u32[]{:S(2)}) collective-permute-start(bf16[2,16,3584]{2,1,0:T(8,128)(2,1)S(1)} %collective-permute-done.refs_4_), channel_id=1, source_target_pairs={{0,3},{1,2},{2,1},{3,0},{4,7},{5,6},{6,5},{7,4},{8,11},{9,10},{10,... | collective-permute-start | bytes 688136 | tf_op jit(solution)/shard_map/ppermute | solution.py:144
  14.6 10.9 %collective-permute-start.4 = (bf16[2,16,3584]{2,1,0:T(8,128)(2,1)S(1)}, bf16[2,16,3584]{2,1,0:T(8,128)(2,1)S(1)}, u32[]{:S(2)}, u32[]{:S(2)}) collective-permute-start(bf16[2,16,3584]{2,1,0:T(8,128)(2,1)S(1)} %collective-permute-done.refs_4_), channel_id=1, source_target_pairs={{0,1},{1,0},{2,3},{3,2},{4,5},{5,4},{6,7},{7,6},{8,9},{9,8},{10,11... | collective-permute-start | bytes 688136 | tf_op jit(solution)/shard_map/ppermute | solution.py:144
  15.5 10.0 %collective-permute-start.3 = (bf16[2,16,3584]{2,1,0:T(8,128)(2,1)S(1)}, bf16[2,16,3584]{2,1,0:T(8,128)(2,1)S(1)}, u32[]{:S(2)}, u32[]{:S(2)}) collective-permute-start(bf16[2,16,3584]{2,1,0:T(8,128)(2,1)S(1)} %collective-permute-done.1.refs_1_), channel_id=1, source_target_pairs={{0,3},{1,2},{2,1},{3,0},{4,7},{5,6},{6,5},{7,4},{8,11},{9,10},{10,... | collective-permute-start | bytes 688136 | tf_op jit(solution)/shard_map/ppermute | solution.py:145
  20.6 5.2 %collective-permute-start.6 = (bf16[2,16,3584]{2,1,0:T(8,128)(2,1)S(1)}, bf16[2,16,3584]{2,1,0:T(8,128)(2,1)S(1)}, u32[]{:S(2)}, u32[]{:S(2)}) collective-permute-start(bf16[2,16,3584]{2,1,0:T(8,128)(2,1)S(1)} %collective-permute-done.5.refs_6_), channel_id=1, source_target_pairs={{0,1},{1,0},{2,3},{3,2},{4,5},{5,4},{6,7},{7,6},{8,9},{9,8},{10,11... | collective-permute-start | bytes 688136 | tf_op jit(solution)/shard_map/ppermute | solution.py:146
  25.9 9.2 %collective-permute-start.7 = (bf16[8,2,16,3584]{3,2,1,0:T(8,128)(2,1)S(1)}, bf16[8,2,16,3584]{3,2,1,0:T(8,128)(2,1)S(1)}, u32[]{:S(2)}, u32[]{:S(2)}) collective-permute-start(bf16[8,2,16,3584]{3,2,1,0:T(8,128)(2,1)S(1)} %arrange.1.own_ref.x_own_ref), channel_id=1, source_target_pairs={{0,8},{8,0},{1,9},{9,1},{2,10},{10,2},{3,11},{11,3},{4,12},{12,4},... | collective-permute-start | bytes 5505032 | tf_op jit(solution)/shard_map/ppermute | solution.py:515
  37.6 3.9 %collective-permute-start.8 = (bf16[2,128,3584]{2,1,0:T(8,128)(2,1)S(1)}, bf16[2,128,3584]{2,1,0:T(8,128)(2,1)S(1)}, u32[]{:S(2)}, u32[]{:S(2)}) collective-permute-start(bf16[2,128,3584]{2,1,0:T(8,128)(2,1)S(1)} %get-tuple-element.80), channel_id=1, source_target_pairs={{0,8},{8,0},{1,9},{9,1},{2,10},{10,2},{3,11},{11,3},{4,12},{12,4},... | collective-permute-start | bytes 5505032 | tf_op jit(solution)/shard_map/ppermute | solution.py:518
  39.9 4.3 %collective-permute-start.9 = (bf16[2,128,3584]{2,1,0:T(8,128)(2,1)S(1)}, bf16[2,128,3584]{2,1,0:T(8,128)(2,1)S(1)}, u32[]{:S(2)}, u32[]{:S(2)}) collective-permute-start(bf16[2,128,3584]{2,1,0:T(8,128)(2,1)S(1)} %get-tuple-element.81), channel_id=1, source_target_pairs={{0,8},{8,0},{1,9},{9,1},{2,10},{10,2},{3,11},{11,3},{4,12},{12,4},... | collective-permute-start | bytes 5505032 | tf_op jit(solution)/shard_map/ppermute | solution.py:520
  44.4 7.7 %collective-permute-start.12 = (bf16[64,3584]{1,0:T(8,128)(2,1)S(1)}, bf16[64,3584]{1,0:T(8,128)(2,1)S(1)}, u32[]{:S(2)}, u32[]{:S(2)}) collective-permute-start(bf16[64,3584]{1,0:T(8,128)(2,1)S(1)} %get-tuple-element.86), channel_id=1, source_target_pairs={{0,1},{1,0},{2,3},{3,2},{4,5},{5,4},{6,7},{7,6},{8,40},{9,41},{10,... | collective-permute-start | bytes 1376264 | tf_op jit(solution)/shard_map/ppermute | solution.py:344
  45.7 8.9 %collective-permute-start.10 = (bf16[64,3584]{1,0:T(8,128)(2,1)S(1)}, bf16[64,3584]{1,0:T(8,128)(2,1)S(1)}, u32[]{:S(2)}, u32[]{:S(2)}) collective-permute-start(bf16[64,3584]{1,0:T(8,128)(2,1)S(1)} %get-tuple-element.84), channel_id=1, source_target_pairs={{0,3},{1,2},{2,1},{3,0},{4,7},{5,6},{6,5},{7,4},{8,104},{9,105},{1... | collective-permute-start | bytes 1376264 | tf_op jit(solution)/shard_map/ppermute | solution.py:345
  52.4 13.8 %collective-permute-start.13 = (bf16[128,3584]{1,0:T(8,128)(2,1)S(1)}, bf16[128,3584]{1,0:T(8,128)(2,1)S(1)}, u32[]{:S(2)}, u32[]{:S(2)}) collective-permute-start(bf16[128,3584]{1,0:T(8,128)(2,1)S(1)} %fold_low.1), channel_id=1, source_target_pairs={{0,3},{1,2},{2,1},{3,0},{4,7},{5,6},{6,5},{7,4},{8,104},{9,105},{1... | collective-permute-start | bytes 2752520 | tf_op jit(solution)/shard_map/ppermute | solution.py:347
  54.9 12.6 %collective-permute-start.11 = (bf16[128,3584]{1,0:T(8,128)(2,1)S(1)}, bf16[128,3584]{1,0:T(8,128)(2,1)S(1)}, u32[]{:S(2)}, u32[]{:S(2)}) collective-permute-start(bf16[128,3584]{1,0:T(8,128)(2,1)S(1)} %fold_high.1), channel_id=1, source_target_pairs={{0,1},{1,0},{2,3},{3,2},{4,5},{5,4},{6,7},{7,6},{8,40},{9,41},{10,... | collective-permute-start | bytes 2752520 | tf_op jit(solution)/shard_map/ppermute | solution.py:351
  55.0 12.8 %collective-permute-start.14 = (bf16[2,3584]{1,0:T(2,128)(2,1)S(1)}, bf16[2,3584]{1,0:T(2,128)(2,1)S(1)}, u32[]{:S(2)}, u32[]{:S(2)}) collective-permute-start(bf16[2,3584]{1,0:T(2,128)(2,1)S(1)} %get-tuple-element.88), channel_id=1, source_target_pairs={{0,1},{1,2},{2,3},{3,0},{4,5},{5,6},{6,7},{7,4},{8,9},{9,10},{10,1... | collective-permute-start | bytes 43016 | tf_op jit(solution)/shard_map/ppermute | solution.py:506
  55.3 12.5 %collective-permute-start.15 = (bf16[2,3584]{1,0:T(2,128)(2,1)S(1)}, bf16[2,3584]{1,0:T(2,128)(2,1)S(1)}, u32[]{:S(2)}, u32[]{:S(2)}) collective-permute-start(bf16[2,3584]{1,0:T(2,128)(2,1)S(1)} %get-tuple-element.89), channel_id=1, source_target_pairs={{0,2},{1,3},{2,0},{3,1},{4,6},{5,7},{6,4},{7,5},{8,10},{9,11},{10,... | collective-permute-start | bytes 43016 | tf_op jit(solution)/shard_map/ppermute | solution.py:506
  56.7 11.1 %collective-permute-start.16 = (bf16[2,3584]{1,0:T(2,128)(2,1)S(1)}, bf16[2,3584]{1,0:T(2,128)(2,1)S(1)}, u32[]{:S(2)}, u32[]{:S(2)}) collective-permute-start(bf16[2,3584]{1,0:T(2,128)(2,1)S(1)} %get-tuple-element.90), channel_id=1, source_target_pairs={{0,3},{1,0},{2,1},{3,2},{4,7},{5,4},{6,5},{7,6},{8,11},{9,8},{10,9... | collective-permute-start | bytes 43016 | tf_op jit(solution)/shard_map/ppermute | solution.py:506
  98.3 21.6 %collective-permute-start.18 = (bf16[128,3584]{1,0:T(8,128)(2,1)S(1)}, bf16[128,3584]{1,0:T(8,128)(2,1)S(1)}, u32[]{:S(2)}, u32[]{:S(2)}) collective-permute-start(bf16[128,3584]{1,0:T(8,128)(2,1)S(1)} %bitcast.2), channel_id=1, source_target_pairs={{0,3},{1,2},{2,1},{3,0},{4,7},{5,6},{6,5},{7,4},{8,104},{9,105},{1... | collective-permute-start | bytes 2752520 | tf_op jit(solution)/shard_map/ppermute | solution.py:374
  98.8 21.1 %collective-permute-start.17 = (bf16[128,3584]{1,0:T(8,128)(2,1)S(1)}, bf16[128,3584]{1,0:T(8,128)(2,1)S(1)}, u32[]{:S(2)}, u32[]{:S(2)}) collective-permute-start(bf16[128,3584]{1,0:T(8,128)(2,1)S(1)} %bitcast.3), channel_id=1, source_target_pairs={{0,1},{1,0},{2,3},{3,2},{4,5},{5,4},{6,7},{7,6},{8,40},{9,41},{10,... | collective-permute-start | bytes 2752520 | tf_op jit(solution)/shard_map/ppermute | solution.py:373
  98.8 4.1 %collective-permute-start.19 = (bf16[2,3584]{1,0:T(2,128)(2,1)S(1)}, bf16[2,3584]{1,0:T(2,128)(2,1)S(1)}, u32[]{:S(2)}, u32[]{:S(2)}) collective-permute-start(bf16[2,3584]{1,0:T(2,128)(2,1)S(1)} %get-tuple-element.103), channel_id=1, source_target_pairs={{0,1},{1,2},{2,3},{3,0},{4,5},{5,6},{6,7},{7,4},{8,9},{9,10},{10,1... | collective-permute-start | bytes 43016 | tf_op jit(solution)/shard_map/ppermute | solution.py:506
  98.8 21.1 %collective-permute-start.20 = (bf16[2,3584]{1,0:T(2,128)(2,1)S(1)}, bf16[2,3584]{1,0:T(2,128)(2,1)S(1)}, u32[]{:S(2)}, u32[]{:S(2)}) collective-permute-start(bf16[2,3584]{1,0:T(2,128)(2,1)S(1)} %get-tuple-element.104), channel_id=1, source_target_pairs={{0,2},{1,3},{2,0},{3,1},{4,6},{5,7},{6,4},{7,5},{8,10},{9,11},{10,... | collective-permute-start | bytes 43016 | tf_op jit(solution)/shard_map/ppermute | solution.py:506
  100.4 19.5 %collective-permute-start.21 = (bf16[2,3584]{1,0:T(2,128)(2,1)S(1)}, bf16[2,3584]{1,0:T(2,128)(2,1)S(1)}, u32[]{:S(2)}, u32[]{:S(2)}) collective-permute-start(bf16[2,3584]{1,0:T(2,128)(2,1)S(1)} %get-tuple-element.105), channel_id=1, source_target_pairs={{0,3},{1,0},{2,1},{3,2},{4,7},{5,4},{6,5},{7,6},{8,11},{9,8},{10,9... | collective-permute-start | bytes 43016 | tf_op jit(solution)/shard_map/ppermute | solution.py:506
  102.9 28.9 %collective-permute-start.24 = (bf16[128,3584]{1,0:T(8,128)(2,1)S(1)}, bf16[128,3584]{1,0:T(8,128)(2,1)S(1)}, u32[]{:S(2)}, u32[]{:S(2)}) collective-permute-start(bf16[128,3584]{1,0:T(8,128)(2,1)S(1)} %bitcast.4), channel_id=1, source_target_pairs={{0,8},{8,0},{1,9},{9,1},{2,10},{10,2},{3,11},{11,3},{4,12},{12,4},... | collective-permute-start | bytes 2752520 | tf_op jit(solution)/shard_map/ppermute | solution.py:381
  120.0 7.7 %collective-permute-start.23 = (bf16[64,3584]{1,0:T(8,128)(2,1)S(1)}, bf16[64,3584]{1,0:T(8,128)(2,1)S(1)}, u32[]{:S(2)}, u32[]{:S(2)}) collective-permute-start(bf16[64,3584]{1,0:T(8,128)(2,1)S(1)} %half_high.1), channel_id=1, source_target_pairs={{0,1},{1,0},{2,3},{3,2},{4,5},{5,4},{6,7},{7,6},{8,40},{9,41},{10,... | collective-permute-start | bytes 1376264 | tf_op jit(solution)/shard_map/ppermute | solution.py:379
  120.5 9.7 %collective-permute-start.22 = (bf16[64,3584]{1,0:T(8,128)(2,1)S(1)}, bf16[64,3584]{1,0:T(8,128)(2,1)S(1)}, u32[]{:S(2)}, u32[]{:S(2)}) collective-permute-start(bf16[64,3584]{1,0:T(8,128)(2,1)S(1)} %half_low.1), channel_id=1, source_target_pairs={{0,3},{1,2},{2,1},{3,0},{4,7},{5,6},{6,5},{7,4},{8,104},{9,105},{1... | collective-permute-start | bytes 1376264 | tf_op jit(solution)/shard_map/ppermute | solution.py:377
  122.3 10.7 %collective-permute-start.25 = (bf16[128,3584]{1,0:T(8,128)(2,1)S(1)}, bf16[128,3584]{1,0:T(8,128)(2,1)S(1)}, u32[]{:S(2)}, u32[]{:S(2)}) collective-permute-start(bf16[128,3584]{1,0:T(8,128)(2,1)S(1)} %collective-permute-done.17.quarter_ref.one_ref), channel_id=1, source_target_pairs={{0,8},{8,0},{1,9},{9,1},{2,10},{10,2},{3,11},{11,3},{4,12},{12,4},... | collective-permute-start | bytes 2752520 | tf_op jit(solution)/shard_map/ppermute | solution.py:381
  122.7 10.2 %collective-permute-start.26 = (bf16[128,3584]{1,0:T(8,128)(2,1)S(1)}, bf16[128,3584]{1,0:T(8,128)(2,1)S(1)}, u32[]{:S(2)}, u32[]{:S(2)}) collective-permute-start(bf16[128,3584]{1,0:T(8,128)(2,1)S(1)} %collective-permute-done.18.quarter_ref.three_ref), channel_id=1, source_target_pairs={{0,8},{8,0},{1,9},{9,1},{2,10},{10,2},{3,11},{11,3},{4,12},{12,4},... | collective-permute-start | bytes 2752520 | tf_op jit(solution)/shard_map/ppermute | solution.py:381
  127.7 4.1 %collective-permute-start.28 = (bf16[64,3584]{1,0:T(8,128)(2,1)S(1)}, bf16[64,3584]{1,0:T(8,128)(2,1)S(1)}, u32[]{:S(2)}, u32[]{:S(2)}) collective-permute-start(bf16[64,3584]{1,0:T(8,128)(2,1)S(1)} %collective-permute-done.23.far3_ref), channel_id=1, source_target_pairs={{0,8},{8,0},{1,9},{9,1},{2,10},{10,2},{3,11},{11,3},{4,12},{12,4},... | collective-permute-start | bytes 1376264 | tf_op jit(solution)/shard_map/ppermute | solution.py:381
  130.2 2.8 %collective-permute-start.27 = (bf16[64,3584]{1,0:T(8,128)(2,1)S(1)}, bf16[64,3584]{1,0:T(8,128)(2,1)S(1)}, u32[]{:S(2)}, u32[]{:S(2)}) collective-permute-start(bf16[64,3584]{1,0:T(8,128)(2,1)S(1)} %collective-permute-done.22.far1_ref), channel_id=1, source_target_pairs={{0,8},{8,0},{1,9},{9,1},{2,10},{10,2},{3,11},{11,3},{4,12},{12,4},... | collective-permute-start | bytes 1376264 | tf_op jit(solution)/shard_map/ppermute | solution.py:381

commit v10 on v9

--- a/solution.py
+++ b/solution.py
@@ -49,7 +49,10 @@
 
 RING = {flip: _ring(flip) for flip in (1, 3)}
 ALONG_Y = {
-    flip: _pairs(lambda x, zl, core, zh, y, flip=flip: (x, zl, core, zh, y ^ flip)) for flip in (1, 3)
+    flip: _pairs(
+        lambda x, zl, core, zh, y, flip=flip: (x, zl, core, zh, y ^ (4 - flip if core else flip))
+    )
+    for flip in (1, 3)
 }
 ACROSS = _pairs(lambda x, zl, core, zh, y: (x, zl ^ 1, core, zh ^ 1, y))
 GROUPS = [
@@ -132,7 +135,9 @@
 
 def _arrange_kernel(*refs):
     zh, y = lax.axis_index("zh"), lax.axis_index("y")
+    core = lax.axis_index("core")
     for piece_ref, (across, flip) in zip(refs[:TILES], TILE_FROM):
+        flip = jnp.where(core == 0, flip, (4 - flip) % 4)
         tile = lax.rem(zh + across, 2) * 4 + lax.bitwise_xor(y, flip)
         refs[TILES][tile] = piece_ref[...]
 

time: 143 us -> 142 us (level)
  starting transfers between devices: 52.5 us -> 45.7 us
  blocking collectives: 30.1 us -> 33.7 us
  waiting for transfers between devices: 36.5 us -> 38.5 us
    ppermute x1, starting transfers between devices: 5.79 us -> 1.7 us  [per_device(): oth = lax.ppermute(own, 'core', SWAP)]
    ppermute x1, waiting for transfers between devices: 0.25 us -> 3.99 us  [_gather_inputs(): far_2 = lax.ppermute(far_3, ALL, ALONG_Y[1])]
    all_to_all x1, blocking collectives: 15.1 us -> 17.7 us  [per_device(): lax.all_to_all(errors, ALL, 0, 0, axis_index_groups=GROUPS)]
where the time goes in v10:
time: 142 us
  starting transfers between devices  45.7 us (32%)
  waiting for transfers between devices  38.5 us (27%)
  blocking collectives  33.7 us (24%)
  Pallas kernels  22.9 us (16%)
    ppermute x5, starting transfers between devices, _gather_ring(): others = [lax.ppermute(piece, 'core', SWAP) for piece in pieces]  20.2 us
    all_to_all x1, blocking collectives, per_device(): lax.all_to_all(errors, ALL, 0, 0, axis_index_groups=GROUPS)  17.7 us
    all_to_all x1, blocking collectives, per_device(): lax.all_to_all(quarter.reshape(16, 8, D), ALL, 0, 0, axis_index_groups=GR...  15.9 us
    pallas_call x1, Pallas kernels, _backward(): pl.pallas_call(_backward_kernel, grid=(PAIRS + 2,), in_specs=[WHOLE] * 11...  9.6 us
    ppermute x1, waiting for transfers between devices, _reduce_ring(): from3 = lax.ppermute(to3, ALL, RING[3])  7.57 us
    ppermute x6, starting transfers between devices, _around_y(): lax.ppermute(pieces[j], 'y', [(i, (i + j) % 4) for i in range(4)])  7.02 us
    pallas_call x1, Pallas kernels, _stage(): pl.pallas_call(_stage_kernel, in_specs=[pl.BlockSpec(memory_space=HBM)] *...  4.74 us
    ppermute x1, waiting for transfers between devices, _gather_ring(): far3 = lax.ppermute(pass1, ALL, RING[1])  4.48 us
  transfers between devices with their start and end apart: 29, of which 13 were waited for; matrix products, arithmetic and copies ran while one was open for 0% of the time, Pallas kernels for 6%

profile of v10, /device:TPU:1, one launch (start us, length us, event | category | flops | bytes accessed | tf_op | source)
XLA Modules:
  0.0 141.5 jit_solution(17206162116029559685)
XLA Ops:
  0.6 1.0 prepare.1
  1.7 2.2 %collective-permute-start.2 = (bf16[2,16,3584]{2,1,0:T(8,128)(2,1)S(1)}, bf16[2,16,3584]{2,1,0:T(8,128)(2,1)S(1)}, u32[]{:S(2)}, u32[]{:S(2)}) collective-permute-start(bf16[2,16,3584]{2,1,0:T(8,128)(2,1)S(1)} %get-tuple-element.64.refs_0_), channel_id=1, source_target_pairs={{0,3},{1,2},{2,1},{3,0},{4,7},{5,6},{6,5},{7,4},{8,9},{9,8},{10,11... | collective-permute-start | bytes 688136 | tf_op jit(solution)/shard_map/ppermute | solution.py:147
  3.9 1.9 %collective-permute-start.1 = (bf16[2,16,3584]{2,1,0:T(8,128)(2,1)S(1)}, bf16[2,16,3584]{2,1,0:T(8,128)(2,1)S(1)}, u32[]{:S(2)}, u32[]{:S(2)}) collective-permute-start(bf16[2,16,3584]{2,1,0:T(8,128)(2,1)S(1)} %get-tuple-element.64.refs_0_), channel_id=1, source_target_pairs={{0,1},{1,0},{2,3},{3,2},{4,5},{5,4},{6,7},{7,6},{8,11},{9,10},{10,... | collective-permute-start | bytes 688136 | tf_op jit(solution)/shard_map/ppermute | solution.py:147
  5.8 3.8 %collective-permute-start = (bf16[2,16,3584]{2,1,0:T(8,128)(2,1)S(1)}, bf16[2,16,3584]{2,1,0:T(8,128)(2,1)S(1)}, u32[]{:S(2)}, u32[]{:S(2)}) collective-permute-start(bf16[2,16,3584]{2,1,0:T(8,128)(2,1)S(1)} %get-tuple-element.64.refs_0_), channel_id=1, source_target_pairs={{0,20},{1,21},{2,22},{3,23},{4,16},{5,17},{6,18},{7,19},{8,28},{9,... | collective-permute-start | bytes 688136 | tf_op jit(solution)/shard_map/ppermute | solution.py:146
  9.5 4.7 %stage.1 = (bf16[2,3584,256]{2,1,0:T(8,128)(2,1)S(1)}, bf16[5,256,3584]{2,1,0:T(8,128)(2,1)S(1)}) custom-call(bf16[2,3584,256]{2,1,0:T(8,128)(2,1)} %enc_hbm, bf16[5,256,3584]{2,1,0:T(8,128)(2,1)} %dec_hbm), custom_call_target="tpu_custom_call" | custom-call | bytes 25690112 | tf_op jit(solution)/shard_map/stage/pallas_call | solution.py:214
  14.3 0.6 collective-permute-done.refs_4_
  14.9 0.8 collective-permute-start.4
  15.8 0.8 collective-permute-start.3
  16.6 3.2 %collective-permute-done.5.refs_6_ = bf16[2,16,3584]{2,1,0:T(8,128)(2,1)S(1)} collective-permute-done((bf16[2,16,3584]{2,1,0:T(8,128)(2,1)S(1)}, bf16[2,16,3584]{2,1,0:T(8,128)(2,1)S(1)}, u32[]{:S(2)}, u32[]{:S(2)}) %collective-permute-start.5) | collective-permute-done | bytes 229408 | tf_op jit(solution)/shard_map/ppermute | solution.py:149
  19.8 0.8 collective-permute-start.6
  20.6 4.1 %collective-permute-done.3.refs_3_ = bf16[2,16,3584]{2,1,0:T(8,128)(2,1)S(1)} collective-permute-done((bf16[2,16,3584]{2,1,0:T(8,128)(2,1)S(1)}, bf16[2,16,3584]{2,1,0:T(8,128)(2,1)S(1)}, u32[]{:S(2)}, u32[]{:S(2)}) %collective-permute-start.3) | collective-permute-done | bytes 229408 | tf_op jit(solution)/shard_map/ppermute | solution.py:150
  24.7 4.0 %collective-permute-done.6.refs_7_ = bf16[2,16,3584]{2,1,0:T(8,128)(2,1)S(1)} collective-permute-done((bf16[2,16,3584]{2,1,0:T(8,128)(2,1)S(1)}, bf16[2,16,3584]{2,1,0:T(8,128)(2,1)S(1)}, u32[]{:S(2)}, u32[]{:S(2)}) %collective-permute-start.6) | collective-permute-done | bytes 229408 | tf_op jit(solution)/shard_map/ppermute | solution.py:151
  28.8 1.7 %collective-permute-start.7 = (bf16[8,2,16,3584]{3,2,1,0:T(8,128)(2,1)S(1)}, bf16[8,2,16,3584]{3,2,1,0:T(8,128)(2,1)S(1)}, u32[]{:S(2)}, u32[]{:S(2)}) collective-permute-start(bf16[8,2,16,3584]{3,2,1,0:T(8,128)(2,1)S(1)} %arrange.1.own_ref.x_own_ref), channel_id=1, source_target_pairs={{0,8},{8,0},{1,9},{9,1},{2,10},{10,2},{3,11},{11,3},{4,12},{12,4},... | collective-permute-start | bytes 5505032 | tf_op jit(solution)/shard_map/ppermute | solution.py:520
  30.5 3.4 %collective-permute-done.7.oth_ref.x_oth_ref = bf16[8,2,16,3584]{3,2,1,0:T(8,128)(2,1)S(1)} collective-permute-done((bf16[8,2,16,3584]{3,2,1,0:T(8,128)(2,1)S(1)}, bf16[8,2,16,3584]{3,2,1,0:T(8,128)(2,1)S(1)}, u32[]{:S(2)}, u32[]{:S(2)}) %collective-permute-start.7) | collective-permute-done | bytes 1835040 | tf_op jit(solution)/shard_map/ppermute | solution.py:520
  33.9 2.5 %forward.1 = (bf16[2,128,3584]{2,1,0:T(8,128)(2,1)S(1)}, bf16[2,128,3584]{2,1,0:T(8,128)(2,1)S(1)}, bf16[2,256,256]{2,1,0:T(8,128)(2,1)S(1)}, bf16[2,256,256]{2,1,0:T(8,128)(2,1)S(1)}, f32[2,256,256]{2,1,0:T(8,128)S(1)}) custom-call(bf16[8,2,16,3584]{3,2,1,0:T(8,128)(2,1)S(1)} %arrange.1.own_ref.x_own_ref, ...), custom_call_target="tpu_custom_call" | custom-call | flops 1879048192 | bytes 3670016 | tf_op jit(solution)/shard_map/forward/pallas_call | solution.py:264
  36.5 0.5 collective-permute-start.8
  36.9 1.8 %forward_high.1 = (bf16[2,128,3584]{2,1,0:T(8,128)(2,1)S(1)}, bf16[2,128,3584]{2,1,0:T(8,128)(2,1)S(1)}) custom-call(bf16[2,256,256]{2,1,0:T(8,128)(2,1)S(1)} %get-tuple-element.78.codes_ref, bf16[5,256,3584]{2,1,0:T(8,128)(2,1)S(1)} %get-tuple-element.74.dec_ref), custom_call_target="tpu_custom_call" | custom-call | flops 1409286144 | bytes 3670016 | tf_op jit(solution)/shard_map/forward_high/pallas_call | solution.py:289
  38.9 1.4 %collective-permute-done.8.got_low_ref = bf16[2,128,3584]{2,1,0:T(8,128)(2,1)S(1)} collective-permute-done((bf16[2,128,3584]{2,1,0:T(8,128)(2,1)S(1)}, bf16[2,128,3584]{2,1,0:T(8,128)(2,1)S(1)}, u32[]{:S(2)}, u32[]{:S(2)}) %collective-permute-start.8) | collective-permute-done | bytes 1835040 | tf_op jit(solution)/shard_map/ppermute | solution.py:523
  40.4 2.6 %collective-permute-done.9.got_ref = bf16[2,128,3584]{2,1,0:T(8,128)(2,1)S(1)} collective-permute-done((bf16[2,128,3584]{2,1,0:T(8,128)(2,1)S(1)}, bf16[2,128,3584]{2,1,0:T(8,128)(2,1)S(1)}, u32[]{:S(2)}, u32[]{:S(2)}) %collective-permute-start.9) | collective-permute-done | bytes 1835040 | tf_op jit(solution)/shard_map/ppermute | solution.py:525
  43.0 0.3 join_far.1
  43.2 1.3 collective-permute-start.12
  44.5 1.4 collective-permute-start.10
  45.9 0.9 join.1
  46.9 4.1 %collective-permute-done.12.got_ref = bf16[64,3584]{1,0:T(8,128)(2,1)S(1)} collective-permute-done((bf16[64,3584]{1,0:T(8,128)(2,1)S(1)}, bf16[64,3584]{1,0:T(8,128)(2,1)S(1)}, u32[]{:S(2)}, u32[]{:S(2)}) %collective-permute-start.12) | collective-permute-done | bytes 458784 | tf_op jit(solution)/shard_map/ppermute | solution.py:349
  50.9 0.4 fold_low.1
  51.3 2.1 %collective-permute-start.13 = (bf16[128,3584]{1,0:T(8,128)(2,1)S(1)}, bf16[128,3584]{1,0:T(8,128)(2,1)S(1)}, u32[]{:S(2)}, u32[]{:S(2)}) collective-permute-start(bf16[128,3584]{1,0:T(8,128)(2,1)S(1)} %fold_low.1), channel_id=1, source_target_pairs={{0,3},{1,2},{2,1},{3,0},{4,7},{5,6},{6,5},{7,4},{8,104},{9,105},{1... | collective-permute-start | bytes 2752520 | tf_op jit(solution)/shard_map/ppermute | solution.py:352
  53.4 0.4 fold_high.1
  53.9 1.2 collective-permute-start.14
  55.1 0.8 collective-permute-start.15
  55.9 1.7 %collective-permute-start.16 = (bf16[2,3584]{1,0:T(2,128)(2,1)S(1)}, bf16[2,3584]{1,0:T(2,128)(2,1)S(1)}, u32[]{:S(2)}, u32[]{:S(2)}) collective-permute-start(bf16[2,3584]{1,0:T(2,128)(2,1)S(1)} %get-tuple-element.90), channel_id=1, source_target_pairs={{0,3},{1,0},{2,1},{3,2},{4,7},{5,4},{6,5},{7,6},{8,11},{9,8},{10,9... | collective-permute-start | bytes 43016 | tf_op jit(solution)/shard_map/ppermute | solution.py:511
  57.6 7.6 %collective-permute-done.13.three_ref = bf16[128,3584]{1,0:T(8,128)(2,1)S(1)} collective-permute-done((bf16[128,3584]{1,0:T(8,128)(2,1)S(1)}, bf16[128,3584]{1,0:T(8,128)(2,1)S(1)}, u32[]{:S(2)}, u32[]{:S(2)}) %collective-permute-start.13) | collective-permute-done | bytes 917536 | tf_op jit(solution)/shard_map/ppermute | solution.py:352
  65.1 1.3 collective-permute-done.11.one_ref
  66.4 0.3 total.1
  66.7 15.9 %all_to_all.10.pieces_ref = bf16[16,8,3584]{2,1,0:T(8,128)(2,1)S(1)} all-to-all(bf16[16,8,3584]{2,1,0:T(8,128)(2,1)S(1)} %bitcast.6), channel_id=1, replica_groups={{0,4,16,20,32,36,48,52,64,68,80,84,96,100,112,116},{1,5,17,21,33,37,49,..., dimensions={0} | all-to-all | bytes 1835008 | tf_op jit(solution)/shard_map/all_to_all | solution.py:528
  82.6 0.3 settle.1
  83.0 17.7 %all_to_all.11 = bf16[16,8,3584]{2,1,0:T(8,128)(2,1)S(1)} all-to-all(bf16[16,8,3584]{2,1,0:T(8,128)(2,1)S(1)} %get-tuple-element.96), channel_id=1, replica_groups={{0,4,16,20,32,36,48,52,64,68,80,84,96,100,112,116},{1,5,17,21,33,37,49,..., dimensions={0} | all-to-all | bytes 1835008 | tf_op jit(solution)/shard_map/all_to_all | solution.py:530
  100.7 2.1 %collective-permute-start.20 = (bf16[2,3584]{1,0:T(2,128)(2,1)S(1)}, bf16[2,3584]{1,0:T(2,128)(2,1)S(1)}, u32[]{:S(2)}, u32[]{:S(2)}) collective-permute-start(bf16[2,3584]{1,0:T(2,128)(2,1)S(1)} %get-tuple-element.104), channel_id=1, source_target_pairs={{0,2},{1,3},{2,0},{3,1},{4,6},{5,7},{6,4},{7,5},{8,10},{9,11},{10,... | collective-permute-start | bytes 43016 | tf_op jit(solution)/shard_map/ppermute | solution.py:511
  102.8 1.2 collective-permute-start.21
  104.1 0.4 collective-permute-done.19.rest_1_
  104.5 14.2 %collective-permute-start.24 = (bf16[128,3584]{1,0:T(8,128)(2,1)S(1)}, bf16[128,3584]{1,0:T(8,128)(2,1)S(1)}, u32[]{:S(2)}, u32[]{:S(2)}) collective-permute-start(bf16[128,3584]{1,0:T(8,128)(2,1)S(1)} %bitcast.4), channel_id=1, source_target_pairs={{0,8},{8,0},{1,9},{9,1},{2,10},{10,2},{3,11},{11,3},{4,12},{12,4},... | collective-permute-start | bytes 2752520 | tf_op jit(solution)/shard_map/ppermute | solution.py:386
  118.9 0.9 collective-permute-start.22
  119.8 2.2 %collective-permute-start.25 = (bf16[128,3584]{1,0:T(8,128)(2,1)S(1)}, bf16[128,3584]{1,0:T(8,128)(2,1)S(1)}, u32[]{:S(2)}, u32[]{:S(2)}) collective-permute-start(bf16[128,3584]{1,0:T(8,128)(2,1)S(1)} %collective-permute-done.17.quarter_ref.one_ref), channel_id=1, source_target_pairs={{0,8},{8,0},{1,9},{9,1},{2,10},{10,2},{3,11},{11,3},{4,12},{12,4},... | collective-permute-start | bytes 2752520 | tf_op jit(solution)/shard_map/ppermute | solution.py:386
  122.0 4.5 %collective-permute-done.23.far3_ref = bf16[64,3584]{1,0:T(8,128)(2,1)S(1)} collective-permute-done((bf16[64,3584]{1,0:T(8,128)(2,1)S(1)}, bf16[64,3584]{1,0:T(8,128)(2,1)S(1)}, u32[]{:S(2)}, u32[]{:S(2)}) %collective-permute-start.23) | collective-permute-done | bytes 458784 | tf_op jit(solution)/shard_map/ppermute | solution.py:384
  126.4 2.5 %collective-permute-start.28 = (bf16[64,3584]{1,0:T(8,128)(2,1)S(1)}, bf16[64,3584]{1,0:T(8,128)(2,1)S(1)}, u32[]{:S(2)}, u32[]{:S(2)}) collective-permute-start(bf16[64,3584]{1,0:T(8,128)(2,1)S(1)} %collective-permute-done.23.far3_ref), channel_id=1, source_target_pairs={{0,8},{8,0},{1,9},{9,1},{2,10},{10,2},{3,11},{11,3},{4,12},{12,4},... | collective-permute-start | bytes 1376264 | tf_op jit(solution)/shard_map/ppermute | solution.py:386
  128.9 1.3 collective-permute-start.27
  130.5 1.2 collective-permute-done.27.far1_ref
  131.7 0.3 assemble_oth.1.oth_ref
  131.9 9.6 %backward.1 = (bf16[5,256,3584]{2,1,0:T(8,128)(2,1)}, bf16[2,3584,256]{2,1,0:T(8,128)(2,1)}, f32[2,256]{1,0:T(2,128)}, bf16[4,2,3584]{2,1,0:T(2,128)(2,1)}) custom-call(bf16[2,256,256]{2,1,0:T(8,128)(2,1)S(1)} %get-tuple-element.75.turned_ref, f32[2,256,256]{2,1,0:T(8,128)S(1)} %get-tuple-element.76.slope_ref, ...), custom_call_target="tpu_custom_call" | custom-call | flops 5637144576 | bytes 12845056 | tf_op jit(solution)/shard_map/backward/pallas_call | solution.py:482
  (32 shorter events, 0.9 us)
Async XLA Ops:
  1.7 12.6 %collective-permute-start.2 = (bf16[2,16,3584]{2,1,0:T(8,128)(2,1)S(1)}, bf16[2,16,3584]{2,1,0:T(8,128)(2,1)S(1)}, u32[]{:S(2)}, u32[]{:S(2)}) collective-permute-start(bf16[2,16,3584]{2,1,0:T(8,128)(2,1)S(1)} %get-tuple-element.64.refs_0_), channel_id=1, source_target_pairs={{0,3},{1,2},{2,1},{3,0},{4,7},{5,6},{6,5},{7,4},{8,9},{9,8},{10,11... | collective-permute-start | bytes 688136 | tf_op jit(solution)/shard_map/ppermute | solution.py:147
  3.9 10.4 %collective-permute-start.1 = (bf16[2,16,3584]{2,1,0:T(8,128)(2,1)S(1)}, bf16[2,16,3584]{2,1,0:T(8,128)(2,1)S(1)}, u32[]{:S(2)}, u32[]{:S(2)}) collective-permute-start(bf16[2,16,3584]{2,1,0:T(8,128)(2,1)S(1)} %get-tuple-element.64.refs_0_), channel_id=1, source_target_pairs={{0,1},{1,0},{2,3},{3,2},{4,5},{5,4},{6,7},{7,6},{8,11},{9,10},{10,... | collective-permute-start | bytes 688136 | tf_op jit(solution)/shard_map/ppermute | solution.py:147
  5.8 9.1 %collective-permute-start = (bf16[2,16,3584]{2,1,0:T(8,128)(2,1)S(1)}, bf16[2,16,3584]{2,1,0:T(8,128)(2,1)S(1)}, u32[]{:S(2)}, u32[]{:S(2)}) collective-permute-start(bf16[2,16,3584]{2,1,0:T(8,128)(2,1)S(1)} %get-tuple-element.64.refs_0_), channel_id=1, source_target_pairs={{0,20},{1,21},{2,22},{3,23},{4,16},{5,17},{6,18},{7,19},{8,28},{9,... | collective-permute-start | bytes 688136 | tf_op jit(solution)/shard_map/ppermute | solution.py:146
  14.9 19.0 %copy-start = (s32[4,8,32]{2,1,0:T(8,128)S(1)}, s32[4,8,32]{2,1,0:T(8,128)}, u32[]{:S(2)}) copy-start(s32[4,8,32]{2,1,0:T(8,128)} %active_ref.1) | copy-start | bytes 12292
  14.9 19.0 %copy-start.1 = (f32[2,256]{1,0:T(2,128)S(1)}, f32[2,256]{1,0:T(2,128)}, u32[]{:S(2)}) copy-start(f32[2,256]{1,0:T(2,128)} %bias_ref.1) | copy-start | bytes 6148
  14.9 4.9 %collective-permute-start.5 = (bf16[2,16,3584]{2,1,0:T(8,128)(2,1)S(1)}, bf16[2,16,3584]{2,1,0:T(8,128)(2,1)S(1)}, u32[]{:S(2)}, u32[]{:S(2)}) collective-permute-start(bf16[2,16,3584]{2,1,0:T(8,128)(2,1)S(1)} %collective-permute-done.refs_4_), channel_id=1, source_target_pairs={{0,3},{1,2},{2,1},{3,0},{4,7},{5,6},{6,5},{7,4},{8,9},{9,8},{10,11... | collective-permute-start | bytes 688136 | tf_op jit(solution)/shard_map/ppermute | solution.py:149
  14.9 9.8 %collective-permute-start.4 = (bf16[2,16,3584]{2,1,0:T(8,128)(2,1)S(1)}, bf16[2,16,3584]{2,1,0:T(8,128)(2,1)S(1)}, u32[]{:S(2)}, u32[]{:S(2)}) collective-permute-start(bf16[2,16,3584]{2,1,0:T(8,128)(2,1)S(1)} %collective-permute-done.refs_4_), channel_id=1, source_target_pairs={{0,1},{1,0},{2,3},{3,2},{4,5},{5,4},{6,7},{7,6},{8,11},{9,10},{10,... | collective-permute-start | bytes 688136 | tf_op jit(solution)/shard_map/ppermute | solution.py:149
  15.8 8.9 %collective-permute-start.3 = (bf16[2,16,3584]{2,1,0:T(8,128)(2,1)S(1)}, bf16[2,16,3584]{2,1,0:T(8,128)(2,1)S(1)}, u32[]{:S(2)}, u32[]{:S(2)}) collective-permute-start(bf16[2,16,3584]{2,1,0:T(8,128)(2,1)S(1)} %collective-permute-done.1.refs_1_), channel_id=1, source_target_pairs={{0,3},{1,2},{2,1},{3,0},{4,7},{5,6},{6,5},{7,4},{8,9},{9,8},{10,11... | collective-permute-start | bytes 688136 | tf_op jit(solution)/shard_map/ppermute | solution.py:150
  19.8 8.9 %collective-permute-start.6 = (bf16[2,16,3584]{2,1,0:T(8,128)(2,1)S(1)}, bf16[2,16,3584]{2,1,0:T(8,128)(2,1)S(1)}, u32[]{:S(2)}, u32[]{:S(2)}) collective-permute-start(bf16[2,16,3584]{2,1,0:T(8,128)(2,1)S(1)} %collective-permute-done.5.refs_6_), channel_id=1, source_target_pairs={{0,1},{1,0},{2,3},{3,2},{4,5},{5,4},{6,7},{7,6},{8,11},{9,10},{10,... | collective-permute-start | bytes 688136 | tf_op jit(solution)/shard_map/ppermute | solution.py:151
  28.8 5.1 %collective-permute-start.7 = (bf16[8,2,16,3584]{3,2,1,0:T(8,128)(2,1)S(1)}, bf16[8,2,16,3584]{3,2,1,0:T(8,128)(2,1)S(1)}, u32[]{:S(2)}, u32[]{:S(2)}) collective-permute-start(bf16[8,2,16,3584]{3,2,1,0:T(8,128)(2,1)S(1)} %arrange.1.own_ref.x_own_ref), channel_id=1, source_target_pairs={{0,8},{8,0},{1,9},{9,1},{2,10},{10,2},{3,11},{11,3},{4,12},{12,4},... | collective-permute-start | bytes 5505032 | tf_op jit(solution)/shard_map/ppermute | solution.py:520
  36.5 3.9 %collective-permute-start.8 = (bf16[2,128,3584]{2,1,0:T(8,128)(2,1)S(1)}, bf16[2,128,3584]{2,1,0:T(8,128)(2,1)S(1)}, u32[]{:S(2)}, u32[]{:S(2)}) collective-permute-start(bf16[2,128,3584]{2,1,0:T(8,128)(2,1)S(1)} %get-tuple-element.80), channel_id=1, source_target_pairs={{0,8},{8,0},{1,9},{9,1},{2,10},{10,2},{3,11},{11,3},{4,12},{12,4},... | collective-permute-start | bytes 5505032 | tf_op jit(solution)/shard_map/ppermute | solution.py:523
  38.7 4.3 %collective-permute-start.9 = (bf16[2,128,3584]{2,1,0:T(8,128)(2,1)S(1)}, bf16[2,128,3584]{2,1,0:T(8,128)(2,1)S(1)}, u32[]{:S(2)}, u32[]{:S(2)}) collective-permute-start(bf16[2,128,3584]{2,1,0:T(8,128)(2,1)S(1)} %get-tuple-element.81), channel_id=1, source_target_pairs={{0,8},{8,0},{1,9},{9,1},{2,10},{10,2},{3,11},{11,3},{4,12},{12,4},... | collective-permute-start | bytes 5505032 | tf_op jit(solution)/shard_map/ppermute | solution.py:525
  43.2 7.7 %collective-permute-start.12 = (bf16[64,3584]{1,0:T(8,128)(2,1)S(1)}, bf16[64,3584]{1,0:T(8,128)(2,1)S(1)}, u32[]{:S(2)}, u32[]{:S(2)}) collective-permute-start(bf16[64,3584]{1,0:T(8,128)(2,1)S(1)} %get-tuple-element.86), channel_id=1, source_target_pairs={{0,1},{1,0},{2,3},{3,2},{4,5},{5,4},{6,7},{7,6},{8,40},{9,41},{10,... | collective-permute-start | bytes 1376264 | tf_op jit(solution)/shard_map/ppermute | solution.py:349
  44.5 8.9 %collective-permute-start.10 = (bf16[64,3584]{1,0:T(8,128)(2,1)S(1)}, bf16[64,3584]{1,0:T(8,128)(2,1)S(1)}, u32[]{:S(2)}, u32[]{:S(2)}) collective-permute-start(bf16[64,3584]{1,0:T(8,128)(2,1)S(1)} %get-tuple-element.84), channel_id=1, source_target_pairs={{0,3},{1,2},{2,1},{3,0},{4,7},{5,6},{6,5},{7,4},{8,104},{9,105},{1... | collective-permute-start | bytes 1376264 | tf_op jit(solution)/shard_map/ppermute | solution.py:350
  51.3 13.8 %collective-permute-start.13 = (bf16[128,3584]{1,0:T(8,128)(2,1)S(1)}, bf16[128,3584]{1,0:T(8,128)(2,1)S(1)}, u32[]{:S(2)}, u32[]{:S(2)}) collective-permute-start(bf16[128,3584]{1,0:T(8,128)(2,1)S(1)} %fold_low.1), channel_id=1, source_target_pairs={{0,3},{1,2},{2,1},{3,0},{4,7},{5,6},{6,5},{7,4},{8,104},{9,105},{1... | collective-permute-start | bytes 2752520 | tf_op jit(solution)/shard_map/ppermute | solution.py:352
  53.8 12.6 %collective-permute-start.11 = (bf16[128,3584]{1,0:T(8,128)(2,1)S(1)}, bf16[128,3584]{1,0:T(8,128)(2,1)S(1)}, u32[]{:S(2)}, u32[]{:S(2)}) collective-permute-start(bf16[128,3584]{1,0:T(8,128)(2,1)S(1)} %fold_high.1), channel_id=1, source_target_pairs={{0,1},{1,0},{2,3},{3,2},{4,5},{5,4},{6,7},{7,6},{8,40},{9,41},{10,... | collective-permute-start | bytes 2752520 | tf_op jit(solution)/shard_map/ppermute | solution.py:356
  53.9 12.8 %collective-permute-start.14 = (bf16[2,3584]{1,0:T(2,128)(2,1)S(1)}, bf16[2,3584]{1,0:T(2,128)(2,1)S(1)}, u32[]{:S(2)}, u32[]{:S(2)}) collective-permute-start(bf16[2,3584]{1,0:T(2,128)(2,1)S(1)} %get-tuple-element.88), channel_id=1, source_target_pairs={{0,1},{1,2},{2,3},{3,0},{4,5},{5,6},{6,7},{7,4},{8,9},{9,10},{10,1... | collective-permute-start | bytes 43016 | tf_op jit(solution)/shard_map/ppermute | solution.py:511
  55.1 11.6 %collective-permute-start.15 = (bf16[2,3584]{1,0:T(2,128)(2,1)S(1)}, bf16[2,3584]{1,0:T(2,128)(2,1)S(1)}, u32[]{:S(2)}, u32[]{:S(2)}) collective-permute-start(bf16[2,3584]{1,0:T(2,128)(2,1)S(1)} %get-tuple-element.89), channel_id=1, source_target_pairs={{0,2},{1,3},{2,0},{3,1},{4,6},{5,7},{6,4},{7,5},{8,10},{9,11},{10,... | collective-permute-start | bytes 43016 | tf_op jit(solution)/shard_map/ppermute | solution.py:511
  55.9 10.8 %collective-permute-start.16 = (bf16[2,3584]{1,0:T(2,128)(2,1)S(1)}, bf16[2,3584]{1,0:T(2,128)(2,1)S(1)}, u32[]{:S(2)}, u32[]{:S(2)}) collective-permute-start(bf16[2,3584]{1,0:T(2,128)(2,1)S(1)} %get-tuple-element.90), channel_id=1, source_target_pairs={{0,3},{1,0},{2,1},{3,2},{4,7},{5,4},{6,5},{7,6},{8,11},{9,8},{10,9... | collective-permute-start | bytes 43016 | tf_op jit(solution)/shard_map/ppermute | solution.py:511
  100.7 18.0 %collective-permute-start.18 = (bf16[128,3584]{1,0:T(8,128)(2,1)S(1)}, bf16[128,3584]{1,0:T(8,128)(2,1)S(1)}, u32[]{:S(2)}, u32[]{:S(2)}) collective-permute-start(bf16[128,3584]{1,0:T(8,128)(2,1)S(1)} %bitcast.2), channel_id=1, source_target_pairs={{0,3},{1,2},{2,1},{3,0},{4,7},{5,6},{6,5},{7,4},{8,104},{9,105},{1... | collective-permute-start | bytes 2752520 | tf_op jit(solution)/shard_map/ppermute | solution.py:379
  100.7 18.0 %collective-permute-start.17 = (bf16[128,3584]{1,0:T(8,128)(2,1)S(1)}, bf16[128,3584]{1,0:T(8,128)(2,1)S(1)}, u32[]{:S(2)}, u32[]{:S(2)}) collective-permute-start(bf16[128,3584]{1,0:T(8,128)(2,1)S(1)} %bitcast.3), channel_id=1, source_target_pairs={{0,1},{1,0},{2,3},{3,2},{4,5},{5,4},{6,7},{7,6},{8,40},{9,41},{10,... | collective-permute-start | bytes 2752520 | tf_op jit(solution)/shard_map/ppermute | solution.py:378
  100.7 3.8 %collective-permute-start.19 = (bf16[2,3584]{1,0:T(2,128)(2,1)S(1)}, bf16[2,3584]{1,0:T(2,128)(2,1)S(1)}, u32[]{:S(2)}, u32[]{:S(2)}) collective-permute-start(bf16[2,3584]{1,0:T(2,128)(2,1)S(1)} %get-tuple-element.103), channel_id=1, source_target_pairs={{0,1},{1,2},{2,3},{3,0},{4,5},{5,6},{6,7},{7,4},{8,9},{9,10},{10,1... | collective-permute-start | bytes 43016 | tf_op jit(solution)/shard_map/ppermute | solution.py:511
  100.7 17.9 %collective-permute-start.20 = (bf16[2,3584]{1,0:T(2,128)(2,1)S(1)}, bf16[2,3584]{1,0:T(2,128)(2,1)S(1)}, u32[]{:S(2)}, u32[]{:S(2)}) collective-permute-start(bf16[2,3584]{1,0:T(2,128)(2,1)S(1)} %get-tuple-element.104), channel_id=1, source_target_pairs={{0,2},{1,3},{2,0},{3,1},{4,6},{5,7},{6,4},{7,5},{8,10},{9,11},{10,... | collective-permute-start | bytes 43016 | tf_op jit(solution)/shard_map/ppermute | solution.py:511
  102.8 15.8 %collective-permute-start.21 = (bf16[2,3584]{1,0:T(2,128)(2,1)S(1)}, bf16[2,3584]{1,0:T(2,128)(2,1)S(1)}, u32[]{:S(2)}, u32[]{:S(2)}) collective-permute-start(bf16[2,3584]{1,0:T(2,128)(2,1)S(1)} %get-tuple-element.105), channel_id=1, source_target_pairs={{0,3},{1,0},{2,1},{3,2},{4,7},{5,4},{6,5},{7,6},{8,11},{9,8},{10,9... | collective-permute-start | bytes 43016 | tf_op jit(solution)/shard_map/ppermute | solution.py:511
  104.5 26.0 %collective-permute-start.24 = (bf16[128,3584]{1,0:T(8,128)(2,1)S(1)}, bf16[128,3584]{1,0:T(8,128)(2,1)S(1)}, u32[]{:S(2)}, u32[]{:S(2)}) collective-permute-start(bf16[128,3584]{1,0:T(8,128)(2,1)S(1)} %bitcast.4), channel_id=1, source_target_pairs={{0,8},{8,0},{1,9},{9,1},{2,10},{10,2},{3,11},{11,3},{4,12},{12,4},... | collective-permute-start | bytes 2752520 | tf_op jit(solution)/shard_map/ppermute | solution.py:386
  118.7 7.7 %collective-permute-start.23 = (bf16[64,3584]{1,0:T(8,128)(2,1)S(1)}, bf16[64,3584]{1,0:T(8,128)(2,1)S(1)}, u32[]{:S(2)}, u32[]{:S(2)}) collective-permute-start(bf16[64,3584]{1,0:T(8,128)(2,1)S(1)} %half_high.1), channel_id=1, source_target_pairs={{0,1},{1,0},{2,3},{3,2},{4,5},{5,4},{6,7},{7,6},{8,40},{9,41},{10,... | collective-permute-start | bytes 1376264 | tf_op jit(solution)/shard_map/ppermute | solution.py:384
  118.9 10.0 %collective-permute-start.22 = (bf16[64,3584]{1,0:T(8,128)(2,1)S(1)}, bf16[64,3584]{1,0:T(8,128)(2,1)S(1)}, u32[]{:S(2)}, u32[]{:S(2)}) collective-permute-start(bf16[64,3584]{1,0:T(8,128)(2,1)S(1)} %half_low.1), channel_id=1, source_target_pairs={{0,3},{1,2},{2,1},{3,0},{4,7},{5,6},{6,5},{7,4},{8,104},{9,105},{1... | collective-permute-start | bytes 1376264 | tf_op jit(solution)/shard_map/ppermute | solution.py:382
  119.8 11.9 %collective-permute-start.25 = (bf16[128,3584]{1,0:T(8,128)(2,1)S(1)}, bf16[128,3584]{1,0:T(8,128)(2,1)S(1)}, u32[]{:S(2)}, u32[]{:S(2)}) collective-permute-start(bf16[128,3584]{1,0:T(8,128)(2,1)S(1)} %collective-permute-done.17.quarter_ref.one_ref), channel_id=1, source_target_pairs={{0,8},{8,0},{1,9},{9,1},{2,10},{10,2},{3,11},{11,3},{4,12},{12,4},... | collective-permute-start | bytes 2752520 | tf_op jit(solution)/shard_map/ppermute | solution.py:386
  121.9 9.7 %collective-permute-start.26 = (bf16[128,3584]{1,0:T(8,128)(2,1)S(1)}, bf16[128,3584]{1,0:T(8,128)(2,1)S(1)}, u32[]{:S(2)}, u32[]{:S(2)}) collective-permute-start(bf16[128,3584]{1,0:T(8,128)(2,1)S(1)} %collective-permute-done.18.quarter_ref.three_ref), channel_id=1, source_target_pairs={{0,8},{8,0},{1,9},{9,1},{2,10},{10,2},{3,11},{11,3},{4,12},{12,4},... | collective-permute-start | bytes 2752520 | tf_op jit(solution)/shard_map/ppermute | solution.py:386
  126.4 4.1 %collective-permute-start.28 = (bf16[64,3584]{1,0:T(8,128)(2,1)S(1)}, bf16[64,3584]{1,0:T(8,128)(2,1)S(1)}, u32[]{:S(2)}, u32[]{:S(2)}) collective-permute-start(bf16[64,3584]{1,0:T(8,128)(2,1)S(1)} %collective-permute-done.23.far3_ref), channel_id=1, source_target_pairs={{0,8},{8,0},{1,9},{9,1},{2,10},{10,2},{3,11},{11,3},{4,12},{12,4},... | collective-permute-start | bytes 1376264 | tf_op jit(solution)/shard_map/ppermute | solution.py:386
  128.9 2.8 %collective-permute-start.27 = (bf16[64,3584]{1,0:T(8,128)(2,1)S(1)}, bf16[64,3584]{1,0:T(8,128)(2,1)S(1)}, u32[]{:S(2)}, u32[]{:S(2)}) collective-permute-start(bf16[64,3584]{1,0:T(8,128)(2,1)S(1)} %collective-permute-done.22.far1_ref), channel_id=1, source_target_pairs={{0,8},{8,0},{1,9},{9,1},{2,10},{10,2},{3,11},{11,3},{4,12},{12,4},... | collective-permute-start | bytes 1376264 | tf_op jit(solution)/shard_map/ppermute | solution.py:386

commit v11 on v10

--- a/solution.py
+++ b/solution.py
@@ -467,25 +467,31 @@
             pre_ref[k] = pre
             bias_ref[k : k + 1] = jnp.sum(pre.astype(F32), axis=0, keepdims=True)
 
-    @pl.when(p >= PAIRS)
-    def _():
-        k = jnp.maximum(p - PAIRS, 0)
-        own, oth = _tokens(x_own_ref, x_oth_ref, k)
-        for rows in CHUNKS:
-            x = jnp.concatenate([own[:, rows], oth[:, rows]], axis=0)
-            genc_ref[0, rows] = lax.dot_general(
-                x, pre_ref[k], (((0,), (0,)), ((), ())), preferred_element_type=F32
-            ).astype(BF)
+    for late in range(2):
+
+        @pl.when(jnp.logical_and(p >= PAIRS, lax.rem(jnp.maximum(p - PAIRS, 0), 2) == late))
+        def _(late=late):
+            k = jnp.maximum(p - PAIRS, 0) // 2
+            own, oth = _tokens(x_own_ref, x_oth_ref, k)
+            for at in range(0, D // 2, W):
+                rows = slice(late * (D // 2) + at, late * (D // 2) + at + W)
+                x = jnp.concatenate([own[:, rows], oth[:, rows]], axis=0)
+                genc_ref[0, at : at + W] = lax.dot_general(
+                    x, pre_ref[k], (((0,), (0,)), ((), ())), preferred_element_type=F32
+                ).astype(BF)
 
 
 def _backward(turned, slope, own, oth, x_own, x_oth, decoder, pieces):
     return pl.pallas_call(
         _backward_kernel,
-        grid=(PAIRS + 2,),
+        grid=(PAIRS + 4,),
         in_specs=[WHOLE] * 11,
         out_specs=[
             pl.BlockSpec((1, W, D), lambda p: (jnp.minimum(p, PAIRS - 1), 0, 0)),
-            pl.BlockSpec((1, D, W), lambda p: (jnp.maximum(p - PAIRS, 0), 0, 0)),
+            pl.BlockSpec(
+                (1, D // 2, W),
+                lambda p: (jnp.maximum(p - PAIRS, 0) // 2, lax.rem(jnp.maximum(p - PAIRS, 0), 2), 0),
+            ),
             pl.BlockSpec((2, W), lambda p: (0, 0)),
             pl.BlockSpec((4, 2, D), lambda p: (0, 0, 0)),
         ],

time: 142 us -> 142 us (level)
  no operation moved by 1% of the time
where the time goes in v11:
time: 142 us
  starting transfers between devices  45.7 us (32%)
  waiting for transfers between devices  38.5 us (27%)
  blocking collectives  33.7 us (24%)
  Pallas kernels  23.6 us (17%)
    ppermute x5, starting transfers between devices, _gather_ring(): others = [lax.ppermute(piece, 'core', SWAP) for piece in pieces]  20.2 us
    all_to_all x1, blocking collectives, per_device(): lax.all_to_all(errors, ALL, 0, 0, axis_index_groups=GROUPS)  17.7 us
    all_to_all x1, blocking collectives, per_device(): lax.all_to_all(quarter.reshape(16, 8, D), ALL, 0, 0, axis_index_groups=GR...  15.9 us
    pallas_call x1, Pallas kernels, _backward(): pl.pallas_call(_backward_kernel, grid=(PAIRS + 4,), in_specs=[WHOLE] * 11...  10.3 us
    ppermute x1, waiting for transfers between devices, _reduce_ring(): from3 = lax.ppermute(to3, ALL, RING[3])  7.57 us
    ppermute x6, starting transfers between devices, _around_y(): lax.ppermute(pieces[j], 'y', [(i, (i + j) % 4) for i in range(4)])  7.02 us
    pallas_call x1, Pallas kernels, _stage(): pl.pallas_call(_stage_kernel, in_specs=[pl.BlockSpec(memory_space=HBM)] *...  4.74 us
    ppermute x1, waiting for transfers between devices, _gather_ring(): far3 = lax.ppermute(pass1, ALL, RING[1])  4.48 us
  transfers between devices with their start and end apart: 29, of which 13 were waited for; matrix products, arithmetic and copies ran while one was open for 0% of the time, Pallas kernels for 6%

profile of v11, /device:TPU:1, one launch (start us, length us, event | category | flops | bytes accessed | tf_op | source)
XLA Modules:
  0.0 142.3 jit_solution(10591384917239154587)
XLA Ops:
  0.6 1.0 prepare.1
  1.7 2.2 %collective-permute-start.2 = (bf16[2,16,3584]{2,1,0:T(8,128)(2,1)S(1)}, bf16[2,16,3584]{2,1,0:T(8,128)(2,1)S(1)}, u32[]{:S(2)}, u32[]{:S(2)}) collective-permute-start(bf16[2,16,3584]{2,1,0:T(8,128)(2,1)S(1)} %get-tuple-element.64.refs_0_), channel_id=1, source_target_pairs={{0,3},{1,2},{2,1},{3,0},{4,7},{5,6},{6,5},{7,4},{8,9},{9,8},{10,11... | collective-permute-start | bytes 688136 | tf_op jit(solution)/shard_map/ppermute | solution.py:147
  3.9 1.9 %collective-permute-start.1 = (bf16[2,16,3584]{2,1,0:T(8,128)(2,1)S(1)}, bf16[2,16,3584]{2,1,0:T(8,128)(2,1)S(1)}, u32[]{:S(2)}, u32[]{:S(2)}) collective-permute-start(bf16[2,16,3584]{2,1,0:T(8,128)(2,1)S(1)} %get-tuple-element.64.refs_0_), channel_id=1, source_target_pairs={{0,1},{1,0},{2,3},{3,2},{4,5},{5,4},{6,7},{7,6},{8,11},{9,10},{10,... | collective-permute-start | bytes 688136 | tf_op jit(solution)/shard_map/ppermute | solution.py:147
  5.8 3.8 %collective-permute-start = (bf16[2,16,3584]{2,1,0:T(8,128)(2,1)S(1)}, bf16[2,16,3584]{2,1,0:T(8,128)(2,1)S(1)}, u32[]{:S(2)}, u32[]{:S(2)}) collective-permute-start(bf16[2,16,3584]{2,1,0:T(8,128)(2,1)S(1)} %get-tuple-element.64.refs_0_), channel_id=1, source_target_pairs={{0,20},{1,21},{2,22},{3,23},{4,16},{5,17},{6,18},{7,19},{8,28},{9,... | collective-permute-start | bytes 688136 | tf_op jit(solution)/shard_map/ppermute | solution.py:146
  9.5 4.7 %stage.1 = (bf16[2,3584,256]{2,1,0:T(8,128)(2,1)S(1)}, bf16[5,256,3584]{2,1,0:T(8,128)(2,1)S(1)}) custom-call(bf16[2,3584,256]{2,1,0:T(8,128)(2,1)} %enc_hbm, bf16[5,256,3584]{2,1,0:T(8,128)(2,1)} %dec_hbm), custom_call_target="tpu_custom_call" | custom-call | bytes 25690112 | tf_op jit(solution)/shard_map/stage/pallas_call | solution.py:214
  14.3 0.6 collective-permute-done.refs_4_
  14.9 0.8 collective-permute-start.4
  15.8 0.8 collective-permute-start.3
  16.6 3.2 %collective-permute-done.5.refs_6_ = bf16[2,16,3584]{2,1,0:T(8,128)(2,1)S(1)} collective-permute-done((bf16[2,16,3584]{2,1,0:T(8,128)(2,1)S(1)}, bf16[2,16,3584]{2,1,0:T(8,128)(2,1)S(1)}, u32[]{:S(2)}, u32[]{:S(2)}) %collective-permute-start.5) | collective-permute-done | bytes 229408 | tf_op jit(solution)/shard_map/ppermute | solution.py:149
  19.8 0.8 collective-permute-start.6
  20.6 4.1 %collective-permute-done.3.refs_3_ = bf16[2,16,3584]{2,1,0:T(8,128)(2,1)S(1)} collective-permute-done((bf16[2,16,3584]{2,1,0:T(8,128)(2,1)S(1)}, bf16[2,16,3584]{2,1,0:T(8,128)(2,1)S(1)}, u32[]{:S(2)}, u32[]{:S(2)}) %collective-permute-start.3) | collective-permute-done | bytes 229408 | tf_op jit(solution)/shard_map/ppermute | solution.py:150
  24.7 4.0 %collective-permute-done.6.refs_7_ = bf16[2,16,3584]{2,1,0:T(8,128)(2,1)S(1)} collective-permute-done((bf16[2,16,3584]{2,1,0:T(8,128)(2,1)S(1)}, bf16[2,16,3584]{2,1,0:T(8,128)(2,1)S(1)}, u32[]{:S(2)}, u32[]{:S(2)}) %collective-permute-start.6) | collective-permute-done | bytes 229408 | tf_op jit(solution)/shard_map/ppermute | solution.py:151
  28.8 1.7 %collective-permute-start.7 = (bf16[8,2,16,3584]{3,2,1,0:T(8,128)(2,1)S(1)}, bf16[8,2,16,3584]{3,2,1,0:T(8,128)(2,1)S(1)}, u32[]{:S(2)}, u32[]{:S(2)}) collective-permute-start(bf16[8,2,16,3584]{3,2,1,0:T(8,128)(2,1)S(1)} %arrange.1.own_ref.x_own_ref), channel_id=1, source_target_pairs={{0,8},{8,0},{1,9},{9,1},{2,10},{10,2},{3,11},{11,3},{4,12},{12,4},... | collective-permute-start | bytes 5505032 | tf_op jit(solution)/shard_map/ppermute | solution.py:526
  30.5 3.4 %collective-permute-done.7.oth_ref.x_oth_ref = bf16[8,2,16,3584]{3,2,1,0:T(8,128)(2,1)S(1)} collective-permute-done((bf16[8,2,16,3584]{3,2,1,0:T(8,128)(2,1)S(1)}, bf16[8,2,16,3584]{3,2,1,0:T(8,128)(2,1)S(1)}, u32[]{:S(2)}, u32[]{:S(2)}) %collective-permute-start.7) | collective-permute-done | bytes 1835040 | tf_op jit(solution)/shard_map/ppermute | solution.py:526
  33.9 2.5 %forward.1 = (bf16[2,128,3584]{2,1,0:T(8,128)(2,1)S(1)}, bf16[2,128,3584]{2,1,0:T(8,128)(2,1)S(1)}, bf16[2,256,256]{2,1,0:T(8,128)(2,1)S(1)}, bf16[2,256,256]{2,1,0:T(8,128)(2,1)S(1)}, f32[2,256,256]{2,1,0:T(8,128)S(1)}) custom-call(bf16[8,2,16,3584]{3,2,1,0:T(8,128)(2,1)S(1)} %arrange.1.own_ref.x_own_ref, ...), custom_call_target="tpu_custom_call" | custom-call | flops 1879048192 | bytes 3670016 | tf_op jit(solution)/shard_map/forward/pallas_call | solution.py:264
  36.5 0.5 collective-permute-start.8
  36.9 1.8 %forward_high.1 = (bf16[2,128,3584]{2,1,0:T(8,128)(2,1)S(1)}, bf16[2,128,3584]{2,1,0:T(8,128)(2,1)S(1)}) custom-call(bf16[2,256,256]{2,1,0:T(8,128)(2,1)S(1)} %get-tuple-element.78.codes_ref, bf16[5,256,3584]{2,1,0:T(8,128)(2,1)S(1)} %get-tuple-element.74.dec_ref), custom_call_target="tpu_custom_call" | custom-call | flops 1409286144 | bytes 3670016 | tf_op jit(solution)/shard_map/forward_high/pallas_call | solution.py:289
  38.9 1.4 collective-permute-done.8.got_low_ref
  40.4 2.6 %collective-permute-done.9.got_ref = bf16[2,128,3584]{2,1,0:T(8,128)(2,1)S(1)} collective-permute-done((bf16[2,128,3584]{2,1,0:T(8,128)(2,1)S(1)}, bf16[2,128,3584]{2,1,0:T(8,128)(2,1)S(1)}, u32[]{:S(2)}, u32[]{:S(2)}) %collective-permute-start.9) | collective-permute-done | bytes 1835040 | tf_op jit(solution)/shard_map/ppermute | solution.py:531
  43.0 0.3 join_far.1
  43.2 1.3 collective-permute-start.12
  44.5 1.4 collective-permute-start.10
  45.9 0.9 join.1
  46.9 4.1 %collective-permute-done.12.got_ref = bf16[64,3584]{1,0:T(8,128)(2,1)S(1)} collective-permute-done((bf16[64,3584]{1,0:T(8,128)(2,1)S(1)}, bf16[64,3584]{1,0:T(8,128)(2,1)S(1)}, u32[]{:S(2)}, u32[]{:S(2)}) %collective-permute-start.12) | collective-permute-done | bytes 458784 | tf_op jit(solution)/shard_map/ppermute | solution.py:349
  50.9 0.4 fold_low.1
  51.3 2.1 %collective-permute-start.13 = (bf16[128,3584]{1,0:T(8,128)(2,1)S(1)}, bf16[128,3584]{1,0:T(8,128)(2,1)S(1)}, u32[]{:S(2)}, u32[]{:S(2)}) collective-permute-start(bf16[128,3584]{1,0:T(8,128)(2,1)S(1)} %fold_low.1), channel_id=1, source_target_pairs={{0,3},{1,2},{2,1},{3,0},{4,7},{5,6},{6,5},{7,4},{8,104},{9,105},{1... | collective-permute-start | bytes 2752520 | tf_op jit(solution)/shard_map/ppermute | solution.py:352
  53.4 0.4 fold_high.1
  53.9 1.2 collective-permute-start.14
  55.1 0.8 collective-permute-start.15
  55.9 1.7 %collective-permute-start.16 = (bf16[2,3584]{1,0:T(2,128)(2,1)S(1)}, bf16[2,3584]{1,0:T(2,128)(2,1)S(1)}, u32[]{:S(2)}, u32[]{:S(2)}) collective-permute-start(bf16[2,3584]{1,0:T(2,128)(2,1)S(1)} %get-tuple-element.90), channel_id=1, source_target_pairs={{0,3},{1,0},{2,1},{3,2},{4,7},{5,4},{6,5},{7,6},{8,11},{9,8},{10,9... | collective-permute-start | bytes 43016 | tf_op jit(solution)/shard_map/ppermute | solution.py:517
  57.6 7.6 %collective-permute-done.13.three_ref = bf16[128,3584]{1,0:T(8,128)(2,1)S(1)} collective-permute-done((bf16[128,3584]{1,0:T(8,128)(2,1)S(1)}, bf16[128,3584]{1,0:T(8,128)(2,1)S(1)}, u32[]{:S(2)}, u32[]{:S(2)}) %collective-permute-start.13) | collective-permute-done | bytes 917536 | tf_op jit(solution)/shard_map/ppermute | solution.py:352
  65.1 1.3 collective-permute-done.11.one_ref
  66.4 0.3 total.1
  66.7 15.9 %all_to_all.10.pieces_ref = bf16[16,8,3584]{2,1,0:T(8,128)(2,1)S(1)} all-to-all(bf16[16,8,3584]{2,1,0:T(8,128)(2,1)S(1)} %bitcast.6), channel_id=1, replica_groups={{0,4,16,20,32,36,48,52,64,68,80,84,96,100,112,116},{1,5,17,21,33,37,49,..., dimensions={0} | all-to-all | bytes 1835008 | tf_op jit(solution)/shard_map/all_to_all | solution.py:534
  82.6 0.3 settle.1
  83.0 17.7 %all_to_all.11 = bf16[16,8,3584]{2,1,0:T(8,128)(2,1)S(1)} all-to-all(bf16[16,8,3584]{2,1,0:T(8,128)(2,1)S(1)} %get-tuple-element.96), channel_id=1, replica_groups={{0,4,16,20,32,36,48,52,64,68,80,84,96,100,112,116},{1,5,17,21,33,37,49,..., dimensions={0} | all-to-all | bytes 1835008 | tf_op jit(solution)/shard_map/all_to_all | solution.py:536
  100.7 2.1 %collective-permute-start.20 = (bf16[2,3584]{1,0:T(2,128)(2,1)S(1)}, bf16[2,3584]{1,0:T(2,128)(2,1)S(1)}, u32[]{:S(2)}, u32[]{:S(2)}) collective-permute-start(bf16[2,3584]{1,0:T(2,128)(2,1)S(1)} %get-tuple-element.104), channel_id=1, source_target_pairs={{0,2},{1,3},{2,0},{3,1},{4,6},{5,7},{6,4},{7,5},{8,10},{9,11},{10,... | collective-permute-start | bytes 43016 | tf_op jit(solution)/shard_map/ppermute | solution.py:517
  102.8 1.2 collective-permute-start.21
  104.1 0.4 collective-permute-done.19.rest_1_
  104.5 14.2 %collective-permute-start.24 = (bf16[128,3584]{1,0:T(8,128)(2,1)S(1)}, bf16[128,3584]{1,0:T(8,128)(2,1)S(1)}, u32[]{:S(2)}, u32[]{:S(2)}) collective-permute-start(bf16[128,3584]{1,0:T(8,128)(2,1)S(1)} %bitcast.4), channel_id=1, source_target_pairs={{0,8},{8,0},{1,9},{9,1},{2,10},{10,2},{3,11},{11,3},{4,12},{12,4},... | collective-permute-start | bytes 2752520 | tf_op jit(solution)/shard_map/ppermute | solution.py:386
  118.9 0.9 collective-permute-start.22
  119.8 2.2 %collective-permute-start.25 = (bf16[128,3584]{1,0:T(8,128)(2,1)S(1)}, bf16[128,3584]{1,0:T(8,128)(2,1)S(1)}, u32[]{:S(2)}, u32[]{:S(2)}) collective-permute-start(bf16[128,3584]{1,0:T(8,128)(2,1)S(1)} %collective-permute-done.17.quarter_ref.one_ref), channel_id=1, source_target_pairs={{0,8},{8,0},{1,9},{9,1},{2,10},{10,2},{3,11},{11,3},{4,12},{12,4},... | collective-permute-start | bytes 2752520 | tf_op jit(solution)/shard_map/ppermute | solution.py:386
  122.0 4.5 %collective-permute-done.23.far3_ref = bf16[64,3584]{1,0:T(8,128)(2,1)S(1)} collective-permute-done((bf16[64,3584]{1,0:T(8,128)(2,1)S(1)}, bf16[64,3584]{1,0:T(8,128)(2,1)S(1)}, u32[]{:S(2)}, u32[]{:S(2)}) %collective-permute-start.23) | collective-permute-done | bytes 458784 | tf_op jit(solution)/shard_map/ppermute | solution.py:384
  126.4 2.5 %collective-permute-start.28 = (bf16[64,3584]{1,0:T(8,128)(2,1)S(1)}, bf16[64,3584]{1,0:T(8,128)(2,1)S(1)}, u32[]{:S(2)}, u32[]{:S(2)}) collective-permute-start(bf16[64,3584]{1,0:T(8,128)(2,1)S(1)} %collective-permute-done.23.far3_ref), channel_id=1, source_target_pairs={{0,8},{8,0},{1,9},{9,1},{2,10},{10,2},{3,11},{11,3},{4,12},{12,4},... | collective-permute-start | bytes 1376264 | tf_op jit(solution)/shard_map/ppermute | solution.py:386
  128.9 1.3 collective-permute-start.27
  130.5 1.2 collective-permute-done.27.far1_ref
  131.7 0.3 assemble_oth.1.oth_ref
  131.9 10.3 %backward.1 = (bf16[5,256,3584]{2,1,0:T(8,128)(2,1)}, bf16[2,3584,256]{2,1,0:T(8,128)(2,1)}, f32[2,256]{1,0:T(2,128)}, bf16[4,2,3584]{2,1,0:T(2,128)(2,1)}) custom-call(bf16[2,256,256]{2,1,0:T(8,128)(2,1)S(1)} %get-tuple-element.75.turned_ref, f32[2,256,256]{2,1,0:T(8,128)S(1)} %get-tuple-element.76.slope_ref, ...), custom_call_target="tpu_custom_call" | custom-call | flops 5637144576 | bytes 12845056 | tf_op jit(solution)/shard_map/backward/pallas_call | solution.py:485
  (32 shorter events, 0.9 us)
Async XLA Ops:
  1.7 12.6 %collective-permute-start.2 = (bf16[2,16,3584]{2,1,0:T(8,128)(2,1)S(1)}, bf16[2,16,3584]{2,1,0:T(8,128)(2,1)S(1)}, u32[]{:S(2)}, u32[]{:S(2)}) collective-permute-start(bf16[2,16,3584]{2,1,0:T(8,128)(2,1)S(1)} %get-tuple-element.64.refs_0_), channel_id=1, source_target_pairs={{0,3},{1,2},{2,1},{3,0},{4,7},{5,6},{6,5},{7,4},{8,9},{9,8},{10,11... | collective-permute-start | bytes 688136 | tf_op jit(solution)/shard_map/ppermute | solution.py:147
  3.9 10.4 %collective-permute-start.1 = (bf16[2,16,3584]{2,1,0:T(8,128)(2,1)S(1)}, bf16[2,16,3584]{2,1,0:T(8,128)(2,1)S(1)}, u32[]{:S(2)}, u32[]{:S(2)}) collective-permute-start(bf16[2,16,3584]{2,1,0:T(8,128)(2,1)S(1)} %get-tuple-element.64.refs_0_), channel_id=1, source_target_pairs={{0,1},{1,0},{2,3},{3,2},{4,5},{5,4},{6,7},{7,6},{8,11},{9,10},{10,... | collective-permute-start | bytes 688136 | tf_op jit(solution)/shard_map/ppermute | solution.py:147
  5.8 9.1 %collective-permute-start = (bf16[2,16,3584]{2,1,0:T(8,128)(2,1)S(1)}, bf16[2,16,3584]{2,1,0:T(8,128)(2,1)S(1)}, u32[]{:S(2)}, u32[]{:S(2)}) collective-permute-start(bf16[2,16,3584]{2,1,0:T(8,128)(2,1)S(1)} %get-tuple-element.64.refs_0_), channel_id=1, source_target_pairs={{0,20},{1,21},{2,22},{3,23},{4,16},{5,17},{6,18},{7,19},{8,28},{9,... | collective-permute-start | bytes 688136 | tf_op jit(solution)/shard_map/ppermute | solution.py:146
  14.9 19.0 %copy-start = (s32[4,8,32]{2,1,0:T(8,128)S(1)}, s32[4,8,32]{2,1,0:T(8,128)}, u32[]{:S(2)}) copy-start(s32[4,8,32]{2,1,0:T(8,128)} %active_ref.1) | copy-start | bytes 12292
  14.9 19.0 %copy-start.1 = (f32[2,256]{1,0:T(2,128)S(1)}, f32[2,256]{1,0:T(2,128)}, u32[]{:S(2)}) copy-start(f32[2,256]{1,0:T(2,128)} %bias_ref.1) | copy-start | bytes 6148
  14.9 4.9 %collective-permute-start.5 = (bf16[2,16,3584]{2,1,0:T(8,128)(2,1)S(1)}, bf16[2,16,3584]{2,1,0:T(8,128)(2,1)S(1)}, u32[]{:S(2)}, u32[]{:S(2)}) collective-permute-start(bf16[2,16,3584]{2,1,0:T(8,128)(2,1)S(1)} %collective-permute-done.refs_4_), channel_id=1, source_target_pairs={{0,3},{1,2},{2,1},{3,0},{4,7},{5,6},{6,5},{7,4},{8,9},{9,8},{10,11... | collective-permute-start | bytes 688136 | tf_op jit(solution)/shard_map/ppermute | solution.py:149
  14.9 9.8 %collective-permute-start.4 = (bf16[2,16,3584]{2,1,0:T(8,128)(2,1)S(1)}, bf16[2,16,3584]{2,1,0:T(8,128)(2,1)S(1)}, u32[]{:S(2)}, u32[]{:S(2)}) collective-permute-start(bf16[2,16,3584]{2,1,0:T(8,128)(2,1)S(1)} %collective-permute-done.refs_4_), channel_id=1, source_target_pairs={{0,1},{1,0},{2,3},{3,2},{4,5},{5,4},{6,7},{7,6},{8,11},{9,10},{10,... | collective-permute-start | bytes 688136 | tf_op jit(solution)/shard_map/ppermute | solution.py:149
  15.8 8.9 %collective-permute-start.3 = (bf16[2,16,3584]{2,1,0:T(8,128)(2,1)S(1)}, bf16[2,16,3584]{2,1,0:T(8,128)(2,1)S(1)}, u32[]{:S(2)}, u32[]{:S(2)}) collective-permute-start(bf16[2,16,3584]{2,1,0:T(8,128)(2,1)S(1)} %collective-permute-done.1.refs_1_), channel_id=1, source_target_pairs={{0,3},{1,2},{2,1},{3,0},{4,7},{5,6},{6,5},{7,4},{8,9},{9,8},{10,11... | collective-permute-start | bytes 688136 | tf_op jit(solution)/shard_map/ppermute | solution.py:150
  19.8 8.9 %collective-permute-start.6 = (bf16[2,16,3584]{2,1,0:T(8,128)(2,1)S(1)}, bf16[2,16,3584]{2,1,0:T(8,128)(2,1)S(1)}, u32[]{:S(2)}, u32[]{:S(2)}) collective-permute-start(bf16[2,16,3584]{2,1,0:T(8,128)(2,1)S(1)} %collective-permute-done.5.refs_6_), channel_id=1, source_target_pairs={{0,1},{1,0},{2,3},{3,2},{4,5},{5,4},{6,7},{7,6},{8,11},{9,10},{10,... | collective-permute-start | bytes 688136 | tf_op jit(solution)/shard_map/ppermute | solution.py:151
  28.8 5.1 %collective-permute-start.7 = (bf16[8,2,16,3584]{3,2,1,0:T(8,128)(2,1)S(1)}, bf16[8,2,16,3584]{3,2,1,0:T(8,128)(2,1)S(1)}, u32[]{:S(2)}, u32[]{:S(2)}) collective-permute-start(bf16[8,2,16,3584]{3,2,1,0:T(8,128)(2,1)S(1)} %arrange.1.own_ref.x_own_ref), channel_id=1, source_target_pairs={{0,8},{8,0},{1,9},{9,1},{2,10},{10,2},{3,11},{11,3},{4,12},{12,4},... | collective-permute-start | bytes 5505032 | tf_op jit(solution)/shard_map/ppermute | solution.py:526
  36.5 3.9 %collective-permute-start.8 = (bf16[2,128,3584]{2,1,0:T(8,128)(2,1)S(1)}, bf16[2,128,3584]{2,1,0:T(8,128)(2,1)S(1)}, u32[]{:S(2)}, u32[]{:S(2)}) collective-permute-start(bf16[2,128,3584]{2,1,0:T(8,128)(2,1)S(1)} %get-tuple-element.80), channel_id=1, source_target_pairs={{0,8},{8,0},{1,9},{9,1},{2,10},{10,2},{3,11},{11,3},{4,12},{12,4},... | collective-permute-start | bytes 5505032 | tf_op jit(solution)/shard_map/ppermute | solution.py:529
  38.7 4.3 %collective-permute-start.9 = (bf16[2,128,3584]{2,1,0:T(8,128)(2,1)S(1)}, bf16[2,128,3584]{2,1,0:T(8,128)(2,1)S(1)}, u32[]{:S(2)}, u32[]{:S(2)}) collective-permute-start(bf16[2,128,3584]{2,1,0:T(8,128)(2,1)S(1)} %get-tuple-element.81), channel_id=1, source_target_pairs={{0,8},{8,0},{1,9},{9,1},{2,10},{10,2},{3,11},{11,3},{4,12},{12,4},... | collective-permute-start | bytes 5505032 | tf_op jit(solution)/shard_map/ppermute | solution.py:531
  43.2 7.7 %collective-permute-start.12 = (bf16[64,3584]{1,0:T(8,128)(2,1)S(1)}, bf16[64,3584]{1,0:T(8,128)(2,1)S(1)}, u32[]{:S(2)}, u32[]{:S(2)}) collective-permute-start(bf16[64,3584]{1,0:T(8,128)(2,1)S(1)} %get-tuple-element.86), channel_id=1, source_target_pairs={{0,1},{1,0},{2,3},{3,2},{4,5},{5,4},{6,7},{7,6},{8,40},{9,41},{10,... | collective-permute-start | bytes 1376264 | tf_op jit(solution)/shard_map/ppermute | solution.py:349
  44.5 8.9 %collective-permute-start.10 = (bf16[64,3584]{1,0:T(8,128)(2,1)S(1)}, bf16[64,3584]{1,0:T(8,128)(2,1)S(1)}, u32[]{:S(2)}, u32[]{:S(2)}) collective-permute-start(bf16[64,3584]{1,0:T(8,128)(2,1)S(1)} %get-tuple-element.84), channel_id=1, source_target_pairs={{0,3},{1,2},{2,1},{3,0},{4,7},{5,6},{6,5},{7,4},{8,104},{9,105},{1... | collective-permute-start | bytes 1376264 | tf_op jit(solution)/shard_map/ppermute | solution.py:350
  51.3 13.8 %collective-permute-start.13 = (bf16[128,3584]{1,0:T(8,128)(2,1)S(1)}, bf16[128,3584]{1,0:T(8,128)(2,1)S(1)}, u32[]{:S(2)}, u32[]{:S(2)}) collective-permute-start(bf16[128,3584]{1,0:T(8,128)(2,1)S(1)} %fold_low.1), channel_id=1, source_target_pairs={{0,3},{1,2},{2,1},{3,0},{4,7},{5,6},{6,5},{7,4},{8,104},{9,105},{1... | collective-permute-start | bytes 2752520 | tf_op jit(solution)/shard_map/ppermute | solution.py:352
  53.8 12.6 %collective-permute-start.11 = (bf16[128,3584]{1,0:T(8,128)(2,1)S(1)}, bf16[128,3584]{1,0:T(8,128)(2,1)S(1)}, u32[]{:S(2)}, u32[]{:S(2)}) collective-permute-start(bf16[128,3584]{1,0:T(8,128)(2,1)S(1)} %fold_high.1), channel_id=1, source_target_pairs={{0,1},{1,0},{2,3},{3,2},{4,5},{5,4},{6,7},{7,6},{8,40},{9,41},{10,... | collective-permute-start | bytes 2752520 | tf_op jit(solution)/shard_map/ppermute | solution.py:356
  53.9 12.8 %collective-permute-start.14 = (bf16[2,3584]{1,0:T(2,128)(2,1)S(1)}, bf16[2,3584]{1,0:T(2,128)(2,1)S(1)}, u32[]{:S(2)}, u32[]{:S(2)}) collective-permute-start(bf16[2,3584]{1,0:T(2,128)(2,1)S(1)} %get-tuple-element.88), channel_id=1, source_target_pairs={{0,1},{1,2},{2,3},{3,0},{4,5},{5,6},{6,7},{7,4},{8,9},{9,10},{10,1... | collective-permute-start | bytes 43016 | tf_op jit(solution)/shard_map/ppermute | solution.py:517
  55.1 11.6 %collective-permute-start.15 = (bf16[2,3584]{1,0:T(2,128)(2,1)S(1)}, bf16[2,3584]{1,0:T(2,128)(2,1)S(1)}, u32[]{:S(2)}, u32[]{:S(2)}) collective-permute-start(bf16[2,3584]{1,0:T(2,128)(2,1)S(1)} %get-tuple-element.89), channel_id=1, source_target_pairs={{0,2},{1,3},{2,0},{3,1},{4,6},{5,7},{6,4},{7,5},{8,10},{9,11},{10,... | collective-permute-start | bytes 43016 | tf_op jit(solution)/shard_map/ppermute | solution.py:517
  55.9 10.8 %collective-permute-start.16 = (bf16[2,3584]{1,0:T(2,128)(2,1)S(1)}, bf16[2,3584]{1,0:T(2,128)(2,1)S(1)}, u32[]{:S(2)}, u32[]{:S(2)}) collective-permute-start(bf16[2,3584]{1,0:T(2,128)(2,1)S(1)} %get-tuple-element.90), channel_id=1, source_target_pairs={{0,3},{1,0},{2,1},{3,2},{4,7},{5,4},{6,5},{7,6},{8,11},{9,8},{10,9... | collective-permute-start | bytes 43016 | tf_op jit(solution)/shard_map/ppermute | solution.py:517
  100.7 18.0 %collective-permute-start.18 = (bf16[128,3584]{1,0:T(8,128)(2,1)S(1)}, bf16[128,3584]{1,0:T(8,128)(2,1)S(1)}, u32[]{:S(2)}, u32[]{:S(2)}) collective-permute-start(bf16[128,3584]{1,0:T(8,128)(2,1)S(1)} %bitcast.2), channel_id=1, source_target_pairs={{0,3},{1,2},{2,1},{3,0},{4,7},{5,6},{6,5},{7,4},{8,104},{9,105},{1... | collective-permute-start | bytes 2752520 | tf_op jit(solution)/shard_map/ppermute | solution.py:379
  100.7 18.0 %collective-permute-start.17 = (bf16[128,3584]{1,0:T(8,128)(2,1)S(1)}, bf16[128,3584]{1,0:T(8,128)(2,1)S(1)}, u32[]{:S(2)}, u32[]{:S(2)}) collective-permute-start(bf16[128,3584]{1,0:T(8,128)(2,1)S(1)} %bitcast.3), channel_id=1, source_target_pairs={{0,1},{1,0},{2,3},{3,2},{4,5},{5,4},{6,7},{7,6},{8,40},{9,41},{10,... | collective-permute-start | bytes 2752520 | tf_op jit(solution)/shard_map/ppermute | solution.py:378
  100.7 3.8 %collective-permute-start.19 = (bf16[2,3584]{1,0:T(2,128)(2,1)S(1)}, bf16[2,3584]{1,0:T(2,128)(2,1)S(1)}, u32[]{:S(2)}, u32[]{:S(2)}) collective-permute-start(bf16[2,3584]{1,0:T(2,128)(2,1)S(1)} %get-tuple-element.103), channel_id=1, source_target_pairs={{0,1},{1,2},{2,3},{3,0},{4,5},{5,6},{6,7},{7,4},{8,9},{9,10},{10,1... | collective-permute-start | bytes 43016 | tf_op jit(solution)/shard_map/ppermute | solution.py:517
  100.7 17.9 %collective-permute-start.20 = (bf16[2,3584]{1,0:T(2,128)(2,1)S(1)}, bf16[2,3584]{1,0:T(2,128)(2,1)S(1)}, u32[]{:S(2)}, u32[]{:S(2)}) collective-permute-start(bf16[2,3584]{1,0:T(2,128)(2,1)S(1)} %get-tuple-element.104), channel_id=1, source_target_pairs={{0,2},{1,3},{2,0},{3,1},{4,6},{5,7},{6,4},{7,5},{8,10},{9,11},{10,... | collective-permute-start | bytes 43016 | tf_op jit(solution)/shard_map/ppermute | solution.py:517
  102.8 15.8 %collective-permute-start.21 = (bf16[2,3584]{1,0:T(2,128)(2,1)S(1)}, bf16[2,3584]{1,0:T(2,128)(2,1)S(1)}, u32[]{:S(2)}, u32[]{:S(2)}) collective-permute-start(bf16[2,3584]{1,0:T(2,128)(2,1)S(1)} %get-tuple-element.105), channel_id=1, source_target_pairs={{0,3},{1,0},{2,1},{3,2},{4,7},{5,4},{6,5},{7,6},{8,11},{9,8},{10,9... | collective-permute-start | bytes 43016 | tf_op jit(solution)/shard_map/ppermute | solution.py:517
  104.5 26.0 %collective-permute-start.24 = (bf16[128,3584]{1,0:T(8,128)(2,1)S(1)}, bf16[128,3584]{1,0:T(8,128)(2,1)S(1)}, u32[]{:S(2)}, u32[]{:S(2)}) collective-permute-start(bf16[128,3584]{1,0:T(8,128)(2,1)S(1)} %bitcast.4), channel_id=1, source_target_pairs={{0,8},{8,0},{1,9},{9,1},{2,10},{10,2},{3,11},{11,3},{4,12},{12,4},... | collective-permute-start | bytes 2752520 | tf_op jit(solution)/shard_map/ppermute | solution.py:386
  118.7 7.7 %collective-permute-start.23 = (bf16[64,3584]{1,0:T(8,128)(2,1)S(1)}, bf16[64,3584]{1,0:T(8,128)(2,1)S(1)}, u32[]{:S(2)}, u32[]{:S(2)}) collective-permute-start(bf16[64,3584]{1,0:T(8,128)(2,1)S(1)} %half_high.1), channel_id=1, source_target_pairs={{0,1},{1,0},{2,3},{3,2},{4,5},{5,4},{6,7},{7,6},{8,40},{9,41},{10,... | collective-permute-start | bytes 1376264 | tf_op jit(solution)/shard_map/ppermute | solution.py:384
  118.9 10.0 %collective-permute-start.22 = (bf16[64,3584]{1,0:T(8,128)(2,1)S(1)}, bf16[64,3584]{1,0:T(8,128)(2,1)S(1)}, u32[]{:S(2)}, u32[]{:S(2)}) collective-permute-start(bf16[64,3584]{1,0:T(8,128)(2,1)S(1)} %half_low.1), channel_id=1, source_target_pairs={{0,3},{1,2},{2,1},{3,0},{4,7},{5,6},{6,5},{7,4},{8,104},{9,105},{1... | collective-permute-start | bytes 1376264 | tf_op jit(solution)/shard_map/ppermute | solution.py:382
  119.8 11.9 %collective-permute-start.25 = (bf16[128,3584]{1,0:T(8,128)(2,1)S(1)}, bf16[128,3584]{1,0:T(8,128)(2,1)S(1)}, u32[]{:S(2)}, u32[]{:S(2)}) collective-permute-start(bf16[128,3584]{1,0:T(8,128)(2,1)S(1)} %collective-permute-done.17.quarter_ref.one_ref), channel_id=1, source_target_pairs={{0,8},{8,0},{1,9},{9,1},{2,10},{10,2},{3,11},{11,3},{4,12},{12,4},... | collective-permute-start | bytes 2752520 | tf_op jit(solution)/shard_map/ppermute | solution.py:386
  121.9 9.7 %collective-permute-start.26 = (bf16[128,3584]{1,0:T(8,128)(2,1)S(1)}, bf16[128,3584]{1,0:T(8,128)(2,1)S(1)}, u32[]{:S(2)}, u32[]{:S(2)}) collective-permute-start(bf16[128,3584]{1,0:T(8,128)(2,1)S(1)} %collective-permute-done.18.quarter_ref.three_ref), channel_id=1, source_target_pairs={{0,8},{8,0},{1,9},{9,1},{2,10},{10,2},{3,11},{11,3},{4,12},{12,4},... | collective-permute-start | bytes 2752520 | tf_op jit(solution)/shard_map/ppermute | solution.py:386
  126.4 4.1 %collective-permute-start.28 = (bf16[64,3584]{1,0:T(8,128)(2,1)S(1)}, bf16[64,3584]{1,0:T(8,128)(2,1)S(1)}, u32[]{:S(2)}, u32[]{:S(2)}) collective-permute-start(bf16[64,3584]{1,0:T(8,128)(2,1)S(1)} %collective-permute-done.23.far3_ref), channel_id=1, source_target_pairs={{0,8},{8,0},{1,9},{9,1},{2,10},{10,2},{3,11},{11,3},{4,12},{12,4},... | collective-permute-start | bytes 1376264 | tf_op jit(solution)/shard_map/ppermute | solution.py:386
  128.9 2.8 %collective-permute-start.27 = (bf16[64,3584]{1,0:T(8,128)(2,1)S(1)}, bf16[64,3584]{1,0:T(8,128)(2,1)S(1)}, u32[]{:S(2)}, u32[]{:S(2)}) collective-permute-start(bf16[64,3584]{1,0:T(8,128)(2,1)S(1)} %collective-permute-done.22.far1_ref), channel_id=1, source_target_pairs={{0,8},{8,0},{1,9},{9,1},{2,10},{10,2},{3,11},{11,3},{4,12},{12,4},... | collective-permute-start | bytes 1376264 | tf_op jit(solution)/shard_map/ppermute | solution.py:386
